TPU v7x, 32 devices: a whole 2x2x4 slice. The times are simulated.
32 devices in a mesh: dp: 8 (over z, x), gate: 4 (over y, core).
Axes of the slice: x: 2, y: 2, z: 4, core: 2. Of those that a mesh axis runs over, the one named last changes fastest.
Arguments:
- inputs: bfloat16 [8, 2048, 2048], P('dp'), may hold values from -6 to 6
- weight: bfloat16 [2048, 6144], P(None, 'gate'), may hold values from -0.125 to 0.125
- ln_gain: float32 [2048], replicated, may hold values from 0.5 to 1.5
- ln_bias: float32 [2048], replicated, may hold values from -3 to 3
- forget_peep: float32 [2048], P('gate'), may hold values from -1 to 1
- reset_peep: float32 [2048], P('gate'), may hold values from -1 to 1
- forget_bias: float32 [2048], P('gate'), may hold values from 0 to 8
- reset_bias: float32 [2048], P('gate'), may hold values from -1 to 1
- resets: int32 [8, 2048], P('dp'), may hold values from 0 to 1, as said below
- padding: int32 [8, 2048], P('dp'), may hold values from 0 to 1, as said below
- grad_out: bfloat16 [8, 2048, 2048], P('dp', None, 'gate'), may hold values from -6 to 6
Outputs:
- hidden_out: bfloat16 [8, 2048, 2048], P('dp', None, 'gate')
- grad_inputs: bfloat16 [8, 2048, 2048], P('dp', None, 'gate')
- grad_weight: float32 [2048, 6144], P(None, 'gate')
- grad_ln_gain: float32 [2048], P('gate')
- grad_ln_bias: float32 [2048], P('gate')
- grad_forget_peep: float32 [2048], P('gate')
- grad_reset_peep: float32 [2048], P('gate')
- grad_forget_bias: float32 [2048], P('gate')
- grad_reset_bias: float32 [2048], P('gate')
Inputs may be any that keep to these rules, and one draw needn't show every extreme that they name: `padding`: each row holds ones followed by zeros, with more than 1536 ones; row 0 is all ones. `resets`: position 0 of every row is 1; row 0 has no other ones.
All inputs are finite; a program needn't handle non-finite values.
Results may differ from a plain program's by a relative error of at most 0.0065.
Values may be sent and summed in bfloat16 or wider, within the bound.
No kernel may reach another device: no remote copies, remote signals or barrier semaphores. Data moves between devices by JAX's collectives and lax.ppermute only.
A program may use at most 192 MiB of HBM per device.

v0:
```python
import math

import jax
import jax.numpy as jnp
from jax import lax
from jax.sharding import PartitionSpec as P

epsilon = 1e-05


def combine(earlier, later):
    early_decay, early_drive = earlier
    late_decay, late_drive = later
    return (early_decay * late_decay, late_decay * early_drive + late_drive)


def chained(decays, drives, backward):
    rows, length, channels = decays.shape
    span = math.gcd(length, 16)
    count = length // span
    dec_blocks = decays.reshape(rows, count, span, channels).transpose(2, 0, 1, 3)
    drv_blocks = drives.reshape(rows, count, span, channels).transpose(2, 0, 1, 3)
    order = list(range(span))
    if backward:
        order = order[::-1]
    run_decay = jnp.ones((rows, count, channels), jnp.float32)
    run_drive = jnp.zeros((rows, count, channels), jnp.float32)
    part_decay = [None] * span
    part_drive = [None] * span
    for step in order:
        run_decay = dec_blocks[step] * run_decay
        run_drive = dec_blocks[step] * run_drive + drv_blocks[step]
        part_decay[step] = run_decay
        part_drive[step] = run_drive
    inclusive = lax.associative_scan(combine, (run_decay, run_drive), reverse=backward, axis=1)[1]
    edge = jnp.zeros((rows, 1, channels), jnp.float32)
    if backward:
        incoming = jnp.concatenate([inclusive[:, 1:], edge], axis=1)
    else:
        incoming = jnp.concatenate([edge, inclusive[:, :-1]], axis=1)
    states = jnp.stack(
        [part_drive[step] + part_decay[step] * incoming for step in range(span)], axis=0
    )
    return states.transpose(1, 2, 0, 3).reshape(rows, length, channels)


def contract(left, right, left_dim, right_dim):
    return lax.dot_general(
        left, right, (((left_dim,), (right_dim,)), ((), ())), preferred_element_type=jnp.float32
    )


def shards(
    inputs,
    weight,
    ln_gain,
    ln_bias,
    forget_peep,
    reset_peep,
    forget_bias,
    reset_bias,
    resets,
    padding,
    grad_out,
):
    rows, length, features = inputs.shape
    tokens = rows * length
    channels = forget_peep.shape[0]
    offset = lax.axis_index("gate") * channels
    flat_rows = inputs.astype(jnp.float32).reshape(tokens, features)
    row_mean = jnp.mean(flat_rows, axis=1, keepdims=True)
    centered = flat_rows - row_mean
    inv_std = lax.rsqrt(jnp.mean(centered * centered, axis=1, keepdims=True) + epsilon)
    unit_rows = centered * inv_std
    normed = (unit_rows * ln_gain + ln_bias).astype(jnp.bfloat16)
    local_cols = jnp.dot(normed, weight, preferred_element_type=jnp.float32).astype(jnp.bfloat16)
    mixed_cols = lax.all_to_all(local_cols, "gate", split_axis=1, concat_axis=1, tiled=True)
    utilde = mixed_cols[:, :channels].astype(jnp.float32).reshape(rows, length, channels)
    uforget = (
        mixed_cols[:, channels : 2 * channels].astype(jnp.float32).reshape(rows, length, channels)
    )
    ureset = mixed_cols[:, 2 * channels :].astype(jnp.float32).reshape(rows, length, channels)
    xslice = lax.dynamic_slice_in_dim(inputs, offset, channels, 2).astype(jnp.float32)
    forget = jax.nn.sigmoid(uforget + forget_peep * xslice + forget_bias)
    reset_gate = jax.nn.sigmoid(ureset + reset_peep * xslice + reset_bias)
    carry_keep = (1 - resets).astype(jnp.float32)[:, :, None]
    decays = forget * carry_keep
    drives = (1.0 - forget) * utilde
    memory = chained(decays, drives, False)
    live_mask = padding.astype(jnp.float32)[:, :, None]
    outputs = live_mask * (reset_gate * memory + (1.0 - reset_gate) * xslice)
    grad_live = grad_out.astype(jnp.float32) * live_mask
    dreset = grad_live * (memory - xslice) * reset_gate * (1.0 - reset_gate)
    dcell_local = grad_live * reset_gate
    edge_zeros = jnp.zeros((rows, 1, channels), jnp.float32)
    decay_next = jnp.concatenate([decays[:, 1:], edge_zeros], axis=1)
    dcells = chained(decay_next, dcell_local, True)
    previous = jnp.concatenate([edge_zeros, memory[:, :-1]], axis=1)
    dtilde = dcells * (1.0 - forget)
    dforget = dcells * (previous * carry_keep - utilde) * forget * (1.0 - forget)
    direct = grad_live * (1.0 - reset_gate) + dforget * forget_peep + dreset * reset_peep
    dstreams = (
        jnp.concatenate([dtilde, dforget, dreset], axis=2)
        .reshape(tokens, 3 * channels)
        .astype(jnp.bfloat16)
    )
    dlocal = lax.all_to_all(dstreams, "gate", split_axis=1, concat_axis=1, tiled=True)
    partial_in = contract(dlocal, weight, 1, 1)
    weight_grad = contract(normed, dlocal, 0, 0)
    dnormed = lax.psum_scatter(partial_in, "gate", scatter_dimension=1, tiled=True)
    unit_slice = lax.dynamic_slice_in_dim(unit_rows, offset, channels, 1)
    gain_slice = lax.dynamic_slice_in_dim(ln_gain, offset, channels, 0)
    grad_unit = dnormed * gain_slice
    first_total, second_total = lax.psum(
        (
            jnp.sum(grad_unit, axis=1, keepdims=True),
            jnp.sum(grad_unit * unit_slice, axis=1, keepdims=True),
        ),
        "gate",
    )
    dx_norm = inv_std * (grad_unit - first_total / features - unit_slice * second_total / features)
    dinputs = (
        (dx_norm + direct.reshape(tokens, channels))
        .astype(jnp.bfloat16)
        .reshape(rows, length, channels)
    )
    totals = lax.psum(
        (
            weight_grad,
            jnp.sum(dnormed * unit_slice, axis=0),
            jnp.sum(dnormed, axis=0),
            jnp.sum(dforget * xslice, axis=(0, 1)),
            jnp.sum(dreset * xslice, axis=(0, 1)),
            jnp.sum(dforget, axis=(0, 1)),
            jnp.sum(dreset, axis=(0, 1)),
        ),
        "dp",
    )
    return (
        outputs.astype(jnp.bfloat16),
        dinputs,
        totals[0],
        totals[1],
        totals[2],
        totals[3],
        totals[4],
        totals[5],
        totals[6],
    )


def solution(mesh):
    return jax.shard_map(
        shards,
        mesh=mesh,
        in_specs=(
            P("dp", None, None),
            P(None, "gate"),
            P(),
            P(),
            P("gate"),
            P("gate"),
            P("gate"),
            P("gate"),
            P("dp", None),
            P("dp", None),
            P("dp", None, "gate"),
        ),
        out_specs=(
            P("dp", None, "gate"),
            P("dp", None, "gate"),
            P(None, "gate"),
            P("gate"),
            P("gate"),
            P("gate"),
            P("gate"),
            P("gate"),
            P("gate"),
        ),
        check_vma=False,
    )
```

profile of v0, /device:TPU:0, one launch (start us, length us, event | category | flops | bytes accessed | tf_op | source)
XLA Modules:
  0.0 1001.1 jit_solution(17736742718394757281)
XLA Ops:
  8.0 4.7 convert_reduce_fusion
  16.6 18.4 %fusion.18 = bf16[2048,1536]{0,1:T(8,128)(2,1)} fusion(bf16[2048,1536]{1,0:T(8,128)(2,1)S(1)} %copy-done.59, f32[2048]{0:T(1024)S(1)} %copy-done.60, f32[2048]{0:T(1024)S(1)} %copy-done.57, bf16[1,2048,2048]{2,1,0:T(8,128)(2,1)} %param.11, f32[2048]{0:T(1024)S(1)} %add_rsqrt_fusion, f32[2048]{0:T(1024)S(1)} %broadcast_multiply_fusion.2), kind=kOutput, calls=%fused_computation.27 | convolution fusion | flops 12913213440 | bytes 21004288 | tf_op jit(solution)/shard_map/dot_general | solution.py:76
  35.0 5.4 all-to-all-start
  40.6 71.2 %all-to-all-done = bf16[2048,4,384]{0,2,1:T(8,128)(2,1)} async-done(((bf16[2048,4,384]{0,2,1:T(8,128)(2,1)}), bf16[2048,4,384]{0,2,1:T(8,128)(2,1)}, u32[]{:S(2)}, u32[]{:S(2)}) %all-to-all-start) | async-done | bytes 6291488 | tf_op jit(solution)/shard_map/all_to_all | solution.py:77
  111.8 5.8 fusion.153
  117.6 3.1 copy.28
  120.7 3.9 copy.29
  124.6 3.9 copy.30
  128.6 7.4 convert_multiply_fusion.5
  138.5 4.3 fusion.93
  142.8 15.9 %fusion.46 = (f32[1,128,512]{2,0,1:T(1,128)S(1)}, f32[1,128,512]{2,0,1:T(1,128)}, f32[1,128,512]{2,0,1:T(1,128)}, f32[1,128,512]{2,0,1:T(1,128)}, f32[1,128,512]...) fusion(f32[16,1,128,512]{3,0,2,1:T(8,128)} %bitcast.786, ...), kind=kLoop, calls=%fused_computation.66 | loop fusion | flops 2097152 | bytes 10485760 | tf_op jit(solution)/shard_map/add | solution.py:32
  164.5 16.6 %fusion.78 = (f32[1,128,512]{2,0,1:T(1,128)S(1)}, f32[1,128,512]{2,0,1:T(1,128)}, f32[1,128,512]{2,0,1:T(1,128)}, f32[1,128,512]{2,0,1:T(1,128)}, f32[1,128,512]...) fusion(f32[16,1,128,512]{3,0,2,1:T(8,128)} %bitcast.771), kind=kLoop, calls=%fused_computation.193 | loop fusion | flops 983040 | bytes 6029312 | tf_op jit(solution)/shard_map/mul | solution.py:31
  181.1 16.4 %fusion.62 = (f32[1,128,512]{2,0,1:T(1,128)S(1)}, f32[1,128,512]{2,0,1:T(1,128)}, f32[1,128,512]{2,0,1:T(1,128)}, f32[1,128,512]{2,0,1:T(1,128)}, f32[1,128,512]...) fusion(f32[16,1,128,512]{3,0,2,1:T(8,128)} %bitcast.782, ...), kind=kLoop, calls=%fused_computation.114 | loop fusion | flops 2097152 | bytes 10485760 | tf_op jit(solution)/shard_map/add | solution.py:32
  211.4 3.2 pad.94
  220.4 4.5 pad.97
  227.8 5.6 pad.99
  234.8 5.5 pad.98
  241.6 11.0 %pad.101 = f32[1,64,512]{2,0,1:T(1,128)S(1)} pad(f32[1,32,512]{2,0,1:T(1,128)} %add.1725, f32[]{:T(128)} %constant.10.clone.1), padding=0_0_0x1_0_1x0_0_0 | pad | bytes 196612 | tf_op jit(solution)/shard_map/pad | solution.py:35
  255.0 11.0 %pad.115 = f32[1,64,512]{2,0,1:T(1,128)S(1)} pad(f32[1,32,512]{2,0,1:T(1,128)} %add.1778, f32[]{:T(128)} %constant.10.clone.1), padding=0_0_0x1_0_1x0_0_0 | pad | bytes 196612 | tf_op jit(solution)/shard_map/pad | solution.py:35
  266.7 28.5 %pad.211 = f32[1,128,512]{2,0,1:T(1,128)} pad(f32[1,64,512]{2,0,1:T(1,128)} %add.1780, f32[]{:T(128)} %constant.10.clone.1), padding=0_0_0x1_0_1x0_0_0 | pad | bytes 393220
  297.2 21.9 %pad.149 = f32[1,127,512]{2,0,1:T(1,128)S(1)} pad(f32[1,64,512]{2,0,1:T(1,128)} %pad_maximum_fusion.2, f32[]{:T(128)} %constant.10.clone.1), padding=0_0_0x0_0_1x0_0_0 | pad | bytes 391172 | tf_op jit(solution)/shard_map/slice | solution.py:38
  322.1 19.8 %pad.210 = f32[1,128,512]{2,0,1:T(1,128)} pad(f32[1,64,512]{2,0,1:T(1,128)S(1)} %add.1727, f32[]{:T(128)} %constant.10.clone.1), padding=0_0_0x1_0_1x0_0_0 | pad | bytes 393220
  342.9 19.8 %pad.147 = f32[1,127,512]{2,0,1:T(1,128)} pad(f32[1,64,512]{2,0,1:T(1,128)S(1)} %pad_maximum_fusion.1, f32[]{:T(128)} %constant.10.clone.1), padding=0_0_0x0_0_1x0_0_0 | pad | bytes 391172 | tf_op jit(solution)/shard_map/slice | solution.py:40
  364.1 7.0 add_bitcast_fusion.17
  371.2 3.3 add_bitcast_fusion.16
  374.6 3.2 add_bitcast_fusion.18
  377.8 5.1 add_bitcast_fusion.19
  383.0 3.1 add_bitcast_fusion.4
  388.6 3.2 add_bitcast_fusion
  391.8 3.2 add_bitcast_fusion.10
  395.1 4.3 add_bitcast_fusion.21
  399.4 13.4 %stack.135 = f32[16,1,128,512]{3,0,2,1:T(8,128)} concatenate(f32[1,1,128,512]{3,0,2,1:T(1,128)} %get-tuple-element.134, f32[1,1,128,512]{3,0,2,1:T(1,128)} %get-tuple-element.68, f32[1,1,128,512]{3,0,2,1:T(1,128)} %get-tuple-element.83, f32[1,1,128,512]{3,0,2,1:T(1,128)} %get-tuple-element.65, f32[1,1,128,512]{3,0,2,1:T(1,128)} %get-tuple-element.93, ...), dimensions={0} | concatenate | bytes 8388608 | tf_op jit(solution)/shard_map/stack | solution.py:41
  412.9 12.9 %stack.118 = f32[16,1,128,512]{3,0,2,1:T(8,128)} concatenate(f32[1,1,128,512]{3,0,2,1:T(1,128)} %get-tuple-element.76, f32[1,1,128,512]{3,0,2,1:T(1,128)} %get-tuple-element.82, f32[1,1,128,512]{3,0,2,1:T(1,128)} %get-tuple-element.73, f32[1,1,128,512]{3,0,2,1:T(1,128)S(1)} %copy-done.34, f32[1,1,128,512]{3,0,2,1:T(1,128)S(1)} %copy-done.32, ...), dimensions={0} | concatenate | bytes 8388608 | tf_op jit(solution)/shard_map/stack | solution.py:41
  425.8 11.7 %fusion.41 = (f32[512]{0:T(512)S(1)}, f32[512]{0:T(512)S(1)}, f32[512]{0:T(512)S(1)}, f32[512]{0:T(512)S(1)}, f32[1,2048,512]{2,1,0:T(8,128)S(1)}, /*index=5*/f3...) fusion(bf16[1,2048,2048]{2,1,0:T(8,128)(2,1)} %param.11, s32[]{:T(128)S(6)} %select_n.2, ...), kind=kLoop, calls=%fused_computation.53 | loop fusion | flops 44038144 | bytes 35682308 | tf_op jit(solution)/shard_map/reduce_sum | solution.py:133
  443.8 11.4 %convert_element_type.48 = bf16[2048,4,384]{2,1,0:T(4,128)(2,1)} reshape(bf16[1,2048,1536]{2,1,0:T(8,128)(2,1)} %pad_maximum_fusion) | data formatting | bytes 12582912 | tf_op jit(solution)/shard_map/convert_element_type | solution.py:105
  455.1 3.6 copy.25
  458.7 74.4 %all_to_all.21 = bf16[2048,4,384]{2,0,1:T(8,128)(2,1)} all-to-all(bf16[2048,4,384]{2,0,1:T(8,128)(2,1)S(1)} %copy.25), channel_id=1, replica_groups=mesh['dp'=8,'gate'=4] {'gate'}, dimensions={1} | all-to-all | bytes 12582912 | tf_op jit(solution)/shard_map/all_to_all | solution.py:107
  533.2 8.7 copy.26
  541.8 20.5 %fusion.160 = f32[2048,2048]{1,0:T(8,128)} fusion(bf16[2048,1536]{0,1:T(8,128)(2,1)} %bitcast.791, bf16[2048,1536]{1,0:T(8,128)(2,1)} %param.12), kind=kOutput, calls=%fused_computation.308 | convolution fusion | flops 12884901888 | bytes 29360128 | tf_op jit(solution)/shard_map/dot_general | solution.py:48
  563.1 23.3 %fusion.10 = f32[2048,1536]{1,0:T(8,128)} fusion(bf16[2048,1536]{0,1:T(8,128)(2,1)} %bitcast.792, bf16[1,2048,2048]{2,1,0:T(8,128)(2,1)} %param.11, f32[2048]{0:T(1024)S(1)} %copy-done.61, f32[2048]{0:T(1024)S(1)} %copy-done.58, f32[2048]{0:T(1024)S(1)} %copy-done.41, f32[2048]{0:T(1024)S(1)} %copy-done.43), kind=kOutput, calls=%fused_computation.20 | convolution fusion | flops 12910067712 | bytes 27295744 | tf_op jit(solution)/shard_map/dot_general | solution.py:48
  586.5 12.6 %fusion.1 = f32[2048,2048]{1,0:T(8,128)} fusion(bf16[1,2048,2048]{2,1,0:T(8,128)(2,1)} %param.11, f32[2048]{0:T(1024)S(1)} %copy-done.41, f32[2048]{0:T(1024)S(1)} %copy-done.43), kind=kLoop, calls=%fused_computation.4 | loop fusion | flops 12582912 | bytes 25182208 | tf_op jit(solution)/shard_map/mul | solution.py:74
  599.1 89.5 %reduce-scatter.2.cloned.1.call-done = f32[2048,512]{1,0:T(8,128)} async-done(((f32[2048,2048]{1,0:T(8,128)}), f32[2048,512]{1,0:T(8,128)}) %reduce-scatter.2.cloned.1.call-update) | async-done | bytes 4194320 | tf_op jit(solution)/shard_map/reduce_scatter | solution.py:110
  688.6 5.1 multiply_reduce_fusion
  693.7 39.1 %all-reduce.32 = (f32[512]{0:T(512)}, f32[512]{0:T(512)}, f32[512]{0:T(512)}, f32[512]{0:T(512)}, f32[512]{0:T(512)}, /*index=5*/f32[512]{0:T(512)}) all-reduce(f32[512]{0:T(512)S(1)} %get-tuple-element.9, f32[512]{0:T(512)S(1)} %get-tuple-element.16, f32[512]{0:T(512)S(1)} %get-tuple-element.12, ...), channel_id=1, replica_groups=mesh['dp'=8,'gate'=4] {'dp'}, use_global_device_ids=true, to_apply=%region_9.0 | all-reduce | flops 3072 | bytes 24576 | tf_op jit(solution)/shard_map/psum | solution.py:127
  732.8 10.6 %all-reduce.33 = (f32[2048]{0:T(1024)S(1)}, f32[2048,1]{0,1:T(1,128)S(1)}) all-reduce(f32[2048]{0:T(1024)S(1)} %get-tuple-element.10, f32[2048,1]{0,1:T(1,128)S(1)} %bitcast.799), channel_id=1, replica_groups=mesh['dp'=8,'gate'=4] {'gate'}, use_global_device_ids=true, to_apply=%region_6.0 | all-reduce | flops 4096 | bytes 32768 | tf_op jit(solution)/shard_map/psum | solution.py:114
  743.3 10.2 %fusion.45 = bf16[1,2048,512]{2,1,0:T(8,128)(2,1)} fusion(f32[1,2048,512]{2,1,0:T(8,128)} %copy-done.7, f32[512]{0:T(512)S(1)} %copy-done.51, f32[1,2048,512]{2,1,0:T(8,128)} %copy-done.6, f32[512]{0:T(512)S(1)} %copy-done.47, f32[2048]{0:T(1024)S(1)} %bitcast.795, bf16[1,2048,512]{2,1,0:T(8,128)(2,1)} %param.21, f32[2048]{0:T(1024)S(1)} %get-tuple-element.23, ...), kind=kLoop, calls=%fused_computation.64 | loop fusion | flops 25165824 | bytes 25206788 | tf_op jit(solution)/shard_map/reshape | solution.py:125
  753.5 229.0 %all-reduce.36.cloned.1.call-done = f32[2048,1536]{1,0:T(8,128)} async-done(((f32[2048,1536]{1,0:T(8,128)}), f32[2048,1536]{1,0:T(8,128)}) %all-reduce.36.cloned.1.call-update) | async-done | bytes 12582928 | tf_op jit(solution)/shard_map/psum | solution.py:127
  982.6 10.6 %copy.32 = f32[2048,1536]{1,0:T(8,128)} copy(f32[2048,1536]{1,0:T(8,128)} %all-reduce.36.cloned.1.call-done) | data formatting | bytes 25165824
  (222 shorter events, 57.4 us)
Async XLA Ops:
  8.0 5.8 copy-start
  16.6 18.4 %copy-start.40 = (f32[2048]{0:T(1024)}, f32[2048]{0:T(1024)S(1)}, u32[]{:S(2)}) copy-start(f32[2048]{0:T(1024)S(1)} %add_rsqrt_fusion) | copy-start | bytes 24580
  35.0 76.8 %all-to-all-start = ((bf16[2048,4,384]{0,2,1:T(8,128)(2,1)}), bf16[2048,4,384]{0,2,1:T(8,128)(2,1)}, u32[]{:S(2)}, u32[]{:S(2)}) async-start(bf16[2048,4,384]{0,2,1:T(8,128)(2,1)} %bitcast.790), calls=%async_computation | async-start | bytes 12582912 | tf_op jit(solution)/shard_map/all_to_all | solution.py:77
  40.4 648.1 %reduce-scatter.2.cloned.1.call-start = ((), (), s32[]{:S(2)}) async-start(), calls=%async_computation.3 | async-start | bytes 20971520 | tf_op jit(solution)/shard_map/reduce_scatter | solution.py:110
  40.5 88.0 %copy-start.37 = (f32[1,2048]{1,0:T(1,128)}, f32[1,2048]{1,0:T(1,128)S(1)}, u32[]{:S(2)}) copy-start(f32[1,2048]{1,0:T(1,128)S(1)} %convert_element_type.40) | copy-start | bytes 24580
  40.6 88.0 %copy-start.44 = (f32[1,2048]{1,0:T(1,128)}, f32[1,2048]{1,0:T(1,128)S(1)}, u32[]{:S(2)}) copy-start(f32[1,2048]{1,0:T(1,128)S(1)} %subtract_convert_fusion) | copy-start | bytes 24580
  120.7 7.9 copy-start.46
  120.7 7.9 copy-start.48
  120.7 7.9 copy-start.50
  120.7 7.9 copy-start.55
  138.5 20.2 %copy-start.4 = (f32[1,2048,512]{2,1,0:T(8,128)}, f32[1,2048,512]{2,1,0:T(8,128)S(1)}, u32[]{:S(2)}) copy-start(f32[1,2048,512]{2,1,0:T(8,128)S(1)} %concatenate.59) | copy-start | bytes 12582916
  161.2 19.9 %copy-start.2 = (f32[1,2048,512]{2,1,0:T(8,128)S(1)}, f32[1,2048,512]{2,1,0:T(8,128)}, u32[]{:S(2)}) copy-start(f32[1,2048,512]{2,1,0:T(8,128)} %copy-done.1) | copy-start | bytes 12582916
  220.4 76.0 %copy-start.52 = (f32[1,1,512]{2,0,1:T(1,128)S(1)}, f32[1,1,512]{2,0,1:T(1,128)}, u32[]{:S(2)}) copy-start(f32[1,1,512]{2,0,1:T(1,128)} %slice.857) | copy-start | bytes 6148
  362.6 8.6 copy-start.19
  362.7 8.6 copy-start.20
  362.7 8.6 copy-start.21
  362.7 8.6 copy-start.22
  362.7 8.6 copy-start.23
  364.1 18.8 %copy-start.8 = (f32[1,2048,512]{2,1,0:T(8,128)S(1)}, f32[1,2048,512]{2,1,0:T(8,128)}, u32[]{:S(2)}) copy-start(f32[1,2048,512]{2,1,0:T(8,128)} %get-tuple-element.77) | copy-start | bytes 12582916
  371.2 6.6 copy-start.3
  371.2 6.6 copy-start.18
  374.5 8.4 copy-start.5
  374.5 8.4 copy-start.12
  374.5 8.4 copy-start.13
  374.5 8.4 copy-start.14
  374.5 8.4 copy-start.15
  374.6 8.4 copy-start.16
  374.6 8.4 copy-start.17
  377.8 8.4 copy-start.9
  377.8 8.4 copy-start.10
  382.9 5.7 copy-start.11
  382.9 5.7 copy-start.26
  382.9 5.7 copy-start.27
  386.2 5.7 copy-start.24
  388.6 6.5 copy-start.28
  388.6 6.5 copy-start.29
  399.4 13.4 %copy-start.30 = (f32[1,1,128,512]{3,0,2,1:T(1,128)S(1)}, f32[1,1,128,512]{3,0,2,1:T(1,128)}, u32[]{:S(2)}) copy-start(f32[1,1,128,512]{3,0,2,1:T(1,128)} %get-tuple-element.69) | copy-start | bytes 786436
  399.4 13.4 %copy-start.31 = (f32[1,1,128,512]{3,0,2,1:T(1,128)S(1)}, f32[1,1,128,512]{3,0,2,1:T(1,128)}, u32[]{:S(2)}) copy-start(f32[1,1,128,512]{3,0,2,1:T(1,128)} %get-tuple-element.70) | copy-start | bytes 786436
  399.4 13.4 %copy-start.32 = (f32[1,1,128,512]{3,0,2,1:T(1,128)S(1)}, f32[1,1,128,512]{3,0,2,1:T(1,128)}, u32[]{:S(2)}) copy-start(f32[1,1,128,512]{3,0,2,1:T(1,128)} %get-tuple-element.71) | copy-start | bytes 786436
  399.4 13.4 %copy-start.33 = (f32[1,1,128,512]{3,0,2,1:T(1,128)S(1)}, f32[1,1,128,512]{3,0,2,1:T(1,128)}, u32[]{:S(2)}) copy-start(f32[1,1,128,512]{3,0,2,1:T(1,128)} %get-tuple-element.96) | copy-start | bytes 786436
  399.4 13.4 %copy-start.34 = (f32[1,1,128,512]{3,0,2,1:T(1,128)S(1)}, f32[1,1,128,512]{3,0,2,1:T(1,128)}, u32[]{:S(2)}) copy-start(f32[1,1,128,512]{3,0,2,1:T(1,128)} %get-tuple-element.97) | copy-start | bytes 786436
  412.9 12.9 %copy-start.38 = (f32[1,2048]{1,0:T(1,128)S(1)}, f32[1,2048]{1,0:T(1,128)}, u32[]{:S(2)}) copy-start(f32[1,2048]{1,0:T(1,128)} %copy-done.37) | copy-start | bytes 24580
  412.9 12.9 %copy-start.45 = (f32[1,2048]{1,0:T(1,128)S(1)}, f32[1,2048]{1,0:T(1,128)}, u32[]{:S(2)}) copy-start(f32[1,2048]{1,0:T(1,128)} %copy-done.44) | copy-start | bytes 24580
  412.9 12.9 %copy-start.47 = (f32[512]{0:T(512)S(1)}, f32[512]{0:T(512)}, u32[]{:S(2)}) copy-start(f32[512]{0:T(512)} %param.15) | copy-start | bytes 6148
  412.9 12.9 %copy-start.49 = (f32[512]{0:T(512)S(1)}, f32[512]{0:T(512)}, u32[]{:S(2)}) copy-start(f32[512]{0:T(512)} %param.18) | copy-start | bytes 6148
  412.9 12.9 %copy-start.51 = (f32[512]{0:T(512)S(1)}, f32[512]{0:T(512)}, u32[]{:S(2)}) copy-start(f32[512]{0:T(512)} %param.16) | copy-start | bytes 6148
  412.9 12.9 %copy-start.56 = (f32[512]{0:T(512)S(1)}, f32[512]{0:T(512)}, u32[]{:S(2)}) copy-start(f32[512]{0:T(512)} %param.17) | copy-start | bytes 6148
  562.4 420.1 %all-reduce.36.cloned.1.call-start = ((), (), s32[]{:S(2)}) async-start(), calls=%async_computation.4 | async-start | bytes 25165824 | tf_op jit(solution)/shard_map/psum | solution.py:127
  (17 other events, 39.1 us)
Sparse Core Ops, SparseCore 0:
  562.6 125.9 reduce-scatter.1
Sparse Core Ops, SparseCore 1:
  586.5 396.0 all-reduce.35
where the time goes:
time: 1020 us; the launch traced here: 1000 us
  waiting for transfers between devices  390 us (38%)
  local copies, waits for them, and re-layouts  232 us (23%)
  other arithmetic  170 us (17%)
  blocking collectives  124 us (12%)
  matrix products  62.2 us (6%)
  between operations  17 us (2%)
    psum x1, waiting for transfers between devices, shards(): lax.psum((weight_grad, jnp.sum(dnormed * unit_slice, axis=0), jnp.sum(dno...  229 us
    reduce_scatter x1, waiting for transfers between devices, shards(): lax.psum_scatter(partial_in, 'gate', scatter_dimension=1, tiled=True)  89.5 us
    unnamed x130, local copies, waits for them, and re-layouts  77.5 us
    all_to_all x1, blocking collectives, shards(): lax.all_to_all(dstreams, 'gate', split_axis=1, concat_axis=1, tiled=True)  74.4 us
    all_to_all x1, waiting for transfers between devices, shards(): lax.all_to_all(local_cols, 'gate', split_axis=1, concat_axis=1, tiled=True)  71.2 us
    pad x20, local copies, waits for them, and re-layouts, chained(): lax.associative_scan(combine, (run_decay, run_drive), reverse=backward, a...  50.7 us
    dot_general x2, matrix products, contract(): lax.dot_general(left, right, (((left_dim,), (right_dim,)), ((), ())), pre...  43.8 us
    psum x1, blocking collectives, shards(): lax.psum((weight_grad, jnp.sum(dnormed * unit_slice, axis=0), jnp.sum(dno...  39.1 us
  transfers between devices with their start and end apart: 3, of which 3 were waited for; matrix products, arithmetic and copies ran while one was open for 5% of the time, Pallas kernels for 0%

commit v1 on v0

v1 whole, which is shorter than its diff:
```python
import functools

import jax
import jax.numpy as jnp
from jax import lax
from jax.experimental import pallas as pl
from jax.experimental.pallas import tpu as pltpu
from jax.sharding import PartitionSpec as P

epsilon = 1e-05
F32 = jnp.float32
BF16 = jnp.bfloat16
LANES = 128
VMEM_LIMIT = 60 * 1024 * 1024


def call(kernel, meta, args, grid, in_specs, out_specs, out_shape, scratch=(), aliases=None, cost=None):
    return pl.pallas_call(
        kernel,
        grid_spec=pltpu.PrefetchScalarGridSpec(
            num_scalar_prefetch=1,
            grid=grid,
            in_specs=in_specs,
            out_specs=out_specs,
            scratch_shapes=list(scratch),
        ),
        out_shape=out_shape,
        input_output_aliases=aliases or {},
        compiler_params=pltpu.CompilerParams(
            dimension_semantics=("arbitrary",) * len(grid), vmem_limit_bytes=VMEM_LIMIT
        ),
        cost_estimate=cost,
    )(meta, *args)


def cost(flops, nbytes, trans=0):
    return pl.CostEstimate(flops=int(flops), bytes_accessed=int(nbytes), transcendentals=int(trans))


def struct(shape, dtype):
    return jax.ShapeDtypeStruct(shape, dtype)


def norm_kernel(meta, x_ref, gain_ref, bias_ref, out_ref, mu_ref, inv_ref):
    x = x_ref[...].astype(F32)
    features = x.shape[1]
    mu = jnp.sum(x, axis=1, keepdims=True) * (1.0 / features)
    centered = x - mu
    inv = lax.rsqrt(jnp.sum(centered * centered, axis=1, keepdims=True) * (1.0 / features) + epsilon)
    out_ref[...] = (centered * inv * gain_ref[...] + bias_ref[...]).astype(BF16)
    mu_ref[...] = jnp.broadcast_to(mu, mu_ref.shape)
    inv_ref[...] = jnp.broadcast_to(inv, inv_ref.shape)


def norm(meta, x, gain, bias, tb=256):
    tokens, features = x.shape
    row = pl.BlockSpec((tb, features), lambda t, m: (t, 0))
    whole = pl.BlockSpec((1, features), lambda t, m: (0, 0))
    stat = pl.BlockSpec((tb, LANES), lambda t, m: (t, 0))
    return call(
        norm_kernel,
        meta,
        (x, gain[None], bias[None]),
        (tokens // tb,),
        [row, whole, whole],
        [row, stat, stat],
        [struct(x.shape, BF16), struct((tokens, LANES), F32), struct((tokens, LANES), F32)],
        cost=cost(8 * tokens * features, 4 * tokens * features),
    )


def swap_halves(value, flag):
    half = value.shape[1] // 2
    swapped = jnp.concatenate([value[:, half:], value[:, :half]], axis=1)
    return jnp.where(flag, swapped, value)


def project_kernel(planes, mixed, meta, normed_ref, *refs):
    weights = refs[: len(planes)]
    out_ref = refs[-1]
    which = pl.program_id(1)
    for number, w_ref in enumerate(weights):

        @pl.when(which == number)
        def _(w_ref=w_ref, number=number):
            value = jnp.dot(normed_ref[...], w_ref[...], preferred_element_type=F32).astype(BF16)
            if mixed[number]:
                value = swap_halves(value, meta[M_CORE] == 1)
            out_ref[0] = value


def project(meta, normed, weights, planes, mixed, earlier, tb=512):
    tokens, features = normed.shape
    width = weights[0].shape[1]
    first = planes[0]
    number = len(weights)

    def where_to(t, n, m):
        return (m[first + n], t, 0)

    in_specs = [pl.BlockSpec((tb, features), lambda t, n, m: (t, 0))]
    in_specs += [pl.BlockSpec((features, width), lambda t, n, m: (0, 0))] * number
    args = [normed, *weights]
    aliases = None
    if earlier is not None:
        in_specs.append(pl.BlockSpec(memory_space=pl.ANY))
        args.append(earlier)
        aliases = {len(args): 0}
    return call(
        functools.partial(project_kernel, planes, mixed),
        meta,
        args,
        (tokens // tb, number),
        in_specs,
        pl.BlockSpec((1, tb, width), where_to),
        struct((3, tokens, width), BF16),
        aliases=aliases,
        cost=cost(2 * tokens * features * width * number, 2 * tokens * (features + width * number)),
    )


def sigmoid(z):
    return 0.5 * jnp.tanh(0.5 * z) + 0.5


def scan_kernel(
    chains,
    meta,
    u_ref,
    x_ref,
    g_ref,
    keep_ref,
    live_ref,
    prm_ref,
    *refs,
):
    hid_ref, ds_ref, direct_ref, vec_ref, A, B, FG, R, PV, D, CE, PE, CI, EI = refs[-14:]
    length = x_ref.shape[0]
    seg = length // (8 * chains)
    tile = 64
    pf, pr, bf, br = (jnp.broadcast_to(prm_ref[i : i + 1, :], (tile, LANES)) for i in range(4))

    def gates(i, carry):
        rows = pl.ds(pl.multiple_of(i * tile, tile), tile)
        x = x_ref[rows, :].astype(F32)
        ut = u_ref[0, rows, :].astype(F32)
        forget = sigmoid(u_ref[1, rows, :].astype(F32) + pf * x + bf)
        reset = sigmoid(u_ref[2, rows, :].astype(F32) + pr * x + br)
        FG[rows, :] = forget
        R[rows, :] = reset
        A[rows, :] = forget * keep_ref[rows, :]
        B[rows, :] = (1.0 - forget) * ut
        D[rows, :] = g_ref[rows, :].astype(F32) * live_ref[rows, :] * reset
        return carry

    lax.fori_loop(0, length // tile, gates, 0)

    def strided(q, i):
        return pl.ds(q * 8 * seg + i, 8, stride=seg)

    zeros = jnp.zeros((8, LANES), F32)
    ones = jnp.ones((8, LANES), F32)

    def summary(i, carry):
        out = []
        for q in range(chains):
            c, p, e = carry[q]
            a = A[strided(q, i), :]
            c = a * c + B[strided(q, i), :]
            p = a * p
            back = seg - 1 - i
            e = A[strided(q, back), :] * (D[strided(q, back), :] + e)
            out.append((c, p, e))
        return tuple(out)

    ends = lax.fori_loop(0, seg, summary, ((zeros, ones, zeros),) * chains, unroll=4)
    for q in range(chains):
        CE[8 * q : 8 * q + 8, :] = ends[q][0]
        PE[8 * q : 8 * q + 8, :] = ends[q][1]
        EI[8 * q : 8 * q + 8, :] = ends[q][2]
    count = 8 * chains
    c = jnp.zeros((1, LANES), F32)
    for j in range(count):
        CI[j : j + 1, :] = c
        c = CE[j : j + 1, :] + PE[j : j + 1, :] * c
    e = jnp.zeros((1, LANES), F32)
    for j in reversed(range(count)):
        own = EI[j : j + 1, :]
        EI[j : j + 1, :] = e
        e = own + PE[j : j + 1, :] * e

    def final(i, carry):
        out = []
        for q in range(chains):
            c, e = carry[q]
            PV[strided(q, i), :] = c
            c = A[strided(q, i), :] * c + B[strided(q, i), :]
            back = seg - 1 - i
            dc = D[strided(q, back), :] + e
            D[strided(q, back), :] = dc
            e = A[strided(q, back), :] * dc
            out.append((c, e))
        return tuple(out)

    starts = tuple((CI[8 * q : 8 * q + 8, :], EI[8 * q : 8 * q + 8, :]) for q in range(chains))
    lax.fori_loop(0, seg, final, starts, unroll=4)

    def fold(v):
        return v.reshape(tile // 8, 8, LANES).sum(axis=0)

    def grads(i, carry):
        rows = pl.ds(pl.multiple_of(i * tile, tile), tile)
        x = x_ref[rows, :].astype(F32)
        ut = u_ref[0, rows, :].astype(F32)
        live = live_ref[rows, :]
        g = g_ref[rows, :].astype(F32) * live
        forget = FG[rows, :]
        reset = R[rows, :]
        prev = PV[rows, :]
        dc = D[rows, :]
        memory = A[rows, :] * prev + B[rows, :]
        gap = memory - x
        hid_ref[rows, :] = (live * (x + reset * gap)).astype(BF16)
        rest = 1.0 - reset
        dreset = g * gap * (reset * rest)
        lose = 1.0 - forget
        dtilde = dc * lose
        dforget = dtilde * forget * (prev * keep_ref[rows, :] - ut)
        ds_ref[0, rows, :] = dtilde.astype(BF16)
        ds_ref[1, rows, :] = dforget.astype(BF16)
        ds_ref[2, rows, :] = dreset.astype(BF16)
        direct_ref[rows, :] = (g * rest + dforget * pf + dreset * pr).astype(BF16)
        s0, s1, s2, s3 = carry
        return (
            s0 + fold(dforget * x),
            s1 + fold(dreset * x),
            s2 + fold(dforget),
            s3 + fold(dreset),
        )

    sums = lax.fori_loop(0, length // tile, grads, (zeros,) * 4)
    for n, s in enumerate(sums):
        vec_ref[n : n + 1, :] = jnp.sum(s, axis=0, keepdims=True)
    vec_ref[4:8, :] = jnp.zeros((4, LANES), F32)


def scan(meta, half, u, x, grad, keep, live, params, earlier):
    length = x.shape[0]
    width = u.shape[2]
    blocks = width // LANES
    channels = grad.shape[1]
    col = lambda k, m: (0, m[half] * blocks + k)
    xcol = lambda k, m: (0, m[M_GATE] * (channels // LANES) + m[half] * blocks + k)
    tall = (length, LANES)
    plane = pl.BlockSpec((3, length, LANES), lambda k, m: (0, 0, k))
    in_specs = [
        plane,
        pl.BlockSpec(tall, xcol),
        pl.BlockSpec(tall, col),
        pl.BlockSpec(tall, lambda k, m: (0, 0)),
        pl.BlockSpec(tall, lambda k, m: (0, 0)),
        pl.BlockSpec((8, LANES), col),
    ]
    args = [u, x, grad, keep, live, params]
    aliases = None
    if earlier is not None:
        aliases = {len(args) + 1: 0, len(args) + 2: 2, len(args) + 3: 3}
        args += list(earlier)
        in_specs += [pl.BlockSpec(memory_space=pl.ANY)] * 3
    chains = 4
    small = pltpu.VMEM((8 * chains, LANES), F32)
    return call(
        functools.partial(scan_kernel, chains),
        meta,
        args,
        (blocks,),
        in_specs,
        [
            pl.BlockSpec(tall, col),
            plane,
            pl.BlockSpec(tall, col),
            pl.BlockSpec((8, LANES), col),
        ],
        [
            struct((length, channels), BF16),
            struct(u.shape, BF16),
            struct((length, channels), BF16),
            struct((8, channels), F32),
        ],
        scratch=[pltpu.VMEM(tall, F32)] * 6 + [small] * 4,
        aliases=aliases,
        cost=cost(60 * length * width, 2 * 9 * length * width, 2 * length * width),
    )


def wgrad_kernel(meta, normed_ref, ds_ref, a_ref, b_ref):
    step = pl.program_id(0)
    half = pl.num_programs(0) // 2
    left = normed_ref[...]
    for s in range(3):
        value = lax.dot_general(
            left, ds_ref[s], (((0,), (0,)), ((), ())), preferred_element_type=F32
        ).astype(BF16)

        @pl.when(step < half)
        def _(value=value, s=s):
            a_ref[s] = value

        @pl.when(step >= half)
        def _(value=value, s=s):
            b_ref[s] = value


def wgrad(meta, normed, ds, first, mb=256):
    tokens, features = normed.shape
    width = ds.shape[2]
    rows = features // 4
    steps = rows // mb

    def lhs(i, m):
        stream = i // steps
        return (0, (stream * 2 + m[first + stream]) * steps + i % steps)

    return call(
        wgrad_kernel,
        meta,
        (normed, ds),
        (2 * steps,),
        [
            pl.BlockSpec((tokens, mb), lhs),
            pl.BlockSpec((3, tokens, width), lambda i, m: (0, 0, 0)),
        ],
        [
            pl.BlockSpec((3, mb, width), lambda i, m: (0, jnp.minimum(i, steps - 1), 0)),
            pl.BlockSpec((3, mb, width), lambda i, m: (0, jnp.maximum(i - steps, 0), 0)),
        ],
        [struct((3, rows, width), BF16)] * 2,
        cost=cost(12 * tokens * rows * width, 2 * tokens * (features // 2 + 3 * width)),
    )


def back_kernel(meta, ds1_ref, ds2_ref, p1, q1, m1, p2, q2, m2, out_ref):
    total = None
    for ds_ref, table, (p, q, m) in ((ds1_ref, M_S1, (p1, q1, m1)), (ds2_ref, M_S2, (p2, q2, m2))):
        for n, w_ref in enumerate((p, q, m)):
            left = ds_ref[meta[table + n]]
            if n == 2:
                left = swap_halves(left, meta[M_CORE] == 1)
            term = lax.dot_general(
                left, w_ref[...], (((1,), (1,)), ((), ())), preferred_element_type=F32
            )
            total = term if total is None else total + term
    out_ref[0] = total.astype(BF16)


def back(meta, ds1, ds2, w1, w2, first, tb=512):
    tokens, width = ds1.shape[1:]
    features = w1[0].shape[0]
    block = features // 4
    dspec = pl.BlockSpec((3, tb, width), lambda n, t, m: (0, t, 0))
    wspec = pl.BlockSpec((block, width), lambda n, t, m: (m[first + n], 0))
    return call(
        back_kernel,
        meta,
        (ds1, ds2, *w1, *w2),
        (2, tokens // tb),
        [dspec, dspec] + [wspec] * 6,
        pl.BlockSpec((1, tb, block), lambda n, t, m: (n, t, 0)),
        struct((2, tokens, block), BF16),
        cost=cost(24 * tokens * block * width, 12 * tokens * width * 2),
    )


def unit_of(x_ref, mu_ref, inv_ref):
    repeat = x_ref.shape[1] // LANES
    mu = jnp.concatenate([mu_ref[...]] * repeat, axis=1)
    inv = jnp.concatenate([inv_ref[...]] * repeat, axis=1)
    return (x_ref[...].astype(F32) - mu) * inv, inv


def tail_sums_kernel(meta, k_ref, rc_ref, ry_ref, x_ref, mu_ref, inv_ref, gain_ref, dn_ref, row_ref, col_ref):
    unit, _ = unit_of(x_ref, mu_ref, inv_ref)
    dn = k_ref[0].astype(F32) + rc_ref[0].astype(F32) + ry_ref[...].astype(F32)
    dn_ref[...] = dn
    gu = dn * gain_ref[...]
    ones = jnp.ones((8, gu.shape[1]), F32)
    dims = (((1,), (1,)), ((), ()))
    first = lax.dot_general(ones, gu, dims, precision=lax.Precision.HIGHEST, preferred_element_type=F32)
    second = lax.dot_general(ones, gu * unit, dims, precision=lax.Precision.HIGHEST, preferred_element_type=F32)
    pick = lax.broadcasted_iota(jnp.int32, first.shape, 0) == 0
    row_ref[...] = jnp.where(pick, first, second)

    @pl.when(pl.program_id(0) == 0)
    def _():
        col_ref[...] = jnp.zeros_like(col_ref)

    col_ref[0:1, :] += jnp.sum(dn * unit, axis=0, keepdims=True)
    col_ref[1:2, :] += jnp.sum(dn, axis=0, keepdims=True)


def tail_sums(meta, keep, got, far, x, mu, inv, gain, tb=512):
    tokens, channels = far.shape
    return call(
        tail_sums_kernel,
        meta,
        (keep, got, far, x, mu, inv, gain[None]),
        (tokens // tb,),
        [
            pl.BlockSpec((1, tb, channels), lambda t, m: (1, t, 0)),
            pl.BlockSpec((1, tb, channels), lambda t, m: (1, t, 0)),
            pl.BlockSpec((tb, channels), lambda t, m: (t, 0)),
            pl.BlockSpec((tb, channels), lambda t, m: (t, m[M_GATE])),
            pl.BlockSpec((tb, LANES), lambda t, m: (t, 0)),
            pl.BlockSpec((tb, LANES), lambda t, m: (t, 0)),
            pl.BlockSpec((1, channels), lambda t, m: (0, m[M_GATE])),
        ],
        [
            pl.BlockSpec((tb, channels), lambda t, m: (t, 0)),
            pl.BlockSpec((8, tb), lambda t, m: (0, t)),
            pl.BlockSpec((8, channels), lambda t, m: (0, 0)),
        ],
        [struct((tokens, channels), F32), struct((8, tokens), F32), struct((8, channels), F32)],
        cost=cost(20 * tokens * channels, 12 * tokens * channels),
    )


def tail_kernel(features, meta, dn_ref, row_ref, x_ref, mu_ref, inv_ref, gain_ref, direct_ref, out_ref):
    unit, inv = unit_of(x_ref, mu_ref, inv_ref)
    rows = row_ref[...] * (1.0 / features)
    shape = (8, 2 * LANES)
    at = lax.broadcasted_iota(jnp.int32, shape, 0)
    lane = lax.broadcasted_iota(jnp.int32, shape, 1)
    pick = jnp.where(at == jnp.where(lane < LANES, 0, 1), 1.0, 0.0).astype(F32)
    means = lax.dot_general(
        rows, pick, (((0,), (0,)), ((), ())), precision=lax.Precision.HIGHEST, preferred_element_type=F32
    )
    repeat = x_ref.shape[1] // LANES
    m1 = jnp.concatenate([means[:, :LANES]] * repeat, axis=1)
    m2 = jnp.concatenate([means[:, LANES:]] * repeat, axis=1)
    gu = dn_ref[...] * gain_ref[...]
    out_ref[...] = (inv * (gu - m1 - unit * m2) + direct_ref[...].astype(F32)).astype(BF16)


def tail(meta, dn, rows, x, mu, inv, gain, direct, features, tb=512):
    tokens, channels = dn.shape
    return call(
        functools.partial(tail_kernel, features),
        meta,
        (dn, rows, x, mu, inv, gain[None], direct),
        (tokens // tb,),
        [
            pl.BlockSpec((tb, channels), lambda t, m: (t, 0)),
            pl.BlockSpec((8, tb), lambda t, m: (0, t)),
            pl.BlockSpec((tb, channels), lambda t, m: (t, m[M_GATE])),
            pl.BlockSpec((tb, LANES), lambda t, m: (t, 0)),
            pl.BlockSpec((tb, LANES), lambda t, m: (t, 0)),
            pl.BlockSpec((1, channels), lambda t, m: (0, m[M_GATE])),
            pl.BlockSpec((tb, channels), lambda t, m: (t, 0)),
        ],
        pl.BlockSpec((tb, channels), lambda t, m: (t, 0)),
        struct((tokens, channels), BF16),
        cost=cost(10 * tokens * channels, 12 * tokens * channels),
    )


def place_kernel(n_dp, meta, *refs):
    out_ref = refs[-1]
    step = pl.program_id(0)
    for stream in range(2):
        for part in range(2):
            low = stream * n_dp + part * (n_dp // 2)

            @pl.when((step >= low) & (step < low + n_dp // 2))
            def _(stream=stream, part=part):
                one = refs[stream * 2 + part]
                two = refs[4 + stream * 2 + part]
                piece = out_ref.shape[1] // 4
                unit = piece // 3
                core = meta[M_CORE]

                def put(owner, single, src, col):
                    base = meta[M_OWN + owner] * piece
                    wide = unit if single else 2 * unit
                    at = base + (jnp.where(core == 0, 2 * unit, 0) if single else core * unit)
                    at = pl.multiple_of(at, LANES)
                    out_ref[:, pl.ds(at, wide)] = src[:, col : col + wide].astype(F32)

                put(0, False, one, 0)
                put(1, False, one, 2 * unit)
                put(2, True, one, 4 * unit)
                put(3, True, one, 5 * unit)
                put(0, True, two, 0)
                put(1, True, two, unit)
                put(2, False, two, 2 * unit)
                put(3, False, two, 4 * unit)


def place(meta, parts1, parts2, n_dp, features, columns):
    rows = features // 2 // n_dp
    half = n_dp // 2
    specs = []
    for _ in range(2):
        for stream in range(2):
            for part in range(2):
                low = stream * n_dp + part * half
                specs.append(
                    pl.BlockSpec(
                        (rows, columns // 2),
                        lambda i, m, low=low: (jnp.clip(i - low, 0, half - 1), 0),
                    )
                )

    def where_to(i, m):
        stream = i // n_dp
        return (stream * n_dp + (i % n_dp ^ m[M_RHO + stream]), 0)

    return call(
        functools.partial(place_kernel, n_dp),
        meta,
        (*parts1, *parts2),
        (2 * n_dp,),
        specs,
        pl.BlockSpec((rows, columns), where_to),
        struct((features, columns), F32),
        cost=cost(features * columns, 6 * features * columns),
    )


M_GATE, M_CORE, M_H1, M_H2 = 0, 1, 2, 3
M_S1, M_S2 = 4, 7
M_SEND, M_KEEP = 10, 12
M_OUT, M_IN = 14, 16
M_OWN, M_RHO = 18, 22


def shards(
    n_dp,
    n_gate,
    inputs,
    weight,
    ln_gain,
    ln_bias,
    forget_peep,
    reset_peep,
    forget_bias,
    reset_bias,
    resets,
    padding,
    grad_out,
):
    rows, tokens, features = inputs.shape
    assert rows == 1 and n_gate == 4
    channels = forget_peep.shape[0]
    unit = channels // 4
    piece = 3 * unit
    bits = n_dp.bit_length() - 1
    assert 1 << bits == n_dp
    gate = lax.axis_index("gate")
    dp = lax.axis_index("dp")
    hi, core = gate // 2, gate % 2
    other = 1 - core

    orders = [list(range(bits)), [1, 0, *range(2, bits)]]

    def bit(b):
        return (dp >> b) & 1

    def rho(order):
        value = 0
        for b in order:
            value = value * 2 + bit(b)
        return value

    def streams(h):
        return [core + h, other + h, 2 * (1 - h)]

    h1, h2 = hi, 1 - hi
    s1, s2 = streams(h1), streams(h2)
    far = (1 - hi) * 2
    meta = jnp.stack(
        [gate, core, h1, h2, *s1, *s2]
        + [1 - bit(order[0]) for order in orders]
        + [bit(order[0]) for order in orders]
        + [far + other, hi * 2 + other, far + core, hi * 2 + core]
        + [gate, hi * 2 + other, far + core, far + other]
        + [rho(order) for order in orders]
    ).astype(jnp.int32)

    def over_gate(value, delta):
        return lax.ppermute(value, "gate", [(g, g ^ delta) for g in range(n_gate)])

    def over_dp(value, b):
        return lax.ppermute(value, "dp", [(d, d ^ (1 << b)) for d in range(n_dp)])

    def columns(start, width):
        return lax.dynamic_slice_in_dim(weight, start, width, 1)

    single = jnp.where(core == 0, 2 * unit, 0)
    pair = core * unit

    sent2 = over_gate(columns((far + core) * piece + single, unit), 2)
    sent3 = over_gate(columns((far + other) * piece + single, unit), 3)
    near = (hi * 2 + other) * piece
    got_pair = over_gate(columns(near + pair, 2 * unit), 1)
    got_single = over_gate(columns(near + single, unit), 1)
    late2 = over_gate(columns((far + core) * piece + pair, 2 * unit), 2)
    late3 = over_gate(columns((far + other) * piece + pair, 2 * unit), 3)
    own_pair = columns(gate * piece + pair, 2 * unit)
    own_single = columns(gate * piece + single, unit)
    w1 = [own_pair, got_pair, jnp.concatenate([sent2, sent3], axis=1)]
    w2 = [late2, late3, jnp.concatenate([own_single, got_single], axis=1)]

    x = inputs.reshape(tokens, features)
    grad = grad_out.reshape(tokens, channels)
    normed, mu, inv = norm(meta, x, ln_gain, ln_bias)

    keep = jnp.broadcast_to((1 - resets).astype(F32).reshape(tokens, 1), (tokens, LANES))
    live = jnp.broadcast_to(padding.astype(F32).reshape(tokens, 1), (tokens, LANES))
    params = jnp.concatenate(
        [jnp.stack([forget_peep, reset_peep, forget_bias, reset_bias]), jnp.zeros((4, channels), F32)]
    )

    u1 = project(meta, normed, w1[:2], [M_S1, M_S1 + 1], [False, False], None)
    u1 = project(meta, normed, w1[2:], [M_S1 + 2], [True], u1)
    hidden, ds1, direct, vecs = scan(meta, M_H1, u1, x, grad, keep, live, params, None)
    send1 = wgrad(meta, normed, ds1, M_SEND)
    keep1 = wgrad(meta, normed, ds1, M_KEEP)
    u2 = project(meta, normed, w2[2:], [M_S2 + 2], [True], None)
    u2 = project(meta, normed, w2[:2], [M_S2, M_S2 + 1], [False, False], u2)
    hidden, ds2, direct, vecs = scan(
        meta, M_H2, u2, x, grad, keep, live, params, (hidden, direct, vecs)
    )
    send2 = wgrad(meta, normed, ds2, M_SEND)
    keep2 = wgrad(meta, normed, ds2, M_KEEP)

    def add(a, b):
        return (a.astype(F32) + b.astype(F32)).astype(BF16)

    def rows_of(v, start, count):
        return lax.dynamic_slice_in_dim(v, start, count, 1)

    def reduce_scatter(send, kept, order):
        got = over_dp(send, order[0])
        for b in order[1:]:
            half = kept.shape[1] // 2
            away, stay = (1 - bit(b)) * half, bit(b) * half
            send = add(rows_of(kept, away, half), rows_of(got, away, half))
            nxt = over_dp(send, b)
            kept = add(rows_of(kept, stay, half), rows_of(got, stay, half))
            got = nxt
        return add(kept, got)

    def lanes(v, start, width):
        return lax.dynamic_slice_in_dim(v, start, width, 1)

    def plane(v, s):
        return lax.dynamic_index_in_dim(v, s, 0, keepdims=False)

    def to_storage(shard, s, late):
        p, q, m = (plane(shard, n) for n in s)
        mine, theirs = lanes(m, core * unit, unit), lanes(m, other * unit, unit)
        if late:
            kept, out = mine, [theirs, p, q]
        else:
            kept, out = p, [q, mine, theirs]
        return jnp.concatenate([kept] + [over_gate(v, n + 1) for n, v in enumerate(out)], axis=1)

    def all_gather(shard, order):
        for b in reversed(order[1:]):
            shard = jnp.concatenate([shard, over_dp(shard, b)], axis=0)
        return [shard, over_dp(shard, order[0])]

    def reduce_all(sends, keeps, s, late):
        parts = [reduce_scatter(a, k, order) for a, k, order in zip(sends, keeps, orders)]
        stored = to_storage(jnp.concatenate(parts, axis=1), s, late)
        each = parts[0].shape[1]
        out = []
        for n, order in enumerate(orders):
            out += all_gather(stored[n * each : (n + 1) * each], order)
        return out

    parts1 = reduce_all(send1, keep1, s1, False)

    send = back(meta, ds1, ds2, w1, w2, M_OUT)
    got = over_gate(send, 1)
    kept = back(meta, ds1, ds2, w1, w2, M_IN)
    far_part = over_gate(add(kept[0], got[0]), 2)

    parts2 = reduce_all(send2, keep2, s2, True)

    dn, row_sums, col_sums = tail_sums(meta, kept, got, far_part, x, mu, inv, ln_gain)
    row_sums = row_sums[:2]
    for delta in (1, 2):
        row_sums = row_sums + over_gate(row_sums, delta)
    row_sums = jnp.concatenate([row_sums, jnp.zeros((6, tokens), F32)])
    dinputs = tail(meta, dn, row_sums, x, mu, inv, ln_gain, direct, features)

    totals = jnp.concatenate([col_sums[:2], vecs[:4]], axis=0)
    for b in range(bits):
        totals = totals + over_dp(totals, b)

    grad_weight = place(meta, parts1, parts2, n_dp, features, weight.shape[1])
    return (
        hidden.reshape(rows, tokens, channels),
        dinputs.reshape(rows, tokens, channels),
        grad_weight,
        totals[0],
        totals[1],
        totals[2],
        totals[3],
        totals[4],
        totals[5],
    )


def solution(mesh):
    return jax.shard_map(
        functools.partial(shards, mesh.shape["dp"], mesh.shape["gate"]),
        mesh=mesh,
        in_specs=(
            P("dp", None, None),
            P(None, "gate"),
            P(),
            P(),
            P("gate"),
            P("gate"),
            P("gate"),
            P("gate"),
            P("dp", None),
            P("dp", None),
            P("dp", None, "gate"),
        ),
        out_specs=(
            P("dp", None, "gate"),
            P("dp", None, "gate"),
            P(None, "gate"),
            P("gate"),
            P("gate"),
            P("gate"),
            P("gate"),
            P("gate"),
            P("gate"),
        ),
        check_vma=False,
    )
```

time: 1020 us -> 403 us (0.40); the launches traced: 1000 us -> 401 us
  waiting for transfers between devices: 390 us -> 122 us
  local copies, waits for them, and re-layouts: 232 us -> 20.1 us
  Pallas kernels: 0 us -> 209 us
  other arithmetic: 170 us -> 11.1 us
  blocking collectives: 124 us -> 0 us
  matrix products: 62.2 us -> 0 us
  starting transfers between devices: 5.51 us -> 37.9 us
  between operations: 17 us -> 1.27 us
    psum x1 -> x0, waiting for transfers between devices: 229 us -> none  [shards(): lax.psum((weight_grad, jnp.sum(dnormed * unit_slice, axis=0), jnp.sum(dno...]
    pallas_call x0 -> x16, Pallas kernels: none -> 209 us  [call(): pl.pallas_call(kernel, grid_spec=pltpu.PrefetchScalarGridSpec(num_scalar_...]
    ppermute x0 -> x43, waiting for transfers between devices: none -> 122 us  [the longest x27 73.2 us: over_dp(): return lax.ppermute(value, 'dp', [(d, d ^ 1 << b) for d in range(n_dp)])]
    reduce_scatter x1 -> x0, waiting for transfers between devices: 89.5 us -> none  [shards(): lax.psum_scatter(partial_in, 'gate', scatter_dimension=1, tiled=True)]
    all_to_all x1 -> x0, blocking collectives: 74.4 us -> none  [shards(): lax.all_to_all(dstreams, 'gate', split_axis=1, concat_axis=1, tiled=True)]
    unnamed x130 -> x43, local copies, waits for them, and re-layouts: 77.5 us -> 6.07 us
    all_to_all x1 -> x0, waiting for transfers between devices: 71.2 us -> none  [shards(): lax.all_to_all(local_cols, 'gate', split_axis=1, concat_axis=1, tiled=True)]
    dot_general x3 -> x0, matrix products: 62.2 us -> none  [the longest x2 43.8 us: contract(): lax.dot_general(left, right, (((left_dim,), (right_dim,)), ((), ())), pre...]
  transfers between devices with their start and end apart: 3 -> 43, of which waited for: 3 -> 13; matrix products, arithmetic and copies ran while one was open for 5% -> 6% of each run, Pallas kernels for 0% -> 40%
where the time goes in v1:
time: 403 us; the launch traced here: 401 us
  Pallas kernels  209 us (52%)
  waiting for transfers between devices  122 us (30%)
  starting transfers between devices  37.9 us (9%)
  local copies, waits for them, and re-layouts  20.1 us (5%)
  other arithmetic  11.1 us (3%)
    pallas_call x16, Pallas kernels, call(): pl.pallas_call(kernel, grid_spec=pltpu.PrefetchScalarGridSpec(num_scalar_...  209 us
    ppermute x27, waiting for transfers between devices, over_dp(): return lax.ppermute(value, 'dp', [(d, d ^ 1 << b) for d in range(n_dp)])  73.2 us
    ppermute x16, waiting for transfers between devices, over_gate(): return lax.ppermute(value, 'gate', [(g, g ^ delta) for g in range(n_gate)])  48.4 us
    ppermute x27, starting transfers between devices, over_dp(): return lax.ppermute(value, 'dp', [(d, d ^ 1 << b) for d in range(n_dp)])  26.2 us
    ppermute x16, starting transfers between devices, over_gate(): return lax.ppermute(value, 'gate', [(g, g ^ delta) for g in range(n_gate)])  11.7 us
  transfers between devices with their start and end apart: 43, of which 13 were waited for; matrix products, arithmetic and copies ran while one was open for 6% of the time, Pallas kernels for 40%

profile of v1, /device:TPU:0, one launch (start us, length us, event | category | flops | bytes accessed | tf_op | source)
XLA Modules:
  0.0 401.1 jit_solution(18420035253020265632)
XLA Ops:
  0.7 2.7 constant_dynamic-slice_fusion.2
  3.9 4.4 %constant_dynamic-slice_fusion = (bf16[2048,256]{1,0:T(8,128)(2,1)}, bf16[2048,256]{1,0:T(8,128)(2,1)}, bf16[2048,256]{1,0:T(8,128)(2,1)}, bf16[2048,256]{1,0:T(8,128)(2,1)}) fusion(bf16[2048,1536]{1,0:T(8,128)(2,1)} %param.12, s32[]{:T(128)S(6)} %select_n.128, s32[]{:T(128)S(6)} %select_n.121, s32[]{:T(128)S(6)} %select_n.120, s32[]{:T(128)S(6)} %select_n.127), kind=kLoop, calls=%fused_computation.66 | loop fusion | bytes 8388624 | tf_op jit(solution)/shard_map/dynamic_slice | solution.py:596
  8.3 3.0 collective-permute-start.3
  14.0 12.0 %shard_map.178 = (bf16[2048,2048]{1,0:T(8,128)(2,1)}, f32[2048,128]{1,0:T(8,128)}, f32[2048,128]{1,0:T(8,128)}) custom-call(s32[24]{0:T(128)} %stack.99.meta, bf16[2048,2048]{1,0:T(8,128)(2,1)} %bitcast.56, f32[1,2048]{1,0:T(1,128)} %bitcast.65, f32[1,2048]{1,0:T(1,128)} %bitcast.70), custom_call_target="tpu_custom_call" | custom-call | flops 33554432 | bytes 16777216 | tf_op jit(solution)/shard_map/pallas_call | solution.py:18
  27.3 2.2 pad_maximum_fusion.refs_0_.m2
  30.6 7.3 %shard_map.179.refs_2_ = bf16[3,2048,256]{2,1,0:T(8,128)(2,1)} custom-call(s32[24]{0:T(128)} %stack.99.meta, bf16[2048,2048]{1,0:T(8,128)(2,1)} %get-tuple-element.31.normed_ref, bf16[2048,256]{1,0:T(8,128)(2,1)} %pad_maximum_fusion.refs_0_.m2), custom_call_target="tpu_custom_call" | custom-call | flops 2147483648 | bytes 9437184 | tf_op jit(solution)/shard_map/pallas_call | solution.py:18
  38.0 12.3 %shard_map.181.refs_1_ = bf16[3,2048,256]{2,1,0:T(8,128)(2,1)} custom-call(s32[24]{0:T(128)} %stack.99.meta, bf16[2048,2048]{1,0:T(8,128)(2,1)} %get-tuple-element.31.normed_ref, bf16[2048,256]{1,0:T(8,128)(2,1)} %get-tuple-element.56.refs_0_.p1, bf16[2048,256]{1,0:T(8,128)(2,1)} %collective-permute-done.5.refs_1_.q1), custom_call_target="tpu_custom_call" | custom-call | flops 4294967296 | bytes 10485760 | tf_op jit(solution)/shard_map/pallas_call | solution.py:18
  50.3 7.3 %shard_map.182.u_ref = bf16[3,2048,256]{2,1,0:T(8,128)(2,1)} custom-call(s32[24]{0:T(128)} %stack.99.meta, bf16[2048,2048]{1,0:T(8,128)(2,1)} %get-tuple-element.31.normed_ref, bf16[2048,256]{1,0:T(8,128)(2,1)} %copy-done.5, bf16[3,2048,256]{2,1,0:T(8,128)(2,1)} %shard_map.181.refs_1_), custom_call_target="tpu_custom_call", output_to_operand_aliasing={{}: (3, {})} | custom-call | flops 2147483648 | bytes 9437184 | tf_op jit(solution)/shard_map/pallas_call | solution.py:18
  60.3 24.5 %shard_map.183 = (bf16[2048,512]{1,0:T(8,128)(2,1)}, bf16[3,2048,256]{2,1,0:T(8,128)(2,1)}, bf16[2048,512]{1,0:T(8,128)(2,1)}, f32[8,512]{1,0:T(8,128)}) custom-call(s32[24]{0:T(128)} %stack.99.meta, bf16[3,2048,256]{2,1,0:T(8,128)(2,1)} %shard_map.182.u_ref, bf16[2048,2048]{1,0:T(8,128)(2,1)} %bitcast.57, bf16[2048,512]{1,0:T(8,128)(2,1)} %bitcast.61, ...), custom_call_target="tpu_custom_call" | custom-call | flops 31457280 | bytes 9437184 | tf_op jit(solution)/shard_map/pallas_call | solution.py:18
  86.8 12.3 %shard_map.180.u_ref = bf16[3,2048,256]{2,1,0:T(8,128)(2,1)} custom-call(s32[24]{0:T(128)} %stack.99.meta, bf16[2048,2048]{1,0:T(8,128)(2,1)} %get-tuple-element.31.normed_ref, bf16[2048,256]{1,0:T(8,128)(2,1)} %copy-done.7, bf16[2048,256]{1,0:T(8,128)(2,1)} %copy-done.8, bf16[3,2048,256]{2,1,0:T(8,128)(2,1)} %shard_map.179.refs_2_), custom_call_target="tpu_custom_call", output_to_operand_aliasing={{}: (4, {})} | custom-call | flops 4294967296 | bytes 10485760 | tf_op jit(solution)/shard_map/pallas_call | solution.py:18
  99.1 24.5 %shard_map.184 = (bf16[2048,512]{1,0:T(8,128)(2,1)}, bf16[3,2048,256]{2,1,0:T(8,128)(2,1)}, bf16[2048,512]{1,0:T(8,128)(2,1)}, f32[8,512]{1,0:T(8,128)}) custom-call(s32[24]{0:T(128)} %stack.99.meta, bf16[3,2048,256]{2,1,0:T(8,128)(2,1)} %shard_map.180.u_ref, ...), custom_call_target="tpu_custom_call", output_to_operand_aliasing={{0}: (7, {}), {2}: (8, {}), {3}: (9, {})} | custom-call | flops 31457280 | bytes 9437184 | tf_op jit(solution)/shard_map/pallas_call | solution.py:18
  123.6 13.8 %shard_map.186 = bf16[2,2048,512]{2,1,0:T(8,128)(2,1)} custom-call(s32[24]{0:T(128)} %stack.99.meta, bf16[3,2048,256]{2,1,0:T(8,128)(2,1)} %get-tuple-element.36.ds1_ref.ds_ref, bf16[3,2048,256]{2,1,0:T(8,128)(2,1)} %get-tuple-element.37.ds2_ref.ds_ref, bf16[2048,256]{1,0:T(8,128)(2,1)} %get-tuple-element.56.refs_0_.p1, ...), custom_call_target="tpu_custom_call" | custom-call | flops 6442450944 | bytes 12582912 | tf_op jit(solution)/shard_map/pallas_call | solution.py:18
  137.8 11.6 %shard_map.192 = (bf16[3,512,256]{2,1,0:T(8,128)(2,1)}, bf16[3,512,256]{2,1,0:T(8,128)(2,1)}) custom-call(s32[24]{0:T(128)} %stack.99.meta, bf16[2048,2048]{1,0:T(8,128)(2,1)} %get-tuple-element.31.normed_ref, bf16[3,2048,256]{2,1,0:T(8,128)(2,1)} %get-tuple-element.37.ds2_ref.ds_ref), custom_call_target="tpu_custom_call" | custom-call | flops 3221225472 | bytes 7340032 | tf_op jit(solution)/shard_map/pallas_call | solution.py:18
  149.4 1.6 collective-permute-start.28
  151.0 1.5 collective-permute-start.25
  152.5 11.7 %shard_map.190 = (bf16[3,512,256]{2,1,0:T(8,128)(2,1)}, bf16[3,512,256]{2,1,0:T(8,128)(2,1)}) custom-call(s32[24]{0:T(128)} %stack.99.meta, bf16[2048,2048]{1,0:T(8,128)(2,1)} %get-tuple-element.31.normed_ref, bf16[3,2048,256]{2,1,0:T(8,128)(2,1)} %get-tuple-element.36.ds1_ref.ds_ref), custom_call_target="tpu_custom_call" | custom-call | flops 3221225472 | bytes 7340032 | tf_op jit(solution)/shard_map/pallas_call | solution.py:18
  165.1 11.6 %shard_map.191 = (bf16[3,512,256]{2,1,0:T(8,128)(2,1)}, bf16[3,512,256]{2,1,0:T(8,128)(2,1)}) custom-call(s32[24]{0:T(128)} %stack.99.meta, bf16[2048,2048]{1,0:T(8,128)(2,1)} %get-tuple-element.31.normed_ref, bf16[3,2048,256]{2,1,0:T(8,128)(2,1)} %get-tuple-element.37.ds2_ref.ds_ref), custom_call_target="tpu_custom_call" | custom-call | flops 3221225472 | bytes 7340032 | tf_op jit(solution)/shard_map/pallas_call | solution.py:18
  176.7 11.8 %shard_map.189 = (bf16[3,512,256]{2,1,0:T(8,128)(2,1)}, bf16[3,512,256]{2,1,0:T(8,128)(2,1)}) custom-call(s32[24]{0:T(128)} %stack.99.meta, bf16[2048,2048]{1,0:T(8,128)(2,1)} %get-tuple-element.31.normed_ref, bf16[3,2048,256]{2,1,0:T(8,128)(2,1)} %get-tuple-element.36.ds1_ref.ds_ref), custom_call_target="tpu_custom_call" | custom-call | flops 3221225472 | bytes 7340032 | tf_op jit(solution)/shard_map/pallas_call | solution.py:18
  188.6 2.2 add_convert_fusion.2
  190.7 1.5 collective-permute-start.29
  193.2 1.6 collective-permute-start.26
  197.0 13.8 %shard_map.185.k_ref = bf16[2,2048,512]{2,1,0:T(8,128)(2,1)} custom-call(s32[24]{0:T(128)} %stack.99.meta, bf16[3,2048,256]{2,1,0:T(8,128)(2,1)} %get-tuple-element.36.ds1_ref.ds_ref, bf16[3,2048,256]{2,1,0:T(8,128)(2,1)} %get-tuple-element.37.ds2_ref.ds_ref, bf16[2048,256]{1,0:T(8,128)(2,1)} %get-tuple-element.56.refs_0_.p1, ...), custom_call_target="tpu_custom_call" | custom-call | flops 6442450944 | bytes 12582912 | tf_op jit(solution)/shard_map/pallas_call | solution.py:18
  210.8 2.6 collective-permute-start.30
  214.0 2.6 collective-permute-start.15
  217.1 17.9 %collective-permute-done.30 = bf16[3,128,256]{2,1,0:T(8,128)(2,1)S(1)} collective-permute-done((bf16[3,128,256]{2,1,0:T(8,128)(2,1)S(1)}, bf16[3,128,256]{2,1,0:T(8,128)(2,1)S(1)}, u32[]{:S(2)}, u32[]{:S(2)}) %collective-permute-start.30) | collective-permute-done | bytes 196640 | tf_op jit(solution)/shard_map/ppermute | solution.py:593
  235.1 4.1 %collective-permute-done.27 = bf16[3,128,256]{2,1,0:T(8,128)(2,1)S(1)} collective-permute-done((bf16[3,128,256]{2,1,0:T(8,128)(2,1)S(1)}, bf16[3,128,256]{2,1,0:T(8,128)(2,1)S(1)}, u32[]{:S(2)}, u32[]{:S(2)}) %collective-permute-start.27) | collective-permute-done | bytes 196640 | tf_op jit(solution)/shard_map/ppermute | solution.py:593
  239.8 1.6 collective-permute-start.32
  241.3 2.1 collective-permute-done.15
  243.6 2.2 fusion
  245.7 1.6 collective-permute-start.7
  248.2 1.6 collective-permute-start.17
  249.9 45.2 %collective-permute-done.17 = bf16[256,128]{1,0:T(8,128)(2,1)S(1)} collective-permute-done((bf16[256,128]{1,0:T(8,128)(2,1)S(1)}, bf16[256,128]{1,0:T(8,128)(2,1)S(1)}, u32[]{:S(2)}, u32[]{:S(2)}) %collective-permute-start.17) | collective-permute-done | bytes 65568 | tf_op jit(solution)/shard_map/ppermute | solution.py:590
  295.1 2.0 collective-permute-done.18
  299.4 2.0 collective-permute-start.19
  301.5 14.5 %collective-permute-done.34 = bf16[128,768]{1,0:T(8,128)(2,1)S(1)} collective-permute-done((bf16[128,768]{1,0:T(8,128)(2,1)S(1)}, bf16[128,768]{1,0:T(8,128)(2,1)S(1)}, u32[]{:S(2)}, u32[]{:S(2)}) %collective-permute-start.34) | collective-permute-done | bytes 196640 | tf_op jit(solution)/shard_map/ppermute | solution.py:593
  316.1 4.2 %collective-permute-done.22 = bf16[128,768]{1,0:T(8,128)(2,1)S(1)} collective-permute-done((bf16[128,768]{1,0:T(8,128)(2,1)S(1)}, bf16[128,768]{1,0:T(8,128)(2,1)S(1)}, u32[]{:S(2)}, u32[]{:S(2)}) %collective-permute-start.22) | collective-permute-done | bytes 196640 | tf_op jit(solution)/shard_map/ppermute | solution.py:593
  320.3 1.6 collective-permute-start.23
  321.9 2.6 collective-permute-done.19
  324.7 2.1 collective-permute-start.39
  326.7 6.2 %collective-permute-done.35 = bf16[256,768]{1,0:T(8,128)(2,1)S(1)} collective-permute-done((bf16[256,768]{1,0:T(8,128)(2,1)S(1)}, bf16[256,768]{1,0:T(8,128)(2,1)S(1)}, u32[]{:S(2)}, u32[]{:S(2)}) %collective-permute-start.35) | collective-permute-done | bytes 393248 | tf_op jit(solution)/shard_map/ppermute | solution.py:593
  333.0 1.6 collective-permute-start.36
  334.7 6.7 %collective-permute-done.20 = bf16[256,768]{1,0:T(8,128)(2,1)S(1)} collective-permute-done((bf16[256,768]{1,0:T(8,128)(2,1)S(1)}, bf16[256,768]{1,0:T(8,128)(2,1)S(1)}, u32[]{:S(2)}, u32[]{:S(2)}) %collective-permute-start.20) | collective-permute-done | bytes 393248 | tf_op jit(solution)/shard_map/ppermute | solution.py:593
  341.4 1.6 collective-permute-start.21
  344.3 11.9 %shard_map.187 = (f32[2048,512]{1,0:T(8,128)}, f32[8,2048]{1,0:T(8,128)}, f32[8,512]{1,0:T(8,128)}) custom-call(s32[24]{0:T(128)} %stack.99.meta, bf16[2,2048,512]{2,1,0:T(8,128)(2,1)} %shard_map.185.k_ref, bf16[2,2048,512]{2,1,0:T(8,128)(2,1)} %collective-permute-done.6.rc_ref, bf16[2048,512]{1,0:T(8,128)(2,1)} %copy-done.6, bf16[2048,2048]{1,0:T(8,128)(2,1)} %bitcast.59, ...), custom_call_target="tpu_custom_call" | custom-call | flops 20971520 | bytes 12582912 | tf_op jit(solution)/shard_map/pallas_call | solution.py:18
  358.4 11.3 %collective-permute-done.40 = f32[6,512]{1,0:T(8,128)S(1)} collective-permute-done((f32[6,512]{1,0:T(8,128)S(1)}, f32[6,512]{1,0:T(8,128)S(1)}, u32[]{:S(2)}, u32[]{:S(2)}) %collective-permute-start.40) | collective-permute-done | bytes 12320 | tf_op jit(solution)/shard_map/ppermute | solution.py:593
  371.7 3.6 collective-permute-done.41
  377.1 14.9 %shard_map.193 = f32[2048,1536]{1,0:T(8,128)} custom-call(s32[24]{0:T(128)} %stack.99.meta, bf16[512,768]{1,0:T(8,128)(2,1)} %copy-done.4, bf16[512,768]{1,0:T(8,128)(2,1)} %collective-permute-done.21.refs_1_, bf16[512,768]{1,0:T(8,128)(2,1)} %copy-done.3, bf16[512,768]{1,0:T(8,128)(2,1)} %collective-permute-done.24.refs_3_, bf16[512,768]{1,0:T(8,128)(2,1)} %copy-done.2, ...), custom_call_target="tpu_custom_call" | custom-call | flops 3145728 | bytes 18874368 | tf_op jit(solution)/shard_map/pallas_call | solution.py:18
  392.6 7.9 %shard_map.188 = bf16[2048,512]{1,0:T(8,128)(2,1)} custom-call(s32[24]{0:T(128)} %stack.99.meta, f32[2048,512]{1,0:T(8,128)} %get-tuple-element.40.dn_ref, f32[8,2048]{1,0:T(8,128)} %concatenate.58.row_ref, bf16[2048,2048]{1,0:T(8,128)(2,1)} %bitcast.60, f32[2048,128]{1,0:T(8,128)} %get-tuple-element.38.mu_ref, f32[2048,128]{1,0:T(8,128)} %get-tuple-element.39.inv_ref, ...), custom_call_target="tpu_custom_call" | custom-call | flops 10485760 | bytes 12582912 | tf_op jit(solution)/shard_map/pallas_call | solution.py:18
  (148 shorter events, 28.9 us)
Async XLA Ops:
  3.4 22.7 %collective-permute-start.2 = (bf16[2048,128]{1,0:T(8,128)(2,1)S(1)}, bf16[2048,128]{1,0:T(8,128)(2,1)S(1)}, u32[]{:S(2)}, u32[]{:S(2)}) collective-permute-start(bf16[2048,128]{1,0:T(8,128)(2,1)S(1)} %get-tuple-element.59), channel_id=1, source_target_pairs={{0,1},{1,0},{2,3},{3,2},{4,5},{5,4},{6,7},{7,6},{8,9},{9,8},{10,11... | collective-permute-start | bytes 1572872 | tf_op jit(solution)/shard_map/ppermute | solution.py:590
  8.3 29.7 %collective-permute-start.5 = (bf16[2048,256]{1,0:T(8,128)(2,1)}, bf16[2048,256]{1,0:T(8,128)(2,1)}, u32[]{:S(2)}, u32[]{:S(2)}) collective-permute-start(bf16[2048,256]{1,0:T(8,128)(2,1)} %get-tuple-element.53), channel_id=1, source_target_pairs={{0,1},{1,0},{2,3},{3,2},{4,5},{5,4},{6,7},{7,6},{8,9},{9,8},{10,11... | collective-permute-start | bytes 3145736 | tf_op jit(solution)/shard_map/ppermute | solution.py:590
  8.3 21.1 %collective-permute-start.3 = (bf16[2048,128]{1,0:T(8,128)(2,1)}, bf16[2048,128]{1,0:T(8,128)(2,1)}, u32[]{:S(2)}, u32[]{:S(2)}) collective-permute-start(bf16[2048,128]{1,0:T(8,128)(2,1)} %get-tuple-element.58), channel_id=1, source_target_pairs={{0,2},{1,3},{2,0},{3,1},{4,6},{5,7},{6,4},{7,5},{8,10},{9,11},{10,... | collective-permute-start | bytes 1572872 | tf_op jit(solution)/shard_map/ppermute | solution.py:590
  11.3 26.5 %collective-permute-start.4 = (bf16[2048,128]{1,0:T(8,128)(2,1)}, bf16[2048,128]{1,0:T(8,128)(2,1)S(1)}, u32[]{:S(2)}, u32[]{:S(2)}) collective-permute-start(bf16[2048,128]{1,0:T(8,128)(2,1)} %get-tuple-element.57), channel_id=1, source_target_pairs={{0,3},{1,2},{2,1},{3,0},{4,7},{5,6},{6,5},{7,4},{8,11},{9,10},{10,... | collective-permute-start | bytes 1572872 | tf_op jit(solution)/shard_map/ppermute | solution.py:590
  11.3 73.4 %collective-permute-start = (bf16[2048,256]{1,0:T(8,128)(2,1)}, bf16[2048,256]{1,0:T(8,128)(2,1)S(1)}, u32[]{:S(2)}, u32[]{:S(2)}) collective-permute-start(bf16[2048,256]{1,0:T(8,128)(2,1)} %get-tuple-element.55), channel_id=1, source_target_pairs={{0,2},{1,3},{2,0},{3,1},{4,6},{5,7},{6,4},{7,5},{8,10},{9,11},{10,... | collective-permute-start | bytes 3145736 | tf_op jit(solution)/shard_map/ppermute | solution.py:590
  26.9 57.9 %collective-permute-start.1 = (bf16[2048,256]{1,0:T(8,128)(2,1)}, bf16[2048,256]{1,0:T(8,128)(2,1)S(1)}, u32[]{:S(2)}, u32[]{:S(2)}) collective-permute-start(bf16[2048,256]{1,0:T(8,128)(2,1)} %get-tuple-element.54), channel_id=1, source_target_pairs={{0,3},{1,2},{2,1},{3,0},{4,7},{5,6},{6,5},{7,4},{8,11},{9,10},{10,... | collective-permute-start | bytes 3145736 | tf_op jit(solution)/shard_map/ppermute | solution.py:590
  137.4 106.1 %collective-permute-start.6 = (bf16[2,2048,512]{2,1,0:T(8,128)(2,1)}, bf16[2,2048,512]{2,1,0:T(8,128)(2,1)}, u32[]{:S(2)}, u32[]{:S(2)}) collective-permute-start(bf16[2,2048,512]{2,1,0:T(8,128)(2,1)} %shard_map.186), channel_id=1, source_target_pairs={{0,1},{1,0},{2,3},{3,2},{4,5},{5,4},{6,7},{7,6},{8,9},{9,8},{10,11... | collective-permute-start | bytes 12582920 | tf_op jit(solution)/shard_map/ppermute | solution.py:590
  149.4 39.1 %collective-permute-start.28 = (bf16[3,512,256]{2,1,0:T(8,128)(2,1)}, bf16[3,512,256]{2,1,0:T(8,128)(2,1)S(1)}, u32[]{:S(2)}, u32[]{:S(2)}) collective-permute-start(bf16[3,512,256]{2,1,0:T(8,128)(2,1)} %get-tuple-element.50), channel_id=1, source_target_pairs={{0,8},{4,12},{8,0},{12,4},{16,24},{20,28},{24,16},{28,20},{1,9},{5... | collective-permute-start | bytes 2359304 | tf_op jit(solution)/shard_map/ppermute | solution.py:593
  151.0 41.3 %collective-permute-start.25 = (bf16[3,512,256]{2,1,0:T(8,128)(2,1)}, bf16[3,512,256]{2,1,0:T(8,128)(2,1)S(1)}, u32[]{:S(2)}, u32[]{:S(2)}) collective-permute-start(bf16[3,512,256]{2,1,0:T(8,128)(2,1)} %get-tuple-element.48), channel_id=1, source_target_pairs={{0,4},{4,0},{8,12},{12,8},{16,20},{20,16},{24,28},{28,24},{1,5},{5... | collective-permute-start | bytes 2359304 | tf_op jit(solution)/shard_map/ppermute | solution.py:593
  164.2 30.6 %collective-permute-start.13 = (bf16[3,512,256]{2,1,0:T(8,128)(2,1)}, bf16[3,512,256]{2,1,0:T(8,128)(2,1)S(1)}, u32[]{:S(2)}, u32[]{:S(2)}) collective-permute-start(bf16[3,512,256]{2,1,0:T(8,128)(2,1)} %get-tuple-element.46), channel_id=1, source_target_pairs={{0,8},{4,12},{8,0},{12,4},{16,24},{20,28},{24,16},{28,20},{1,9},{5... | collective-permute-start | bytes 2359304 | tf_op jit(solution)/shard_map/ppermute | solution.py:593
  164.6 31.6 %collective-permute-start.10 = (bf16[3,512,256]{2,1,0:T(8,128)(2,1)}, bf16[3,512,256]{2,1,0:T(8,128)(2,1)S(1)}, u32[]{:S(2)}, u32[]{:S(2)}) collective-permute-start(bf16[3,512,256]{2,1,0:T(8,128)(2,1)} %get-tuple-element.44), channel_id=1, source_target_pairs={{0,4},{4,0},{8,12},{12,8},{16,20},{20,16},{24,28},{28,24},{1,5},{5... | collective-permute-start | bytes 2359304 | tf_op jit(solution)/shard_map/ppermute | solution.py:593
  190.7 20.0 %collective-permute-start.29 = (bf16[3,256,256]{2,1,0:T(8,128)(2,1)}, bf16[3,256,256]{2,1,0:T(8,128)(2,1)S(1)}, u32[]{:S(2)}, u32[]{:S(2)}) collective-permute-start(bf16[3,256,256]{2,1,0:T(8,128)(2,1)} %get-tuple-element.62), channel_id=1, source_target_pairs={{0,4},{4,0},{8,12},{12,8},{16,20},{20,16},{24,28},{28,24},{1,5},{5... | collective-permute-start | bytes 1179656 | tf_op jit(solution)/shard_map/ppermute | solution.py:593
  193.2 20.3 %collective-permute-start.26 = (bf16[3,256,256]{2,1,0:T(8,128)(2,1)}, bf16[3,256,256]{2,1,0:T(8,128)(2,1)S(1)}, u32[]{:S(2)}, u32[]{:S(2)}) collective-permute-start(bf16[3,256,256]{2,1,0:T(8,128)(2,1)} %get-tuple-element.64), channel_id=1, source_target_pairs={{0,8},{4,12},{8,0},{12,4},{16,24},{20,28},{24,16},{28,20},{1,9},{5... | collective-permute-start | bytes 1179656 | tf_op jit(solution)/shard_map/ppermute | solution.py:593
  195.7 18.2 %collective-permute-start.14 = (bf16[3,256,256]{2,1,0:T(8,128)(2,1)}, bf16[3,256,256]{2,1,0:T(8,128)(2,1)S(1)}, u32[]{:S(2)}, u32[]{:S(2)}) collective-permute-start(bf16[3,256,256]{2,1,0:T(8,128)(2,1)} %get-tuple-element.66), channel_id=1, source_target_pairs={{0,4},{4,0},{8,12},{12,8},{16,20},{20,16},{24,28},{28,24},{1,5},{5... | collective-permute-start | bytes 1179656 | tf_op jit(solution)/shard_map/ppermute | solution.py:593
  196.4 20.2 %collective-permute-start.11 = (bf16[3,256,256]{2,1,0:T(8,128)(2,1)S(1)}, bf16[3,256,256]{2,1,0:T(8,128)(2,1)S(1)}, u32[]{:S(2)}, u32[]{:S(2)}) collective-permute-start(bf16[3,256,256]{2,1,0:T(8,128)(2,1)S(1)} %get-tuple-element.68), channel_id=1, source_target_pairs={{0,8},{4,12},{8,0},{12,4},{16,24},{20,28},{24,16},{28,20},{1,9},{5... | collective-permute-start | bytes 1179656 | tf_op jit(solution)/shard_map/ppermute | solution.py:593
  210.8 24.2 %collective-permute-start.30 = (bf16[3,128,256]{2,1,0:T(8,128)(2,1)S(1)}, bf16[3,128,256]{2,1,0:T(8,128)(2,1)S(1)}, u32[]{:S(2)}, u32[]{:S(2)}) collective-permute-start(bf16[3,128,256]{2,1,0:T(8,128)(2,1)S(1)} %add_convert_fusion.10), channel_id=1, source_target_pairs={{0,16},{4,20},{8,24},{12,28},{16,0},{20,4},{24,8},{28,12},{1,17},{... | collective-permute-start | bytes 589832 | tf_op jit(solution)/shard_map/ppermute | solution.py:593
  213.5 25.7 %collective-permute-start.27 = (bf16[3,128,256]{2,1,0:T(8,128)(2,1)S(1)}, bf16[3,128,256]{2,1,0:T(8,128)(2,1)S(1)}, u32[]{:S(2)}, u32[]{:S(2)}) collective-permute-start(bf16[3,128,256]{2,1,0:T(8,128)(2,1)S(1)} %add_convert_fusion.13), channel_id=1, source_target_pairs={{0,16},{4,20},{8,24},{12,28},{16,0},{20,4},{24,8},{28,12},{1,17},{... | collective-permute-start | bytes 589832 | tf_op jit(solution)/shard_map/ppermute | solution.py:593
  214.0 29.6 %copy-start = (bf16[2,2048,512]{2,1,0:T(8,128)(2,1)S(1)}, bf16[2,2048,512]{2,1,0:T(8,128)(2,1)}, u32[]{:S(2)}) copy-start(bf16[2,2048,512]{2,1,0:T(8,128)(2,1)} %shard_map.185.k_ref) | copy-start | bytes 12582916
  214.0 29.4 %collective-permute-start.15 = (bf16[3,128,256]{2,1,0:T(8,128)(2,1)S(1)}, bf16[3,128,256]{2,1,0:T(8,128)(2,1)S(1)}, u32[]{:S(2)}, u32[]{:S(2)}) collective-permute-start(bf16[3,128,256]{2,1,0:T(8,128)(2,1)S(1)} %add_convert_fusion.16), channel_id=1, source_target_pairs={{0,16},{4,20},{8,24},{12,28},{16,0},{20,4},{24,8},{28,12},{1,17},{... | collective-permute-start | bytes 589832 | tf_op jit(solution)/shard_map/ppermute | solution.py:593
  216.7 30.6 %collective-permute-start.12 = (bf16[3,128,256]{2,1,0:T(8,128)(2,1)S(1)}, bf16[3,128,256]{2,1,0:T(8,128)(2,1)S(1)}, u32[]{:S(2)}, u32[]{:S(2)}) collective-permute-start(bf16[3,128,256]{2,1,0:T(8,128)(2,1)S(1)} %add_convert_fusion.19), channel_id=1, source_target_pairs={{0,16},{4,20},{8,24},{12,28},{16,0},{20,4},{24,8},{28,12},{1,17},{... | collective-permute-start | bytes 589832 | tf_op jit(solution)/shard_map/ppermute | solution.py:593
  239.6 8.5 %collective-permute-start.31 = (bf16[256,128]{1,0:T(8,128)(2,1)S(1)}, bf16[256,128]{1,0:T(8,128)(2,1)S(1)}, u32[]{:S(2)}, u32[]{:S(2)}) collective-permute-start(bf16[256,128]{1,0:T(8,128)(2,1)S(1)} %get-tuple-element.72), channel_id=1, source_target_pairs={{0,1},{1,0},{2,3},{3,2},{4,5},{5,4},{6,7},{7,6},{8,9},{9,8},{10,11... | collective-permute-start | bytes 196616 | tf_op jit(solution)/shard_map/ppermute | solution.py:590
  239.8 10.0 %collective-permute-start.32 = (bf16[256,256]{1,0:T(8,128)(2,1)S(1)}, bf16[256,256]{1,0:T(8,128)(2,1)S(1)}, u32[]{:S(2)}, u32[]{:S(2)}) collective-permute-start(bf16[256,256]{1,0:T(8,128)(2,1)S(1)} %get-tuple-element.73), channel_id=1, source_target_pairs={{0,2},{1,3},{2,0},{3,1},{4,6},{5,7},{6,4},{7,5},{8,10},{9,11},{10,... | collective-permute-start | bytes 393224 | tf_op jit(solution)/shard_map/ppermute | solution.py:590
  243.4 6.3 %collective-permute-start.33 = (bf16[256,256]{1,0:T(8,128)(2,1)S(1)}, bf16[256,256]{1,0:T(8,128)(2,1)S(1)}, u32[]{:S(2)}, u32[]{:S(2)}) collective-permute-start(bf16[256,256]{1,0:T(8,128)(2,1)S(1)} %get-tuple-element.74), channel_id=1, source_target_pairs={{0,3},{1,2},{2,1},{3,0},{4,7},{5,6},{6,5},{7,4},{8,11},{9,10},{10,... | collective-permute-start | bytes 393224 | tf_op jit(solution)/shard_map/ppermute | solution.py:590
  245.7 97.2 %collective-permute-start.7 = (bf16[2048,512]{1,0:T(8,128)(2,1)S(1)}, bf16[2048,512]{1,0:T(8,128)(2,1)S(1)}, u32[]{:S(2)}, u32[]{:S(2)}) collective-permute-start(bf16[2048,512]{1,0:T(8,128)(2,1)S(1)} %fusion), channel_id=1, source_target_pairs={{0,2},{1,3},{2,0},{3,1},{4,6},{5,7},{6,4},{7,5},{8,10},{9,11},{10,... | collective-permute-start | bytes 6291464 | tf_op jit(solution)/shard_map/ppermute | solution.py:590
  247.4 49.7 %collective-permute-start.16 = (bf16[256,256]{1,0:T(8,128)(2,1)S(1)}, bf16[256,256]{1,0:T(8,128)(2,1)S(1)}, u32[]{:S(2)}, u32[]{:S(2)}) collective-permute-start(bf16[256,256]{1,0:T(8,128)(2,1)S(1)} %get-tuple-element.78), channel_id=1, source_target_pairs={{0,1},{1,0},{2,3},{3,2},{4,5},{5,4},{6,7},{7,6},{8,9},{9,8},{10,11... | collective-permute-start | bytes 393224 | tf_op jit(solution)/shard_map/ppermute | solution.py:590
  248.2 46.9 %collective-permute-start.17 = (bf16[256,128]{1,0:T(8,128)(2,1)S(1)}, bf16[256,128]{1,0:T(8,128)(2,1)S(1)}, u32[]{:S(2)}, u32[]{:S(2)}) collective-permute-start(bf16[256,128]{1,0:T(8,128)(2,1)S(1)} %get-tuple-element.79), channel_id=1, source_target_pairs={{0,2},{1,3},{2,0},{3,1},{4,6},{5,7},{6,4},{7,5},{8,10},{9,11},{10,... | collective-permute-start | bytes 196616 | tf_op jit(solution)/shard_map/ppermute | solution.py:590
  249.7 47.4 %collective-permute-start.18 = (bf16[256,128]{1,0:T(8,128)(2,1)S(1)}, bf16[256,128]{1,0:T(8,128)(2,1)S(1)}, u32[]{:S(2)}, u32[]{:S(2)}) collective-permute-start(bf16[256,128]{1,0:T(8,128)(2,1)S(1)} %get-tuple-element.80), channel_id=1, source_target_pairs={{0,3},{1,2},{2,1},{3,0},{4,7},{5,6},{6,5},{7,4},{8,11},{9,10},{10,... | collective-permute-start | bytes 196616 | tf_op jit(solution)/shard_map/ppermute | solution.py:590
  249.8 72.0 %copy-start.14 = (f32[8,512]{1,0:T(8,128)S(1)}, f32[8,512]{1,0:T(8,128)}, u32[]{:S(2)}) copy-start(f32[8,512]{1,0:T(8,128)} %get-tuple-element.52) | copy-start | bytes 49156
  249.8 48.3 %collective-permute-start.37 = (bf16[128,768]{1,0:T(8,128)(2,1)S(1)}, bf16[128,768]{1,0:T(8,128)(2,1)S(1)}, u32[]{:S(2)}, u32[]{:S(2)}) collective-permute-start(bf16[128,768]{1,0:T(8,128)(2,1)S(1)} %get-tuple-element.69), channel_id=1, source_target_pairs={{0,16},{4,20},{8,24},{12,28},{16,0},{20,4},{24,8},{28,12},{1,17},{... | collective-permute-start | bytes 589832 | tf_op jit(solution)/shard_map/ppermute | solution.py:593
  295.1 20.9 %collective-permute-start.34 = (bf16[128,768]{1,0:T(8,128)(2,1)S(1)}, bf16[128,768]{1,0:T(8,128)(2,1)S(1)}, u32[]{:S(2)}, u32[]{:S(2)}) collective-permute-start(bf16[128,768]{1,0:T(8,128)(2,1)S(1)} %get-tuple-element.70), channel_id=1, source_target_pairs={{0,16},{4,20},{8,24},{12,28},{16,0},{20,4},{24,8},{28,12},{1,17},{... | collective-permute-start | bytes 589832 | tf_op jit(solution)/shard_map/ppermute | solution.py:593
  297.2 23.1 %collective-permute-start.22 = (bf16[128,768]{1,0:T(8,128)(2,1)S(1)}, bf16[128,768]{1,0:T(8,128)(2,1)S(1)}, u32[]{:S(2)}, u32[]{:S(2)}) collective-permute-start(bf16[128,768]{1,0:T(8,128)(2,1)S(1)} %get-tuple-element.75), channel_id=1, source_target_pairs={{0,16},{4,20},{8,24},{12,28},{16,0},{20,4},{24,8},{28,12},{1,17},{... | collective-permute-start | bytes 589832 | tf_op jit(solution)/shard_map/ppermute | solution.py:593
  298.2 26.4 %collective-permute-start.38 = (bf16[256,768]{1,0:T(8,128)(2,1)S(1)}, bf16[256,768]{1,0:T(8,128)(2,1)S(1)}, u32[]{:S(2)}, u32[]{:S(2)}) collective-permute-start(bf16[256,768]{1,0:T(8,128)(2,1)S(1)} %pad_maximum_fusion.10), channel_id=1, source_target_pairs={{0,4},{4,0},{8,12},{12,8},{16,20},{20,16},{24,28},{28,24},{1,5},{5... | collective-permute-start | bytes 1179656 | tf_op jit(solution)/shard_map/ppermute | solution.py:593
  299.4 25.1 %collective-permute-start.19 = (bf16[128,768]{1,0:T(8,128)(2,1)S(1)}, bf16[128,768]{1,0:T(8,128)(2,1)S(1)}, u32[]{:S(2)}, u32[]{:S(2)}) collective-permute-start(bf16[128,768]{1,0:T(8,128)(2,1)S(1)} %get-tuple-element.76), channel_id=1, source_target_pairs={{0,16},{4,20},{8,24},{12,28},{16,0},{20,4},{24,8},{28,12},{1,17},{... | collective-permute-start | bytes 589832 | tf_op jit(solution)/shard_map/ppermute | solution.py:593
  316.0 16.9 %collective-permute-start.35 = (bf16[256,768]{1,0:T(8,128)(2,1)S(1)}, bf16[256,768]{1,0:T(8,128)(2,1)S(1)}, u32[]{:S(2)}, u32[]{:S(2)}) collective-permute-start(bf16[256,768]{1,0:T(8,128)(2,1)S(1)} %pad_maximum_fusion.9), channel_id=1, source_target_pairs={{0,8},{4,12},{8,0},{12,4},{16,24},{20,28},{24,16},{28,20},{1,9},{5... | collective-permute-start | bytes 1179656 | tf_op jit(solution)/shard_map/ppermute | solution.py:593
  320.3 14.2 %collective-permute-start.23 = (bf16[256,768]{1,0:T(8,128)(2,1)S(1)}, bf16[256,768]{1,0:T(8,128)(2,1)S(1)}, u32[]{:S(2)}, u32[]{:S(2)}) collective-permute-start(bf16[256,768]{1,0:T(8,128)(2,1)S(1)} %pad_maximum_fusion.7), channel_id=1, source_target_pairs={{0,4},{4,0},{8,12},{12,8},{16,20},{20,16},{24,28},{28,24},{1,5},{5... | collective-permute-start | bytes 1179656 | tf_op jit(solution)/shard_map/ppermute | solution.py:593
  324.5 16.8 %collective-permute-start.20 = (bf16[256,768]{1,0:T(8,128)(2,1)S(1)}, bf16[256,768]{1,0:T(8,128)(2,1)S(1)}, u32[]{:S(2)}, u32[]{:S(2)}) collective-permute-start(bf16[256,768]{1,0:T(8,128)(2,1)S(1)} %pad_maximum_fusion.6), channel_id=1, source_target_pairs={{0,8},{4,12},{8,0},{12,4},{16,24},{20,28},{24,16},{28,20},{1,9},{5... | collective-permute-start | bytes 1179656 | tf_op jit(solution)/shard_map/ppermute | solution.py:593
  324.7 16.7 %copy-start.1 = (bf16[512,768]{1,0:T(8,128)(2,1)}, bf16[512,768]{1,0:T(8,128)(2,1)S(1)}, u32[]{:S(2)}) copy-start(bf16[512,768]{1,0:T(8,128)(2,1)S(1)} %pad_maximum_fusion.4.refs_6_) | copy-start | bytes 2359300
  324.7 51.6 %collective-permute-start.39 = (bf16[512,768]{1,0:T(8,128)(2,1)S(1)}, bf16[512,768]{1,0:T(8,128)(2,1)S(1)}, u32[]{:S(2)}, u32[]{:S(2)}) collective-permute-start(bf16[512,768]{1,0:T(8,128)(2,1)S(1)} %pad_maximum_fusion.4.refs_6_), channel_id=1, source_target_pairs={{0,8},{4,12},{8,0},{12,4},{16,24},{20,28},{24,16},{28,20},{1,9},{5... | collective-permute-start | bytes 2359304 | tf_op jit(solution)/shard_map/ppermute | solution.py:593
  332.9 23.2 %copy-start.2 = (bf16[512,768]{1,0:T(8,128)(2,1)}, bf16[512,768]{1,0:T(8,128)(2,1)S(1)}, u32[]{:S(2)}) copy-start(bf16[512,768]{1,0:T(8,128)(2,1)S(1)} %pad_maximum_fusion.3.refs_4_) | copy-start | bytes 2359300
  333.0 43.4 %collective-permute-start.36 = (bf16[512,768]{1,0:T(8,128)(2,1)S(1)}, bf16[512,768]{1,0:T(8,128)(2,1)}, u32[]{:S(2)}, u32[]{:S(2)}) collective-permute-start(bf16[512,768]{1,0:T(8,128)(2,1)S(1)} %pad_maximum_fusion.3.refs_4_), channel_id=1, source_target_pairs={{0,4},{4,0},{8,12},{12,8},{16,20},{20,16},{24,28},{28,24},{1,5},{5... | collective-permute-start | bytes 2359304 | tf_op jit(solution)/shard_map/ppermute | solution.py:593
  334.6 21.6 %copy-start.3 = (bf16[512,768]{1,0:T(8,128)(2,1)}, bf16[512,768]{1,0:T(8,128)(2,1)S(1)}, u32[]{:S(2)}) copy-start(bf16[512,768]{1,0:T(8,128)(2,1)S(1)} %pad_maximum_fusion.2.refs_2_) | copy-start | bytes 2359300
  334.6 41.8 %collective-permute-start.24 = (bf16[512,768]{1,0:T(8,128)(2,1)S(1)}, bf16[512,768]{1,0:T(8,128)(2,1)}, u32[]{:S(2)}, u32[]{:S(2)}) collective-permute-start(bf16[512,768]{1,0:T(8,128)(2,1)S(1)} %pad_maximum_fusion.2.refs_2_), channel_id=1, source_target_pairs={{0,8},{4,12},{8,0},{12,4},{16,24},{20,28},{24,16},{28,20},{1,9},{5... | collective-permute-start | bytes 2359304 | tf_op jit(solution)/shard_map/ppermute | solution.py:593
  341.4 35.0 %collective-permute-start.21 = (bf16[512,768]{1,0:T(8,128)(2,1)S(1)}, bf16[512,768]{1,0:T(8,128)(2,1)}, u32[]{:S(2)}, u32[]{:S(2)}) collective-permute-start(bf16[512,768]{1,0:T(8,128)(2,1)S(1)} %pad_maximum_fusion.1.refs_0_), channel_id=1, source_target_pairs={{0,4},{4,0},{8,12},{12,8},{16,20},{20,16},{24,28},{28,24},{1,5},{5... | collective-permute-start | bytes 2359304 | tf_op jit(solution)/shard_map/ppermute | solution.py:593
  356.9 12.7 %collective-permute-start.40 = (f32[6,512]{1,0:T(8,128)S(1)}, f32[6,512]{1,0:T(8,128)S(1)}, u32[]{:S(2)}, u32[]{:S(2)}) collective-permute-start(f32[6,512]{1,0:T(8,128)S(1)} %pad_maximum_fusion.11), channel_id=1, source_target_pairs={{0,4},{4,0},{8,12},{12,8},{16,20},{20,16},{24,28},{28,24},{1,5},{5... | collective-permute-start | bytes 36872 | tf_op jit(solution)/shard_map/ppermute | solution.py:593
  369.6 1.2 collective-permute-start.8
  370.8 4.5 %collective-permute-start.41 = (f32[6,512]{1,0:T(8,128)S(1)}, f32[6,512]{1,0:T(8,128)S(1)}, u32[]{:S(2)}, u32[]{:S(2)}) collective-permute-start(f32[6,512]{1,0:T(8,128)S(1)} %fusion.17), channel_id=1, source_target_pairs={{0,8},{4,12},{8,0},{12,4},{16,24},{20,28},{24,16},{28,20},{1,9},{5... | collective-permute-start | bytes 36872 | tf_op jit(solution)/shard_map/ppermute | solution.py:593
  375.3 16.7 %collective-permute-start.9 = (f32[2,2048]{1,0:T(2,128)S(1)}, f32[2,2048]{1,0:T(2,128)S(1)}, u32[]{:S(2)}, u32[]{:S(2)}) collective-permute-start(f32[2,2048]{1,0:T(2,128)S(1)} %slice_add_fusion), channel_id=1, source_target_pairs={{0,2},{1,3},{2,0},{3,1},{4,6},{5,7},{6,4},{7,5},{8,10},{9,11},{10,... | collective-permute-start | bytes 49160 | tf_op jit(solution)/shard_map/ppermute | solution.py:590
  376.3 24.3 %collective-permute-start.42 = (f32[6,512]{1,0:T(8,128)S(1)}, f32[6,512]{1,0:T(8,128)S(1)}, u32[]{:S(2)}, u32[]{:S(2)}) collective-permute-start(f32[6,512]{1,0:T(8,128)S(1)} %add.328), channel_id=1, source_target_pairs={{0,16},{4,20},{8,24},{12,28},{16,0},{20,4},{24,8},{28,12},{1,17},{... | collective-permute-start | bytes 36872 | tf_op jit(solution)/shard_map/ppermute | solution.py:593
  (16 other events, 99.1 us)

commit v2 on v0

v2 whole, which is shorter than its diff:
```python
import functools

import jax
import jax.numpy as jnp
from jax import lax
from jax.experimental import pallas as pl
from jax.experimental.pallas import tpu as pltpu
from jax.sharding import PartitionSpec as P

epsilon = 1e-05
F32 = jnp.float32
BF16 = jnp.bfloat16
LANES = 128
VMEM_LIMIT = 60 * 1024 * 1024


def call(kernel, meta, args, grid, in_specs, out_specs, out_shape, scratch=(), aliases=None, cost=None):
    return pl.pallas_call(
        kernel,
        grid_spec=pltpu.PrefetchScalarGridSpec(
            num_scalar_prefetch=1,
            grid=grid,
            in_specs=in_specs,
            out_specs=out_specs,
            scratch_shapes=list(scratch),
        ),
        out_shape=out_shape,
        input_output_aliases=aliases or {},
        compiler_params=pltpu.CompilerParams(
            dimension_semantics=("arbitrary",) * len(grid), vmem_limit_bytes=VMEM_LIMIT
        ),
        cost_estimate=cost,
    )(meta, *args)


def cost(flops, nbytes, trans=0):
    return pl.CostEstimate(flops=int(flops), bytes_accessed=int(nbytes), transcendentals=int(trans))


def struct(shape, dtype):
    return jax.ShapeDtypeStruct(shape, dtype)


TILE = 256


def order_matrix():
    row = lax.broadcasted_iota(jnp.int32, (TILE, TILE), 0)
    token = lax.broadcasted_iota(jnp.int32, (TILE, TILE), 1)
    return jnp.where(token == (row % 8) * (TILE // 8) + row // 8, 1.0, 0.0).astype(BF16)


def to_rows(order, value):
    return jnp.dot(order, value, preferred_element_type=F32)


def to_tokens(order, value):
    return lax.dot_general(order, value, (((0,), (0,)), ((), ())), preferred_element_type=F32)


def norm_kernel(
    meta, x_ref, gain_ref, bias_ref, res_ref, pad_ref, out_ref, mu_ref, inv_ref, own_ref, keep_ref, live_ref, PM, XP, S1, S2
):
    @pl.when(pl.program_id(0) == 0)
    def _():
        PM[...] = order_matrix()

    order = PM[...]
    features = x_ref.shape[1]
    groups = features // LANES
    wide = 2 * LANES
    ones = jnp.ones((TILE, LANES), BF16)
    keep_ref[...] = jnp.dot(order * (1 - res_ref[0]).astype(F32).astype(BF16), ones, preferred_element_type=F32)
    live_ref[...] = jnp.dot(order * pad_ref[0].astype(F32).astype(BF16), ones, preferred_element_type=F32)
    shift = None
    first = second = None
    for g in range(0, features, wide):
        value = to_rows(order, x_ref[:, g : g + wide])
        XP[:, g : g + wide] = value
        if shift is None:
            shift = jnp.broadcast_to(value[:, 0:1], (TILE, LANES))
            S1[...] = shift
        one, two = value[:, :LANES] - shift, value[:, LANES:] - shift
        first = one + two if first is None else first + (one + two)
        squares = one * one + two * two
        second = squares if second is None else second + squares
    drift = jnp.sum(first, axis=1, keepdims=True) * (1.0 / features)
    spread = jnp.sum(second, axis=1, keepdims=True) * (1.0 / features) - drift * drift
    mu_ref[...] = shift + drift
    inv_ref[...] = jnp.broadcast_to(lax.rsqrt(jnp.maximum(spread, 0.0) + epsilon), inv_ref.shape)
    tall = 16

    def scaled(i, carry):
        rows = pl.ds(pl.multiple_of(i * tall, tall), tall)
        mean = mu_ref[rows, :]
        scale = inv_ref[rows, :]
        for g in range(groups):
            at = slice(g * LANES, (g + 1) * LANES)
            value = (XP[rows, at] - mean) * scale * gain_ref[0:1, at] + bias_ref[0:1, at]
            out_ref[rows, at] = value.astype(BF16)
        return carry

    lax.fori_loop(0, TILE // tall, scaled, 0, unroll=2)
    channels = own_ref.shape[1]
    own_ref[...] = XP[:, pl.ds(pl.multiple_of(meta[M_GATE] * channels, channels), channels)].astype(BF16)


def norm(meta, x, gain, bias, resets, padding, channels):
    tokens, features = x.shape
    tiles = tokens // TILE
    row = pl.BlockSpec((TILE, features), lambda t, m: (t, 0))
    whole = pl.BlockSpec((1, features), lambda t, m: (0, 0))
    flag = pl.BlockSpec((1, 1, TILE), lambda t, m: (t, 0, 0))
    stat = pl.BlockSpec((TILE, LANES), lambda t, m: (t, 0))
    stats = struct((tokens, LANES), F32)
    return call(
        norm_kernel,
        meta,
        (x, gain[None], bias[None], resets.reshape(tiles, 1, TILE), padding.reshape(tiles, 1, TILE)),
        (tiles,),
        [row, whole, whole, flag, flag],
        [row, stat, stat, pl.BlockSpec((TILE, channels), lambda t, m: (t, 0)), stat, stat],
        [struct(x.shape, BF16), stats, stats, struct((tokens, channels), BF16), stats, stats],
        scratch=[pltpu.VMEM((TILE, TILE), BF16), pltpu.VMEM((TILE, features), F32)] + [pltpu.VMEM((TILE, LANES), F32)] * 2,
        cost=cost(8 * tokens * features, 4 * tokens * features),
    )


def column_of(meta, table, plane, block):
    blk = block ^ meta[M_CORE] if plane == 2 else block
    return pl.multiple_of((blk * 3 + meta[table + plane]) * LANES, LANES)


def cut_kernel(widths, meta, *refs):
    for n, width in enumerate(widths):
        out_ref = refs[sum(widths) + n]
        for b in range(width):
            out_ref[:, b * LANES : (b + 1) * LANES] = refs[sum(widths[:n]) + b][...]


def cut(meta, weight, pieces, tb=512):
    rows = weight.shape[0]
    widths = [width for _, width in pieces]
    specs = [
        pl.BlockSpec((tb, LANES), lambda t, m, at=at, b=b: (t, m[at] + b)) for at, width in pieces for b in range(width)
    ]
    return call(
        functools.partial(cut_kernel, widths),
        meta,
        [weight] * len(specs),
        (rows // tb,),
        specs,
        [pl.BlockSpec((tb, width * LANES), lambda t, m: (t, 0)) for width in widths],
        [struct((rows, width * LANES), BF16) for width in widths],
        cost=cost(0, 4 * rows * LANES * sum(widths)),
    )


def unit_specs(units, rows, row_of):
    return [pl.BlockSpec((rows, LANES), lambda *i, at=at, b=b: (row_of(*i), (i[-1][at] if at else 0) + b)) for _, at, b in units]


def gather_units(meta, table, refs, W, base):
    for n, ref in enumerate(refs):
        at = pl.multiple_of(base + column_of(meta, table, n // 2, n % 2), LANES)
        W[:, pl.ds(at, LANES)] = ref[...]


def project_kernel(table, meta, normed_ref, *refs):
    out_ref, W = refs[-2:]

    @pl.when(pl.program_id(0) == 0)
    def _():
        gather_units(meta, table, refs[:6], W, 0)

    out_ref[...] = jnp.dot(normed_ref[...], W[...], preferred_element_type=F32).astype(BF16)


def project(meta, table, normed, units, tb=512):
    tokens, features = normed.shape
    columns = 6 * LANES
    return call(
        functools.partial(project_kernel, table),
        meta,
        [normed] + [array for array, _, _ in units],
        (tokens // tb,),
        [pl.BlockSpec((tb, features), lambda t, m: (t, 0))] + unit_specs(units, features, lambda t, m: 0),
        pl.BlockSpec((tb, columns), lambda t, m: (t, 0)),
        struct((tokens, columns), BF16),
        scratch=[pltpu.VMEM((features, columns), BF16)],
        cost=cost(2 * tokens * features * columns, 2 * tokens * (features + 2 * columns)),
    )


def sigmoid(z):
    return 0.5 * jnp.tanh(0.5 * z) + 0.5


def scan_kernel(meta, u_ref, x_ref, g_ref, keep_ref, live_ref, prm_ref, *refs):
    (hid_ref, ds_ref, direct_ref, vec_ref, PM, A, B, FG, R, PV, GL, XF, UT, HP, CE, PE, CI, EI) = refs[-18:]
    length = x_ref.shape[0]
    tiles = length // TILE
    seg = TILE // 8
    rows_in = 64
    each = TILE // rows_in
    groups = rows_in // 8
    pf, pr, bf, br = (jnp.broadcast_to(prm_ref[i : i + 1, :], (rows_in, LANES)) for i in range(4))

    @pl.when(pl.program_id(0) == 0)
    def _():
        PM[...] = order_matrix()

    order = PM[...]
    for q in range(tiles):
        GL[q * TILE : (q + 1) * TILE, :] = to_rows(order, g_ref[q * TILE : (q + 1) * TILE, :])

    zeros = jnp.zeros((8, LANES), F32)
    ones = jnp.ones((8, LANES), F32)

    def rows_at(i):
        return pl.ds(pl.multiple_of(i * rows_in, rows_in), rows_in)

    def tile_at(i):
        return pl.ds(pl.multiple_of((i // each) * 8, 8), 8)

    def gates(i, carry):
        rows = rows_at(i)
        x = x_ref[rows, :].astype(F32)
        ut = u_ref[rows, 0:LANES].astype(F32)
        forget = sigmoid(u_ref[rows, LANES : 2 * LANES].astype(F32) + pf * x + bf)
        reset = sigmoid(u_ref[rows, 2 * LANES :].astype(F32) + pr * x + br)
        a = forget * keep_ref[rows, :]
        b = (1.0 - forget) * ut
        gl = GL[rows, :] * live_ref[rows, :]
        d = gl * reset
        XF[rows, :] = x
        UT[rows, :] = ut
        FG[rows, :] = forget
        R[rows, :] = reset
        A[rows, :] = a
        B[rows, :] = b
        GL[rows, :] = gl
        fresh = i % each == 0
        c, p, e = (jnp.where(fresh, start, old) for start, old in zip((zeros, ones, zeros), carry))
        for j in range(groups):
            at = slice(8 * j, 8 * j + 8)
            c = a[at] * c + b[at]
            p = a[at] * p
            e = e + p * d[at]
        CE[tile_at(i), :] = c
        PE[tile_at(i), :] = p
        EI[tile_at(i), :] = e
        return (c, p, e)

    lax.fori_loop(0, tiles * each, gates, (zeros, ones, zeros))

    count = 8 * tiles
    c = jnp.zeros((1, LANES), F32)
    e = jnp.zeros((1, LANES), F32)
    for j in range(count):
        CI[j : j + 1, :] = c
        c = CE[j : j + 1, :] + PE[j : j + 1, :] * c
        r = count - 1 - j
        own = EI[r : r + 1, :]
        EI[r : r + 1, :] = e
        e = own + PE[r : r + 1, :] * e

    def forward(i, carry):
        out = []
        for q in range(tiles):
            rows = pl.ds(pl.multiple_of(q * TILE + i * 8, 8), 8)
            PV[rows, :] = carry[q]
            out.append(A[rows, :] * carry[q] + B[rows, :])
        return tuple(out)

    lax.fori_loop(0, seg, forward, tuple(CI[8 * q : 8 * q + 8, :] for q in range(tiles)), unroll=4)

    def fold(v):
        return v.reshape(groups, 8, LANES).sum(axis=0)

    def grads(n, carry):
        i = tiles * each - 1 - n
        rows = rows_at(i)
        e, s0, s1, s2, s3 = carry
        e = jnp.where(n % each == 0, EI[tile_at(i), :], e)
        g = GL[rows, :]
        reset = R[rows, :]
        a = A[rows, :]
        d = g * reset
        dcs = [None] * groups
        for j in reversed(range(groups)):
            at = slice(8 * j, 8 * j + 8)
            dcs[j] = d[at] + e
            e = a[at] * dcs[j]
        dc = jnp.concatenate(dcs, axis=0)
        x = XF[rows, :]
        forget = FG[rows, :]
        prev = PV[rows, :]
        gap = a * prev + B[rows, :] - x
        HP[rows, :] = (live_ref[rows, :] * (x + reset * gap)).astype(BF16)
        rest = 1.0 - reset
        dreset = g * gap * (reset * rest)
        dtilde = dc * (1.0 - forget)
        dforget = dtilde * forget * (prev * keep_ref[rows, :] - UT[rows, :])
        ds_ref[rows, 0:LANES] = dtilde.astype(BF16)
        ds_ref[rows, LANES : 2 * LANES] = dforget.astype(BF16)
        ds_ref[rows, 2 * LANES :] = dreset.astype(BF16)
        direct_ref[rows, :] = (g * rest + dforget * pf + dreset * pr).astype(BF16)
        return (e, s0 + fold(dforget * x), s1 + fold(dreset * x), s2 + fold(dforget), s3 + fold(dreset))

    sums = lax.fori_loop(0, tiles * each, grads, (zeros,) * 5)[1:]
    for n, s in enumerate(sums):
        vec_ref[n : n + 1, :] = jnp.sum(s, axis=0, keepdims=True)
    vec_ref[4:8, :] = jnp.zeros((4, LANES), F32)
    for q in range(tiles):
        at = slice(q * TILE, (q + 1) * TILE)
        hid_ref[at, :] = to_tokens(order, HP[at, :]).astype(BF16)


def scan(meta, half, u, x, grad, keep, live, params, earlier):
    length, channels = x.shape
    blocks = u.shape[1] // (3 * LANES)
    col = lambda k, m: (0, m[half] * blocks + k)
    tall = (length, LANES)
    chunk = pl.BlockSpec((length, 3 * LANES), lambda k, m: (0, k))
    fixed = pl.BlockSpec(tall, lambda k, m: (0, 0))
    own = pl.BlockSpec(tall, col)
    small = pl.BlockSpec((8, LANES), col)
    in_specs = [chunk, own, own, fixed, fixed, small]
    args = [u, x, grad, keep, live, params]
    aliases = None
    if earlier is not None:
        aliases = {len(args) + 1: 0, len(args) + 2: 2, len(args) + 3: 3}
        args += list(earlier)
        in_specs += [pl.BlockSpec(memory_space=pl.ANY)] * 3
    ends = pltpu.VMEM((8 * length // TILE, LANES), F32)
    return call(
        scan_kernel,
        meta,
        args,
        (blocks,),
        in_specs,
        [own, chunk, own, small],
        [
            struct((length, channels), BF16),
            struct(u.shape, BF16),
            struct((length, channels), BF16),
            struct((8, channels), F32),
        ],
        scratch=[pltpu.VMEM((TILE, TILE), BF16)]
        + [pltpu.VMEM(tall, F32)] * 8
        + [pltpu.VMEM(tall, BF16)]
        + [ends] * 4,
        aliases=aliases,
        cost=cost(60 * length * channels // 2, 9 * length * channels, length * channels),
    )


def wgrad_kernel(meta, normed_ref, ds_ref, a_ref, b_ref):
    first = pl.program_id(0) < pl.num_programs(0) // 2
    dims = (((0,), (0,)), ((), ()))

    @pl.when(first)
    def _():
        a_ref[...] = lax.dot_general(normed_ref[...], ds_ref[...], dims, preferred_element_type=F32).astype(BF16)

    @pl.when(jnp.logical_not(first))
    def _():
        b_ref[...] = lax.dot_general(normed_ref[...], ds_ref[...], dims, preferred_element_type=F32).astype(BF16)


def wgrad(meta, normed, ds, first, mb=512):
    tokens, features = normed.shape
    width = ds.shape[1]
    rows = features // 4
    steps = rows // mb

    def lhs(i, m):
        return (0, m[first + i // steps] * steps + i % steps)

    return call(
        wgrad_kernel,
        meta,
        (normed, ds),
        (2 * steps,),
        [
            pl.BlockSpec((tokens, mb), lhs),
            pl.BlockSpec((tokens, width), lambda i, m: (0, 0)),
        ],
        [
            pl.BlockSpec((mb, width), lambda i, m: (jnp.minimum(i, steps - 1), 0)),
            pl.BlockSpec((mb, width), lambda i, m: (jnp.maximum(i - steps, 0), 0)),
        ],
        [struct((rows, width), BF16)] * 2,
        cost=cost(4 * tokens * rows * width, 2 * tokens * (features // 2 + width)),
    )


def back_kernel(meta, ds1_ref, ds2_ref, *refs):
    out_ref, W = refs[-2:]
    chunk = ds1_ref.shape[1]

    @pl.when(pl.program_id(1) == 0)
    def _():
        gather_units(meta, M_S1, refs[:6], W, 0)
        gather_units(meta, M_S2, refs[6:12], W, chunk)

    dims = (((1,), (1,)), ((), ()))
    value = lax.dot_general(ds1_ref[...], W[:, :chunk], dims, preferred_element_type=F32)
    value += lax.dot_general(ds2_ref[...], W[:, chunk:], dims, preferred_element_type=F32)
    out_ref[0] = value.astype(BF16)


def back(meta, ds1, ds2, units, first, tb=1024):
    tokens, width = ds1.shape
    features = units[0][0].shape[0]
    block = features // 4
    dspec = pl.BlockSpec((tb, width), lambda n, t, m: (t, 0))
    return call(
        back_kernel,
        meta,
        [ds1, ds2] + [array for array, _, _ in units],
        (2, tokens // tb),
        [dspec, dspec] + unit_specs(units, block, lambda n, t, m: m[first + n]),
        pl.BlockSpec((1, tb, block), lambda n, t, m: (n, t, 0)),
        struct((2, tokens, block), BF16),
        scratch=[pltpu.VMEM((block, 2 * width), BF16)],
        cost=cost(8 * tokens * block * width, 8 * tokens * width),
    )


def unit_of(x_ref, mu_ref, inv_ref):
    repeat = x_ref.shape[1] // LANES
    mu = jnp.concatenate([mu_ref[...]] * repeat, axis=1)
    inv = jnp.concatenate([inv_ref[...]] * repeat, axis=1)
    return (x_ref[...].astype(F32) - mu) * inv, inv


def lane_sums(value):
    part = value[:, :LANES]
    for g in range(1, value.shape[1] // LANES):
        part = part + value[:, g * LANES : (g + 1) * LANES]
    return jnp.sum(part.T, axis=0, keepdims=True)


def tail_sums_kernel(meta, k_ref, rc_ref, ry_ref, x_ref, mu_ref, inv_ref, gain_ref, dn_ref, row_ref, col_ref):
    unit, _ = unit_of(x_ref, mu_ref, inv_ref)
    dn = k_ref[0].astype(F32) + rc_ref[0].astype(F32) + ry_ref[...].astype(F32)
    dn_ref[...] = dn
    gu = dn * gain_ref[...]
    row_ref[0:1, :] = lane_sums(gu)
    row_ref[1:2, :] = lane_sums(gu * unit)
    row_ref[2:8, :] = jnp.zeros((6, row_ref.shape[1]), F32)

    @pl.when(pl.program_id(0) == 0)
    def _():
        col_ref[...] = jnp.zeros_like(col_ref)

    col_ref[0:1, :] += jnp.sum(dn * unit, axis=0, keepdims=True)
    col_ref[1:2, :] += jnp.sum(dn, axis=0, keepdims=True)


def tail_sums(meta, keep, got, far, x, mu, inv, gain, tb=512):
    tokens, channels = far.shape
    part = pl.BlockSpec((1, tb, channels), lambda t, m: (1, t, 0))
    wide = pl.BlockSpec((tb, channels), lambda t, m: (t, 0))
    stat = pl.BlockSpec((tb, LANES), lambda t, m: (t, 0))
    return call(
        tail_sums_kernel,
        meta,
        (keep, got, far, x, mu, inv, gain[None]),
        (tokens // tb,),
        [part, part, wide, wide, stat, stat, pl.BlockSpec((1, channels), lambda t, m: (0, m[M_GATE]))],
        [
            wide,
            pl.BlockSpec((8, tb), lambda t, m: (0, t)),
            pl.BlockSpec((8, channels), lambda t, m: (0, 0)),
        ],
        [struct((tokens, channels), F32), struct((8, tokens), F32), struct((8, channels), F32)],
        cost=cost(20 * tokens * channels, 12 * tokens * channels),
    )


def tail_kernel(features, meta, dn_ref, row_ref, x_ref, mu_ref, inv_ref, gain_ref, direct_ref, out_ref, PM):
    @pl.when(pl.program_id(0) == 0)
    def _():
        PM[...] = order_matrix()

    unit, inv = unit_of(x_ref, mu_ref, inv_ref)
    repeat = x_ref.shape[1] // LANES
    tb = x_ref.shape[0]

    def mean(n):
        row = row_ref[n : n + 1, :] * (1.0 / features)
        return jnp.concatenate([jnp.broadcast_to(row, (LANES, tb)).T] * repeat, axis=1)

    gu = dn_ref[...] * gain_ref[...]
    value = (inv * (gu - mean(0) - unit * mean(1)) + direct_ref[...].astype(F32)).astype(BF16)
    for q in range(tb // TILE):
        at = slice(q * TILE, (q + 1) * TILE)
        out_ref[at, :] = to_tokens(PM[...], value[at]).astype(BF16)


def tail(meta, dn, rows, x, mu, inv, gain, direct, features, tb=512):
    tokens, channels = dn.shape
    wide = pl.BlockSpec((tb, channels), lambda t, m: (t, 0))
    stat = pl.BlockSpec((tb, LANES), lambda t, m: (t, 0))
    return call(
        functools.partial(tail_kernel, features),
        meta,
        (dn, rows, x, mu, inv, gain[None], direct),
        (tokens // tb,),
        [
            wide,
            pl.BlockSpec((rows.shape[0], tb), lambda t, m: (0, t)),
            wide,
            stat,
            stat,
            pl.BlockSpec((1, channels), lambda t, m: (0, m[M_GATE])),
            wide,
        ],
        wide,
        struct((tokens, channels), BF16),
        scratch=[pltpu.VMEM((TILE, TILE), BF16)],
        cost=cost(10 * tokens * channels, 12 * tokens * channels),
    )


def halve_kernel(meta, *refs):
    ins, (away_ref, stay_ref) = refs[:-2], refs[-2:]
    for n, out_ref in ((0, away_ref), (1, stay_ref)):
        part = ins[n * len(ins) // 2 : (n + 1) * len(ins) // 2]
        if len(part) == 4:
            for o in range(2):
                out_ref[o] = (part[o][...].astype(F32) + part[2 + o][...].astype(F32)).astype(BF16)
        else:
            out_ref[...] = (part[0][...].astype(F32) + part[1][...].astype(F32)).astype(BF16)


def halve(meta, at, kept, got, parts=2):
    if len(kept) == 2:
        rows, width = kept[0].shape
        lead = ()
    else:
        lead, rows, width = kept[0].shape
        lead = (lead,)
    half = rows // 2
    tb = half // parts
    zeros = (0,) * len(lead)
    specs, args = [], []
    for side in range(2):
        for array in (*kept, *got):
            specs.append(
                pl.BlockSpec((*lead, tb, width), lambda i, m, side=side: (*zeros, (m[at] ^ (1 - side)) * parts + i, 0))
            )
            args.append(array)
    out = pl.BlockSpec((2, tb, width), lambda i, m: (0, i, 0))
    return call(
        halve_kernel,
        meta,
        args,
        (parts,),
        specs,
        [out, out],
        [struct((2, half, width), BF16)] * 2,
        cost=cost(4 * rows * width, 12 * rows * width),
    )


def split_kernel(late, half, meta, a_ref, b_ref, near_ref, far_ref):
    core = meta[M_CORE]
    h = meta[half]
    pair_ref, single_ref = (far_ref, near_ref) if late else (near_ref, far_ref)

    def take(owner, stream, block):
        col = pl.ds(pl.multiple_of((block * 3 + stream) * LANES, LANES), LANES)
        return (a_ref[owner, :, col].astype(F32) + b_ref[owner, :, col].astype(F32)).astype(BF16)

    for store in range(2):
        k = core ^ store
        for owner in range(2):
            for block in range(2):
                at = (2 * owner + block) * LANES
                pair_ref[store, :, at : at + LANES] = take(owner, k + h, block)
            single_ref[store, :, owner * LANES : (owner + 1) * LANES] = take(owner, 2 * (1 - h), k)


def split(meta, half, late, kept, got):
    _, rows, width = kept.shape
    pair, single = 4 * LANES, 2 * LANES
    widths = (single, pair) if late else (pair, single)
    whole = pl.BlockSpec((2, rows, width), lambda i, m: (0, 0, 0))
    return call(
        functools.partial(split_kernel, late, half),
        meta,
        (kept, got),
        (1,),
        [whole] * 2,
        [pl.BlockSpec((2, rows, w), lambda i, m: (0, 0, 0)) for w in widths],
        [struct((2, rows, w), BF16) for w in widths],
        cost=cost(2 * rows * width, 12 * rows * width),
    )


def join_kernel(meta, a_ref, b_ref, *outs):
    rows = a_ref.shape[1]
    for n, out_ref in enumerate(outs):
        out_ref[:rows, :] = a_ref[n]
        out_ref[rows:, :] = b_ref[n]


def join(meta, a, b):
    _, rows, width = a.shape
    whole = pl.BlockSpec((2, rows, width), lambda i, m: (0, 0, 0))
    out = pl.BlockSpec((2 * rows, width), lambda i, m: (0, 0))
    return call(
        join_kernel,
        meta,
        (a, b),
        (1,),
        [whole] * 2,
        [out] * 2,
        [struct((2 * rows, width), BF16)] * 2,
        cost=cost(0, 16 * rows * width),
    )


def place_kernel(blocks, meta, *refs):
    out_ref = refs[-1]
    step = pl.program_id(0)
    piece = out_ref.shape[1] // 4
    unit = piece // 3
    rows = out_ref.shape[0] // blocks
    core = meta[M_CORE]
    for stream in range(2):
        for part in range(2):

            @pl.when(step == stream * 2 + part)
            def _(stream=stream, part=part):
                one = refs[stream * 2 + part]
                two = refs[4 + stream * 2 + part]
                inner = meta[M_RHO + stream] % blocks

                def put(owner, single, src, col):
                    base = meta[M_OWN + (owner ^ stream)] * piece
                    wide = unit if single else 2 * unit
                    at = base + (jnp.where(core == 0, 2 * unit, 0) if single else core * unit)
                    at = pl.ds(pl.multiple_of(at, LANES), wide)
                    for j in range(blocks):
                        to = pl.ds(pl.multiple_of((inner ^ j) * rows, rows), rows)
                        out_ref[to, at] = src[j * rows : (j + 1) * rows, col : col + wide].astype(F32)

                put(0, False, one, 0)
                put(1, False, one, 2 * unit)
                put(2, True, one, 4 * unit)
                put(3, True, one, 5 * unit)
                put(0, True, two, 0)
                put(1, True, two, unit)
                put(2, False, two, 2 * unit)
                put(3, False, two, 4 * unit)


def place(meta, parts1, parts2, n_dp, features, columns):
    blocks = n_dp // 2
    whole = pl.BlockSpec((features // 4, columns // 2), lambda i, m: (0, 0))

    def where_to(i, m):
        stream = i // 2
        return ((m[M_CORE] ^ stream) * 2 + (i % 2 ^ m[M_RHO + stream] // blocks), 0)

    return call(
        functools.partial(place_kernel, blocks),
        meta,
        (*parts1, *parts2),
        (4,),
        [whole] * 8,
        pl.BlockSpec((features // 4, columns), where_to),
        struct((features, columns), F32),
        cost=cost(features * columns, 6 * features * columns),
    )


M_GATE, M_CORE, M_H1, M_H2 = 0, 1, 2, 3
M_S1, M_S2 = 4, 7
M_SEND, M_KEEP = 10, 12
M_OUT, M_IN = 14, 16
M_OWN, M_RHO = 18, 22
M_TO2, M_TO3, M_NEAR, M_LATE2, M_LATE3 = 24, 25, 26, 27, 28
M_PAIR, M_SINGLE, M_GOT_PAIR, M_GOT_SINGLE = 29, 30, 31, 32
M_BIT = 33


def shards(
    n_dp,
    n_gate,
    inputs,
    weight,
    ln_gain,
    ln_bias,
    forget_peep,
    reset_peep,
    forget_bias,
    reset_bias,
    resets,
    padding,
    grad_out,
):
    rows, tokens, features = inputs.shape
    assert rows == 1 and n_gate == 4
    channels = forget_peep.shape[0]
    assert channels == 4 * LANES
    bits = n_dp.bit_length() - 1
    assert 1 << bits == n_dp
    gate = lax.axis_index("gate")
    dp = lax.axis_index("dp")
    hi, core = gate // 2, gate % 2
    other = 1 - core

    orders = [list(range(bits)), [1, 0, *range(2, bits)]]

    def bit(stream, step):
        return (dp >> jnp.where(stream == 0, orders[0][step], orders[1][step])) & 1

    def rho(stream):
        value = 0
        for step in range(bits):
            value = value * 2 + bit(stream, step)
        return value

    def streams(h):
        return [core + h, other + h, 2 * (1 - h)]

    h1, h2 = hi, 1 - hi
    far = (1 - hi) * 2
    single, pair = 2 * other, core
    meta = jnp.stack(
        [gate, core, h1, h2, *streams(h1), *streams(h2)]
        + [other * 2 + 1 - bit(other, 0), core * 2 + 1 - bit(core, 0)]
        + [other * 2 + bit(other, 0), core * 2 + bit(core, 0)]
        + [far + other, hi * 2 + other, far + core, hi * 2 + core]
        + [gate, hi * 2 + other, far + core, far + other]
        + [rho(core), rho(other)]
        + [(far + core) * 3 + single, (far + other) * 3 + single, (hi * 2 + other) * 3]
        + [(far + core) * 3 + pair, (far + other) * 3 + pair]
        + [gate * 3 + pair, gate * 3 + single, other, 2 * core]
        + [bit(core, step) for step in range(bits)]
    ).astype(jnp.int32)

    def over_gate(value, delta):
        return lax.ppermute(value, "gate", [(g, g ^ delta) for g in range(n_gate)])

    def over_dp(value, step):
        pairs = [
            (d * n_gate + g, (d ^ (1 << orders[g % 2][step])) * n_gate + g) for d in range(n_dp) for g in range(n_gate)
        ]
        return lax.ppermute(value, ("dp", "gate"), pairs)

    def after(value, *others):
        return lax.optimization_barrier((value, *others))[0]

    x = inputs.reshape(tokens, features)
    grad = grad_out.reshape(tokens, channels)
    params = jnp.concatenate(
        [jnp.stack([forget_peep, reset_peep, forget_bias, reset_bias]), jnp.zeros((4, channels), F32)]
    )

    to2, to3 = cut(meta, weight, [(M_TO2, 1), (M_TO3, 1)])
    sent2, sent3 = over_gate(to2, 2), over_gate(to3, 3)
    normed, mu, inv, own_x, keep, live = norm(
        after(meta, to2, to3), x, ln_gain, ln_bias, resets, padding, channels
    )
    near, away2, away3 = cut(after(meta, normed), weight, [(M_NEAR, 3), (M_LATE2, 2), (M_LATE3, 2)])
    near = over_gate(near, 1)
    late2, late3 = over_gate(away2, 2), over_gate(away3, 3)
    units1 = [(weight, M_PAIR, 0), (weight, M_PAIR, 1), (near, M_GOT_PAIR, 0), (near, M_GOT_PAIR, 1)]
    units1 += [(sent2, None, 0), (sent3, None, 0)]
    units2 = [(late2, None, 0), (late2, None, 1), (late3, None, 0), (late3, None, 1)]
    units2 += [(weight, M_SINGLE, 0), (near, M_GOT_SINGLE, 0)]
    units = units1 + units2

    def first_sends(meta, ds):
        theirs, mine = wgrad(meta, normed, ds, M_SEND)
        return mine, [over_dp(mine, 0), over_dp(over_gate(theirs, 1), 0)]

    def first_keeps(meta, ds):
        theirs, mine = wgrad(meta, normed, ds, M_KEEP)
        return [mine, over_gate(theirs, 1)]

    def gathered(meta, half, late, kept, got):
        near, far = split(meta, half, late, kept, got)
        return near, over_gate(far, 2)

    def last_steps(meta, shard):
        for step in reversed(range(2, bits)):
            shard = jnp.concatenate([shard, over_dp(shard, step)], axis=1)
        return shard

    u1 = project(after(meta, away2, away3), M_S1, normed, units1)
    hidden, ds1, direct, vecs = scan(meta, M_H1, u1, own_x, grad, keep, live, params, None)
    mine1, got1 = first_sends(meta, ds1)
    kept1 = first_keeps(after(meta, mine1), ds1)
    u2 = project(after(meta, kept1[0]), M_S2, normed, units2)
    away1, stay1 = halve(after(meta, u2), M_BIT + 1, kept1, got1)
    step1 = over_dp(away1, 1)
    hidden, ds2, direct, vecs = scan(
        after(meta, away1), M_H2, u2, own_x, grad, keep, live, params, (hidden, direct, vecs)
    )
    for step in range(2, bits):
        away1, stay1 = halve(after(meta, ds2), M_BIT + step, [stay1], [step1])
        step1 = over_dp(away1, step)
    mine2, got2 = first_sends(after(meta, away1), ds2)
    kept2 = first_keeps(after(meta, mine2), ds2)
    send = back(after(meta, kept2[0]), ds1, ds2, units, M_OUT)
    got = over_gate(send, 1)
    near1, far1 = gathered(after(meta, send), M_H1, False, stay1, step1)
    away2, stay2 = halve(after(meta, near1), M_BIT + 1, kept2, got2)
    step2 = over_dp(away2, 1)
    shard1 = jnp.concatenate([near1, far1], axis=2)
    kept = back(after(meta, away2, shard1), ds1, ds2, units, M_IN)
    far_send = (kept[0].astype(F32) + got[0].astype(F32)).astype(BF16)
    far_part = over_gate(far_send, 2)

    def all_gather(meta, shard):
        for step in reversed(range(2, bits)):
            shard = jnp.concatenate([shard, over_dp(shard, step)], axis=1)
        mine, theirs = join(meta, shard, over_dp(shard, 1))
        moved = over_dp(theirs, 0)
        return [mine, over_dp(mine, 0), over_gate(theirs, 1), over_gate(moved, 1)]

    for step in range(2, bits):
        away2, stay2 = halve(after(meta, kept), M_BIT + step, [stay2], [step2])
        step2 = over_dp(away2, step)
    parts1 = all_gather(meta, shard1)
    near2, far2 = gathered(meta, M_H2, True, stay2, step2)
    shard2 = jnp.concatenate([near2, far2], axis=2)
    parts2 = all_gather(meta, shard2)

    dn, row_sums, col_sums = tail_sums(meta, kept, got, far_part, own_x, mu, inv, ln_gain)
    for delta in (1, 2):
        row_sums = row_sums + over_gate(row_sums, delta)
    dinputs = tail(meta, dn, row_sums, own_x, mu, inv, ln_gain, direct, features)

    totals = jnp.concatenate([col_sums[:2], vecs[:4]], axis=0)
    for step in range(bits):
        totals = totals + lax.ppermute(totals, "dp", [(d, d ^ (1 << step)) for d in range(n_dp)])

    grad_weight = place(meta, parts1, parts2, n_dp, features, weight.shape[1])
    return (
        hidden.reshape(rows, tokens, channels),
        dinputs.reshape(rows, tokens, channels),
        grad_weight,
        totals[0],
        totals[1],
        totals[2],
        totals[3],
        totals[4],
        totals[5],
    )


def solution(mesh):
    return jax.shard_map(
        functools.partial(shards, mesh.shape["dp"], mesh.shape["gate"]),
        mesh=mesh,
        in_specs=(
            P("dp", None, None),
            P(None, "gate"),
            P(),
            P(),
            P("gate"),
            P("gate"),
            P("gate"),
            P("gate"),
            P("dp", None),
            P("dp", None),
            P("dp", None, "gate"),
        ),
        out_specs=(
            P("dp", None, "gate"),
            P("dp", None, "gate"),
            P(None, "gate"),
            P("gate"),
            P("gate"),
            P("gate"),
            P("gate"),
            P("gate"),
            P("gate"),
        ),
        check_vma=False,
    )
```

time: 1020 us -> 353 us (0.35); the launches traced: 1000 us -> 352 us
  waiting for transfers between devices: 390 us -> 107 us
  local copies, waits for them, and re-layouts: 232 us -> 13.1 us
  Pallas kernels: 0 us -> 182 us
  other arithmetic: 170 us -> 3.58 us
  blocking collectives: 124 us -> 0 us
  matrix products: 62.2 us -> 0 us
  starting transfers between devices: 5.51 us -> 45.8 us
  between operations: 17 us -> 1.12 us
    psum x1 -> x0, waiting for transfers between devices: 229 us -> none  [shards(): lax.psum((weight_grad, jnp.sum(dnormed * unit_slice, axis=0), jnp.sum(dno...]
    pallas_call x0 -> x24, Pallas kernels: none -> 182 us  [call(): pl.pallas_call(kernel, grid_spec=pltpu.PrefetchScalarGridSpec(num_scalar_...]
    ppermute x0 -> x38, waiting for transfers between devices: none -> 107 us  [the longest x16 68.9 us: over_dp(): return lax.ppermute(value, ('dp', 'gate'), pairs)]
    reduce_scatter x1 -> x0, waiting for transfers between devices: 89.5 us -> none  [shards(): lax.psum_scatter(partial_in, 'gate', scatter_dimension=1, tiled=True)]
    all_to_all x1 -> x0, blocking collectives: 74.4 us -> none  [shards(): lax.all_to_all(dstreams, 'gate', split_axis=1, concat_axis=1, tiled=True)]
    all_to_all x1 -> x0, waiting for transfers between devices: 71.2 us -> none  [shards(): lax.all_to_all(local_cols, 'gate', split_axis=1, concat_axis=1, tiled=True)]
    unnamed x130 -> x64, local copies, waits for them, and re-layouts: 77.5 us -> 10.5 us
    dot_general x3 -> x0, matrix products: 62.2 us -> none  [the longest x2 43.8 us: contract(): lax.dot_general(left, right, (((left_dim,), (right_dim,)), ((), ())), pre...]
  transfers between devices with their start and end apart: 3 -> 38, of which waited for: 3 -> 13; matrix products, arithmetic and copies ran while one was open for 5% -> 1% of each run, Pallas kernels for 0% -> 32%
where the time goes in v2:
time: 353 us; the launch traced here: 352 us
  Pallas kernels  182 us (52%)
  waiting for transfers between devices  107 us (30%)
  starting transfers between devices  45.8 us (13%)
  local copies, waits for them, and re-layouts  13.1 us (4%)
  other arithmetic  3.58 us (1%)
    pallas_call x24, Pallas kernels, call(): pl.pallas_call(kernel, grid_spec=pltpu.PrefetchScalarGridSpec(num_scalar_...  182 us
    ppermute x16, waiting for transfers between devices, over_dp(): return lax.ppermute(value, ('dp', 'gate'), pairs)  68.9 us
    ppermute x19, waiting for transfers between devices, over_gate(): return lax.ppermute(value, 'gate', [(g, g ^ delta) for g in range(n_gate)])  35.7 us
    ppermute x16, starting transfers between devices, over_dp(): return lax.ppermute(value, ('dp', 'gate'), pairs)  21.7 us
    ppermute x19, starting transfers between devices, over_gate(): return lax.ppermute(value, 'gate', [(g, g ^ delta) for g in range(n_gate)])  17.1 us
    unnamed x64, local copies, waits for them, and re-layouts  10.5 us
  transfers between devices with their start and end apart: 38, of which 13 were waited for; matrix products, arithmetic and copies ran while one was open for 1% of the time, Pallas kernels for 32%

profile of v2, /device:TPU:0, one launch (start us, length us, event | category | flops | bytes accessed | tf_op | source)
XLA Modules:
  0.0 351.9 jit_solution(7826200284774008750)
XLA Ops:
  1.4 4.1 %shard_map.178 = (bf16[2048,128]{1,0:T(8,128)(2,1)}, bf16[2048,128]{1,0:T(8,128)(2,1)}) custom-call(s32[36]{0:T(128)} %stack.147.meta, bf16[2048,1536]{1,0:T(8,128)(2,1)} %refs_10_.3, bf16[2048,1536]{1,0:T(8,128)(2,1)} %refs_10_.3), custom_call_target="tpu_custom_call" | custom-call | bytes 2097152 | tf_op jit(solution)/shard_map/pallas_call | solution.py:18
  5.4 14.9 %shard_map.179 = (bf16[2048,2048]{1,0:T(8,128)(2,1)}, f32[2048,128]{1,0:T(8,128)}, f32[2048,128]{1,0:T(8,128)}, bf16[2048,512]{1,0:T(8,128)(2,1)}, f32[2048,128]{1,0:T(8,128)}, /*index=5*/f32[2048,128]{1,0:T(8,128)}) custom-call(s32[36]{0:T(128)} %stack.147.meta, bf16[2048,2048]{1,0:T(8,128)(2,1)} %bitcast.52, f32[1,2048]{1,0:T(1,128)} %bitcast.57, ...), custom_call_target="tpu_custom_call" | custom-call | flops 33554432 | bytes 16777216 | tf_op jit(solution)/shard_map/pallas_call | solution.py:18
  20.3 5.6 %shard_map.180 = (bf16[2048,384]{1,0:T(8,128)(2,1)}, bf16[2048,256]{1,0:T(8,128)(2,1)}, bf16[2048,256]{1,0:T(8,128)(2,1)}) custom-call(s32[36]{0:T(128)} %stack.147.meta, bf16[2048,1536]{1,0:T(8,128)(2,1)} %refs_10_.3, bf16[2048,1536]{1,0:T(8,128)(2,1)} %refs_10_.3, bf16[2048,1536]{1,0:T(8,128)(2,1)} %refs_10_.3, bf16[2048,1536]{1,0:T(8,128)(2,1)} %refs_10_.3, ...), custom_call_target="tpu_custom_call" | custom-call | bytes 7340032 | tf_op jit(solution)/shard_map/pallas_call | solution.py:18
  26.5 2.6 collective-permute-start.1
  29.1 1.7 collective-permute-start.3
  31.5 10.5 %collective-permute-done.1.refs_4_ = bf16[2048,128]{1,0:T(8,128)(2,1)S(1)} collective-permute-done((bf16[2048,128]{1,0:T(8,128)(2,1)}, bf16[2048,128]{1,0:T(8,128)(2,1)S(1)}, u32[]{:S(2)}, u32[]{:S(2)}) %collective-permute-start.1) | collective-permute-done | bytes 524320 | tf_op jit(solution)/shard_map/ppermute | solution.py:750
  42.0 10.9 %collective-permute-done.2.refs_5_ = bf16[2048,128]{1,0:T(8,128)(2,1)} collective-permute-done((bf16[2048,128]{1,0:T(8,128)(2,1)}, bf16[2048,128]{1,0:T(8,128)(2,1)}, u32[]{:S(2)}, u32[]{:S(2)}) %collective-permute-start.2) | collective-permute-done | bytes 524320 | tf_op jit(solution)/shard_map/ppermute | solution.py:750
  54.1 12.0 %shard_map.181.u_ref = bf16[2048,768]{1,0:T(8,128)(2,1)} custom-call(s32[36]{0:T(128)} %stack.147.meta, bf16[2048,2048]{1,0:T(8,128)(2,1)} %get-tuple-element.73.normed_ref, bf16[2048,1536]{1,0:T(8,128)(2,1)} %refs_10_.3, bf16[2048,1536]{1,0:T(8,128)(2,1)} %refs_10_.3, bf16[2048,384]{1,0:T(8,128)(2,1)} %copy-done, bf16[2048,384]{1,0:T(8,128)(2,1)} %copy-done, ...), custom_call_target="tpu_custom_call" | custom-call | flops 6442450944 | bytes 14680064 | tf_op jit(solution)/shard_map/pallas_call | solution.py:18
  66.0 12.4 %shard_map.182 = (bf16[2048,512]{1,0:T(8,128)(2,1)}, bf16[2048,768]{1,0:T(8,128)(2,1)}, bf16[2048,512]{1,0:T(8,128)(2,1)}, f32[8,512]{1,0:T(8,128)}) custom-call(s32[36]{0:T(128)} %stack.147.meta, bf16[2048,768]{1,0:T(8,128)(2,1)} %shard_map.181.u_ref, bf16[2048,512]{1,0:T(8,128)(2,1)} %get-tuple-element.79.x_ref, bf16[2048,512]{1,0:T(8,128)(2,1)} %bitcast.53, ...), custom_call_target="tpu_custom_call" | custom-call | flops 31457280 | bytes 9437184 | tf_op jit(solution)/shard_map/pallas_call | solution.py:18
  78.4 8.1 %shard_map.183 = (bf16[512,768]{1,0:T(8,128)(2,1)}, bf16[512,768]{1,0:T(8,128)(2,1)}) custom-call(s32[36]{0:T(128)} %stack.147.meta, bf16[2048,2048]{1,0:T(8,128)(2,1)} %get-tuple-element.73.normed_ref, bf16[2048,768]{1,0:T(8,128)(2,1)} %get-tuple-element.82.ds_ref.ds1_ref), custom_call_target="tpu_custom_call" | custom-call | flops 3221225472 | bytes 7340032 | tf_op jit(solution)/shard_map/pallas_call | solution.py:18
  86.9 2.0 collective-permute-start.6
  88.9 8.2 %shard_map.184 = (bf16[512,768]{1,0:T(8,128)(2,1)}, bf16[512,768]{1,0:T(8,128)(2,1)}) custom-call(s32[36]{0:T(128)} %stack.147.meta, bf16[2048,2048]{1,0:T(8,128)(2,1)} %get-tuple-element.73.normed_ref, bf16[2048,768]{1,0:T(8,128)(2,1)} %get-tuple-element.82.ds_ref.ds1_ref), custom_call_target="tpu_custom_call" | custom-call | flops 3221225472 | bytes 7340032 | tf_op jit(solution)/shard_map/pallas_call | solution.py:18
  99.3 12.1 %shard_map.185.u_ref = bf16[2048,768]{1,0:T(8,128)(2,1)} custom-call(s32[36]{0:T(128)} %stack.147.meta, bf16[2048,2048]{1,0:T(8,128)(2,1)} %get-tuple-element.73.normed_ref, bf16[2048,256]{1,0:T(8,128)(2,1)} %copy-done.1, bf16[2048,256]{1,0:T(8,128)(2,1)} %copy-done.1, bf16[2048,256]{1,0:T(8,128)(2,1)} %collective-permute-done.4.refs_2_.refs_3_.refs_8_.refs_9_, ...), custom_call_target="tpu_custom_call" | custom-call | flops 6442450944 | bytes 14680064 | tf_op jit(solution)/shard_map/pallas_call | solution.py:18
  113.5 3.7 %shard_map.186 = (bf16[2,256,768]{2,1,0:T(8,128)(2,1)}, bf16[2,256,768]{2,1,0:T(8,128)(2,1)}) custom-call(s32[36]{0:T(128)} %stack.147.meta, bf16[512,768]{1,0:T(8,128)(2,1)} %get-tuple-element.85.refs_0_.refs_4_, bf16[512,768]{1,0:T(8,128)(2,1)} %copy-done.7, bf16[512,768]{1,0:T(8,128)(2,1)} %copy-done.5, bf16[512,768]{1,0:T(8,128)(2,1)} %copy-done.8, ...), custom_call_target="tpu_custom_call" | custom-call | flops 1572864 | bytes 4718592 | tf_op jit(solution)/shard_map/pallas_call | solution.py:18
  118.1 12.4 %shard_map.187 = (bf16[2048,512]{1,0:T(8,128)(2,1)}, bf16[2048,768]{1,0:T(8,128)(2,1)}, bf16[2048,512]{1,0:T(8,128)(2,1)}, f32[8,512]{1,0:T(8,128)}) custom-call(s32[36]{0:T(128)} %stack.147.meta, bf16[2048,768]{1,0:T(8,128)(2,1)} %shard_map.185.u_ref, ...), custom_call_target="tpu_custom_call", output_to_operand_aliasing={{0}: (7, {}), {2}: (8, {}), {3}: (9, {})} | custom-call | flops 31457280 | bytes 9437184 | tf_op jit(solution)/shard_map/pallas_call | solution.py:18
  131.5 3.0 shard_map.188
  134.5 8.1 %shard_map.189 = (bf16[512,768]{1,0:T(8,128)(2,1)}, bf16[512,768]{1,0:T(8,128)(2,1)}) custom-call(s32[36]{0:T(128)} %stack.147.meta, bf16[2048,2048]{1,0:T(8,128)(2,1)} %get-tuple-element.73.normed_ref, bf16[2048,768]{1,0:T(8,128)(2,1)} %get-tuple-element.96.ds_ref.ds2_ref), custom_call_target="tpu_custom_call" | custom-call | flops 3221225472 | bytes 7340032 | tf_op jit(solution)/shard_map/pallas_call | solution.py:18
  142.6 8.2 %shard_map.190 = (bf16[512,768]{1,0:T(8,128)(2,1)}, bf16[512,768]{1,0:T(8,128)(2,1)}) custom-call(s32[36]{0:T(128)} %stack.147.meta, bf16[2048,2048]{1,0:T(8,128)(2,1)} %get-tuple-element.73.normed_ref, bf16[2048,768]{1,0:T(8,128)(2,1)} %get-tuple-element.96.ds_ref.ds2_ref), custom_call_target="tpu_custom_call" | custom-call | flops 3221225472 | bytes 7340032 | tf_op jit(solution)/shard_map/pallas_call | solution.py:18
  150.8 13.2 %shard_map.191 = bf16[2,2048,512]{2,1,0:T(8,128)(2,1)} custom-call(s32[36]{0:T(128)} %stack.147.meta, bf16[2048,768]{1,0:T(8,128)(2,1)} %get-tuple-element.82.ds_ref.ds1_ref, bf16[2048,768]{1,0:T(8,128)(2,1)} %get-tuple-element.96.ds_ref.ds2_ref, bf16[2048,1536]{1,0:T(8,128)(2,1)} %refs_10_.3, bf16[2048,1536]{1,0:T(8,128)(2,1)} %refs_10_.3, ...), custom_call_target="tpu_custom_call" | custom-call | flops 6442450944 | bytes 12582912 | tf_op jit(solution)/shard_map/pallas_call | solution.py:18
  166.1 6.6 %collective-permute-done.13 = bf16[512,768]{1,0:T(8,128)(2,1)} collective-permute-done((bf16[512,768]{1,0:T(8,128)(2,1)S(1)}, bf16[512,768]{1,0:T(8,128)(2,1)}, u32[]{:S(2)}, u32[]{:S(2)}) %collective-permute-start.13) | collective-permute-done | bytes 786464 | tf_op jit(solution)/shard_map/ppermute | solution.py:750
  174.2 2.6 collective-permute-start.10
  176.8 13.1 %collective-permute-done.10.b_ref = bf16[2,128,768]{2,1,0:T(8,128)(2,1)S(1)} collective-permute-done((bf16[2,128,768]{2,1,0:T(8,128)(2,1)S(1)}, bf16[2,128,768]{2,1,0:T(8,128)(2,1)S(1)}, u32[]{:S(2)}, u32[]{:S(2)}) %collective-permute-start.10) | collective-permute-done | bytes 393248 | tf_op jit(solution)/shard_map/ppermute | solution.py:756
  190.6 2.6 shard_map.192
  196.9 3.8 %shard_map.193 = (bf16[2,256,768]{2,1,0:T(8,128)(2,1)}, bf16[2,256,768]{2,1,0:T(8,128)(2,1)}) custom-call(s32[36]{0:T(128)} %stack.147.meta, bf16[512,768]{1,0:T(8,128)(2,1)} %get-tuple-element.103.refs_0_.refs_4_, bf16[512,768]{1,0:T(8,128)(2,1)} %copy-done.4, bf16[512,768]{1,0:T(8,128)(2,1)} %copy-done.3, bf16[512,768]{1,0:T(8,128)(2,1)} %copy-done.6, ...), custom_call_target="tpu_custom_call" | custom-call | flops 1572864 | bytes 4718592 | tf_op jit(solution)/shard_map/pallas_call | solution.py:18
  200.6 4.3 %collective-permute-start.26 = (bf16[2,256,768]{2,1,0:T(8,128)(2,1)}, bf16[2,256,768]{2,1,0:T(8,128)(2,1)S(1)}, u32[]{:S(2)}, u32[]{:S(2)}) collective-permute-start(bf16[2,256,768]{2,1,0:T(8,128)(2,1)} %get-tuple-element.111), channel_id=1, source_target_pairs={{0,8},{1,5},{2,10},{3,7},{4,12},{5,1},{6,14},{7,3},{8,0},{9,13},{1... | collective-permute-start | bytes 2359304 | tf_op jit(solution)/shard_map/ppermute | solution.py:756
  205.0 13.0 %shard_map.194.k_ref = bf16[2,2048,512]{2,1,0:T(8,128)(2,1)} custom-call(s32[36]{0:T(128)} %stack.147.meta, bf16[2048,768]{1,0:T(8,128)(2,1)} %get-tuple-element.82.ds_ref.ds1_ref, bf16[2048,768]{1,0:T(8,128)(2,1)} %get-tuple-element.96.ds_ref.ds2_ref, bf16[2048,1536]{1,0:T(8,128)(2,1)} %refs_10_.3, bf16[2048,1536]{1,0:T(8,128)(2,1)} %refs_10_.3, ...), custom_call_target="tpu_custom_call" | custom-call | flops 6442450944 | bytes 12582912 | tf_op jit(solution)/shard_map/pallas_call | solution.py:18
  218.9 3.0 shard_map.198
  221.9 3.4 collective-permute-start.27
  225.4 26.5 %collective-permute-done.27.b_ref = bf16[2,128,768]{2,1,0:T(8,128)(2,1)S(1)} collective-permute-done((bf16[2,128,768]{2,1,0:T(8,128)(2,1)}, bf16[2,128,768]{2,1,0:T(8,128)(2,1)S(1)}, u32[]{:S(2)}, u32[]{:S(2)}) %collective-permute-start.27) | collective-permute-done | bytes 393248 | tf_op jit(solution)/shard_map/ppermute | solution.py:756
  252.6 2.6 shard_map.199
  255.8 2.8 fusion
  258.6 1.6 collective-permute-start.17
  260.2 4.5 %collective-permute-done.28 = bf16[2,128,512]{2,1,0:T(8,128)(2,1)S(1)} collective-permute-done((bf16[2,128,512]{2,1,0:T(8,128)(2,1)}, bf16[2,128,512]{2,1,0:T(8,128)(2,1)S(1)}, u32[]{:S(2)}, u32[]{:S(2)}) %collective-permute-start.28) | collective-permute-done | bytes 262176 | tf_op jit(solution)/shard_map/ppermute | solution.py:750
  266.0 11.0 %collective-permute-done.29 = bf16[2,128,768]{2,1,0:T(8,128)(2,1)S(1)} collective-permute-done((bf16[2,128,768]{2,1,0:T(8,128)(2,1)S(1)}, bf16[2,128,768]{2,1,0:T(8,128)(2,1)S(1)}, u32[]{:S(2)}, u32[]{:S(2)}) %collective-permute-start.29) | collective-permute-done | bytes 393248 | tf_op jit(solution)/shard_map/ppermute | solution.py:756
  277.2 5.7 %collective-permute-done.21.b_ref = bf16[2,256,768]{2,1,0:T(8,128)(2,1)} collective-permute-done((bf16[2,256,768]{2,1,0:T(8,128)(2,1)S(1)}, bf16[2,256,768]{2,1,0:T(8,128)(2,1)}, u32[]{:S(2)}, u32[]{:S(2)}) %collective-permute-start.21) | collective-permute-done | bytes 786464 | tf_op jit(solution)/shard_map/ppermute | solution.py:756
  282.9 3.3 shard_map.197
  286.6 1.6 collective-permute-start.22
  288.2 11.5 %collective-permute-done.30.b_ref = bf16[2,256,768]{2,1,0:T(8,128)(2,1)} collective-permute-done((bf16[2,256,768]{2,1,0:T(8,128)(2,1)S(1)}, bf16[2,256,768]{2,1,0:T(8,128)(2,1)}, u32[]{:S(2)}, u32[]{:S(2)}) %collective-permute-start.30) | collective-permute-done | bytes 786464 | tf_op jit(solution)/shard_map/ppermute | solution.py:756
  299.7 3.3 shard_map.200
  303.5 8.0 %shard_map.195 = (f32[2048,512]{1,0:T(8,128)}, f32[8,2048]{1,0:T(8,128)}, f32[8,512]{1,0:T(8,128)}) custom-call(s32[36]{0:T(128)} %stack.147.meta, bf16[2,2048,512]{2,1,0:T(8,128)(2,1)} %shard_map.194.k_ref, bf16[2,2048,512]{2,1,0:T(8,128)(2,1)} %collective-permute-done.16.rc_ref, bf16[2048,512]{1,0:T(8,128)(2,1)} %collective-permute-done.17.ry_ref, ...), custom_call_target="tpu_custom_call" | custom-call | flops 20971520 | bytes 12582912 | tf_op jit(solution)/shard_map/pallas_call | solution.py:18
  312.2 1.7 collective-permute-start.35
  316.9 2.3 collective-permute-start.36
  319.1 1.9 collective-permute-done.36
  321.0 5.8 %collective-permute-start.18 = (f32[8,2048]{1,0:T(8,128)}, f32[8,2048]{1,0:T(8,128)S(1)}, u32[]{:S(2)}, u32[]{:S(2)}) collective-permute-start(f32[8,2048]{1,0:T(8,128)} %get-tuple-element.117), channel_id=1, source_target_pairs={{0,1},{1,0},{2,3},{3,2},{4,5},{5,4},{6,7},{7,6},{8,9},{9,8},{10,11... | collective-permute-start | bytes 196616 | tf_op jit(solution)/shard_map/ppermute | solution.py:750
  326.9 3.0 collective-permute-start.37
  330.9 8.5 %shard_map.201 = f32[2048,1536]{1,0:T(8,128)} custom-call(s32[36]{0:T(128)} %stack.147.meta, bf16[512,768]{1,0:T(8,128)(2,1)} %get-tuple-element.119.refs_0_, bf16[512,768]{1,0:T(8,128)(2,1)} %copy-done.13, bf16[512,768]{1,0:T(8,128)(2,1)} %copy-done.15, bf16[512,768]{1,0:T(8,128)(2,1)} %copy-done.16, bf16[512,768]{1,0:T(8,128)(2,1)} %get-tuple-element.127.refs_4_, ...), custom_call_target="tpu_custom_call" | custom-call | flops 3145728 | bytes 18874368 | tf_op jit(solution)/shard_map/pallas_call | solution.py:18
  340.6 3.2 collective-permute-done.19
  344.4 7.4 %shard_map.196 = bf16[2048,512]{1,0:T(8,128)(2,1)} custom-call(s32[36]{0:T(128)} %stack.147.meta, f32[2048,512]{1,0:T(8,128)} %get-tuple-element.116.dn_ref, f32[8,2048]{1,0:T(8,128)} %add.123.row_ref, bf16[2048,512]{1,0:T(8,128)(2,1)} %get-tuple-element.79.x_ref, f32[2048,128]{1,0:T(8,128)} %get-tuple-element.114.mu_ref, ...), custom_call_target="tpu_custom_call" | custom-call | flops 10485760 | bytes 12582912 | tf_op jit(solution)/shard_map/pallas_call | solution.py:18
  (133 shorter events, 28.3 us)
Async XLA Ops:
  25.9 27.0 %collective-permute-start = (bf16[2048,384]{1,0:T(8,128)(2,1)}, bf16[2048,384]{1,0:T(8,128)(2,1)S(1)}, u32[]{:S(2)}, u32[]{:S(2)}) collective-permute-start(bf16[2048,384]{1,0:T(8,128)(2,1)} %get-tuple-element.78), channel_id=1, source_target_pairs={{0,1},{1,0},{2,3},{3,2},{4,5},{5,4},{6,7},{7,6},{8,9},{9,8},{10,11... | collective-permute-start | bytes 4718600 | tf_op jit(solution)/shard_map/ppermute | solution.py:750
  26.5 15.6 %collective-permute-start.1 = (bf16[2048,128]{1,0:T(8,128)(2,1)}, bf16[2048,128]{1,0:T(8,128)(2,1)S(1)}, u32[]{:S(2)}, u32[]{:S(2)}) collective-permute-start(bf16[2048,128]{1,0:T(8,128)(2,1)} %get-tuple-element.70), channel_id=1, source_target_pairs={{0,2},{1,3},{2,0},{3,1},{4,6},{5,7},{6,4},{7,5},{8,10},{9,11},{10,... | collective-permute-start | bytes 1572872 | tf_op jit(solution)/shard_map/ppermute | solution.py:750
  29.0 23.9 %collective-permute-start.2 = (bf16[2048,128]{1,0:T(8,128)(2,1)}, bf16[2048,128]{1,0:T(8,128)(2,1)}, u32[]{:S(2)}, u32[]{:S(2)}) collective-permute-start(bf16[2048,128]{1,0:T(8,128)(2,1)} %get-tuple-element.71), channel_id=1, source_target_pairs={{0,3},{1,2},{2,1},{3,0},{4,7},{5,6},{6,5},{7,4},{8,11},{9,10},{10,... | collective-permute-start | bytes 1572872 | tf_op jit(solution)/shard_map/ppermute | solution.py:750
  29.1 69.3 %collective-permute-start.3 = (bf16[2048,256]{1,0:T(8,128)(2,1)}, bf16[2048,256]{1,0:T(8,128)(2,1)S(1)}, u32[]{:S(2)}, u32[]{:S(2)}) collective-permute-start(bf16[2048,256]{1,0:T(8,128)(2,1)} %get-tuple-element.75), channel_id=1, source_target_pairs={{0,2},{1,3},{2,0},{3,1},{4,6},{5,7},{6,4},{7,5},{8,10},{9,11},{10,... | collective-permute-start | bytes 3145736 | tf_op jit(solution)/shard_map/ppermute | solution.py:750
  30.8 67.5 %collective-permute-start.4 = (bf16[2048,256]{1,0:T(8,128)(2,1)}, bf16[2048,256]{1,0:T(8,128)(2,1)}, u32[]{:S(2)}, u32[]{:S(2)}) collective-permute-start(bf16[2048,256]{1,0:T(8,128)(2,1)} %get-tuple-element.76), channel_id=1, source_target_pairs={{0,3},{1,2},{2,1},{3,0},{4,7},{5,6},{6,5},{7,4},{8,11},{9,10},{10,... | collective-permute-start | bytes 3145736 | tf_op jit(solution)/shard_map/ppermute | solution.py:750
  86.6 10.5 %collective-permute-start.7 = (bf16[512,768]{1,0:T(8,128)(2,1)}, bf16[512,768]{1,0:T(8,128)(2,1)}, u32[]{:S(2)}, u32[]{:S(2)}) collective-permute-start(bf16[512,768]{1,0:T(8,128)(2,1)} %get-tuple-element.89), channel_id=1, source_target_pairs={{0,1},{1,0},{2,3},{3,2},{4,5},{5,4},{6,7},{7,6},{8,9},{9,8},{10,11... | collective-permute-start | bytes 2359304 | tf_op jit(solution)/shard_map/ppermute | solution.py:750
  86.9 24.6 %collective-permute-start.6 = (bf16[512,768]{1,0:T(8,128)(2,1)}, bf16[512,768]{1,0:T(8,128)(2,1)S(1)}, u32[]{:S(2)}, u32[]{:S(2)}) collective-permute-start(bf16[512,768]{1,0:T(8,128)(2,1)} %get-tuple-element.83), channel_id=1, source_target_pairs={{0,4},{1,9},{2,6},{3,11},{4,0},{5,13},{6,2},{7,15},{8,12},{9,1},{1... | collective-permute-start | bytes 2359304 | tf_op jit(solution)/shard_map/ppermute | solution.py:756
  97.0 14.4 %collective-permute-start.5 = (bf16[512,768]{1,0:T(8,128)(2,1)}, bf16[512,768]{1,0:T(8,128)(2,1)S(1)}, u32[]{:S(2)}, u32[]{:S(2)}) collective-permute-start(bf16[512,768]{1,0:T(8,128)(2,1)} %get-tuple-element.88), channel_id=1, source_target_pairs={{0,1},{1,0},{2,3},{3,2},{4,5},{5,4},{6,7},{7,6},{8,9},{9,8},{10,11... | collective-permute-start | bytes 2359304 | tf_op jit(solution)/shard_map/ppermute | solution.py:750
  97.1 14.4 %collective-permute-start.8 = (bf16[512,768]{1,0:T(8,128)(2,1)}, bf16[512,768]{1,0:T(8,128)(2,1)S(1)}, u32[]{:S(2)}, u32[]{:S(2)}) collective-permute-start(bf16[512,768]{1,0:T(8,128)(2,1)} %collective-permute-done.7), channel_id=1, source_target_pairs={{0,4},{1,9},{2,6},{3,11},{4,0},{5,13},{6,2},{7,15},{8,12},{9,1},{1... | collective-permute-start | bytes 2359304 | tf_op jit(solution)/shard_map/ppermute | solution.py:756
  117.3 13.3 %collective-permute-start.9 = (bf16[2,256,768]{2,1,0:T(8,128)(2,1)}, bf16[2,256,768]{2,1,0:T(8,128)(2,1)S(1)}, u32[]{:S(2)}, u32[]{:S(2)}) collective-permute-start(bf16[2,256,768]{2,1,0:T(8,128)(2,1)} %get-tuple-element.90), channel_id=1, source_target_pairs={{0,8},{1,5},{2,10},{3,7},{4,12},{5,1},{6,14},{7,3},{8,0},{9,13},{1... | collective-permute-start | bytes 2359304 | tf_op jit(solution)/shard_map/ppermute | solution.py:756
  150.8 13.3 %copy-start.29 = (bf16[512,768]{1,0:T(8,128)(2,1)S(1)}, bf16[512,768]{1,0:T(8,128)(2,1)}, u32[]{:S(2)}) copy-start(bf16[512,768]{1,0:T(8,128)(2,1)} %get-tuple-element.110) | copy-start | bytes 2359300
  150.8 13.8 %copy-start.28 = (bf16[512,768]{1,0:T(8,128)(2,1)S(1)}, bf16[512,768]{1,0:T(8,128)(2,1)}, u32[]{:S(2)}) copy-start(bf16[512,768]{1,0:T(8,128)(2,1)} %get-tuple-element.101) | copy-start | bytes 2359300
  150.8 23.4 %copy-start.30 = (bf16[2,128,768]{2,1,0:T(8,128)(2,1)S(1)}, bf16[2,128,768]{2,1,0:T(8,128)(2,1)}, u32[]{:S(2)}) copy-start(bf16[2,128,768]{2,1,0:T(8,128)(2,1)} %get-tuple-element.99) | copy-start | bytes 1179652
  164.0 91.8 %collective-permute-start.16 = (bf16[2,2048,512]{2,1,0:T(8,128)(2,1)}, bf16[2,2048,512]{2,1,0:T(8,128)(2,1)}, u32[]{:S(2)}, u32[]{:S(2)}) collective-permute-start(bf16[2,2048,512]{2,1,0:T(8,128)(2,1)} %shard_map.191), channel_id=1, source_target_pairs={{0,1},{1,0},{2,3},{3,2},{4,5},{5,4},{6,7},{7,6},{8,9},{9,8},{10,11... | collective-permute-start | bytes 12582920 | tf_op jit(solution)/shard_map/ppermute | solution.py:750
  164.1 8.6 %collective-permute-start.13 = (bf16[512,768]{1,0:T(8,128)(2,1)S(1)}, bf16[512,768]{1,0:T(8,128)(2,1)}, u32[]{:S(2)}, u32[]{:S(2)}) collective-permute-start(bf16[512,768]{1,0:T(8,128)(2,1)S(1)} %copy-done.29), channel_id=1, source_target_pairs={{0,1},{1,0},{2,3},{3,2},{4,5},{5,4},{6,7},{7,6},{8,9},{9,8},{10,11... | collective-permute-start | bytes 2359304 | tf_op jit(solution)/shard_map/ppermute | solution.py:750
  164.6 30.2 %collective-permute-start.12 = (bf16[512,768]{1,0:T(8,128)(2,1)S(1)}, bf16[512,768]{1,0:T(8,128)(2,1)S(1)}, u32[]{:S(2)}, u32[]{:S(2)}) collective-permute-start(bf16[512,768]{1,0:T(8,128)(2,1)S(1)} %copy-done.28), channel_id=1, source_target_pairs={{0,4},{1,9},{2,6},{3,11},{4,0},{5,13},{6,2},{7,15},{8,12},{9,1},{1... | collective-permute-start | bytes 2359304 | tf_op jit(solution)/shard_map/ppermute | solution.py:756
  166.1 28.7 %collective-permute-start.11 = (bf16[512,768]{1,0:T(8,128)(2,1)}, bf16[512,768]{1,0:T(8,128)(2,1)S(1)}, u32[]{:S(2)}, u32[]{:S(2)}) collective-permute-start(bf16[512,768]{1,0:T(8,128)(2,1)} %get-tuple-element.109), channel_id=1, source_target_pairs={{0,1},{1,0},{2,3},{3,2},{4,5},{5,4},{6,7},{7,6},{8,9},{9,8},{10,11... | collective-permute-start | bytes 2359304 | tf_op jit(solution)/shard_map/ppermute | solution.py:750
  172.7 22.1 %collective-permute-start.14 = (bf16[512,768]{1,0:T(8,128)(2,1)}, bf16[512,768]{1,0:T(8,128)(2,1)S(1)}, u32[]{:S(2)}, u32[]{:S(2)}) collective-permute-start(bf16[512,768]{1,0:T(8,128)(2,1)} %collective-permute-done.13), channel_id=1, source_target_pairs={{0,4},{1,9},{2,6},{3,11},{4,0},{5,13},{6,2},{7,15},{8,12},{9,1},{1... | collective-permute-start | bytes 2359304 | tf_op jit(solution)/shard_map/ppermute | solution.py:756
  174.2 15.7 %collective-permute-start.10 = (bf16[2,128,768]{2,1,0:T(8,128)(2,1)S(1)}, bf16[2,128,768]{2,1,0:T(8,128)(2,1)S(1)}, u32[]{:S(2)}, u32[]{:S(2)}) collective-permute-start(bf16[2,128,768]{2,1,0:T(8,128)(2,1)S(1)} %copy-done.30), channel_id=1, source_target_pairs={{0,16},{1,17},{2,18},{3,19},{4,20},{5,21},{6,22},{7,23},{8,24},{9,... | collective-permute-start | bytes 1179656 | tf_op jit(solution)/shard_map/ppermute | solution.py:756
  193.3 11.7 %collective-permute-start.15 = (bf16[2,128,256]{2,1,0:T(8,128)(2,1)}, bf16[2,128,256]{2,1,0:T(8,128)(2,1)S(1)}, u32[]{:S(2)}, u32[]{:S(2)}) collective-permute-start(bf16[2,128,256]{2,1,0:T(8,128)(2,1)} %get-tuple-element.112), channel_id=1, source_target_pairs={{0,2},{1,3},{2,0},{3,1},{4,6},{5,7},{6,4},{7,5},{8,10},{9,11},{10,... | collective-permute-start | bytes 393224 | tf_op jit(solution)/shard_map/ppermute | solution.py:750
  200.6 17.4 %collective-permute-start.26 = (bf16[2,256,768]{2,1,0:T(8,128)(2,1)}, bf16[2,256,768]{2,1,0:T(8,128)(2,1)S(1)}, u32[]{:S(2)}, u32[]{:S(2)}) collective-permute-start(bf16[2,256,768]{2,1,0:T(8,128)(2,1)} %get-tuple-element.111), channel_id=1, source_target_pairs={{0,8},{1,5},{2,10},{3,7},{4,12},{5,1},{6,14},{7,3},{8,0},{9,13},{1... | collective-permute-start | bytes 2359304 | tf_op jit(solution)/shard_map/ppermute | solution.py:756
  221.9 30.0 %collective-permute-start.27 = (bf16[2,128,768]{2,1,0:T(8,128)(2,1)}, bf16[2,128,768]{2,1,0:T(8,128)(2,1)S(1)}, u32[]{:S(2)}, u32[]{:S(2)}) collective-permute-start(bf16[2,128,768]{2,1,0:T(8,128)(2,1)} %get-tuple-element.124), channel_id=1, source_target_pairs={{0,16},{1,17},{2,18},{3,19},{4,20},{5,21},{6,22},{7,23},{8,24},{9,... | collective-permute-start | bytes 1179656 | tf_op jit(solution)/shard_map/ppermute | solution.py:756
  225.3 39.5 %collective-permute-start.20 = (bf16[2,128,768]{2,1,0:T(8,128)(2,1)S(1)}, bf16[2,128,768]{2,1,0:T(8,128)(2,1)S(1)}, u32[]{:S(2)}, u32[]{:S(2)}) collective-permute-start(bf16[2,128,768]{2,1,0:T(8,128)(2,1)S(1)} %constant_dynamic-update-slice_fusion), channel_id=1, source_target_pairs={{0,16},{1,17},{2,18},{3,19},{4,20},{5,21},{6,22},{7,23},{8,24},{9,... | collective-permute-start | bytes 1179656 | tf_op jit(solution)/shard_map/ppermute | solution.py:756
  255.3 9.4 %collective-permute-start.28 = (bf16[2,128,512]{2,1,0:T(8,128)(2,1)}, bf16[2,128,512]{2,1,0:T(8,128)(2,1)S(1)}, u32[]{:S(2)}, u32[]{:S(2)}) collective-permute-start(bf16[2,128,512]{2,1,0:T(8,128)(2,1)} %get-tuple-element.126), channel_id=1, source_target_pairs={{0,2},{1,3},{2,0},{3,1},{4,6},{5,7},{6,4},{7,5},{8,10},{9,11},{10,... | collective-permute-start | bytes 786440 | tf_op jit(solution)/shard_map/ppermute | solution.py:750
  258.6 44.9 %collective-permute-start.17 = (bf16[2048,512]{1,0:T(8,128)(2,1)S(1)}, bf16[2048,512]{1,0:T(8,128)(2,1)}, u32[]{:S(2)}, u32[]{:S(2)}) collective-permute-start(bf16[2048,512]{1,0:T(8,128)(2,1)S(1)} %fusion), channel_id=1, source_target_pairs={{0,2},{1,3},{2,0},{3,1},{4,6},{5,7},{6,4},{7,5},{8,10},{9,11},{10,... | collective-permute-start | bytes 6291464 | tf_op jit(solution)/shard_map/ppermute | solution.py:750
  264.7 12.3 %collective-permute-start.29 = (bf16[2,128,768]{2,1,0:T(8,128)(2,1)S(1)}, bf16[2,128,768]{2,1,0:T(8,128)(2,1)S(1)}, u32[]{:S(2)}, u32[]{:S(2)}) collective-permute-start(bf16[2,128,768]{2,1,0:T(8,128)(2,1)S(1)} %constant_dynamic-update-slice_fusion.2), channel_id=1, source_target_pairs={{0,16},{1,17},{2,18},{3,19},{4,20},{5,21},{6,22},{7,23},{8,24},{9,... | collective-permute-start | bytes 1179656 | tf_op jit(solution)/shard_map/ppermute | solution.py:756
  264.8 18.1 %copy-start.10 = (bf16[2,256,768]{2,1,0:T(8,128)(2,1)}, bf16[2,256,768]{2,1,0:T(8,128)(2,1)S(1)}, u32[]{:S(2)}) copy-start(bf16[2,256,768]{2,1,0:T(8,128)(2,1)S(1)} %pad_maximum_fusion.a_ref) | copy-start | bytes 2359300
  264.8 38.6 %copy-start.23 = (f32[8,512]{1,0:T(8,128)S(1)}, f32[8,512]{1,0:T(8,128)}, u32[]{:S(2)}) copy-start(f32[8,512]{1,0:T(8,128)} %get-tuple-element.130) | copy-start | bytes 49156
  264.8 18.0 %collective-permute-start.21 = (bf16[2,256,768]{2,1,0:T(8,128)(2,1)S(1)}, bf16[2,256,768]{2,1,0:T(8,128)(2,1)}, u32[]{:S(2)}, u32[]{:S(2)}) collective-permute-start(bf16[2,256,768]{2,1,0:T(8,128)(2,1)S(1)} %pad_maximum_fusion.a_ref), channel_id=1, source_target_pairs={{0,8},{1,5},{2,10},{3,7},{4,12},{5,1},{6,14},{7,3},{8,0},{9,13},{1... | collective-permute-start | bytes 2359304 | tf_op jit(solution)/shard_map/ppermute | solution.py:756
  277.1 22.7 %copy-start.9 = (bf16[2,256,768]{2,1,0:T(8,128)(2,1)}, bf16[2,256,768]{2,1,0:T(8,128)(2,1)S(1)}, u32[]{:S(2)}) copy-start(bf16[2,256,768]{2,1,0:T(8,128)(2,1)S(1)} %pad_maximum_fusion.1.a_ref) | copy-start | bytes 2359300
  277.1 22.7 %collective-permute-start.30 = (bf16[2,256,768]{2,1,0:T(8,128)(2,1)S(1)}, bf16[2,256,768]{2,1,0:T(8,128)(2,1)}, u32[]{:S(2)}, u32[]{:S(2)}) collective-permute-start(bf16[2,256,768]{2,1,0:T(8,128)(2,1)S(1)} %pad_maximum_fusion.1.a_ref), channel_id=1, source_target_pairs={{0,8},{1,5},{2,10},{3,7},{4,12},{5,1},{6,14},{7,3},{8,0},{9,13},{1... | collective-permute-start | bytes 2359304 | tf_op jit(solution)/shard_map/ppermute | solution.py:756
  286.2 27.7 %collective-permute-start.24 = (bf16[512,768]{1,0:T(8,128)(2,1)}, bf16[512,768]{1,0:T(8,128)(2,1)}, u32[]{:S(2)}, u32[]{:S(2)}) collective-permute-start(bf16[512,768]{1,0:T(8,128)(2,1)} %get-tuple-element.120), channel_id=1, source_target_pairs={{0,4},{1,9},{2,6},{3,11},{4,0},{5,13},{6,2},{7,15},{8,12},{9,1},{1... | collective-permute-start | bytes 2359304 | tf_op jit(solution)/shard_map/ppermute | solution.py:756
  286.6 27.4 %collective-permute-start.22 = (bf16[512,768]{1,0:T(8,128)(2,1)}, bf16[512,768]{1,0:T(8,128)(2,1)S(1)}, u32[]{:S(2)}, u32[]{:S(2)}) collective-permute-start(bf16[512,768]{1,0:T(8,128)(2,1)} %get-tuple-element.119.refs_0_), channel_id=1, source_target_pairs={{0,4},{1,9},{2,6},{3,11},{4,0},{5,13},{6,2},{7,15},{8,12},{9,1},{1... | collective-permute-start | bytes 2359304 | tf_op jit(solution)/shard_map/ppermute | solution.py:756
  303.0 12.3 %collective-permute-start.33 = (bf16[512,768]{1,0:T(8,128)(2,1)}, bf16[512,768]{1,0:T(8,128)(2,1)}, u32[]{:S(2)}, u32[]{:S(2)}) collective-permute-start(bf16[512,768]{1,0:T(8,128)(2,1)} %get-tuple-element.128), channel_id=1, source_target_pairs={{0,4},{1,9},{2,6},{3,11},{4,0},{5,13},{6,2},{7,15},{8,12},{9,1},{1... | collective-permute-start | bytes 2359304 | tf_op jit(solution)/shard_map/ppermute | solution.py:756
  303.4 13.4 %collective-permute-start.23 = (bf16[512,768]{1,0:T(8,128)(2,1)}, bf16[512,768]{1,0:T(8,128)(2,1)S(1)}, u32[]{:S(2)}, u32[]{:S(2)}) collective-permute-start(bf16[512,768]{1,0:T(8,128)(2,1)} %get-tuple-element.120), channel_id=1, source_target_pairs={{0,1},{1,0},{2,3},{3,2},{4,5},{5,4},{6,7},{7,6},{8,9},{9,8},{10,11... | collective-permute-start | bytes 2359304 | tf_op jit(solution)/shard_map/ppermute | solution.py:750
  303.5 11.9 %copy-start.14 = (bf16[512,768]{1,0:T(8,128)(2,1)S(1)}, bf16[512,768]{1,0:T(8,128)(2,1)}, u32[]{:S(2)}) copy-start(bf16[512,768]{1,0:T(8,128)(2,1)} %get-tuple-element.127.refs_4_) | copy-start | bytes 2359300
  312.2 3.8 %collective-permute-start.35 = (f32[6,512]{1,0:T(8,128)S(1)}, f32[6,512]{1,0:T(8,128)S(1)}, u32[]{:S(2)}, u32[]{:S(2)}) collective-permute-start(f32[6,512]{1,0:T(8,128)S(1)} %pad_maximum_fusion.2), channel_id=1, source_target_pairs={{0,4},{4,0},{8,12},{12,8},{16,20},{20,16},{24,28},{28,24},{1,5},{5... | collective-permute-start | bytes 36872 | tf_op jit(solution)/shard_map/ppermute | solution.py:845
  313.8 13.0 %collective-permute-start.25 = (bf16[512,768]{1,0:T(8,128)(2,1)}, bf16[512,768]{1,0:T(8,128)(2,1)S(1)}, u32[]{:S(2)}, u32[]{:S(2)}) collective-permute-start(bf16[512,768]{1,0:T(8,128)(2,1)} %collective-permute-done.24), channel_id=1, source_target_pairs={{0,1},{1,0},{2,3},{3,2},{4,5},{5,4},{6,7},{7,6},{8,9},{9,8},{10,11... | collective-permute-start | bytes 2359304 | tf_op jit(solution)/shard_map/ppermute | solution.py:750
  314.1 16.8 %copy-start.13 = (bf16[512,768]{1,0:T(8,128)(2,1)}, bf16[512,768]{1,0:T(8,128)(2,1)S(1)}, u32[]{:S(2)}) copy-start(bf16[512,768]{1,0:T(8,128)(2,1)S(1)} %collective-permute-done.22.refs_1_) | copy-start | bytes 2359300
  314.1 16.8 %collective-permute-start.32 = (bf16[512,768]{1,0:T(8,128)(2,1)}, bf16[512,768]{1,0:T(8,128)(2,1)}, u32[]{:S(2)}, u32[]{:S(2)}) collective-permute-start(bf16[512,768]{1,0:T(8,128)(2,1)} %get-tuple-element.128), channel_id=1, source_target_pairs={{0,1},{1,0},{2,3},{3,2},{4,5},{5,4},{6,7},{7,6},{8,9},{9,8},{10,11... | collective-permute-start | bytes 2359304 | tf_op jit(solution)/shard_map/ppermute | solution.py:750
  315.3 14.6 %collective-permute-start.31 = (bf16[512,768]{1,0:T(8,128)(2,1)S(1)}, bf16[512,768]{1,0:T(8,128)(2,1)S(1)}, u32[]{:S(2)}, u32[]{:S(2)}) collective-permute-start(bf16[512,768]{1,0:T(8,128)(2,1)S(1)} %copy-done.14), channel_id=1, source_target_pairs={{0,4},{1,9},{2,6},{3,11},{4,0},{5,13},{6,2},{7,15},{8,12},{9,1},{1... | collective-permute-start | bytes 2359304 | tf_op jit(solution)/shard_map/ppermute | solution.py:756
  316.0 14.9 %collective-permute-start.34 = (bf16[512,768]{1,0:T(8,128)(2,1)}, bf16[512,768]{1,0:T(8,128)(2,1)}, u32[]{:S(2)}, u32[]{:S(2)}) collective-permute-start(bf16[512,768]{1,0:T(8,128)(2,1)} %collective-permute-done.33), channel_id=1, source_target_pairs={{0,1},{1,0},{2,3},{3,2},{4,5},{5,4},{6,7},{7,6},{8,9},{9,8},{10,11... | collective-permute-start | bytes 2359304 | tf_op jit(solution)/shard_map/ppermute | solution.py:750
  316.9 14.0 %copy-start.15 = (bf16[512,768]{1,0:T(8,128)(2,1)}, bf16[512,768]{1,0:T(8,128)(2,1)S(1)}, u32[]{:S(2)}) copy-start(bf16[512,768]{1,0:T(8,128)(2,1)S(1)} %collective-permute-done.23.refs_2_) | copy-start | bytes 2359300
  316.9 4.2 %collective-permute-start.36 = (f32[6,512]{1,0:T(8,128)S(1)}, f32[6,512]{1,0:T(8,128)S(1)}, u32[]{:S(2)}, u32[]{:S(2)}) collective-permute-start(f32[6,512]{1,0:T(8,128)S(1)} %fusion.1), channel_id=1, source_target_pairs={{0,8},{4,12},{8,0},{12,4},{16,24},{20,28},{24,16},{28,20},{1,9},{5... | collective-permute-start | bytes 36872 | tf_op jit(solution)/shard_map/ppermute | solution.py:845
  321.0 18.4 %collective-permute-start.18 = (f32[8,2048]{1,0:T(8,128)}, f32[8,2048]{1,0:T(8,128)S(1)}, u32[]{:S(2)}, u32[]{:S(2)}) collective-permute-start(f32[8,2048]{1,0:T(8,128)} %get-tuple-element.117), channel_id=1, source_target_pairs={{0,1},{1,0},{2,3},{3,2},{4,5},{5,4},{6,7},{7,6},{8,9},{9,8},{10,11... | collective-permute-start | bytes 196616 | tf_op jit(solution)/shard_map/ppermute | solution.py:750
  326.9 12.6 %copy-start.22 = (f32[8,2048]{1,0:T(8,128)S(1)}, f32[8,2048]{1,0:T(8,128)}, u32[]{:S(2)}) copy-start(f32[8,2048]{1,0:T(8,128)} %get-tuple-element.117) | copy-start | bytes 196612
  326.9 12.5 %collective-permute-start.37 = (f32[6,512]{1,0:T(8,128)S(1)}, f32[6,512]{1,0:T(8,128)S(1)}, u32[]{:S(2)}, u32[]{:S(2)}) collective-permute-start(f32[6,512]{1,0:T(8,128)S(1)} %add.125), channel_id=1, source_target_pairs={{0,16},{4,20},{8,24},{12,28},{16,0},{20,4},{24,8},{28,12},{1,17},{... | collective-permute-start | bytes 36872 | tf_op jit(solution)/shard_map/ppermute | solution.py:845
  339.5 4.3 %collective-permute-start.19 = (f32[8,2048]{1,0:T(8,128)S(1)}, f32[8,2048]{1,0:T(8,128)S(1)}, u32[]{:S(2)}, u32[]{:S(2)}) collective-permute-start(f32[8,2048]{1,0:T(8,128)S(1)} %add.122), channel_id=1, source_target_pairs={{0,2},{1,3},{2,0},{3,1},{4,6},{5,7},{6,4},{7,5},{8,10},{9,11},{10,... | collective-permute-start | bytes 196616 | tf_op jit(solution)/shard_map/ppermute | solution.py:750
  (21 other events, 84.3 us)

commit v3 on v2

--- a/solution.py
+++ b/solution.py
@@ -12,6 +12,7 @@
 BF16 = jnp.bfloat16
 LANES = 128
 VMEM_LIMIT = 60 * 1024 * 1024
+COVER = 20
 
 
 def call(kernel, meta, args, grid, in_specs, out_specs, out_shape, scratch=(), aliases=None, cost=None):
@@ -33,8 +34,8 @@
     )(meta, *args)
 
 
-def cost(flops, nbytes, trans=0):
-    return pl.CostEstimate(flops=int(flops), bytes_accessed=int(nbytes), transcendentals=int(trans))
+def cost(flops, nbytes, trans=0, weight=1):
+    return pl.CostEstimate(flops=int(weight * flops), bytes_accessed=int(weight * nbytes), transcendentals=int(trans))
 
 
 def struct(shape, dtype):
@@ -122,7 +123,7 @@
         [row, stat, stat, pl.BlockSpec((TILE, channels), lambda t, m: (t, 0)), stat, stat],
         [struct(x.shape, BF16), stats, stats, struct((tokens, channels), BF16), stats, stats],
         scratch=[pltpu.VMEM((TILE, TILE), BF16), pltpu.VMEM((TILE, features), F32)] + [pltpu.VMEM((TILE, LANES), F32)] * 2,
-        cost=cost(8 * tokens * features, 4 * tokens * features),
+        cost=cost(8 * tokens * features, 4 * tokens * features, weight=COVER),
     )
 
 
@@ -188,7 +189,7 @@
         pl.BlockSpec((tb, columns), lambda t, m: (t, 0)),
         struct((tokens, columns), BF16),
         scratch=[pltpu.VMEM((features, columns), BF16)],
-        cost=cost(2 * tokens * features * columns, 2 * tokens * (features + 2 * columns)),
+        cost=cost(2 * tokens * features * columns, 2 * tokens * (features + 2 * columns), weight=COVER),
     )
 
 
@@ -352,7 +353,7 @@
         + [pltpu.VMEM(tall, BF16)]
         + [ends] * 4,
         aliases=aliases,
-        cost=cost(60 * length * channels // 2, 9 * length * channels, length * channels),
+        cost=cost(60 * length * channels // 2, 9 * length * channels, length * channels, weight=COVER),
     )
 
 
@@ -392,7 +393,7 @@
             pl.BlockSpec((mb, width), lambda i, m: (jnp.maximum(i - steps, 0), 0)),
         ],
         [struct((rows, width), BF16)] * 2,
-        cost=cost(4 * tokens * rows * width, 2 * tokens * (features // 2 + width)),
+        cost=cost(4 * tokens * rows * width, 2 * tokens * (features // 2 + width), weight=COVER),
     )
 
 
@@ -411,7 +412,7 @@
     out_ref[0] = value.astype(BF16)
 
 
-def back(meta, ds1, ds2, units, first, tb=1024):
+def back(meta, ds1, ds2, units, first, count, tb=1024):
     tokens, width = ds1.shape
     features = units[0][0].shape[0]
     block = features // 4
@@ -420,12 +421,12 @@
         back_kernel,
         meta,
         [ds1, ds2] + [array for array, _, _ in units],
-        (2, tokens // tb),
+        (count, tokens // tb),
         [dspec, dspec] + unit_specs(units, block, lambda n, t, m: m[first + n]),
         pl.BlockSpec((1, tb, block), lambda n, t, m: (n, t, 0)),
-        struct((2, tokens, block), BF16),
+        struct((count, tokens, block), BF16),
         scratch=[pltpu.VMEM((block, 2 * width), BF16)],
-        cost=cost(8 * tokens * block * width, 8 * tokens * width),
+        cost=cost(4 * count * tokens * block * width, 4 * count * tokens * width, weight=COVER),
     )
 
 
@@ -443,9 +444,11 @@
     return jnp.sum(part.T, axis=0, keepdims=True)
 
 
-def tail_sums_kernel(meta, k_ref, rc_ref, ry_ref, x_ref, mu_ref, inv_ref, gain_ref, dn_ref, row_ref, col_ref):
+def tail_sums_kernel(meta, k_ref, rc_ref, r1_ref, r2_ref, x_ref, mu_ref, inv_ref, gain_ref, dn_ref, row_ref, col_ref):
     unit, _ = unit_of(x_ref, mu_ref, inv_ref)
-    dn = k_ref[0].astype(F32) + rc_ref[0].astype(F32) + ry_ref[...].astype(F32)
+    early = pl.program_id(0) < pl.num_programs(0) // 2
+    far = jnp.where(early, r1_ref[...].astype(F32), r2_ref[...].astype(F32))
+    dn = k_ref[0].astype(F32) + rc_ref[0].astype(F32) + far
     dn_ref[...] = dn
     gu = dn * gain_ref[...]
     row_ref[0:1, :] = lane_sums(gu)
@@ -461,16 +464,25 @@
 
 
 def tail_sums(meta, keep, got, far, x, mu, inv, gain, tb=512):
-    tokens, channels = far.shape
-    part = pl.BlockSpec((1, tb, channels), lambda t, m: (1, t, 0))
+    tokens, channels = x.shape
+    half = tokens // tb // 2
     wide = pl.BlockSpec((tb, channels), lambda t, m: (t, 0))
     stat = pl.BlockSpec((tb, LANES), lambda t, m: (t, 0))
     return call(
         tail_sums_kernel,
         meta,
-        (keep, got, far, x, mu, inv, gain[None]),
+        (keep, got, *far, x, mu, inv, gain[None]),
         (tokens // tb,),
-        [part, part, wide, wide, stat, stat, pl.BlockSpec((1, channels), lambda t, m: (0, m[M_GATE]))],
+        [
+            pl.BlockSpec((1, tb, channels), lambda t, m: (0, t, 0)),
+            pl.BlockSpec((1, tb, channels), lambda t, m: (1, t, 0)),
+            pl.BlockSpec((tb, channels), lambda t, m: (jnp.minimum(t, half - 1), 0)),
+            pl.BlockSpec((tb, channels), lambda t, m: (jnp.maximum(t - half, 0), 0)),
+            wide,
+            stat,
+            stat,
+            pl.BlockSpec((1, channels), lambda t, m: (0, m[M_GATE])),
+        ],
         [
             wide,
             pl.BlockSpec((8, tb), lambda t, m: (0, t)),
@@ -764,13 +776,12 @@
         [jnp.stack([forget_peep, reset_peep, forget_bias, reset_bias]), jnp.zeros((4, channels), F32)]
     )
 
-    to2, to3 = cut(meta, weight, [(M_TO2, 1), (M_TO3, 1)])
-    sent2, sent3 = over_gate(to2, 2), over_gate(to3, 3)
+    to2, to3, near = cut(meta, weight, [(M_TO2, 1), (M_TO3, 1), (M_NEAR, 3)])
+    sent2, sent3, near = over_gate(to2, 2), over_gate(to3, 3), over_gate(near, 1)
     normed, mu, inv, own_x, keep, live = norm(
         after(meta, to2, to3), x, ln_gain, ln_bias, resets, padding, channels
     )
-    near, away2, away3 = cut(after(meta, normed), weight, [(M_NEAR, 3), (M_LATE2, 2), (M_LATE3, 2)])
-    near = over_gate(near, 1)
+    away2, away3 = cut(after(meta, normed), weight, [(M_LATE2, 2), (M_LATE3, 2)])
     late2, late3 = over_gate(away2, 2), over_gate(away3, 3)
     units1 = [(weight, M_PAIR, 0), (weight, M_PAIR, 1), (near, M_GOT_PAIR, 0), (near, M_GOT_PAIR, 1)]
     units1 += [(sent2, None, 0), (sent3, None, 0)]
@@ -790,9 +801,9 @@
         near, far = split(meta, half, late, kept, got)
         return near, over_gate(far, 2)
 
-    def last_steps(meta, shard):
+    def last_steps(shard, *others):
         for step in reversed(range(2, bits)):
-            shard = jnp.concatenate([shard, over_dp(shard, step)], axis=1)
+            shard = jnp.concatenate([after(shard, *others), over_dp(shard, step)], axis=1)
         return shard
 
     u1 = project(after(meta, away2, away3), M_S1, normed, units1)
@@ -810,30 +821,31 @@
         step1 = over_dp(away1, step)
     mine2, got2 = first_sends(after(meta, away1), ds2)
     kept2 = first_keeps(after(meta, mine2), ds2)
-    send = back(after(meta, kept2[0]), ds1, ds2, units, M_OUT)
+    send = back(after(meta, kept2[0]), ds1, ds2, units, M_OUT, 2)
     got = over_gate(send, 1)
     near1, far1 = gathered(after(meta, send), M_H1, False, stay1, step1)
     away2, stay2 = halve(after(meta, near1), M_BIT + 1, kept2, got2)
     step2 = over_dp(away2, 1)
     shard1 = jnp.concatenate([near1, far1], axis=2)
-    kept = back(after(meta, away2, shard1), ds1, ds2, units, M_IN)
-    far_send = (kept[0].astype(F32) + got[0].astype(F32)).astype(BF16)
-    far_part = over_gate(far_send, 2)
-
-    def all_gather(meta, shard):
-        for step in reversed(range(2, bits)):
-            shard = jnp.concatenate([shard, over_dp(shard, step)], axis=1)
+
+    def last_doubling(meta, shard):
         mine, theirs = join(meta, shard, over_dp(shard, 1))
         moved = over_dp(theirs, 0)
         return [mine, over_dp(mine, 0), over_gate(theirs, 1), over_gate(moved, 1)]
 
+    kept_far = back(after(meta, away2, shard1), ds1, ds2, units, M_IN, 1)
+    half = tokens // 2
+    far_send = [(kept_far[0, at : at + half].astype(F32) + got[0, at : at + half].astype(F32)).astype(BF16) for at in (0, half)]
+    far_part = [over_gate(part, 2) for part in far_send]
+    kept = back(after(meta, *far_send), ds1, ds2, units, M_IN + 1, 1)
+    shard1 = last_steps(shard1, kept)
     for step in range(2, bits):
-        away2, stay2 = halve(after(meta, kept), M_BIT + step, [stay2], [step2])
+        away2, stay2 = halve(after(meta, shard1, kept), M_BIT + step, [stay2], [step2])
         step2 = over_dp(away2, step)
-    parts1 = all_gather(meta, shard1)
-    near2, far2 = gathered(meta, M_H2, True, stay2, step2)
-    shard2 = jnp.concatenate([near2, far2], axis=2)
-    parts2 = all_gather(meta, shard2)
+    near2, far2 = gathered(after(meta, far_part[0]), M_H2, True, stay2, step2)
+    parts1 = last_doubling(after(meta, near2), shard1)
+    shard2 = last_steps(jnp.concatenate([near2, far2], axis=2))
+    parts2 = last_doubling(meta, shard2)
 
     dn, row_sums, col_sums = tail_sums(meta, kept, got, far_part, own_x, mu, inv, ln_gain)
     for delta in (1, 2):

time: 353 us -> 308 us (0.87)
  waiting for transfers between devices: 107 us -> 68.4 us
  starting transfers between devices: 45.8 us -> 33.6 us
    ppermute x16, waiting for transfers between devices: 68.9 us -> 37.9 us  [over_dp(): return lax.ppermute(value, ('dp', 'gate'), pairs)]
    ppermute x19 -> x20, waiting for transfers between devices: 35.7 us -> 21.4 us  [over_gate(): return lax.ppermute(value, 'gate', [(g, g ^ delta) for g in range(n_gate)])]
    ppermute x3, waiting for transfers between devices: 2.1 us -> 9.02 us  [shards(): lax.ppermute(totals, 'dp', [(d, d ^ 1 << step) for d in range(n_dp)])]
    ppermute x3, starting transfers between devices: 6.98 us -> 1.23 us  [shards(): lax.ppermute(totals, 'dp', [(d, d ^ 1 << step) for d in range(n_dp)])]
    ppermute x19 -> x20, starting transfers between devices: 17.1 us -> 11.8 us  [over_gate(): return lax.ppermute(value, 'gate', [(g, g ^ delta) for g in range(n_gate)])]
    pallas_call x24 -> x25, Pallas kernels: 182 us -> 185 us  [call(): pl.pallas_call(kernel, grid_spec=pltpu.PrefetchScalarGridSpec(num_scalar_...]
    unnamed x64 -> x49, local copies, waits for them, and re-layouts: 10.5 us -> 11.1 us
  transfers between devices with their start and end apart: 38 -> 39, of which waited for: 13 -> 14; matrix products, arithmetic and copies ran while one was open for 1% -> 3% of each run, Pallas kernels for 32% -> 53%
where the time goes in v3:
time: 308 us; the launch traced here: 307 us
  Pallas kernels  185 us (60%)
  waiting for transfers between devices  68.4 us (22%)
  starting transfers between devices  33.6 us (11%)
  local copies, waits for them, and re-layouts  14.7 us (5%)
  other arithmetic  4.32 us (1%)
    pallas_call x25, Pallas kernels, call(): pl.pallas_call(kernel, grid_spec=pltpu.PrefetchScalarGridSpec(num_scalar_...  185 us
    ppermute x16, waiting for transfers between devices, over_dp(): return lax.ppermute(value, ('dp', 'gate'), pairs)  37.9 us
    ppermute x20, waiting for transfers between devices, over_gate(): return lax.ppermute(value, 'gate', [(g, g ^ delta) for g in range(n_gate)])  21.4 us
    ppermute x16, starting transfers between devices, over_dp(): return lax.ppermute(value, ('dp', 'gate'), pairs)  20.6 us
    ppermute x20, starting transfers between devices, over_gate(): return lax.ppermute(value, 'gate', [(g, g ^ delta) for g in range(n_gate)])  11.8 us
    unnamed x49, local copies, waits for them, and re-layouts  11.1 us
    ppermute x3, waiting for transfers between devices, shards(): lax.ppermute(totals, 'dp', [(d, d ^ 1 << step) for d in range(n_dp)])  9.02 us
  transfers between devices with their start and end apart: 39, of which 14 were waited for; matrix products, arithmetic and copies ran while one was open for 3% of the time, Pallas kernels for 53%

profile of v3, /device:TPU:0, one launch (start us, length us, event | category | flops | bytes accessed | tf_op | source)
XLA Modules:
  0.0 306.6 jit_solution(5031625949886123595)
XLA Ops:
  1.3 4.8 %shard_map.178 = (bf16[2048,128]{1,0:T(8,128)(2,1)}, bf16[2048,128]{1,0:T(8,128)(2,1)}, bf16[2048,384]{1,0:T(8,128)(2,1)}) custom-call(s32[36]{0:T(128)} %stack.147.meta, bf16[2048,1536]{1,0:T(8,128)(2,1)} %refs_10_.5, bf16[2048,1536]{1,0:T(8,128)(2,1)} %refs_10_.5, bf16[2048,1536]{1,0:T(8,128)(2,1)} %refs_10_.5, bf16[2048,1536]{1,0:T(8,128)(2,1)} %refs_10_.5, ...), custom_call_target="tpu_custom_call" | custom-call | bytes 5242880 | tf_op jit(solution)/shard_map/pallas_call | solution.py:19
  6.6 2.6 collective-permute-start.1
  9.3 14.8 %shard_map.179 = (bf16[2048,2048]{1,0:T(8,128)(2,1)}, f32[2048,128]{1,0:T(8,128)}, f32[2048,128]{1,0:T(8,128)}, bf16[2048,512]{1,0:T(8,128)(2,1)}, f32[2048,128]{1,0:T(8,128)}, /*index=5*/f32[2048,128]{1,0:T(8,128)}) custom-call(s32[36]{0:T(128)} %stack.147.meta, bf16[2048,2048]{1,0:T(8,128)(2,1)} %bitcast.54, f32[1,2048]{1,0:T(1,128)} %bitcast.59, ...), custom_call_target="tpu_custom_call" | custom-call | flops 671088640 | bytes 335544320 | tf_op jit(solution)/shard_map/pallas_call | solution.py:19
  24.2 4.8 %shard_map.180 = (bf16[2048,256]{1,0:T(8,128)(2,1)}, bf16[2048,256]{1,0:T(8,128)(2,1)}) custom-call(s32[36]{0:T(128)} %stack.147.meta, bf16[2048,1536]{1,0:T(8,128)(2,1)} %refs_10_.5, bf16[2048,1536]{1,0:T(8,128)(2,1)} %refs_10_.5, bf16[2048,1536]{1,0:T(8,128)(2,1)} %refs_10_.5, bf16[2048,1536]{1,0:T(8,128)(2,1)} %refs_10_.5), custom_call_target="tpu_custom_call" | custom-call | bytes 4194304 | tf_op jit(solution)/shard_map/pallas_call | solution.py:19
  29.0 1.7 collective-permute-start.3
  31.4 1.7 collective-permute-done.2.refs_5_
  35.0 12.0 %shard_map.181.u_ref = bf16[2048,768]{1,0:T(8,128)(2,1)} custom-call(s32[36]{0:T(128)} %stack.147.meta, bf16[2048,2048]{1,0:T(8,128)(2,1)} %get-tuple-element.77.normed_ref, bf16[2048,1536]{1,0:T(8,128)(2,1)} %refs_10_.5, bf16[2048,1536]{1,0:T(8,128)(2,1)} %refs_10_.5, bf16[2048,384]{1,0:T(8,128)(2,1)} %copy-done.19, bf16[2048,384]{1,0:T(8,128)(2,1)} %copy-done.19, ...), custom_call_target="tpu_custom_call" | custom-call | flops 128849018880 | bytes 293601280 | tf_op jit(solution)/shard_map/pallas_call | solution.py:19
  47.0 12.4 %shard_map.182 = (bf16[2048,512]{1,0:T(8,128)(2,1)}, bf16[2048,768]{1,0:T(8,128)(2,1)}, bf16[2048,512]{1,0:T(8,128)(2,1)}, f32[8,512]{1,0:T(8,128)}) custom-call(s32[36]{0:T(128)} %stack.147.meta, bf16[2048,768]{1,0:T(8,128)(2,1)} %shard_map.181.u_ref, bf16[2048,512]{1,0:T(8,128)(2,1)} %get-tuple-element.83.x_ref, bf16[2048,512]{1,0:T(8,128)(2,1)} %bitcast.55, ...), custom_call_target="tpu_custom_call" | custom-call | flops 629145600 | bytes 188743680 | tf_op jit(solution)/shard_map/pallas_call | solution.py:19
  59.4 8.1 %shard_map.183 = (bf16[512,768]{1,0:T(8,128)(2,1)}, bf16[512,768]{1,0:T(8,128)(2,1)}) custom-call(s32[36]{0:T(128)} %stack.147.meta, bf16[2048,2048]{1,0:T(8,128)(2,1)} %get-tuple-element.77.normed_ref, bf16[2048,768]{1,0:T(8,128)(2,1)} %get-tuple-element.86.ds_ref.ds1_ref), custom_call_target="tpu_custom_call" | custom-call | flops 64424509440 | bytes 146800640 | tf_op jit(solution)/shard_map/pallas_call | solution.py:19
  69.5 8.1 %shard_map.184 = (bf16[512,768]{1,0:T(8,128)(2,1)}, bf16[512,768]{1,0:T(8,128)(2,1)}) custom-call(s32[36]{0:T(128)} %stack.147.meta, bf16[2048,2048]{1,0:T(8,128)(2,1)} %get-tuple-element.77.normed_ref, bf16[2048,768]{1,0:T(8,128)(2,1)} %get-tuple-element.86.ds_ref.ds1_ref), custom_call_target="tpu_custom_call" | custom-call | flops 64424509440 | bytes 146800640 | tf_op jit(solution)/shard_map/pallas_call | solution.py:19
  77.7 1.5 collective-permute-start.8
  79.2 12.1 %shard_map.185.u_ref = bf16[2048,768]{1,0:T(8,128)(2,1)} custom-call(s32[36]{0:T(128)} %stack.147.meta, bf16[2048,2048]{1,0:T(8,128)(2,1)} %get-tuple-element.77.normed_ref, bf16[2048,256]{1,0:T(8,128)(2,1)} %collective-permute-done.3.refs_0_.refs_1_.refs_6_.refs_7_, bf16[2048,256]{1,0:T(8,128)(2,1)} %collective-permute-done.3.refs_0_.refs_1_.refs_6_.refs_7_, ...), custom_call_target="tpu_custom_call" | custom-call | flops 128849018880 | bytes 293601280 | tf_op jit(solution)/shard_map/pallas_call | solution.py:19
  93.2 3.7 %shard_map.186 = (bf16[2,256,768]{2,1,0:T(8,128)(2,1)}, bf16[2,256,768]{2,1,0:T(8,128)(2,1)}) custom-call(s32[36]{0:T(128)} %stack.147.meta, bf16[512,768]{1,0:T(8,128)(2,1)} %get-tuple-element.89.refs_0_.refs_4_, bf16[512,768]{1,0:T(8,128)(2,1)} %copy-done.2, bf16[512,768]{1,0:T(8,128)(2,1)} %collective-permute-done.6.refs_2_.refs_6_, ...), custom_call_target="tpu_custom_call" | custom-call | flops 1572864 | bytes 4718592 | tf_op jit(solution)/shard_map/pallas_call | solution.py:19
  97.5 12.4 %shard_map.187 = (bf16[2048,512]{1,0:T(8,128)(2,1)}, bf16[2048,768]{1,0:T(8,128)(2,1)}, bf16[2048,512]{1,0:T(8,128)(2,1)}, f32[8,512]{1,0:T(8,128)}) custom-call(s32[36]{0:T(128)} %stack.147.meta, bf16[2048,768]{1,0:T(8,128)(2,1)} %shard_map.185.u_ref, ...), custom_call_target="tpu_custom_call", output_to_operand_aliasing={{0}: (7, {}), {2}: (8, {}), {3}: (9, {})} | custom-call | flops 629145600 | bytes 188743680 | tf_op jit(solution)/shard_map/pallas_call | solution.py:19
  110.8 3.0 shard_map.188
  113.8 2.6 collective-permute-start.10
  116.4 8.1 %shard_map.189 = (bf16[512,768]{1,0:T(8,128)(2,1)}, bf16[512,768]{1,0:T(8,128)(2,1)}) custom-call(s32[36]{0:T(128)} %stack.147.meta, bf16[2048,2048]{1,0:T(8,128)(2,1)} %get-tuple-element.77.normed_ref, bf16[2048,768]{1,0:T(8,128)(2,1)} %get-tuple-element.100.ds_ref.ds2_ref), custom_call_target="tpu_custom_call" | custom-call | flops 64424509440 | bytes 146800640 | tf_op jit(solution)/shard_map/pallas_call | solution.py:19
  124.5 1.5 collective-permute-start.12
  126.0 8.1 %shard_map.190 = (bf16[512,768]{1,0:T(8,128)(2,1)}, bf16[512,768]{1,0:T(8,128)(2,1)}) custom-call(s32[36]{0:T(128)} %stack.147.meta, bf16[2048,2048]{1,0:T(8,128)(2,1)} %get-tuple-element.77.normed_ref, bf16[2048,768]{1,0:T(8,128)(2,1)} %get-tuple-element.100.ds_ref.ds2_ref), custom_call_target="tpu_custom_call" | custom-call | flops 64424509440 | bytes 146800640 | tf_op jit(solution)/shard_map/pallas_call | solution.py:19
  135.2 13.0 %shard_map.191 = bf16[2,2048,512]{2,1,0:T(8,128)(2,1)} custom-call(s32[36]{0:T(128)} %stack.147.meta, bf16[2048,768]{1,0:T(8,128)(2,1)} %get-tuple-element.86.ds_ref.ds1_ref, bf16[2048,768]{1,0:T(8,128)(2,1)} %get-tuple-element.100.ds_ref.ds2_ref, bf16[2048,1536]{1,0:T(8,128)(2,1)} %refs_10_.5, bf16[2048,1536]{1,0:T(8,128)(2,1)} %refs_10_.5, ...), custom_call_target="tpu_custom_call" | custom-call | flops 128849018880 | bytes 251658240 | tf_op jit(solution)/shard_map/pallas_call | solution.py:19
  148.2 2.6 shard_map.192
  153.2 3.0 collective-permute-done.15
  158.4 4.0 %shard_map.193 = (bf16[2,256,768]{2,1,0:T(8,128)(2,1)}, bf16[2,256,768]{2,1,0:T(8,128)(2,1)}) custom-call(s32[36]{0:T(128)} %stack.147.meta, bf16[512,768]{1,0:T(8,128)(2,1)} %get-tuple-element.107.refs_0_.refs_4_, bf16[512,768]{1,0:T(8,128)(2,1)} %copy-done, bf16[512,768]{1,0:T(8,128)(2,1)} %collective-permute-done.12.refs_2_.refs_6_, ...), custom_call_target="tpu_custom_call" | custom-call | flops 1572864 | bytes 4718592 | tf_op jit(solution)/shard_map/pallas_call | solution.py:19
  162.4 1.5 collective-permute-start.22
  163.9 8.0 %shard_map.194 = bf16[1,2048,512]{2,1,0:T(8,128)(2,1)} custom-call(s32[36]{0:T(128)} %stack.147.meta, bf16[2048,768]{1,0:T(8,128)(2,1)} %get-tuple-element.86.ds_ref.ds1_ref, bf16[2048,768]{1,0:T(8,128)(2,1)} %get-tuple-element.100.ds_ref.ds2_ref, bf16[2048,1536]{1,0:T(8,128)(2,1)} %refs_10_.5, bf16[2048,1536]{1,0:T(8,128)(2,1)} %refs_10_.5, ...), custom_call_target="tpu_custom_call" | custom-call | flops 64424509440 | bytes 125829120 | tf_op jit(solution)/shard_map/pallas_call | solution.py:19
  172.0 2.8 fusion.1
  174.8 1.6 collective-permute-start.17
  176.4 8.1 %shard_map.195.k_ref = bf16[1,2048,512]{2,1,0:T(8,128)(2,1)} custom-call(s32[36]{0:T(128)} %stack.147.meta, bf16[2048,768]{1,0:T(8,128)(2,1)} %get-tuple-element.86.ds_ref.ds1_ref, bf16[2048,768]{1,0:T(8,128)(2,1)} %get-tuple-element.100.ds_ref.ds2_ref, bf16[2048,1536]{1,0:T(8,128)(2,1)} %refs_10_.5, bf16[2048,1536]{1,0:T(8,128)(2,1)} %refs_10_.5, ...), custom_call_target="tpu_custom_call" | custom-call | flops 64424509440 | bytes 125829120 | tf_op jit(solution)/shard_map/pallas_call | solution.py:19
  186.5 3.0 shard_map.198
  189.5 2.6 collective-permute-start.23
  192.1 6.3 %collective-permute-done.17.r1_ref = bf16[1024,512]{1,0:T(8,128)(2,1)} collective-permute-done((bf16[1024,512]{1,0:T(8,128)(2,1)S(1)}, bf16[1024,512]{1,0:T(8,128)(2,1)}, u32[]{:S(2)}, u32[]{:S(2)}) %collective-permute-start.17) | collective-permute-done | bytes 1048608 | tf_op jit(solution)/shard_map/ppermute | solution.py:762
  198.5 9.6 %collective-permute-done.23.b_ref = bf16[2,128,768]{2,1,0:T(8,128)(2,1)S(1)} collective-permute-done((bf16[2,128,768]{2,1,0:T(8,128)(2,1)}, bf16[2,128,768]{2,1,0:T(8,128)(2,1)S(1)}, u32[]{:S(2)}, u32[]{:S(2)}) %collective-permute-start.23) | collective-permute-done | bytes 393248 | tf_op jit(solution)/shard_map/ppermute | solution.py:768
  208.8 2.6 shard_map.199
  212.9 6.9 %collective-permute-done.29 = bf16[2,128,512]{2,1,0:T(8,128)(2,1)S(1)} collective-permute-done((bf16[2,128,512]{2,1,0:T(8,128)(2,1)}, bf16[2,128,512]{2,1,0:T(8,128)(2,1)S(1)}, u32[]{:S(2)}, u32[]{:S(2)}) %collective-permute-start.29) | collective-permute-done | bytes 262176 | tf_op jit(solution)/shard_map/ppermute | solution.py:762
  220.0 1.9 collective-permute-start.24
  221.8 15.1 %collective-permute-done.30 = bf16[2,128,768]{2,1,0:T(8,128)(2,1)S(1)} collective-permute-done((bf16[2,128,768]{2,1,0:T(8,128)(2,1)S(1)}, bf16[2,128,768]{2,1,0:T(8,128)(2,1)S(1)}, u32[]{:S(2)}, u32[]{:S(2)}) %collective-permute-start.30) | collective-permute-done | bytes 393248 | tf_op jit(solution)/shard_map/ppermute | solution.py:768
  238.3 2.2 collective-permute-done.24.b_ref
  240.5 3.3 %shard_map.200 = (bf16[512,768]{1,0:T(8,128)(2,1)}, bf16[512,768]{1,0:T(8,128)(2,1)}) custom-call(s32[36]{0:T(128)} %stack.147.meta, bf16[2,256,768]{2,1,0:T(8,128)(2,1)} %copy-done.7, bf16[2,256,768]{2,1,0:T(8,128)(2,1)} %collective-permute-done.24.b_ref), custom_call_target="tpu_custom_call" | custom-call | bytes 3145728 | tf_op jit(solution)/shard_map/pallas_call | solution.py:19
  245.8 8.2 %collective-permute-done.31.b_ref = bf16[2,256,768]{2,1,0:T(8,128)(2,1)} collective-permute-done((bf16[2,256,768]{2,1,0:T(8,128)(2,1)S(1)}, bf16[2,256,768]{2,1,0:T(8,128)(2,1)}, u32[]{:S(2)}, u32[]{:S(2)}) %collective-permute-start.31) | collective-permute-done | bytes 786464 | tf_op jit(solution)/shard_map/ppermute | solution.py:768
  254.0 3.3 %shard_map.201 = (bf16[512,768]{1,0:T(8,128)(2,1)}, bf16[512,768]{1,0:T(8,128)(2,1)}) custom-call(s32[36]{0:T(128)} %stack.147.meta, bf16[2,256,768]{2,1,0:T(8,128)(2,1)} %copy-done.4, bf16[2,256,768]{2,1,0:T(8,128)(2,1)} %collective-permute-done.31.b_ref), custom_call_target="tpu_custom_call" | custom-call | bytes 3145728 | tf_op jit(solution)/shard_map/pallas_call | solution.py:19
  257.2 3.2 %collective-permute-start.34 = (bf16[512,768]{1,0:T(8,128)(2,1)}, bf16[512,768]{1,0:T(8,128)(2,1)}, u32[]{:S(2)}, u32[]{:S(2)}) collective-permute-start(bf16[512,768]{1,0:T(8,128)(2,1)} %get-tuple-element.136), channel_id=1, source_target_pairs={{0,4},{1,9},{2,6},{3,11},{4,0},{5,13},{6,2},{7,15},{8,12},{9,1},{1... | collective-permute-start | bytes 2359304 | tf_op jit(solution)/shard_map/ppermute | solution.py:768
  260.4 2.7 collective-permute-done.18.r2_ref
  264.2 7.9 %shard_map.196 = (f32[2048,512]{1,0:T(8,128)}, f32[8,2048]{1,0:T(8,128)}, f32[8,512]{1,0:T(8,128)}) custom-call(s32[36]{0:T(128)} %stack.147.meta, bf16[1,2048,512]{2,1,0:T(8,128)(2,1)} %shard_map.195.k_ref, bf16[2,2048,512]{2,1,0:T(8,128)(2,1)} %collective-permute-done.16.rc_ref, bf16[1024,512]{1,0:T(8,128)(2,1)} %collective-permute-done.17.r1_ref, ...), custom_call_target="tpu_custom_call" | custom-call | flops 20971520 | bytes 12582912 | tf_op jit(solution)/shard_map/pallas_call | solution.py:19
  276.9 3.7 %collective-permute-done.37 = f32[6,512]{1,0:T(8,128)S(1)} collective-permute-done((f32[6,512]{1,0:T(8,128)S(1)}, f32[6,512]{1,0:T(8,128)S(1)}, u32[]{:S(2)}, u32[]{:S(2)}) %collective-permute-start.37) | collective-permute-done | bytes 12320 | tf_op jit(solution)/shard_map/ppermute | solution.py:857
  281.2 4.1 %collective-permute-done.38 = f32[6,512]{1,0:T(8,128)S(1)} collective-permute-done((f32[6,512]{1,0:T(8,128)S(1)}, f32[6,512]{1,0:T(8,128)S(1)}, u32[]{:S(2)}, u32[]{:S(2)}) %collective-permute-start.38) | collective-permute-done | bytes 12320 | tf_op jit(solution)/shard_map/ppermute | solution.py:857
  287.7 7.4 %shard_map.197 = bf16[2048,512]{1,0:T(8,128)(2,1)} custom-call(s32[36]{0:T(128)} %stack.147.meta, f32[2048,512]{1,0:T(8,128)} %get-tuple-element.121.dn_ref, f32[8,2048]{1,0:T(8,128)} %add.128.row_ref, bf16[2048,512]{1,0:T(8,128)(2,1)} %get-tuple-element.83.x_ref, f32[2048,128]{1,0:T(8,128)} %get-tuple-element.119.mu_ref, ...), custom_call_target="tpu_custom_call" | custom-call | flops 10485760 | bytes 12582912 | tf_op jit(solution)/shard_map/pallas_call | solution.py:19
  295.2 2.8 collective-permute-done.32.refs_5_
  298.0 8.5 %shard_map.202 = f32[2048,1536]{1,0:T(8,128)} custom-call(s32[36]{0:T(128)} %stack.147.meta, bf16[512,768]{1,0:T(8,128)(2,1)} %get-tuple-element.132.refs_0_, bf16[512,768]{1,0:T(8,128)(2,1)} %copy-done.9, bf16[512,768]{1,0:T(8,128)(2,1)} %copy-done.11, bf16[512,768]{1,0:T(8,128)(2,1)} %copy-done.12, bf16[512,768]{1,0:T(8,128)(2,1)} %get-tuple-element.135.refs_4_, ...), custom_call_target="tpu_custom_call" | custom-call | flops 3145728 | bytes 18874368 | tf_op jit(solution)/shard_map/pallas_call | solution.py:19
  (121 shorter events, 31.1 us)
Async XLA Ops:
  6.2 26.9 %collective-permute-start = (bf16[2048,384]{1,0:T(8,128)(2,1)}, bf16[2048,384]{1,0:T(8,128)(2,1)S(1)}, u32[]{:S(2)}, u32[]{:S(2)}) collective-permute-start(bf16[2048,384]{1,0:T(8,128)(2,1)} %get-tuple-element.82), channel_id=1, source_target_pairs={{0,1},{1,0},{2,3},{3,2},{4,5},{5,4},{6,7},{7,6},{8,9},{9,8},{10,11... | collective-permute-start | bytes 4718600 | tf_op jit(solution)/shard_map/ppermute | solution.py:762
  6.6 24.7 %collective-permute-start.1 = (bf16[2048,128]{1,0:T(8,128)(2,1)}, bf16[2048,128]{1,0:T(8,128)(2,1)S(1)}, u32[]{:S(2)}, u32[]{:S(2)}) collective-permute-start(bf16[2048,128]{1,0:T(8,128)(2,1)} %get-tuple-element.74), channel_id=1, source_target_pairs={{0,2},{1,3},{2,0},{3,1},{4,6},{5,7},{6,4},{7,5},{8,10},{9,11},{10,... | collective-permute-start | bytes 1572872 | tf_op jit(solution)/shard_map/ppermute | solution.py:762
  9.2 23.9 %collective-permute-start.2 = (bf16[2048,128]{1,0:T(8,128)(2,1)}, bf16[2048,128]{1,0:T(8,128)(2,1)S(1)}, u32[]{:S(2)}, u32[]{:S(2)}) collective-permute-start(bf16[2048,128]{1,0:T(8,128)(2,1)} %get-tuple-element.75), channel_id=1, source_target_pairs={{0,3},{1,2},{2,1},{3,0},{4,7},{5,6},{6,5},{7,4},{8,11},{9,10},{10,... | collective-permute-start | bytes 1572872 | tf_op jit(solution)/shard_map/ppermute | solution.py:762
  24.1 6.6 %copy-start.15 = (f32[512]{0:T(512)S(1)}, f32[512]{0:T(512)}, u32[]{:S(2)}) copy-start(f32[512]{0:T(512)} %param.15) | copy-start | bytes 6148
  24.1 6.6 %copy-start.16 = (f32[512]{0:T(512)S(1)}, f32[512]{0:T(512)}, u32[]{:S(2)}) copy-start(f32[512]{0:T(512)} %param.16) | copy-start | bytes 6148
  24.1 6.6 %copy-start.17 = (f32[512]{0:T(512)S(1)}, f32[512]{0:T(512)}, u32[]{:S(2)}) copy-start(f32[512]{0:T(512)} %param.17) | copy-start | bytes 6148
  29.0 50.3 %collective-permute-start.3 = (bf16[2048,256]{1,0:T(8,128)(2,1)}, bf16[2048,256]{1,0:T(8,128)(2,1)}, u32[]{:S(2)}, u32[]{:S(2)}) collective-permute-start(bf16[2048,256]{1,0:T(8,128)(2,1)} %get-tuple-element.79), channel_id=1, source_target_pairs={{0,2},{1,3},{2,0},{3,1},{4,6},{5,7},{6,4},{7,5},{8,10},{9,11},{10,... | collective-permute-start | bytes 3145736 | tf_op jit(solution)/shard_map/ppermute | solution.py:762
  30.7 48.5 %collective-permute-start.4 = (bf16[2048,256]{1,0:T(8,128)(2,1)}, bf16[2048,256]{1,0:T(8,128)(2,1)}, u32[]{:S(2)}, u32[]{:S(2)}) collective-permute-start(bf16[2048,256]{1,0:T(8,128)(2,1)} %get-tuple-element.80), channel_id=1, source_target_pairs={{0,3},{1,2},{2,1},{3,0},{4,7},{5,6},{6,5},{7,4},{8,11},{9,10},{10,... | collective-permute-start | bytes 3145736 | tf_op jit(solution)/shard_map/ppermute | solution.py:762
  67.6 23.8 %collective-permute-start.6 = (bf16[512,768]{1,0:T(8,128)(2,1)}, bf16[512,768]{1,0:T(8,128)(2,1)}, u32[]{:S(2)}, u32[]{:S(2)}) collective-permute-start(bf16[512,768]{1,0:T(8,128)(2,1)} %get-tuple-element.87), channel_id=1, source_target_pairs={{0,4},{1,9},{2,6},{3,11},{4,0},{5,13},{6,2},{7,15},{8,12},{9,1},{1... | collective-permute-start | bytes 2359304 | tf_op jit(solution)/shard_map/ppermute | solution.py:768
  69.1 8.6 %collective-permute-start.7 = (bf16[512,768]{1,0:T(8,128)(2,1)}, bf16[512,768]{1,0:T(8,128)(2,1)S(1)}, u32[]{:S(2)}, u32[]{:S(2)}) collective-permute-start(bf16[512,768]{1,0:T(8,128)(2,1)} %get-tuple-element.93), channel_id=1, source_target_pairs={{0,1},{1,0},{2,3},{3,2},{4,5},{5,4},{6,7},{7,6},{8,9},{9,8},{10,11... | collective-permute-start | bytes 2359304 | tf_op jit(solution)/shard_map/ppermute | solution.py:762
  77.6 13.7 %collective-permute-start.5 = (bf16[512,768]{1,0:T(8,128)(2,1)}, bf16[512,768]{1,0:T(8,128)(2,1)S(1)}, u32[]{:S(2)}, u32[]{:S(2)}) collective-permute-start(bf16[512,768]{1,0:T(8,128)(2,1)} %get-tuple-element.92), channel_id=1, source_target_pairs={{0,1},{1,0},{2,3},{3,2},{4,5},{5,4},{6,7},{7,6},{8,9},{9,8},{10,11... | collective-permute-start | bytes 2359304 | tf_op jit(solution)/shard_map/ppermute | solution.py:762
  77.7 13.7 %collective-permute-start.8 = (bf16[512,768]{1,0:T(8,128)(2,1)S(1)}, bf16[512,768]{1,0:T(8,128)(2,1)S(1)}, u32[]{:S(2)}, u32[]{:S(2)}) collective-permute-start(bf16[512,768]{1,0:T(8,128)(2,1)S(1)} %collective-permute-done.7), channel_id=1, source_target_pairs={{0,4},{1,9},{2,6},{3,11},{4,0},{5,13},{6,2},{7,15},{8,12},{9,1},{1... | collective-permute-start | bytes 2359304 | tf_op jit(solution)/shard_map/ppermute | solution.py:768
  96.9 13.0 %collective-permute-start.9 = (bf16[2,256,768]{2,1,0:T(8,128)(2,1)}, bf16[2,256,768]{2,1,0:T(8,128)(2,1)S(1)}, u32[]{:S(2)}, u32[]{:S(2)}) collective-permute-start(bf16[2,256,768]{2,1,0:T(8,128)(2,1)} %get-tuple-element.94), channel_id=1, source_target_pairs={{0,8},{1,5},{2,10},{3,7},{4,12},{5,1},{6,14},{7,3},{8,0},{9,13},{1... | collective-permute-start | bytes 2359304 | tf_op jit(solution)/shard_map/ppermute | solution.py:768
  113.8 34.3 %collective-permute-start.10 = (bf16[2,128,768]{2,1,0:T(8,128)(2,1)}, bf16[2,128,768]{2,1,0:T(8,128)(2,1)}, u32[]{:S(2)}, u32[]{:S(2)}) collective-permute-start(bf16[2,128,768]{2,1,0:T(8,128)(2,1)} %get-tuple-element.103), channel_id=1, source_target_pairs={{0,16},{1,17},{2,18},{3,19},{4,20},{5,21},{6,22},{7,23},{8,24},{9,... | collective-permute-start | bytes 1179656 | tf_op jit(solution)/shard_map/ppermute | solution.py:768
  124.5 32.1 %collective-permute-start.12 = (bf16[512,768]{1,0:T(8,128)(2,1)}, bf16[512,768]{1,0:T(8,128)(2,1)}, u32[]{:S(2)}, u32[]{:S(2)}) collective-permute-start(bf16[512,768]{1,0:T(8,128)(2,1)} %get-tuple-element.105), channel_id=1, source_target_pairs={{0,4},{1,9},{2,6},{3,11},{4,0},{5,13},{6,2},{7,15},{8,12},{9,1},{1... | collective-permute-start | bytes 2359304 | tf_op jit(solution)/shard_map/ppermute | solution.py:768
  126.0 8.7 %collective-permute-start.13 = (bf16[512,768]{1,0:T(8,128)(2,1)}, bf16[512,768]{1,0:T(8,128)(2,1)S(1)}, u32[]{:S(2)}, u32[]{:S(2)}) collective-permute-start(bf16[512,768]{1,0:T(8,128)(2,1)} %get-tuple-element.114), channel_id=1, source_target_pairs={{0,1},{1,0},{2,3},{3,2},{4,5},{5,4},{6,7},{7,6},{8,9},{9,8},{10,11... | collective-permute-start | bytes 2359304 | tf_op jit(solution)/shard_map/ppermute | solution.py:762
  134.2 22.4 %collective-permute-start.11 = (bf16[512,768]{1,0:T(8,128)(2,1)}, bf16[512,768]{1,0:T(8,128)(2,1)S(1)}, u32[]{:S(2)}, u32[]{:S(2)}) collective-permute-start(bf16[512,768]{1,0:T(8,128)(2,1)} %get-tuple-element.113), channel_id=1, source_target_pairs={{0,1},{1,0},{2,3},{3,2},{4,5},{5,4},{6,7},{7,6},{8,9},{9,8},{10,11... | collective-permute-start | bytes 2359304 | tf_op jit(solution)/shard_map/ppermute | solution.py:762
  134.7 21.9 %collective-permute-start.14 = (bf16[512,768]{1,0:T(8,128)(2,1)S(1)}, bf16[512,768]{1,0:T(8,128)(2,1)S(1)}, u32[]{:S(2)}, u32[]{:S(2)}) collective-permute-start(bf16[512,768]{1,0:T(8,128)(2,1)S(1)} %collective-permute-done.13), channel_id=1, source_target_pairs={{0,4},{1,9},{2,6},{3,11},{4,0},{5,13},{6,2},{7,15},{8,12},{9,1},{1... | collective-permute-start | bytes 2359304 | tf_op jit(solution)/shard_map/ppermute | solution.py:768
  150.8 5.4 %collective-permute-start.15 = (bf16[2,128,256]{2,1,0:T(8,128)(2,1)}, bf16[2,128,256]{2,1,0:T(8,128)(2,1)S(1)}, u32[]{:S(2)}, u32[]{:S(2)}) collective-permute-start(bf16[2,128,256]{2,1,0:T(8,128)(2,1)} %get-tuple-element.116), channel_id=1, source_target_pairs={{0,2},{1,3},{2,0},{3,1},{4,6},{5,7},{6,4},{7,5},{8,10},{9,11},{10,... | collective-permute-start | bytes 393224 | tf_op jit(solution)/shard_map/ppermute | solution.py:762
  152.2 19.7 %collective-permute-start.16 = (bf16[2,2048,512]{2,1,0:T(8,128)(2,1)}, bf16[2,2048,512]{2,1,0:T(8,128)(2,1)}, u32[]{:S(2)}, u32[]{:S(2)}) collective-permute-start(bf16[2,2048,512]{2,1,0:T(8,128)(2,1)} %shard_map.191), channel_id=1, source_target_pairs={{0,1},{1,0},{2,3},{3,2},{4,5},{5,4},{6,7},{7,6},{8,9},{9,8},{10,11... | collective-permute-start | bytes 12582920 | tf_op jit(solution)/shard_map/ppermute | solution.py:762
  156.2 28.3 %collective-permute-start.21 = (bf16[2,128,768]{2,1,0:T(8,128)(2,1)S(1)}, bf16[2,128,768]{2,1,0:T(8,128)(2,1)}, u32[]{:S(2)}, u32[]{:S(2)}) collective-permute-start(bf16[2,128,768]{2,1,0:T(8,128)(2,1)S(1)} %constant_dynamic-update-slice_fusion), channel_id=1, source_target_pairs={{0,16},{1,17},{2,18},{3,19},{4,20},{5,21},{6,22},{7,23},{8,24},{9,... | collective-permute-start | bytes 1179656 | tf_op jit(solution)/shard_map/ppermute | solution.py:768
  162.4 23.2 %collective-permute-start.22 = (bf16[2,256,768]{2,1,0:T(8,128)(2,1)}, bf16[2,256,768]{2,1,0:T(8,128)(2,1)S(1)}, u32[]{:S(2)}, u32[]{:S(2)}) collective-permute-start(bf16[2,256,768]{2,1,0:T(8,128)(2,1)} %get-tuple-element.115), channel_id=1, source_target_pairs={{0,8},{1,5},{2,10},{3,7},{4,12},{5,1},{6,14},{7,3},{8,0},{9,13},{1... | collective-permute-start | bytes 2359304 | tf_op jit(solution)/shard_map/ppermute | solution.py:768
  174.8 23.7 %collective-permute-start.17 = (bf16[1024,512]{1,0:T(8,128)(2,1)S(1)}, bf16[1024,512]{1,0:T(8,128)(2,1)}, u32[]{:S(2)}, u32[]{:S(2)}) collective-permute-start(bf16[1024,512]{1,0:T(8,128)(2,1)S(1)} %get-tuple-element.140), channel_id=1, source_target_pairs={{0,2},{1,3},{2,0},{3,1},{4,6},{5,7},{6,4},{7,5},{8,10},{9,11},{10,... | collective-permute-start | bytes 3145736 | tf_op jit(solution)/shard_map/ppermute | solution.py:762
  185.6 54.9 %copy-start.7 = (bf16[2,256,768]{2,1,0:T(8,128)(2,1)}, bf16[2,256,768]{2,1,0:T(8,128)(2,1)S(1)}, u32[]{:S(2)}) copy-start(bf16[2,256,768]{2,1,0:T(8,128)(2,1)S(1)} %constant_dynamic-update-slice_fusion.2.a_ref) | copy-start | bytes 2359300
  189.5 18.5 %collective-permute-start.23 = (bf16[2,128,768]{2,1,0:T(8,128)(2,1)}, bf16[2,128,768]{2,1,0:T(8,128)(2,1)S(1)}, u32[]{:S(2)}, u32[]{:S(2)}) collective-permute-start(bf16[2,128,768]{2,1,0:T(8,128)(2,1)} %get-tuple-element.129), channel_id=1, source_target_pairs={{0,16},{1,17},{2,18},{3,19},{4,20},{5,21},{6,22},{7,23},{8,24},{9,... | collective-permute-start | bytes 1179656 | tf_op jit(solution)/shard_map/ppermute | solution.py:768
  211.4 8.4 %collective-permute-start.29 = (bf16[2,128,512]{2,1,0:T(8,128)(2,1)}, bf16[2,128,512]{2,1,0:T(8,128)(2,1)S(1)}, u32[]{:S(2)}, u32[]{:S(2)}) collective-permute-start(bf16[2,128,512]{2,1,0:T(8,128)(2,1)} %get-tuple-element.134), channel_id=1, source_target_pairs={{0,2},{1,3},{2,0},{3,1},{4,6},{5,7},{6,4},{7,5},{8,10},{9,11},{10,... | collective-permute-start | bytes 786440 | tf_op jit(solution)/shard_map/ppermute | solution.py:762
  219.9 40.5 %copy-start.14 = (f32[8,512]{1,0:T(8,128)S(1)}, f32[8,512]{1,0:T(8,128)}, u32[]{:S(2)}) copy-start(f32[8,512]{1,0:T(8,128)} %get-tuple-element.138) | copy-start | bytes 49156
  219.9 17.1 %collective-permute-start.30 = (bf16[2,128,768]{2,1,0:T(8,128)(2,1)S(1)}, bf16[2,128,768]{2,1,0:T(8,128)(2,1)S(1)}, u32[]{:S(2)}, u32[]{:S(2)}) collective-permute-start(bf16[2,128,768]{2,1,0:T(8,128)(2,1)S(1)} %constant_dynamic-update-slice_fusion.4), channel_id=1, source_target_pairs={{0,16},{1,17},{2,18},{3,19},{4,20},{5,21},{6,22},{7,23},{8,24},{9,... | collective-permute-start | bytes 1179656 | tf_op jit(solution)/shard_map/ppermute | solution.py:768
  220.0 20.5 %collective-permute-start.24 = (bf16[2,256,768]{2,1,0:T(8,128)(2,1)S(1)}, bf16[2,256,768]{2,1,0:T(8,128)(2,1)}, u32[]{:S(2)}, u32[]{:S(2)}) collective-permute-start(bf16[2,256,768]{2,1,0:T(8,128)(2,1)S(1)} %constant_dynamic-update-slice_fusion.2.a_ref), channel_id=1, source_target_pairs={{0,8},{1,5},{2,10},{3,7},{4,12},{5,1},{6,14},{7,3},{8,0},{9,13},{1... | collective-permute-start | bytes 2359304 | tf_op jit(solution)/shard_map/ppermute | solution.py:768
  237.0 16.9 %copy-start.4 = (bf16[2,256,768]{2,1,0:T(8,128)(2,1)}, bf16[2,256,768]{2,1,0:T(8,128)(2,1)S(1)}, u32[]{:S(2)}) copy-start(bf16[2,256,768]{2,1,0:T(8,128)(2,1)S(1)} %pad_maximum_fusion.a_ref) | copy-start | bytes 2359300
  237.1 16.9 %collective-permute-start.31 = (bf16[2,256,768]{2,1,0:T(8,128)(2,1)S(1)}, bf16[2,256,768]{2,1,0:T(8,128)(2,1)}, u32[]{:S(2)}, u32[]{:S(2)}) collective-permute-start(bf16[2,256,768]{2,1,0:T(8,128)(2,1)S(1)} %pad_maximum_fusion.a_ref), channel_id=1, source_target_pairs={{0,8},{1,5},{2,10},{3,7},{4,12},{5,1},{6,14},{7,3},{8,0},{9,13},{1... | collective-permute-start | bytes 2359304 | tf_op jit(solution)/shard_map/ppermute | solution.py:768
  237.1 26.0 %collective-permute-start.18 = (bf16[1024,512]{1,0:T(8,128)(2,1)S(1)}, bf16[1024,512]{1,0:T(8,128)(2,1)S(1)}, u32[]{:S(2)}, u32[]{:S(2)}) collective-permute-start(bf16[1024,512]{1,0:T(8,128)(2,1)S(1)} %get-tuple-element.139), channel_id=1, source_target_pairs={{0,2},{1,3},{2,0},{3,1},{4,6},{5,7},{6,4},{7,5},{8,10},{9,11},{10,... | collective-permute-start | bytes 3145736 | tf_op jit(solution)/shard_map/ppermute | solution.py:762
  243.8 41.5 %collective-permute-start.27 = (bf16[512,768]{1,0:T(8,128)(2,1)}, bf16[512,768]{1,0:T(8,128)(2,1)}, u32[]{:S(2)}, u32[]{:S(2)}) collective-permute-start(bf16[512,768]{1,0:T(8,128)(2,1)} %get-tuple-element.133), channel_id=1, source_target_pairs={{0,4},{1,9},{2,6},{3,11},{4,0},{5,13},{6,2},{7,15},{8,12},{9,1},{1... | collective-permute-start | bytes 2359304 | tf_op jit(solution)/shard_map/ppermute | solution.py:768
  244.9 40.9 %collective-permute-start.25 = (bf16[512,768]{1,0:T(8,128)(2,1)}, bf16[512,768]{1,0:T(8,128)(2,1)S(1)}, u32[]{:S(2)}, u32[]{:S(2)}) collective-permute-start(bf16[512,768]{1,0:T(8,128)(2,1)} %get-tuple-element.132.refs_0_), channel_id=1, source_target_pairs={{0,4},{1,9},{2,6},{3,11},{4,0},{5,13},{6,2},{7,15},{8,12},{9,1},{1... | collective-permute-start | bytes 2359304 | tf_op jit(solution)/shard_map/ppermute | solution.py:768
  257.2 29.3 %collective-permute-start.34 = (bf16[512,768]{1,0:T(8,128)(2,1)}, bf16[512,768]{1,0:T(8,128)(2,1)}, u32[]{:S(2)}, u32[]{:S(2)}) collective-permute-start(bf16[512,768]{1,0:T(8,128)(2,1)} %get-tuple-element.136), channel_id=1, source_target_pairs={{0,4},{1,9},{2,6},{3,11},{4,0},{5,13},{6,2},{7,15},{8,12},{9,1},{1... | collective-permute-start | bytes 2359304 | tf_op jit(solution)/shard_map/ppermute | solution.py:768
  264.2 21.1 %copy-start.20 = (bf16[512,768]{1,0:T(8,128)(2,1)S(1)}, bf16[512,768]{1,0:T(8,128)(2,1)}, u32[]{:S(2)}) copy-start(bf16[512,768]{1,0:T(8,128)(2,1)} %get-tuple-element.133) | copy-start | bytes 2359300
  264.2 21.7 %copy-start.10 = (bf16[512,768]{1,0:T(8,128)(2,1)S(1)}, bf16[512,768]{1,0:T(8,128)(2,1)}, u32[]{:S(2)}) copy-start(bf16[512,768]{1,0:T(8,128)(2,1)} %get-tuple-element.135.refs_4_) | copy-start | bytes 2359300
  272.8 1.5 collective-permute-start.19
  273.0 3.8 %collective-permute-start.36 = (f32[6,512]{1,0:T(8,128)S(1)}, f32[6,512]{1,0:T(8,128)S(1)}, u32[]{:S(2)}, u32[]{:S(2)}) collective-permute-start(f32[6,512]{1,0:T(8,128)S(1)} %pad_maximum_fusion.1), channel_id=1, source_target_pairs={{0,4},{4,0},{8,12},{12,8},{16,20},{20,16},{24,28},{28,24},{1,5},{5... | collective-permute-start | bytes 36872 | tf_op jit(solution)/shard_map/ppermute | solution.py:857
  275.1 10.7 %collective-permute-start.20 = (f32[8,2048]{1,0:T(8,128)S(1)}, f32[8,2048]{1,0:T(8,128)S(1)}, u32[]{:S(2)}, u32[]{:S(2)}) collective-permute-start(f32[8,2048]{1,0:T(8,128)S(1)} %add.127), channel_id=1, source_target_pairs={{0,2},{1,3},{2,0},{3,1},{4,6},{5,7},{6,4},{7,5},{8,10},{9,11},{10,... | collective-permute-start | bytes 196616 | tf_op jit(solution)/shard_map/ppermute | solution.py:762
  276.8 3.8 %collective-permute-start.37 = (f32[6,512]{1,0:T(8,128)S(1)}, f32[6,512]{1,0:T(8,128)S(1)}, u32[]{:S(2)}, u32[]{:S(2)}) collective-permute-start(f32[6,512]{1,0:T(8,128)S(1)} %fusion.2), channel_id=1, source_target_pairs={{0,8},{4,12},{8,0},{12,4},{16,24},{20,28},{24,16},{28,20},{1,9},{5... | collective-permute-start | bytes 36872 | tf_op jit(solution)/shard_map/ppermute | solution.py:857
  280.6 4.6 %collective-permute-start.38 = (f32[6,512]{1,0:T(8,128)S(1)}, f32[6,512]{1,0:T(8,128)S(1)}, u32[]{:S(2)}, u32[]{:S(2)}) collective-permute-start(f32[6,512]{1,0:T(8,128)S(1)} %add.130), channel_id=1, source_target_pairs={{0,16},{4,20},{8,24},{12,28},{16,0},{20,4},{24,8},{28,12},{1,17},{... | collective-permute-start | bytes 36872 | tf_op jit(solution)/shard_map/ppermute | solution.py:857
  285.3 9.9 %collective-permute-start.26 = (bf16[512,768]{1,0:T(8,128)(2,1)S(1)}, bf16[512,768]{1,0:T(8,128)(2,1)S(1)}, u32[]{:S(2)}, u32[]{:S(2)}) collective-permute-start(bf16[512,768]{1,0:T(8,128)(2,1)S(1)} %copy-done.20), channel_id=1, source_target_pairs={{0,1},{1,0},{2,3},{3,2},{4,5},{5,4},{6,7},{7,6},{8,9},{9,8},{10,11... | collective-permute-start | bytes 2359304 | tf_op jit(solution)/shard_map/ppermute | solution.py:762
  285.3 9.9 %collective-permute-start.28 = (bf16[512,768]{1,0:T(8,128)(2,1)}, bf16[512,768]{1,0:T(8,128)(2,1)S(1)}, u32[]{:S(2)}, u32[]{:S(2)}) collective-permute-start(bf16[512,768]{1,0:T(8,128)(2,1)} %collective-permute-done.27), channel_id=1, source_target_pairs={{0,1},{1,0},{2,3},{3,2},{4,5},{5,4},{6,7},{7,6},{8,9},{9,8},{10,11... | collective-permute-start | bytes 2359304 | tf_op jit(solution)/shard_map/ppermute | solution.py:762
  285.8 12.2 %collective-permute-start.33 = (bf16[512,768]{1,0:T(8,128)(2,1)}, bf16[512,768]{1,0:T(8,128)(2,1)}, u32[]{:S(2)}, u32[]{:S(2)}) collective-permute-start(bf16[512,768]{1,0:T(8,128)(2,1)} %get-tuple-element.136), channel_id=1, source_target_pairs={{0,1},{1,0},{2,3},{3,2},{4,5},{5,4},{6,7},{7,6},{8,9},{9,8},{10,11... | collective-permute-start | bytes 2359304 | tf_op jit(solution)/shard_map/ppermute | solution.py:762
  285.9 9.3 %copy-start.9 = (bf16[512,768]{1,0:T(8,128)(2,1)}, bf16[512,768]{1,0:T(8,128)(2,1)S(1)}, u32[]{:S(2)}) copy-start(bf16[512,768]{1,0:T(8,128)(2,1)S(1)} %collective-permute-done.25.refs_1_) | copy-start | bytes 2359300
  285.9 12.2 %collective-permute-start.32 = (bf16[512,768]{1,0:T(8,128)(2,1)S(1)}, bf16[512,768]{1,0:T(8,128)(2,1)}, u32[]{:S(2)}, u32[]{:S(2)}) collective-permute-start(bf16[512,768]{1,0:T(8,128)(2,1)S(1)} %copy-done.10), channel_id=1, source_target_pairs={{0,4},{1,9},{2,6},{3,11},{4,0},{5,13},{6,2},{7,15},{8,12},{9,1},{1... | collective-permute-start | bytes 2359304 | tf_op jit(solution)/shard_map/ppermute | solution.py:768
  286.5 11.5 %collective-permute-start.35 = (bf16[512,768]{1,0:T(8,128)(2,1)}, bf16[512,768]{1,0:T(8,128)(2,1)}, u32[]{:S(2)}, u32[]{:S(2)}) collective-permute-start(bf16[512,768]{1,0:T(8,128)(2,1)} %collective-permute-done.34), channel_id=1, source_target_pairs={{0,1},{1,0},{2,3},{3,2},{4,5},{5,4},{6,7},{7,6},{8,9},{9,8},{10,11... | collective-permute-start | bytes 2359304 | tf_op jit(solution)/shard_map/ppermute | solution.py:762
  (14 other events, 23.2 us)

commit v4 on v3

--- a/solution.py
+++ b/solution.py
@@ -13,6 +13,7 @@
 LANES = 128
 VMEM_LIMIT = 60 * 1024 * 1024
 COVER = 20
+FIRST = 2
 
 
 def call(kernel, meta, args, grid, in_specs, out_specs, out_shape, scratch=(), aliases=None, cost=None):
@@ -398,7 +399,7 @@
 
 
 def back_kernel(meta, ds1_ref, ds2_ref, *refs):
-    out_ref, W = refs[-2:]
+    outs, W = refs[-3:-1], refs[-1]
     chunk = ds1_ref.shape[1]
 
     @pl.when(pl.program_id(1) == 0)
@@ -407,26 +408,34 @@
         gather_units(meta, M_S2, refs[6:12], W, chunk)
 
     dims = (((1,), (1,)), ((), ()))
-    value = lax.dot_general(ds1_ref[...], W[:, :chunk], dims, preferred_element_type=F32)
-    value += lax.dot_general(ds2_ref[...], W[:, chunk:], dims, preferred_element_type=F32)
-    out_ref[0] = value.astype(BF16)
-
-
-def back(meta, ds1, ds2, units, first, count, tb=1024):
+    for n, out_ref in enumerate(outs):
+
+        @pl.when(pl.program_id(0) == n)
+        def _(out_ref=out_ref):
+            value = lax.dot_general(ds1_ref[...], W[:, :chunk], dims, preferred_element_type=F32)
+            value += lax.dot_general(ds2_ref[...], W[:, chunk:], dims, preferred_element_type=F32)
+            out_ref[...] = value.astype(BF16)
+
+
+def back(meta, ds1, ds2, units, first, tb=1024):
     tokens, width = ds1.shape
     features = units[0][0].shape[0]
     block = features // 4
+    steps = tokens // tb
     dspec = pl.BlockSpec((tb, width), lambda n, t, m: (t, 0))
     return call(
         back_kernel,
         meta,
         [ds1, ds2] + [array for array, _, _ in units],
-        (count, tokens // tb),
+        (2, steps),
         [dspec, dspec] + unit_specs(units, block, lambda n, t, m: m[first + n]),
-        pl.BlockSpec((1, tb, block), lambda n, t, m: (n, t, 0)),
-        struct((count, tokens, block), BF16),
+        [
+            pl.BlockSpec((tb, block), lambda n, t, m: (jnp.where(n == 0, t, steps - 1), 0)),
+            pl.BlockSpec((tb, block), lambda n, t, m: (jnp.where(n == 0, 0, t), 0)),
+        ],
+        [struct((tokens, block), BF16)] * 2,
         scratch=[pltpu.VMEM((block, 2 * width), BF16)],
-        cost=cost(4 * count * tokens * block * width, 4 * count * tokens * width, weight=COVER),
+        cost=cost(8 * tokens * block * width, 8 * tokens * width, weight=COVER),
     )
 
 
@@ -446,9 +455,9 @@
 
 def tail_sums_kernel(meta, k_ref, rc_ref, r1_ref, r2_ref, x_ref, mu_ref, inv_ref, gain_ref, dn_ref, row_ref, col_ref):
     unit, _ = unit_of(x_ref, mu_ref, inv_ref)
-    early = pl.program_id(0) < pl.num_programs(0) // 2
+    early = pl.program_id(0) < pl.num_programs(0) * FIRST // 4
     far = jnp.where(early, r1_ref[...].astype(F32), r2_ref[...].astype(F32))
-    dn = k_ref[0].astype(F32) + rc_ref[0].astype(F32) + far
+    dn = k_ref[...].astype(F32) + rc_ref[...].astype(F32) + far
     dn_ref[...] = dn
     gu = dn * gain_ref[...]
     row_ref[0:1, :] = lane_sums(gu)
@@ -465,7 +474,7 @@
 
 def tail_sums(meta, keep, got, far, x, mu, inv, gain, tb=512):
     tokens, channels = x.shape
-    half = tokens // tb // 2
+    first = tokens // tb * FIRST // 4
     wide = pl.BlockSpec((tb, channels), lambda t, m: (t, 0))
     stat = pl.BlockSpec((tb, LANES), lambda t, m: (t, 0))
     return call(
@@ -474,10 +483,10 @@
         (keep, got, *far, x, mu, inv, gain[None]),
         (tokens // tb,),
         [
-            pl.BlockSpec((1, tb, channels), lambda t, m: (0, t, 0)),
-            pl.BlockSpec((1, tb, channels), lambda t, m: (1, t, 0)),
-            pl.BlockSpec((tb, channels), lambda t, m: (jnp.minimum(t, half - 1), 0)),
-            pl.BlockSpec((tb, channels), lambda t, m: (jnp.maximum(t - half, 0), 0)),
+            wide,
+            wide,
+            pl.BlockSpec((tb, channels), lambda t, m: (jnp.minimum(t, first - 1), 0)),
+            pl.BlockSpec((tb, channels), lambda t, m: (jnp.maximum(t - first, 0), 0)),
             wide,
             stat,
             stat,
@@ -695,7 +704,7 @@
 M_GATE, M_CORE, M_H1, M_H2 = 0, 1, 2, 3
 M_S1, M_S2 = 4, 7
 M_SEND, M_KEEP = 10, 12
-M_OUT, M_IN = 14, 16
+M_FAR, M_HERE = 14, 16
 M_OWN, M_RHO = 18, 22
 M_TO2, M_TO3, M_NEAR, M_LATE2, M_LATE3 = 24, 25, 26, 27, 28
 M_PAIR, M_SINGLE, M_GOT_PAIR, M_GOT_SINGLE = 29, 30, 31, 32
@@ -749,7 +758,7 @@
         [gate, core, h1, h2, *streams(h1), *streams(h2)]
         + [other * 2 + 1 - bit(other, 0), core * 2 + 1 - bit(core, 0)]
         + [other * 2 + bit(other, 0), core * 2 + bit(core, 0)]
-        + [far + other, hi * 2 + other, far + core, hi * 2 + core]
+        + [far + other, far + core, hi * 2 + other, hi * 2 + core]
         + [gate, hi * 2 + other, far + core, far + other]
         + [rho(core), rho(other)]
         + [(far + core) * 3 + single, (far + other) * 3 + single, (hi * 2 + other) * 3]
@@ -821,36 +830,39 @@
         step1 = over_dp(away1, step)
     mine2, got2 = first_sends(after(meta, away1), ds2)
     kept2 = first_keeps(after(meta, mine2), ds2)
-    send = back(after(meta, kept2[0]), ds1, ds2, units, M_OUT, 2)
-    got = over_gate(send, 1)
-    near1, far1 = gathered(after(meta, send), M_H1, False, stay1, step1)
+    far_theirs, far_mine = back(after(meta, kept2[0]), ds1, ds2, units, M_FAR)
+    far_got = over_gate(far_theirs, 1)
+    near1, far1 = gathered(after(meta, far_mine), M_H1, False, stay1, step1)
     away2, stay2 = halve(after(meta, near1), M_BIT + 1, kept2, got2)
     step2 = over_dp(away2, 1)
     shard1 = jnp.concatenate([near1, far1], axis=2)
+    theirs, mine = back(after(meta, away2, shard1), ds1, ds2, units, M_HERE)
+    cut_at = tokens * FIRST // 4
+    far_send = [
+        (far_mine[at].astype(F32) + far_got[at].astype(F32)).astype(BF16) for at in (slice(cut_at), slice(cut_at, None))
+    ]
+    far_part = [over_gate(part, 2) for part in far_send]
+    shard1 = last_steps(shard1, mine)
+    for step in range(2, bits):
+        away2, stay2 = halve(after(meta, shard1, *far_send), M_BIT + step, [stay2], [step2])
+        step2 = over_dp(away2, step)
+
+    got = over_gate(after(theirs, away2), 1)
 
     def last_doubling(meta, shard):
         mine, theirs = join(meta, shard, over_dp(shard, 1))
         moved = over_dp(theirs, 0)
         return [mine, over_dp(mine, 0), over_gate(theirs, 1), over_gate(moved, 1)]
 
-    kept_far = back(after(meta, away2, shard1), ds1, ds2, units, M_IN, 1)
-    half = tokens // 2
-    far_send = [(kept_far[0, at : at + half].astype(F32) + got[0, at : at + half].astype(F32)).astype(BF16) for at in (0, half)]
-    far_part = [over_gate(part, 2) for part in far_send]
-    kept = back(after(meta, *far_send), ds1, ds2, units, M_IN + 1, 1)
-    shard1 = last_steps(shard1, kept)
-    for step in range(2, bits):
-        away2, stay2 = halve(after(meta, shard1, kept), M_BIT + step, [stay2], [step2])
-        step2 = over_dp(away2, step)
-    near2, far2 = gathered(after(meta, far_part[0]), M_H2, True, stay2, step2)
+    near2, far2 = gathered(after(meta, shard1, far_part[0]), M_H2, True, stay2, step2)
     parts1 = last_doubling(after(meta, near2), shard1)
-    shard2 = last_steps(jnp.concatenate([near2, far2], axis=2))
+    dn, row_sums, col_sums = tail_sums(after(meta, parts1[0]), mine, got, far_part, own_x, mu, inv, ln_gain)
+    shard2 = last_steps(jnp.concatenate([near2, far2], axis=2), dn)
     parts2 = last_doubling(meta, shard2)
 
-    dn, row_sums, col_sums = tail_sums(meta, kept, got, far_part, own_x, mu, inv, ln_gain)
     for delta in (1, 2):
         row_sums = row_sums + over_gate(row_sums, delta)
-    dinputs = tail(meta, dn, row_sums, own_x, mu, inv, ln_gain, direct, features)
+    dinputs = tail(after(meta, parts2[0]), dn, row_sums, own_x, mu, inv, ln_gain, direct, features)
 
     totals = jnp.concatenate([col_sums[:2], vecs[:4]], axis=0)
     for step in range(bits):

time: 308 us -> 336 us (1.091)
  waiting for transfers between devices: 68.4 us -> 91.4 us
  local copies, waits for them, and re-layouts: 14.7 us -> 18.7 us
    ppermute x20 -> x21, waiting for transfers between devices: 21.4 us -> 47 us  [over_gate(): return lax.ppermute(value, 'gate', [(g, g ^ delta) for g in range(n_gate)])]
    ppermute x16, waiting for transfers between devices: 37.9 us -> 30.6 us  [over_dp(): return lax.ppermute(value, ('dp', 'gate'), pairs)]
    ppermute x3, waiting for transfers between devices: 9.02 us -> 13.8 us  [shards(): lax.ppermute(totals, 'dp', [(d, d ^ 1 << step) for d in range(n_dp)])]
    unnamed x49 -> x58, local copies, waits for them, and re-layouts: 11.1 us -> 13.2 us
    pallas_call x25 -> x24, Pallas kernels: 185 us -> 183 us  [call(): pl.pallas_call(kernel, grid_spec=pltpu.PrefetchScalarGridSpec(num_scalar_...]
    ppermute x20 -> x21, starting transfers between devices: 11.8 us -> 12.8 us  [over_gate(): return lax.ppermute(value, 'gate', [(g, g ^ delta) for g in range(n_gate)])]
  transfers between devices with their start and end apart: 39 -> 40, of which waited for: 14 -> 10; matrix products, arithmetic and copies ran while one was open for 3% -> 4% of each run, Pallas kernels for 53% -> 48%
where the time goes in v4:
time: 336 us; the launch traced here: 335 us
  Pallas kernels  183 us (54%)
  waiting for transfers between devices  91.4 us (27%)
  starting transfers between devices  36.6 us (11%)
  local copies, waits for them, and re-layouts  18.7 us (6%)
  other arithmetic  4.42 us (1%)
    pallas_call x24, Pallas kernels, call(): pl.pallas_call(kernel, grid_spec=pltpu.PrefetchScalarGridSpec(num_scalar_...  183 us
    ppermute x21, waiting for transfers between devices, over_gate(): return lax.ppermute(value, 'gate', [(g, g ^ delta) for g in range(n_gate)])  47 us
    ppermute x16, waiting for transfers between devices, over_dp(): return lax.ppermute(value, ('dp', 'gate'), pairs)  30.6 us
    ppermute x16, starting transfers between devices, over_dp(): return lax.ppermute(value, ('dp', 'gate'), pairs)  20.2 us
    ppermute x3, waiting for transfers between devices, shards(): lax.ppermute(totals, 'dp', [(d, d ^ 1 << step) for d in range(n_dp)])  13.8 us
    unnamed x58, local copies, waits for them, and re-layouts  13.2 us
    ppermute x21, starting transfers between devices, over_gate(): return lax.ppermute(value, 'gate', [(g, g ^ delta) for g in range(n_gate)])  12.8 us
  transfers between devices with their start and end apart: 40, of which 10 were waited for; matrix products, arithmetic and copies ran while one was open for 4% of the time, Pallas kernels for 48%

profile of v4, /device:TPU:0, one launch (start us, length us, event | category | flops | bytes accessed | tf_op | source)
XLA Modules:
  0.0 334.7 jit_solution(3467730229941597185)
XLA Ops:
  1.4 4.8 %shard_map.178 = (bf16[2048,128]{1,0:T(8,128)(2,1)}, bf16[2048,128]{1,0:T(8,128)(2,1)}, bf16[2048,384]{1,0:T(8,128)(2,1)}) custom-call(s32[36]{0:T(128)} %stack.147.meta, bf16[2048,1536]{1,0:T(8,128)(2,1)} %refs_10_.3, bf16[2048,1536]{1,0:T(8,128)(2,1)} %refs_10_.3, bf16[2048,1536]{1,0:T(8,128)(2,1)} %refs_10_.3, bf16[2048,1536]{1,0:T(8,128)(2,1)} %refs_10_.3, ...), custom_call_target="tpu_custom_call" | custom-call | bytes 5242880 | tf_op jit(solution)/shard_map/pallas_call | solution.py:20
  6.7 2.6 collective-permute-start.1
  9.3 14.9 %shard_map.179 = (bf16[2048,2048]{1,0:T(8,128)(2,1)}, f32[2048,128]{1,0:T(8,128)}, f32[2048,128]{1,0:T(8,128)}, bf16[2048,512]{1,0:T(8,128)(2,1)}, f32[2048,128]{1,0:T(8,128)}, /*index=5*/f32[2048,128]{1,0:T(8,128)}) custom-call(s32[36]{0:T(128)} %stack.147.meta, bf16[2048,2048]{1,0:T(8,128)(2,1)} %bitcast.50, f32[1,2048]{1,0:T(1,128)} %bitcast.55, ...), custom_call_target="tpu_custom_call" | custom-call | flops 671088640 | bytes 335544320 | tf_op jit(solution)/shard_map/pallas_call | solution.py:20
  24.2 4.8 %shard_map.180 = (bf16[2048,256]{1,0:T(8,128)(2,1)}, bf16[2048,256]{1,0:T(8,128)(2,1)}) custom-call(s32[36]{0:T(128)} %stack.147.meta, bf16[2048,1536]{1,0:T(8,128)(2,1)} %refs_10_.3, bf16[2048,1536]{1,0:T(8,128)(2,1)} %refs_10_.3, bf16[2048,1536]{1,0:T(8,128)(2,1)} %refs_10_.3, bf16[2048,1536]{1,0:T(8,128)(2,1)} %refs_10_.3), custom_call_target="tpu_custom_call" | custom-call | bytes 4194304 | tf_op jit(solution)/shard_map/pallas_call | solution.py:20
  29.1 1.7 collective-permute-start.3
  31.5 1.7 collective-permute-done.2.refs_5_
  35.1 12.0 %shard_map.181.u_ref = bf16[2048,768]{1,0:T(8,128)(2,1)} custom-call(s32[36]{0:T(128)} %stack.147.meta, bf16[2048,2048]{1,0:T(8,128)(2,1)} %get-tuple-element.84.normed_ref, bf16[2048,1536]{1,0:T(8,128)(2,1)} %refs_10_.3, bf16[2048,1536]{1,0:T(8,128)(2,1)} %refs_10_.3, bf16[2048,384]{1,0:T(8,128)(2,1)} %copy-done.23, bf16[2048,384]{1,0:T(8,128)(2,1)} %copy-done.23, ...), custom_call_target="tpu_custom_call" | custom-call | flops 128849018880 | bytes 293601280 | tf_op jit(solution)/shard_map/pallas_call | solution.py:20
  47.1 12.4 %shard_map.182 = (bf16[2048,512]{1,0:T(8,128)(2,1)}, bf16[2048,768]{1,0:T(8,128)(2,1)}, bf16[2048,512]{1,0:T(8,128)(2,1)}, f32[8,512]{1,0:T(8,128)}) custom-call(s32[36]{0:T(128)} %stack.147.meta, bf16[2048,768]{1,0:T(8,128)(2,1)} %shard_map.181.u_ref, bf16[2048,512]{1,0:T(8,128)(2,1)} %get-tuple-element.90.x_ref, bf16[2048,512]{1,0:T(8,128)(2,1)} %bitcast.51, ...), custom_call_target="tpu_custom_call" | custom-call | flops 629145600 | bytes 188743680 | tf_op jit(solution)/shard_map/pallas_call | solution.py:20
  59.5 8.2 %shard_map.183 = (bf16[512,768]{1,0:T(8,128)(2,1)}, bf16[512,768]{1,0:T(8,128)(2,1)}) custom-call(s32[36]{0:T(128)} %stack.147.meta, bf16[2048,2048]{1,0:T(8,128)(2,1)} %get-tuple-element.84.normed_ref, bf16[2048,768]{1,0:T(8,128)(2,1)} %get-tuple-element.93.ds_ref.ds1_ref), custom_call_target="tpu_custom_call" | custom-call | flops 64424509440 | bytes 146800640 | tf_op jit(solution)/shard_map/pallas_call | solution.py:20
  69.7 8.2 %shard_map.184 = (bf16[512,768]{1,0:T(8,128)(2,1)}, bf16[512,768]{1,0:T(8,128)(2,1)}) custom-call(s32[36]{0:T(128)} %stack.147.meta, bf16[2048,2048]{1,0:T(8,128)(2,1)} %get-tuple-element.84.normed_ref, bf16[2048,768]{1,0:T(8,128)(2,1)} %get-tuple-element.93.ds_ref.ds1_ref), custom_call_target="tpu_custom_call" | custom-call | flops 64424509440 | bytes 146800640 | tf_op jit(solution)/shard_map/pallas_call | solution.py:20
  77.8 1.5 collective-permute-start.8
  79.4 12.1 %shard_map.185.u_ref = bf16[2048,768]{1,0:T(8,128)(2,1)} custom-call(s32[36]{0:T(128)} %stack.147.meta, bf16[2048,2048]{1,0:T(8,128)(2,1)} %get-tuple-element.84.normed_ref, bf16[2048,256]{1,0:T(8,128)(2,1)} %collective-permute-done.3.refs_0_.refs_1_.refs_6_.refs_7_, bf16[2048,256]{1,0:T(8,128)(2,1)} %collective-permute-done.3.refs_0_.refs_1_.refs_6_.refs_7_, ...), custom_call_target="tpu_custom_call" | custom-call | flops 128849018880 | bytes 293601280 | tf_op jit(solution)/shard_map/pallas_call | solution.py:20
  93.3 3.7 %shard_map.186 = (bf16[2,256,768]{2,1,0:T(8,128)(2,1)}, bf16[2,256,768]{2,1,0:T(8,128)(2,1)}) custom-call(s32[36]{0:T(128)} %stack.147.meta, bf16[512,768]{1,0:T(8,128)(2,1)} %get-tuple-element.96.refs_0_.refs_4_, bf16[512,768]{1,0:T(8,128)(2,1)} %copy-done.2, bf16[512,768]{1,0:T(8,128)(2,1)} %collective-permute-done.6.refs_2_.refs_6_, ...), custom_call_target="tpu_custom_call" | custom-call | flops 1572864 | bytes 4718592 | tf_op jit(solution)/shard_map/pallas_call | solution.py:20
  97.6 12.4 %shard_map.187 = (bf16[2048,512]{1,0:T(8,128)(2,1)}, bf16[2048,768]{1,0:T(8,128)(2,1)}, bf16[2048,512]{1,0:T(8,128)(2,1)}, f32[8,512]{1,0:T(8,128)}) custom-call(s32[36]{0:T(128)} %stack.147.meta, bf16[2048,768]{1,0:T(8,128)(2,1)} %shard_map.185.u_ref, ...), custom_call_target="tpu_custom_call", output_to_operand_aliasing={{0}: (7, {}), {2}: (8, {}), {3}: (9, {})} | custom-call | flops 629145600 | bytes 188743680 | tf_op jit(solution)/shard_map/pallas_call | solution.py:20
  110.9 3.0 shard_map.188
  114.0 2.6 collective-permute-start.10
  116.6 8.2 %shard_map.189 = (bf16[512,768]{1,0:T(8,128)(2,1)}, bf16[512,768]{1,0:T(8,128)(2,1)}) custom-call(s32[36]{0:T(128)} %stack.147.meta, bf16[2048,2048]{1,0:T(8,128)(2,1)} %get-tuple-element.84.normed_ref, bf16[2048,768]{1,0:T(8,128)(2,1)} %get-tuple-element.107.ds_ref.ds2_ref), custom_call_target="tpu_custom_call" | custom-call | flops 64424509440 | bytes 146800640 | tf_op jit(solution)/shard_map/pallas_call | solution.py:20
  124.8 1.5 collective-permute-start.13
  126.3 8.1 %shard_map.190 = (bf16[512,768]{1,0:T(8,128)(2,1)}, bf16[512,768]{1,0:T(8,128)(2,1)}) custom-call(s32[36]{0:T(128)} %stack.147.meta, bf16[2048,2048]{1,0:T(8,128)(2,1)} %get-tuple-element.84.normed_ref, bf16[2048,768]{1,0:T(8,128)(2,1)} %get-tuple-element.107.ds_ref.ds2_ref), custom_call_target="tpu_custom_call" | custom-call | flops 64424509440 | bytes 146800640 | tf_op jit(solution)/shard_map/pallas_call | solution.py:20
  135.4 13.6 %shard_map.191 = (bf16[2048,512]{1,0:T(8,128)(2,1)}, bf16[2048,512]{1,0:T(8,128)(2,1)}) custom-call(s32[36]{0:T(128)} %stack.147.meta, bf16[2048,768]{1,0:T(8,128)(2,1)} %get-tuple-element.93.ds_ref.ds1_ref, bf16[2048,768]{1,0:T(8,128)(2,1)} %get-tuple-element.107.ds_ref.ds2_ref, bf16[2048,1536]{1,0:T(8,128)(2,1)} %refs_10_.3, bf16[2048,1536]{1,0:T(8,128)(2,1)} %refs_10_.3, ...), custom_call_target="tpu_custom_call" | custom-call | flops 128849018880 | bytes 251658240 | tf_op jit(solution)/shard_map/pallas_call | solution.py:20
  149.0 2.6 shard_map.192
  154.1 3.0 collective-permute-done.11
  159.3 3.8 %shard_map.193 = (bf16[2,256,768]{2,1,0:T(8,128)(2,1)}, bf16[2,256,768]{2,1,0:T(8,128)(2,1)}) custom-call(s32[36]{0:T(128)} %stack.147.meta, bf16[512,768]{1,0:T(8,128)(2,1)} %get-tuple-element.114.refs_0_.refs_4_, bf16[512,768]{1,0:T(8,128)(2,1)} %copy-done, bf16[512,768]{1,0:T(8,128)(2,1)} %collective-permute-done.13.refs_2_.refs_6_, ...), custom_call_target="tpu_custom_call" | custom-call | flops 1572864 | bytes 4718592 | tf_op jit(solution)/shard_map/pallas_call | solution.py:20
  163.0 1.5 collective-permute-start.19
  164.6 13.5 %shard_map.194 = (bf16[2048,512]{1,0:T(8,128)(2,1)}, bf16[2048,512]{1,0:T(8,128)(2,1)}) custom-call(s32[36]{0:T(128)} %stack.147.meta, bf16[2048,768]{1,0:T(8,128)(2,1)} %get-tuple-element.93.ds_ref.ds1_ref, bf16[2048,768]{1,0:T(8,128)(2,1)} %get-tuple-element.107.ds_ref.ds2_ref, bf16[2048,1536]{1,0:T(8,128)(2,1)} %refs_10_.3, bf16[2048,1536]{1,0:T(8,128)(2,1)} %refs_10_.3, ...), custom_call_target="tpu_custom_call" | custom-call | flops 128849018880 | bytes 251658240 | tf_op jit(solution)/shard_map/pallas_call | solution.py:20
  179.2 3.7 %add_convert_fusion = (bf16[1024,512]{1,0:T(8,128)(2,1)}, bf16[1024,512]{1,0:T(8,128)(2,1)}) fusion(bf16[2048,512]{1,0:T(8,128)(2,1)} %collective-permute-done.17, bf16[2048,512]{1,0:T(8,128)(2,1)S(1)} %copy-done.6), kind=kLoop, calls=%fused_computation | loop fusion | flops 4194304 | bytes 6291456 | tf_op jit(solution)/shard_map/convert_element_type | solution.py:842
  183.8 3.1 shard_map.195
  186.9 1.6 collective-permute-start.18
  189.0 2.6 collective-permute-start.20
  192.7 20.6 %collective-permute-done.18.r1_ref = bf16[1024,512]{1,0:T(8,128)(2,1)} collective-permute-done((bf16[1024,512]{1,0:T(8,128)(2,1)}, bf16[1024,512]{1,0:T(8,128)(2,1)}, u32[]{:S(2)}, u32[]{:S(2)}) %collective-permute-start.18) | collective-permute-done | bytes 1048608 | tf_op jit(solution)/shard_map/ppermute | solution.py:771
  213.3 2.6 shard_map.196
  215.9 1.6 collective-permute-start.21
  217.5 1.6 constant_dynamic-update-slice_fusion.5
  219.1 21.7 %collective-permute-done.21 = bf16[2,128,512]{2,1,0:T(8,128)(2,1)S(1)} collective-permute-done((bf16[2,128,512]{2,1,0:T(8,128)(2,1)}, bf16[2,128,512]{2,1,0:T(8,128)(2,1)S(1)}, u32[]{:S(2)}, u32[]{:S(2)}) %collective-permute-start.21) | collective-permute-done | bytes 262176 | tf_op jit(solution)/shard_map/ppermute | solution.py:771
  241.5 2.6 collective-permute-start.25
  244.1 3.3 shard_map.197
  248.7 7.9 %shard_map.198 = (f32[2048,512]{1,0:T(8,128)}, f32[8,2048]{1,0:T(8,128)}, f32[8,512]{1,0:T(8,128)}) custom-call(s32[36]{0:T(128)} %stack.147.meta, bf16[2048,512]{1,0:T(8,128)(2,1)} %get-tuple-element.126.k_ref, bf16[2048,512]{1,0:T(8,128)(2,1)} %copy-done.7, bf16[1024,512]{1,0:T(8,128)(2,1)} %collective-permute-done.18.r1_ref, ...), custom_call_target="tpu_custom_call" | custom-call | flops 20971520 | bytes 12582912 | tf_op jit(solution)/shard_map/pallas_call | solution.py:20
  257.8 4.0 %collective-permute-done.25 = bf16[2,128,768]{2,1,0:T(8,128)(2,1)} collective-permute-done((bf16[2,128,768]{2,1,0:T(8,128)(2,1)}, bf16[2,128,768]{2,1,0:T(8,128)(2,1)}, u32[]{:S(2)}, u32[]{:S(2)}) %collective-permute-start.25) | collective-permute-done | bytes 393248 | tf_op jit(solution)/shard_map/ppermute | solution.py:777
  264.4 18.7 %collective-permute-done.26.b_ref = bf16[2,256,768]{2,1,0:T(8,128)(2,1)S(1)} collective-permute-done((bf16[2,256,768]{2,1,0:T(8,128)(2,1)S(1)}, bf16[2,256,768]{2,1,0:T(8,128)(2,1)S(1)}, u32[]{:S(2)}, u32[]{:S(2)}) %collective-permute-start.26) | collective-permute-done | bytes 786464 | tf_op jit(solution)/shard_map/ppermute | solution.py:777
  284.0 3.3 shard_map.199
  290.2 1.7 collective-permute-start.28
  291.9 8.0 %collective-permute-done.37 = f32[6,512]{1,0:T(8,128)S(1)} collective-permute-done((f32[6,512]{1,0:T(8,128)S(1)}, f32[6,512]{1,0:T(8,128)S(1)}, u32[]{:S(2)}, u32[]{:S(2)}) %collective-permute-start.37) | collective-permute-done | bytes 12320 | tf_op jit(solution)/shard_map/ppermute | solution.py:869
  300.3 3.6 %collective-permute-done.38 = f32[6,512]{1,0:T(8,128)S(1)} collective-permute-done((f32[6,512]{1,0:T(8,128)S(1)}, f32[6,512]{1,0:T(8,128)S(1)}, u32[]{:S(2)}, u32[]{:S(2)}) %collective-permute-start.38) | collective-permute-done | bytes 12320 | tf_op jit(solution)/shard_map/ppermute | solution.py:869
  303.9 1.8 collective-permute-start.39
  306.4 2.2 collective-permute-done.39
  310.7 7.4 %shard_map.200 = bf16[2048,512]{1,0:T(8,128)(2,1)} custom-call(s32[36]{0:T(128)} %stack.147.meta, f32[2048,512]{1,0:T(8,128)} %get-tuple-element.143.dn_ref, f32[8,2048]{1,0:T(8,128)} %add.126.row_ref, bf16[2048,512]{1,0:T(8,128)(2,1)} %get-tuple-element.90.x_ref, f32[2048,128]{1,0:T(8,128)} %get-tuple-element.141.mu_ref, ...), custom_call_target="tpu_custom_call" | custom-call | flops 10485760 | bytes 12582912 | tf_op jit(solution)/shard_map/pallas_call | solution.py:20
  318.3 7.9 %collective-permute-done.33.refs_5_ = bf16[512,768]{1,0:T(8,128)(2,1)} collective-permute-done((bf16[512,768]{1,0:T(8,128)(2,1)}, bf16[512,768]{1,0:T(8,128)(2,1)}, u32[]{:S(2)}, u32[]{:S(2)}) %collective-permute-start.33) | collective-permute-done | bytes 786464 | tf_op jit(solution)/shard_map/ppermute | solution.py:777
  326.2 8.5 %shard_map.201 = f32[2048,1536]{1,0:T(8,128)} custom-call(s32[36]{0:T(128)} %stack.147.meta, bf16[512,768]{1,0:T(8,128)(2,1)} %get-tuple-element.137.refs_0_, bf16[512,768]{1,0:T(8,128)(2,1)} %copy-done.13, bf16[512,768]{1,0:T(8,128)(2,1)} %copy-done.12, bf16[512,768]{1,0:T(8,128)(2,1)} %copy-done.14, bf16[512,768]{1,0:T(8,128)(2,1)} %get-tuple-element.145.refs_4_, ...), custom_call_target="tpu_custom_call" | custom-call | flops 3145728 | bytes 18874368 | tf_op jit(solution)/shard_map/pallas_call | solution.py:20
  (131 shorter events, 31.0 us)
Async XLA Ops:
  6.2 26.9 %collective-permute-start = (bf16[2048,384]{1,0:T(8,128)(2,1)}, bf16[2048,384]{1,0:T(8,128)(2,1)S(1)}, u32[]{:S(2)}, u32[]{:S(2)}) collective-permute-start(bf16[2048,384]{1,0:T(8,128)(2,1)} %get-tuple-element.89), channel_id=1, source_target_pairs={{0,1},{1,0},{2,3},{3,2},{4,5},{5,4},{6,7},{7,6},{8,9},{9,8},{10,11... | collective-permute-start | bytes 4718600 | tf_op jit(solution)/shard_map/ppermute | solution.py:771
  6.7 24.8 %collective-permute-start.1 = (bf16[2048,128]{1,0:T(8,128)(2,1)}, bf16[2048,128]{1,0:T(8,128)(2,1)S(1)}, u32[]{:S(2)}, u32[]{:S(2)}) collective-permute-start(bf16[2048,128]{1,0:T(8,128)(2,1)} %get-tuple-element.81), channel_id=1, source_target_pairs={{0,2},{1,3},{2,0},{3,1},{4,6},{5,7},{6,4},{7,5},{8,10},{9,11},{10,... | collective-permute-start | bytes 1572872 | tf_op jit(solution)/shard_map/ppermute | solution.py:771
  9.3 23.9 %collective-permute-start.2 = (bf16[2048,128]{1,0:T(8,128)(2,1)}, bf16[2048,128]{1,0:T(8,128)(2,1)S(1)}, u32[]{:S(2)}, u32[]{:S(2)}) collective-permute-start(bf16[2048,128]{1,0:T(8,128)(2,1)} %get-tuple-element.82), channel_id=1, source_target_pairs={{0,3},{1,2},{2,1},{3,0},{4,7},{5,6},{6,5},{7,4},{8,11},{9,10},{10,... | collective-permute-start | bytes 1572872 | tf_op jit(solution)/shard_map/ppermute | solution.py:771
  29.1 50.3 %collective-permute-start.3 = (bf16[2048,256]{1,0:T(8,128)(2,1)}, bf16[2048,256]{1,0:T(8,128)(2,1)}, u32[]{:S(2)}, u32[]{:S(2)}) collective-permute-start(bf16[2048,256]{1,0:T(8,128)(2,1)} %get-tuple-element.86), channel_id=1, source_target_pairs={{0,2},{1,3},{2,0},{3,1},{4,6},{5,7},{6,4},{7,5},{8,10},{9,11},{10,... | collective-permute-start | bytes 3145736 | tf_op jit(solution)/shard_map/ppermute | solution.py:771
  30.8 48.6 %collective-permute-start.4 = (bf16[2048,256]{1,0:T(8,128)(2,1)}, bf16[2048,256]{1,0:T(8,128)(2,1)}, u32[]{:S(2)}, u32[]{:S(2)}) collective-permute-start(bf16[2048,256]{1,0:T(8,128)(2,1)} %get-tuple-element.87), channel_id=1, source_target_pairs={{0,3},{1,2},{2,1},{3,0},{4,7},{5,6},{6,5},{7,4},{8,11},{9,10},{10,... | collective-permute-start | bytes 3145736 | tf_op jit(solution)/shard_map/ppermute | solution.py:771
  67.7 23.8 %collective-permute-start.6 = (bf16[512,768]{1,0:T(8,128)(2,1)}, bf16[512,768]{1,0:T(8,128)(2,1)}, u32[]{:S(2)}, u32[]{:S(2)}) collective-permute-start(bf16[512,768]{1,0:T(8,128)(2,1)} %get-tuple-element.94), channel_id=1, source_target_pairs={{0,4},{1,9},{2,6},{3,11},{4,0},{5,13},{6,2},{7,15},{8,12},{9,1},{1... | collective-permute-start | bytes 2359304 | tf_op jit(solution)/shard_map/ppermute | solution.py:777
  69.2 8.7 %collective-permute-start.7 = (bf16[512,768]{1,0:T(8,128)(2,1)}, bf16[512,768]{1,0:T(8,128)(2,1)S(1)}, u32[]{:S(2)}, u32[]{:S(2)}) collective-permute-start(bf16[512,768]{1,0:T(8,128)(2,1)} %get-tuple-element.100), channel_id=1, source_target_pairs={{0,1},{1,0},{2,3},{3,2},{4,5},{5,4},{6,7},{7,6},{8,9},{9,8},{10,11... | collective-permute-start | bytes 2359304 | tf_op jit(solution)/shard_map/ppermute | solution.py:771
  77.8 13.7 %collective-permute-start.5 = (bf16[512,768]{1,0:T(8,128)(2,1)}, bf16[512,768]{1,0:T(8,128)(2,1)S(1)}, u32[]{:S(2)}, u32[]{:S(2)}) collective-permute-start(bf16[512,768]{1,0:T(8,128)(2,1)} %get-tuple-element.99), channel_id=1, source_target_pairs={{0,1},{1,0},{2,3},{3,2},{4,5},{5,4},{6,7},{7,6},{8,9},{9,8},{10,11... | collective-permute-start | bytes 2359304 | tf_op jit(solution)/shard_map/ppermute | solution.py:771
  77.8 13.7 %collective-permute-start.8 = (bf16[512,768]{1,0:T(8,128)(2,1)S(1)}, bf16[512,768]{1,0:T(8,128)(2,1)S(1)}, u32[]{:S(2)}, u32[]{:S(2)}) collective-permute-start(bf16[512,768]{1,0:T(8,128)(2,1)S(1)} %collective-permute-done.7), channel_id=1, source_target_pairs={{0,4},{1,9},{2,6},{3,11},{4,0},{5,13},{6,2},{7,15},{8,12},{9,1},{1... | collective-permute-start | bytes 2359304 | tf_op jit(solution)/shard_map/ppermute | solution.py:777
  97.0 13.0 %collective-permute-start.9 = (bf16[2,256,768]{2,1,0:T(8,128)(2,1)}, bf16[2,256,768]{2,1,0:T(8,128)(2,1)S(1)}, u32[]{:S(2)}, u32[]{:S(2)}) collective-permute-start(bf16[2,256,768]{2,1,0:T(8,128)(2,1)} %get-tuple-element.101), channel_id=1, source_target_pairs={{0,8},{1,5},{2,10},{3,7},{4,12},{5,1},{6,14},{7,3},{8,0},{9,13},{1... | collective-permute-start | bytes 2359304 | tf_op jit(solution)/shard_map/ppermute | solution.py:777
  114.0 35.1 %collective-permute-start.10 = (bf16[2,128,768]{2,1,0:T(8,128)(2,1)}, bf16[2,128,768]{2,1,0:T(8,128)(2,1)}, u32[]{:S(2)}, u32[]{:S(2)}) collective-permute-start(bf16[2,128,768]{2,1,0:T(8,128)(2,1)} %get-tuple-element.110), channel_id=1, source_target_pairs={{0,16},{1,17},{2,18},{3,19},{4,20},{5,21},{6,22},{7,23},{8,24},{9,... | collective-permute-start | bytes 1179656 | tf_op jit(solution)/shard_map/ppermute | solution.py:777
  124.8 32.7 %collective-permute-start.13 = (bf16[512,768]{1,0:T(8,128)(2,1)}, bf16[512,768]{1,0:T(8,128)(2,1)}, u32[]{:S(2)}, u32[]{:S(2)}) collective-permute-start(bf16[512,768]{1,0:T(8,128)(2,1)} %get-tuple-element.112), channel_id=1, source_target_pairs={{0,4},{1,9},{2,6},{3,11},{4,0},{5,13},{6,2},{7,15},{8,12},{9,1},{1... | collective-permute-start | bytes 2359304 | tf_op jit(solution)/shard_map/ppermute | solution.py:777
  126.3 8.6 %collective-permute-start.14 = (bf16[512,768]{1,0:T(8,128)(2,1)}, bf16[512,768]{1,0:T(8,128)(2,1)S(1)}, u32[]{:S(2)}, u32[]{:S(2)}) collective-permute-start(bf16[512,768]{1,0:T(8,128)(2,1)} %get-tuple-element.123), channel_id=1, source_target_pairs={{0,1},{1,0},{2,3},{3,2},{4,5},{5,4},{6,7},{7,6},{8,9},{9,8},{10,11... | collective-permute-start | bytes 2359304 | tf_op jit(solution)/shard_map/ppermute | solution.py:771
  134.4 23.1 %collective-permute-start.12 = (bf16[512,768]{1,0:T(8,128)(2,1)}, bf16[512,768]{1,0:T(8,128)(2,1)S(1)}, u32[]{:S(2)}, u32[]{:S(2)}) collective-permute-start(bf16[512,768]{1,0:T(8,128)(2,1)} %get-tuple-element.122), channel_id=1, source_target_pairs={{0,1},{1,0},{2,3},{3,2},{4,5},{5,4},{6,7},{7,6},{8,9},{9,8},{10,11... | collective-permute-start | bytes 2359304 | tf_op jit(solution)/shard_map/ppermute | solution.py:771
  134.9 22.6 %collective-permute-start.15 = (bf16[512,768]{1,0:T(8,128)(2,1)S(1)}, bf16[512,768]{1,0:T(8,128)(2,1)S(1)}, u32[]{:S(2)}, u32[]{:S(2)}) collective-permute-start(bf16[512,768]{1,0:T(8,128)(2,1)S(1)} %collective-permute-done.14), channel_id=1, source_target_pairs={{0,4},{1,9},{2,6},{3,11},{4,0},{5,13},{6,2},{7,15},{8,12},{9,1},{1... | collective-permute-start | bytes 2359304 | tf_op jit(solution)/shard_map/ppermute | solution.py:777
  151.7 5.4 %collective-permute-start.11 = (bf16[2,128,256]{2,1,0:T(8,128)(2,1)}, bf16[2,128,256]{2,1,0:T(8,128)(2,1)S(1)}, u32[]{:S(2)}, u32[]{:S(2)}) collective-permute-start(bf16[2,128,256]{2,1,0:T(8,128)(2,1)} %get-tuple-element.120), channel_id=1, source_target_pairs={{0,2},{1,3},{2,0},{3,1},{4,6},{5,7},{6,4},{7,5},{8,10},{9,11},{10,... | collective-permute-start | bytes 393224 | tf_op jit(solution)/shard_map/ppermute | solution.py:771
  153.1 26.1 %collective-permute-start.17 = (bf16[2048,512]{1,0:T(8,128)(2,1)}, bf16[2048,512]{1,0:T(8,128)(2,1)}, u32[]{:S(2)}, u32[]{:S(2)}) collective-permute-start(bf16[2048,512]{1,0:T(8,128)(2,1)} %get-tuple-element.128), channel_id=1, source_target_pairs={{0,1},{1,0},{2,3},{3,2},{4,5},{5,4},{6,7},{7,6},{8,9},{9,8},{10,11... | collective-permute-start | bytes 6291464 | tf_op jit(solution)/shard_map/ppermute | solution.py:771
  157.1 21.0 %collective-permute-start.16 = (bf16[2,128,768]{2,1,0:T(8,128)(2,1)S(1)}, bf16[2,128,768]{2,1,0:T(8,128)(2,1)}, u32[]{:S(2)}, u32[]{:S(2)}) collective-permute-start(bf16[2,128,768]{2,1,0:T(8,128)(2,1)S(1)} %constant_dynamic-update-slice_fusion), channel_id=1, source_target_pairs={{0,16},{1,17},{2,18},{3,19},{4,20},{5,21},{6,22},{7,23},{8,24},{9,... | collective-permute-start | bytes 1179656 | tf_op jit(solution)/shard_map/ppermute | solution.py:777
  163.0 19.9 %collective-permute-start.19 = (bf16[2,256,768]{2,1,0:T(8,128)(2,1)}, bf16[2,256,768]{2,1,0:T(8,128)(2,1)S(1)}, u32[]{:S(2)}, u32[]{:S(2)}) collective-permute-start(bf16[2,256,768]{2,1,0:T(8,128)(2,1)} %get-tuple-element.124), channel_id=1, source_target_pairs={{0,8},{1,5},{2,10},{3,7},{4,12},{5,1},{6,14},{7,3},{8,0},{9,13},{1... | collective-permute-start | bytes 2359304 | tf_op jit(solution)/shard_map/ppermute | solution.py:777
  164.6 14.6 %copy-start.6 = (bf16[2048,512]{1,0:T(8,128)(2,1)S(1)}, bf16[2048,512]{1,0:T(8,128)(2,1)}, u32[]{:S(2)}) copy-start(bf16[2048,512]{1,0:T(8,128)(2,1)} %get-tuple-element.116) | copy-start | bytes 6291460
  179.1 12.4 %copy-start.8 = (bf16[2,256,768]{2,1,0:T(8,128)(2,1)}, bf16[2,256,768]{2,1,0:T(8,128)(2,1)S(1)}, u32[]{:S(2)}) copy-start(bf16[2,256,768]{2,1,0:T(8,128)(2,1)S(1)} %constant_dynamic-update-slice_fusion.2.a_ref) | copy-start | bytes 2359300
  186.9 60.5 %collective-permute-start.23 = (bf16[2048,512]{1,0:T(8,128)(2,1)}, bf16[2048,512]{1,0:T(8,128)(2,1)S(1)}, u32[]{:S(2)}, u32[]{:S(2)}) collective-permute-start(bf16[2048,512]{1,0:T(8,128)(2,1)} %get-tuple-element.140), channel_id=1, source_target_pairs={{0,1},{1,0},{2,3},{3,2},{4,5},{5,4},{6,7},{7,6},{8,9},{9,8},{10,11... | collective-permute-start | bytes 6291464 | tf_op jit(solution)/shard_map/ppermute | solution.py:771
  186.9 26.4 %collective-permute-start.18 = (bf16[1024,512]{1,0:T(8,128)(2,1)}, bf16[1024,512]{1,0:T(8,128)(2,1)}, u32[]{:S(2)}, u32[]{:S(2)}) collective-permute-start(bf16[1024,512]{1,0:T(8,128)(2,1)} %get-tuple-element.154), channel_id=1, source_target_pairs={{0,2},{1,3},{2,0},{3,1},{4,6},{5,7},{6,4},{7,5},{8,10},{9,11},{10,... | collective-permute-start | bytes 3145736 | tf_op jit(solution)/shard_map/ppermute | solution.py:771
  188.6 58.8 %collective-permute-start.24 = (bf16[1024,512]{1,0:T(8,128)(2,1)S(1)}, bf16[1024,512]{1,0:T(8,128)(2,1)}, u32[]{:S(2)}, u32[]{:S(2)}) collective-permute-start(bf16[1024,512]{1,0:T(8,128)(2,1)S(1)} %copy-done.10), channel_id=1, source_target_pairs={{0,2},{1,3},{2,0},{3,1},{4,6},{5,7},{6,4},{7,5},{8,10},{9,11},{10,... | collective-permute-start | bytes 3145736 | tf_op jit(solution)/shard_map/ppermute | solution.py:771
  189.0 24.3 %collective-permute-start.20 = (bf16[2,128,768]{2,1,0:T(8,128)(2,1)}, bf16[2,128,768]{2,1,0:T(8,128)(2,1)}, u32[]{:S(2)}, u32[]{:S(2)}) collective-permute-start(bf16[2,128,768]{2,1,0:T(8,128)(2,1)} %get-tuple-element.133), channel_id=1, source_target_pairs={{0,16},{1,17},{2,18},{3,19},{4,20},{5,21},{6,22},{7,23},{8,24},{9,... | collective-permute-start | bytes 1179656 | tf_op jit(solution)/shard_map/ppermute | solution.py:777
  191.6 52.5 %collective-permute-start.22 = (bf16[2,256,768]{2,1,0:T(8,128)(2,1)S(1)}, bf16[2,256,768]{2,1,0:T(8,128)(2,1)}, u32[]{:S(2)}, u32[]{:S(2)}) collective-permute-start(bf16[2,256,768]{2,1,0:T(8,128)(2,1)S(1)} %constant_dynamic-update-slice_fusion.2.a_ref), channel_id=1, source_target_pairs={{0,8},{1,5},{2,10},{3,7},{4,12},{5,1},{6,14},{7,3},{8,0},{9,13},{1... | collective-permute-start | bytes 2359304 | tf_op jit(solution)/shard_map/ppermute | solution.py:777
  215.9 24.8 %collective-permute-start.21 = (bf16[2,128,512]{2,1,0:T(8,128)(2,1)}, bf16[2,128,512]{2,1,0:T(8,128)(2,1)S(1)}, u32[]{:S(2)}, u32[]{:S(2)}) collective-permute-start(bf16[2,128,512]{2,1,0:T(8,128)(2,1)} %get-tuple-element.135), channel_id=1, source_target_pairs={{0,2},{1,3},{2,0},{3,1},{4,6},{5,7},{6,4},{7,5},{8,10},{9,11},{10,... | collective-permute-start | bytes 786440 | tf_op jit(solution)/shard_map/ppermute | solution.py:771
  241.5 20.2 %collective-permute-start.25 = (bf16[2,128,768]{2,1,0:T(8,128)(2,1)}, bf16[2,128,768]{2,1,0:T(8,128)(2,1)}, u32[]{:S(2)}, u32[]{:S(2)}) collective-permute-start(bf16[2,128,768]{2,1,0:T(8,128)(2,1)} %constant_dynamic-update-slice_fusion.4), channel_id=1, source_target_pairs={{0,16},{1,17},{2,18},{3,19},{4,20},{5,21},{6,22},{7,23},{8,24},{9,... | collective-permute-start | bytes 1179656 | tf_op jit(solution)/shard_map/ppermute | solution.py:777
  248.7 14.5 %copy-start.24 = (bf16[512,768]{1,0:T(8,128)(2,1)S(1)}, bf16[512,768]{1,0:T(8,128)(2,1)}, u32[]{:S(2)}) copy-start(bf16[512,768]{1,0:T(8,128)(2,1)} %get-tuple-element.149) | copy-start | bytes 2359300
  256.6 31.4 %copy-start.18 = (f32[8,512]{1,0:T(8,128)S(1)}, f32[8,512]{1,0:T(8,128)}, u32[]{:S(2)}) copy-start(f32[8,512]{1,0:T(8,128)} %get-tuple-element.152) | copy-start | bytes 49156
  256.7 32.1 %copy-start.17 = (f32[8,2048]{1,0:T(8,128)S(1)}, f32[8,2048]{1,0:T(8,128)}, u32[]{:S(2)}) copy-start(f32[8,2048]{1,0:T(8,128)} %get-tuple-element.147) | copy-start | bytes 196612
  256.7 49.0 %copy-start.11 = (bf16[512,768]{1,0:T(8,128)(2,1)S(1)}, bf16[512,768]{1,0:T(8,128)(2,1)}, u32[]{:S(2)}) copy-start(bf16[512,768]{1,0:T(8,128)(2,1)} %get-tuple-element.137.refs_0_) | copy-start | bytes 2359300
  262.8 20.3 %copy-start.9 = (bf16[2,256,768]{2,1,0:T(8,128)(2,1)}, bf16[2,256,768]{2,1,0:T(8,128)(2,1)S(1)}, u32[]{:S(2)}) copy-start(bf16[2,256,768]{2,1,0:T(8,128)(2,1)S(1)} %constant_dynamic-update-slice_fusion.6.a_ref) | copy-start | bytes 2359300
  262.8 20.3 %collective-permute-start.26 = (bf16[2,256,768]{2,1,0:T(8,128)(2,1)S(1)}, bf16[2,256,768]{2,1,0:T(8,128)(2,1)S(1)}, u32[]{:S(2)}, u32[]{:S(2)}) collective-permute-start(bf16[2,256,768]{2,1,0:T(8,128)(2,1)S(1)} %constant_dynamic-update-slice_fusion.6.a_ref), channel_id=1, source_target_pairs={{0,8},{1,5},{2,10},{3,7},{4,12},{5,1},{6,14},{7,3},{8,0},{9,13},{1... | collective-permute-start | bytes 2359304 | tf_op jit(solution)/shard_map/ppermute | solution.py:777
  263.2 42.4 %collective-permute-start.31 = (bf16[512,768]{1,0:T(8,128)(2,1)S(1)}, bf16[512,768]{1,0:T(8,128)(2,1)}, u32[]{:S(2)}, u32[]{:S(2)}) collective-permute-start(bf16[512,768]{1,0:T(8,128)(2,1)S(1)} %copy-done.24), channel_id=1, source_target_pairs={{0,4},{1,9},{2,6},{3,11},{4,0},{5,13},{6,2},{7,15},{8,12},{9,1},{1... | collective-permute-start | bytes 2359304 | tf_op jit(solution)/shard_map/ppermute | solution.py:777
  264.4 42.0 %collective-permute-start.30 = (bf16[512,768]{1,0:T(8,128)(2,1)S(1)}, bf16[512,768]{1,0:T(8,128)(2,1)S(1)}, u32[]{:S(2)}, u32[]{:S(2)}) collective-permute-start(bf16[512,768]{1,0:T(8,128)(2,1)S(1)} %copy-done.24), channel_id=1, source_target_pairs={{0,1},{1,0},{2,3},{3,2},{4,5},{5,4},{6,7},{7,6},{8,9},{9,8},{10,11... | collective-permute-start | bytes 2359304 | tf_op jit(solution)/shard_map/ppermute | solution.py:771
  287.3 22.0 %collective-permute-start.35 = (bf16[512,768]{1,0:T(8,128)(2,1)}, bf16[512,768]{1,0:T(8,128)(2,1)}, u32[]{:S(2)}, u32[]{:S(2)}) collective-permute-start(bf16[512,768]{1,0:T(8,128)(2,1)} %get-tuple-element.150), channel_id=1, source_target_pairs={{0,4},{1,9},{2,6},{3,11},{4,0},{5,13},{6,2},{7,15},{8,12},{9,1},{1... | collective-permute-start | bytes 2359304 | tf_op jit(solution)/shard_map/ppermute | solution.py:777
  288.8 1.4 collective-permute-start.27
  288.8 11.1 %collective-permute-start.37 = (f32[6,512]{1,0:T(8,128)S(1)}, f32[6,512]{1,0:T(8,128)S(1)}, u32[]{:S(2)}, u32[]{:S(2)}) collective-permute-start(f32[6,512]{1,0:T(8,128)S(1)} %pad_maximum_fusion), channel_id=1, source_target_pairs={{0,4},{4,0},{8,12},{12,8},{16,20},{20,16},{24,28},{28,24},{1,5},{5... | collective-permute-start | bytes 36872 | tf_op jit(solution)/shard_map/ppermute | solution.py:869
  290.2 18.5 %collective-permute-start.28 = (f32[8,2048]{1,0:T(8,128)S(1)}, f32[8,2048]{1,0:T(8,128)S(1)}, u32[]{:S(2)}, u32[]{:S(2)}) collective-permute-start(f32[8,2048]{1,0:T(8,128)S(1)} %add.125), channel_id=1, source_target_pairs={{0,2},{1,3},{2,0},{3,1},{4,6},{5,7},{6,4},{7,5},{8,10},{9,11},{10,... | collective-permute-start | bytes 196616 | tf_op jit(solution)/shard_map/ppermute | solution.py:771
  299.9 4.0 %collective-permute-start.38 = (f32[6,512]{1,0:T(8,128)S(1)}, f32[6,512]{1,0:T(8,128)S(1)}, u32[]{:S(2)}, u32[]{:S(2)}) collective-permute-start(f32[6,512]{1,0:T(8,128)S(1)} %fusion), channel_id=1, source_target_pairs={{0,8},{4,12},{8,0},{12,4},{16,24},{20,28},{24,16},{28,20},{1,9},{5... | collective-permute-start | bytes 36872 | tf_op jit(solution)/shard_map/ppermute | solution.py:869
  303.9 4.8 %collective-permute-start.39 = (f32[6,512]{1,0:T(8,128)S(1)}, f32[6,512]{1,0:T(8,128)S(1)}, u32[]{:S(2)}, u32[]{:S(2)}) collective-permute-start(f32[6,512]{1,0:T(8,128)S(1)} %add.128), channel_id=1, source_target_pairs={{0,16},{4,20},{8,24},{12,28},{16,0},{20,4},{24,8},{28,12},{1,17},{... | collective-permute-start | bytes 36872 | tf_op jit(solution)/shard_map/ppermute | solution.py:869
  305.6 12.6 %collective-permute-start.29 = (bf16[512,768]{1,0:T(8,128)(2,1)S(1)}, bf16[512,768]{1,0:T(8,128)(2,1)S(1)}, u32[]{:S(2)}, u32[]{:S(2)}) collective-permute-start(bf16[512,768]{1,0:T(8,128)(2,1)S(1)} %copy-done.11), channel_id=1, source_target_pairs={{0,4},{1,9},{2,6},{3,11},{4,0},{5,13},{6,2},{7,15},{8,12},{9,1},{1... | collective-permute-start | bytes 2359304 | tf_op jit(solution)/shard_map/ppermute | solution.py:777
  306.4 11.8 %copy-start.12 = (bf16[512,768]{1,0:T(8,128)(2,1)}, bf16[512,768]{1,0:T(8,128)(2,1)S(1)}, u32[]{:S(2)}) copy-start(bf16[512,768]{1,0:T(8,128)(2,1)S(1)} %collective-permute-done.30.refs_2_) | copy-start | bytes 2359300
  306.4 11.8 %collective-permute-start.32 = (bf16[512,768]{1,0:T(8,128)(2,1)}, bf16[512,768]{1,0:T(8,128)(2,1)S(1)}, u32[]{:S(2)}, u32[]{:S(2)}) collective-permute-start(bf16[512,768]{1,0:T(8,128)(2,1)} %collective-permute-done.31), channel_id=1, source_target_pairs={{0,1},{1,0},{2,3},{3,2},{4,5},{5,4},{6,7},{7,6},{8,9},{9,8},{10,11... | collective-permute-start | bytes 2359304 | tf_op jit(solution)/shard_map/ppermute | solution.py:771
  308.6 9.6 %collective-permute-start.34 = (bf16[512,768]{1,0:T(8,128)(2,1)}, bf16[512,768]{1,0:T(8,128)(2,1)S(1)}, u32[]{:S(2)}, u32[]{:S(2)}) collective-permute-start(bf16[512,768]{1,0:T(8,128)(2,1)} %get-tuple-element.150), channel_id=1, source_target_pairs={{0,1},{1,0},{2,3},{3,2},{4,5},{5,4},{6,7},{7,6},{8,9},{9,8},{10,11... | collective-permute-start | bytes 2359304 | tf_op jit(solution)/shard_map/ppermute | solution.py:771
  308.6 17.5 %collective-permute-start.33 = (bf16[512,768]{1,0:T(8,128)(2,1)}, bf16[512,768]{1,0:T(8,128)(2,1)}, u32[]{:S(2)}, u32[]{:S(2)}) collective-permute-start(bf16[512,768]{1,0:T(8,128)(2,1)} %get-tuple-element.145.refs_4_), channel_id=1, source_target_pairs={{0,4},{1,9},{2,6},{3,11},{4,0},{5,13},{6,2},{7,15},{8,12},{9,1},{1... | collective-permute-start | bytes 2359304 | tf_op jit(solution)/shard_map/ppermute | solution.py:777
  309.3 16.8 %collective-permute-start.36 = (bf16[512,768]{1,0:T(8,128)(2,1)}, bf16[512,768]{1,0:T(8,128)(2,1)}, u32[]{:S(2)}, u32[]{:S(2)}) collective-permute-start(bf16[512,768]{1,0:T(8,128)(2,1)} %collective-permute-done.35), channel_id=1, source_target_pairs={{0,1},{1,0},{2,3},{3,2},{4,5},{5,4},{6,7},{7,6},{8,9},{9,8},{10,11... | collective-permute-start | bytes 2359304 | tf_op jit(solution)/shard_map/ppermute | solution.py:771
  (19 other events, 67.1 us)

commit v5 on v4

--- a/solution.py
+++ b/solution.py
@@ -399,43 +399,35 @@
 
 
 def back_kernel(meta, ds1_ref, ds2_ref, *refs):
-    outs, W = refs[-3:-1], refs[-1]
+    out_ref, W = refs[-2:]
     chunk = ds1_ref.shape[1]
 
-    @pl.when(pl.program_id(1) == 0)
+    @pl.when(pl.program_id(0) == 0)
     def _():
         gather_units(meta, M_S1, refs[:6], W, 0)
         gather_units(meta, M_S2, refs[6:12], W, chunk)
 
     dims = (((1,), (1,)), ((), ()))
-    for n, out_ref in enumerate(outs):
-
-        @pl.when(pl.program_id(0) == n)
-        def _(out_ref=out_ref):
-            value = lax.dot_general(ds1_ref[...], W[:, :chunk], dims, preferred_element_type=F32)
-            value += lax.dot_general(ds2_ref[...], W[:, chunk:], dims, preferred_element_type=F32)
-            out_ref[...] = value.astype(BF16)
-
-
-def back(meta, ds1, ds2, units, first, tb=1024):
+    value = lax.dot_general(ds1_ref[...], W[:, :chunk], dims, preferred_element_type=F32)
+    value += lax.dot_general(ds2_ref[...], W[:, chunk:], dims, preferred_element_type=F32)
+    out_ref[...] = value.astype(BF16)
+
+
+def back(meta, ds1, ds2, units, at, tb=1024):
     tokens, width = ds1.shape
     features = units[0][0].shape[0]
     block = features // 4
-    steps = tokens // tb
-    dspec = pl.BlockSpec((tb, width), lambda n, t, m: (t, 0))
+    dspec = pl.BlockSpec((tb, width), lambda t, m: (t, 0))
     return call(
         back_kernel,
         meta,
         [ds1, ds2] + [array for array, _, _ in units],
-        (2, steps),
-        [dspec, dspec] + unit_specs(units, block, lambda n, t, m: m[first + n]),
-        [
-            pl.BlockSpec((tb, block), lambda n, t, m: (jnp.where(n == 0, t, steps - 1), 0)),
-            pl.BlockSpec((tb, block), lambda n, t, m: (jnp.where(n == 0, 0, t), 0)),
-        ],
-        [struct((tokens, block), BF16)] * 2,
+        (tokens // tb,),
+        [dspec, dspec] + unit_specs(units, block, lambda t, m: m[at]),
+        pl.BlockSpec((tb, block), lambda t, m: (t, 0)),
+        struct((tokens, block), BF16),
         scratch=[pltpu.VMEM((block, 2 * width), BF16)],
-        cost=cost(8 * tokens * block * width, 8 * tokens * width, weight=COVER),
+        cost=cost(4 * tokens * block * width, 4 * tokens * width, weight=COVER),
     )
 
 
@@ -455,7 +447,7 @@
 
 def tail_sums_kernel(meta, k_ref, rc_ref, r1_ref, r2_ref, x_ref, mu_ref, inv_ref, gain_ref, dn_ref, row_ref, col_ref):
     unit, _ = unit_of(x_ref, mu_ref, inv_ref)
-    early = pl.program_id(0) < pl.num_programs(0) * FIRST // 4
+    early = pl.program_id(0) < pl.num_programs(0) * FIRST // 8
     far = jnp.where(early, r1_ref[...].astype(F32), r2_ref[...].astype(F32))
     dn = k_ref[...].astype(F32) + rc_ref[...].astype(F32) + far
     dn_ref[...] = dn
@@ -472,9 +464,9 @@
     col_ref[1:2, :] += jnp.sum(dn, axis=0, keepdims=True)
 
 
-def tail_sums(meta, keep, got, far, x, mu, inv, gain, tb=512):
+def tail_sums(meta, keep, got, far, x, mu, inv, gain, tb=256):
     tokens, channels = x.shape
-    first = tokens // tb * FIRST // 4
+    first = tokens // tb * FIRST // 8
     wide = pl.BlockSpec((tb, channels), lambda t, m: (t, 0))
     stat = pl.BlockSpec((tb, LANES), lambda t, m: (t, 0))
     return call(
@@ -830,36 +822,37 @@
         step1 = over_dp(away1, step)
     mine2, got2 = first_sends(after(meta, away1), ds2)
     kept2 = first_keeps(after(meta, mine2), ds2)
-    far_theirs, far_mine = back(after(meta, kept2[0]), ds1, ds2, units, M_FAR)
+    far_theirs = back(after(meta, kept2[0]), ds1, ds2, units, M_FAR)
     far_got = over_gate(far_theirs, 1)
-    near1, far1 = gathered(after(meta, far_mine), M_H1, False, stay1, step1)
-    away2, stay2 = halve(after(meta, near1), M_BIT + 1, kept2, got2)
+    away2, stay2 = halve(after(meta, far_theirs), M_BIT + 1, kept2, got2)
     step2 = over_dp(away2, 1)
-    shard1 = jnp.concatenate([near1, far1], axis=2)
-    theirs, mine = back(after(meta, away2, shard1), ds1, ds2, units, M_HERE)
-    cut_at = tokens * FIRST // 4
+    near1, far1 = gathered(after(meta, away2), M_H1, False, stay1, step1)
+    far_mine = back(after(meta, near1), ds1, ds2, units, M_FAR + 1)
+    for step in range(2, bits):
+        away2, stay2 = halve(after(meta, far_mine), M_BIT + step, [stay2], [step2])
+        step2 = over_dp(away2, step)
+    far_mine = after(far_mine, away2)
+    cut_at = tokens * FIRST // 8
     far_send = [
         (far_mine[at].astype(F32) + far_got[at].astype(F32)).astype(BF16) for at in (slice(cut_at), slice(cut_at, None))
     ]
     far_part = [over_gate(part, 2) for part in far_send]
-    shard1 = last_steps(shard1, mine)
-    for step in range(2, bits):
-        away2, stay2 = halve(after(meta, shard1, *far_send), M_BIT + step, [stay2], [step2])
-        step2 = over_dp(away2, step)
-
-    got = over_gate(after(theirs, away2), 1)
+    theirs = back(after(meta, away2, *far_send), ds1, ds2, units, M_HERE)
+    got = over_gate(theirs, 1)
+    shard1 = jnp.concatenate([after(near1, theirs), far1], axis=2)
+    mine = back(after(meta, theirs, shard1), ds1, ds2, units, M_HERE + 1)
 
     def last_doubling(meta, shard):
         mine, theirs = join(meta, shard, over_dp(shard, 1))
         moved = over_dp(theirs, 0)
         return [mine, over_dp(mine, 0), over_gate(theirs, 1), over_gate(moved, 1)]
 
-    near2, far2 = gathered(after(meta, shard1, far_part[0]), M_H2, True, stay2, step2)
-    parts1 = last_doubling(after(meta, near2), shard1)
-    dn, row_sums, col_sums = tail_sums(after(meta, parts1[0]), mine, got, far_part, own_x, mu, inv, ln_gain)
-    shard2 = last_steps(jnp.concatenate([near2, far2], axis=2), dn)
-    parts2 = last_doubling(meta, shard2)
-
+    near2, far2 = gathered(after(meta, mine, far_part[0]), M_H2, True, stay2, step2)
+    shard1 = last_steps(shard1, near2)
+    shard2 = last_steps(jnp.concatenate([after(near2, shard1), far2], axis=2))
+    parts1 = last_doubling(after(meta, shard2), shard1)
+    parts2 = last_doubling(after(meta, parts1[0]), shard2)
+    dn, row_sums, col_sums = tail_sums(after(meta, parts2[0]), mine, got, far_part, own_x, mu, inv, ln_gain)
     for delta in (1, 2):
         row_sums = row_sums + over_gate(row_sums, delta)
     dinputs = tail(after(meta, parts2[0]), dn, row_sums, own_x, mu, inv, ln_gain, direct, features)

time: 336 us -> 301 us (0.90)
  waiting for transfers between devices: 91.4 us -> 55.6 us
  local copies, waits for them, and re-layouts: 18.7 us -> 12.5 us
  Pallas kernels: 183 us -> 189 us
    ppermute x21, waiting for transfers between devices: 47 us -> 2.69 us  [over_gate(): return lax.ppermute(value, 'gate', [(g, g ^ delta) for g in range(n_gate)])]
    ppermute x16, waiting for transfers between devices: 30.6 us -> 45.4 us  [over_dp(): return lax.ppermute(value, ('dp', 'gate'), pairs)]
    pallas_call x24 -> x26, Pallas kernels: 183 us -> 189 us  [call(): pl.pallas_call(kernel, grid_spec=pltpu.PrefetchScalarGridSpec(num_scalar_...]
    ppermute x3, waiting for transfers between devices: 13.8 us -> 7.51 us  [shards(): lax.ppermute(totals, 'dp', [(d, d ^ 1 << step) for d in range(n_dp)])]
    unnamed x58 -> x53, local copies, waits for them, and re-layouts: 13.2 us -> 8.84 us
  transfers between devices with their start and end apart: 40 -> 40, of which waited for: 10 -> 13; matrix products, arithmetic and copies ran while one was open for 4% -> 4% of each run, Pallas kernels for 48% -> 56%
where the time goes in v5:
time: 301 us; the launch traced here: 300 us
  Pallas kernels  189 us (63%)
  waiting for transfers between devices  55.6 us (18%)
  starting transfers between devices  34.8 us (12%)
  local copies, waits for them, and re-layouts  12.5 us (4%)
  other arithmetic  6.51 us (2%)
    pallas_call x26, Pallas kernels, call(): pl.pallas_call(kernel, grid_spec=pltpu.PrefetchScalarGridSpec(num_scalar_...  189 us
    ppermute x16, waiting for transfers between devices, over_dp(): return lax.ppermute(value, ('dp', 'gate'), pairs)  45.4 us
    ppermute x16, starting transfers between devices, over_dp(): return lax.ppermute(value, ('dp', 'gate'), pairs)  18.1 us
    ppermute x21, starting transfers between devices, over_gate(): return lax.ppermute(value, 'gate', [(g, g ^ delta) for g in range(n_gate)])  14.2 us
    unnamed x53, local copies, waits for them, and re-layouts  8.84 us
    ppermute x3, waiting for transfers between devices, shards(): lax.ppermute(totals, 'dp', [(d, d ^ 1 << step) for d in range(n_dp)])  7.51 us
  transfers between devices with their start and end apart: 40, of which 13 were waited for; matrix products, arithmetic and copies ran while one was open for 4% of the time, Pallas kernels for 56%

profile of v5, /device:TPU:0, one launch (start us, length us, event | category | flops | bytes accessed | tf_op | source)
XLA Modules:
  0.0 299.8 jit_solution(1746204684231267847)
XLA Ops:
  1.4 4.8 %shard_map.178 = (bf16[2048,128]{1,0:T(8,128)(2,1)}, bf16[2048,128]{1,0:T(8,128)(2,1)}, bf16[2048,384]{1,0:T(8,128)(2,1)}) custom-call(s32[36]{0:T(128)} %stack.147.meta, bf16[2048,1536]{1,0:T(8,128)(2,1)} %refs_10_.7, bf16[2048,1536]{1,0:T(8,128)(2,1)} %refs_10_.7, bf16[2048,1536]{1,0:T(8,128)(2,1)} %refs_10_.7, bf16[2048,1536]{1,0:T(8,128)(2,1)} %refs_10_.7, ...), custom_call_target="tpu_custom_call" | custom-call | bytes 5242880 | tf_op jit(solution)/shard_map/pallas_call | solution.py:20
  6.7 2.6 collective-permute-start.1
  9.3 14.8 %shard_map.179 = (bf16[2048,2048]{1,0:T(8,128)(2,1)}, f32[2048,128]{1,0:T(8,128)}, f32[2048,128]{1,0:T(8,128)}, bf16[2048,512]{1,0:T(8,128)(2,1)}, f32[2048,128]{1,0:T(8,128)}, /*index=5*/f32[2048,128]{1,0:T(8,128)}) custom-call(s32[36]{0:T(128)} %stack.147.meta, bf16[2048,2048]{1,0:T(8,128)(2,1)} %bitcast.50, f32[1,2048]{1,0:T(1,128)} %bitcast.55, ...), custom_call_target="tpu_custom_call" | custom-call | flops 671088640 | bytes 335544320 | tf_op jit(solution)/shard_map/pallas_call | solution.py:20
  24.2 4.8 %shard_map.180 = (bf16[2048,256]{1,0:T(8,128)(2,1)}, bf16[2048,256]{1,0:T(8,128)(2,1)}) custom-call(s32[36]{0:T(128)} %stack.147.meta, bf16[2048,1536]{1,0:T(8,128)(2,1)} %refs_10_.7, bf16[2048,1536]{1,0:T(8,128)(2,1)} %refs_10_.7, bf16[2048,1536]{1,0:T(8,128)(2,1)} %refs_10_.7, bf16[2048,1536]{1,0:T(8,128)(2,1)} %refs_10_.7), custom_call_target="tpu_custom_call" | custom-call | bytes 4194304 | tf_op jit(solution)/shard_map/pallas_call | solution.py:20
  29.0 1.7 collective-permute-start.3
  31.4 1.7 collective-permute-done.2.refs_5_
  35.0 12.0 %shard_map.181.u_ref = bf16[2048,768]{1,0:T(8,128)(2,1)} custom-call(s32[36]{0:T(128)} %stack.147.meta, bf16[2048,2048]{1,0:T(8,128)(2,1)} %get-tuple-element.83.normed_ref, bf16[2048,1536]{1,0:T(8,128)(2,1)} %refs_10_.7, bf16[2048,1536]{1,0:T(8,128)(2,1)} %refs_10_.7, bf16[2048,384]{1,0:T(8,128)(2,1)} %copy-done.22, bf16[2048,384]{1,0:T(8,128)(2,1)} %copy-done.22, ...), custom_call_target="tpu_custom_call" | custom-call | flops 128849018880 | bytes 293601280 | tf_op jit(solution)/shard_map/pallas_call | solution.py:20
  47.0 12.4 %shard_map.182 = (bf16[2048,512]{1,0:T(8,128)(2,1)}, bf16[2048,768]{1,0:T(8,128)(2,1)}, bf16[2048,512]{1,0:T(8,128)(2,1)}, f32[8,512]{1,0:T(8,128)}) custom-call(s32[36]{0:T(128)} %stack.147.meta, bf16[2048,768]{1,0:T(8,128)(2,1)} %shard_map.181.u_ref, bf16[2048,512]{1,0:T(8,128)(2,1)} %get-tuple-element.89.x_ref, bf16[2048,512]{1,0:T(8,128)(2,1)} %bitcast.51, ...), custom_call_target="tpu_custom_call" | custom-call | flops 629145600 | bytes 188743680 | tf_op jit(solution)/shard_map/pallas_call | solution.py:20
  59.4 8.1 %shard_map.183 = (bf16[512,768]{1,0:T(8,128)(2,1)}, bf16[512,768]{1,0:T(8,128)(2,1)}) custom-call(s32[36]{0:T(128)} %stack.147.meta, bf16[2048,2048]{1,0:T(8,128)(2,1)} %get-tuple-element.83.normed_ref, bf16[2048,768]{1,0:T(8,128)(2,1)} %get-tuple-element.92.ds_ref.ds1_ref), custom_call_target="tpu_custom_call" | custom-call | flops 64424509440 | bytes 146800640 | tf_op jit(solution)/shard_map/pallas_call | solution.py:20
  67.6 1.5 collective-permute-start.6
  69.5 8.1 %shard_map.184 = (bf16[512,768]{1,0:T(8,128)(2,1)}, bf16[512,768]{1,0:T(8,128)(2,1)}) custom-call(s32[36]{0:T(128)} %stack.147.meta, bf16[2048,2048]{1,0:T(8,128)(2,1)} %get-tuple-element.83.normed_ref, bf16[2048,768]{1,0:T(8,128)(2,1)} %get-tuple-element.92.ds_ref.ds1_ref), custom_call_target="tpu_custom_call" | custom-call | flops 64424509440 | bytes 146800640 | tf_op jit(solution)/shard_map/pallas_call | solution.py:20
  77.7 1.5 collective-permute-start.8
  79.2 12.1 %shard_map.185.u_ref = bf16[2048,768]{1,0:T(8,128)(2,1)} custom-call(s32[36]{0:T(128)} %stack.147.meta, bf16[2048,2048]{1,0:T(8,128)(2,1)} %get-tuple-element.83.normed_ref, bf16[2048,256]{1,0:T(8,128)(2,1)} %collective-permute-done.3.refs_0_.refs_1_.refs_6_.refs_7_, bf16[2048,256]{1,0:T(8,128)(2,1)} %collective-permute-done.3.refs_0_.refs_1_.refs_6_.refs_7_, ...), custom_call_target="tpu_custom_call" | custom-call | flops 128849018880 | bytes 293601280 | tf_op jit(solution)/shard_map/pallas_call | solution.py:20
  93.1 3.7 %shard_map.186 = (bf16[2,256,768]{2,1,0:T(8,128)(2,1)}, bf16[2,256,768]{2,1,0:T(8,128)(2,1)}) custom-call(s32[36]{0:T(128)} %stack.147.meta, bf16[512,768]{1,0:T(8,128)(2,1)} %get-tuple-element.95.refs_0_.refs_4_, bf16[512,768]{1,0:T(8,128)(2,1)} %copy-done.1, bf16[512,768]{1,0:T(8,128)(2,1)} %collective-permute-done.6.refs_2_.refs_6_, ...), custom_call_target="tpu_custom_call" | custom-call | flops 1572864 | bytes 4718592 | tf_op jit(solution)/shard_map/pallas_call | solution.py:20
  97.4 12.4 %shard_map.187 = (bf16[2048,512]{1,0:T(8,128)(2,1)}, bf16[2048,768]{1,0:T(8,128)(2,1)}, bf16[2048,512]{1,0:T(8,128)(2,1)}, f32[8,512]{1,0:T(8,128)}) custom-call(s32[36]{0:T(128)} %stack.147.meta, bf16[2048,768]{1,0:T(8,128)(2,1)} %shard_map.185.u_ref, ...), custom_call_target="tpu_custom_call", output_to_operand_aliasing={{0}: (7, {}), {2}: (8, {}), {3}: (9, {})} | custom-call | flops 629145600 | bytes 188743680 | tf_op jit(solution)/shard_map/pallas_call | solution.py:20
  110.8 3.0 %shard_map.188 = (bf16[2,128,768]{2,1,0:T(8,128)(2,1)}, bf16[2,128,768]{2,1,0:T(8,128)(2,1)}) custom-call(s32[36]{0:T(128)} %stack.147.meta, bf16[2,256,768]{2,1,0:T(8,128)(2,1)} %get-tuple-element.108.refs_0_.refs_2_, bf16[2,256,768]{2,1,0:T(8,128)(2,1)} %copy-done.7, bf16[2,256,768]{2,1,0:T(8,128)(2,1)} %get-tuple-element.108.refs_0_.refs_2_, ...), custom_call_target="tpu_custom_call" | custom-call | flops 786432 | bytes 2359296 | tf_op jit(solution)/shard_map/pallas_call | solution.py:20
  113.8 2.6 collective-permute-start.14
  116.4 8.1 %shard_map.189 = (bf16[512,768]{1,0:T(8,128)(2,1)}, bf16[512,768]{1,0:T(8,128)(2,1)}) custom-call(s32[36]{0:T(128)} %stack.147.meta, bf16[2048,2048]{1,0:T(8,128)(2,1)} %get-tuple-element.83.normed_ref, bf16[2048,768]{1,0:T(8,128)(2,1)} %get-tuple-element.106.ds_ref.ds2_ref), custom_call_target="tpu_custom_call" | custom-call | flops 64424509440 | bytes 146800640 | tf_op jit(solution)/shard_map/pallas_call | solution.py:20
  124.5 1.5 collective-permute-start.11
  126.0 8.1 %shard_map.190 = (bf16[512,768]{1,0:T(8,128)(2,1)}, bf16[512,768]{1,0:T(8,128)(2,1)}) custom-call(s32[36]{0:T(128)} %stack.147.meta, bf16[2048,2048]{1,0:T(8,128)(2,1)} %get-tuple-element.83.normed_ref, bf16[2048,768]{1,0:T(8,128)(2,1)} %get-tuple-element.106.ds_ref.ds2_ref), custom_call_target="tpu_custom_call" | custom-call | flops 64424509440 | bytes 146800640 | tf_op jit(solution)/shard_map/pallas_call | solution.py:20
  135.2 8.0 %shard_map.191 = bf16[2048,512]{1,0:T(8,128)(2,1)} custom-call(s32[36]{0:T(128)} %stack.147.meta, bf16[2048,768]{1,0:T(8,128)(2,1)} %get-tuple-element.92.ds_ref.ds1_ref, bf16[2048,768]{1,0:T(8,128)(2,1)} %get-tuple-element.106.ds_ref.ds2_ref, bf16[2048,1536]{1,0:T(8,128)(2,1)} %refs_10_.7, bf16[2048,1536]{1,0:T(8,128)(2,1)} %refs_10_.7, ...), custom_call_target="tpu_custom_call" | custom-call | flops 64424509440 | bytes 125829120 | tf_op jit(solution)/shard_map/pallas_call | solution.py:20
  143.3 3.4 %collective-permute-done.13.refs_3_.refs_7_ = bf16[512,768]{1,0:T(8,128)(2,1)S(1)} collective-permute-done((bf16[512,768]{1,0:T(8,128)(2,1)S(1)}, bf16[512,768]{1,0:T(8,128)(2,1)S(1)}, u32[]{:S(2)}, u32[]{:S(2)}) %collective-permute-start.13) | collective-permute-done | bytes 786464 | tf_op jit(solution)/shard_map/ppermute | solution.py:769
  147.6 3.7 %shard_map.192 = (bf16[2,256,768]{2,1,0:T(8,128)(2,1)}, bf16[2,256,768]{2,1,0:T(8,128)(2,1)}) custom-call(s32[36]{0:T(128)} %stack.147.meta, bf16[512,768]{1,0:T(8,128)(2,1)} %get-tuple-element.113.refs_0_.refs_4_, bf16[512,768]{1,0:T(8,128)(2,1)} %copy-done.2, bf16[512,768]{1,0:T(8,128)(2,1)} %copy-done, bf16[512,768]{1,0:T(8,128)(2,1)} %copy-done.4, ...), custom_call_target="tpu_custom_call" | custom-call | flops 1572864 | bytes 4718592 | tf_op jit(solution)/shard_map/pallas_call | solution.py:20
  151.8 2.6 shard_map.193
  154.4 1.5 collective-permute-start.17
  156.0 8.3 %shard_map.194 = bf16[2048,512]{1,0:T(8,128)(2,1)} custom-call(s32[36]{0:T(128)} %stack.147.meta, bf16[2048,768]{1,0:T(8,128)(2,1)} %get-tuple-element.92.ds_ref.ds1_ref, bf16[2048,768]{1,0:T(8,128)(2,1)} %get-tuple-element.106.ds_ref.ds2_ref, bf16[2048,1536]{1,0:T(8,128)(2,1)} %refs_10_.7, bf16[2048,1536]{1,0:T(8,128)(2,1)} %refs_10_.7, ...), custom_call_target="tpu_custom_call" | custom-call | flops 64424509440 | bytes 125829120 | tf_op jit(solution)/shard_map/pallas_call | solution.py:20
  165.1 3.2 %shard_map.195 = (bf16[2,128,768]{2,1,0:T(8,128)(2,1)}, bf16[2,128,768]{2,1,0:T(8,128)(2,1)}) custom-call(s32[36]{0:T(128)} %stack.147.meta, bf16[2,256,768]{2,1,0:T(8,128)(2,1)} %get-tuple-element.124.refs_0_.refs_2_, bf16[2,256,768]{2,1,0:T(8,128)(2,1)} %copy-done.6, bf16[2,256,768]{2,1,0:T(8,128)(2,1)} %get-tuple-element.124.refs_0_.refs_2_, ...), custom_call_target="tpu_custom_call" | custom-call | flops 786432 | bytes 2359296 | tf_op jit(solution)/shard_map/pallas_call | solution.py:20
  168.6 2.0 add_convert_fusion.1
  171.1 3.0 add_convert_fusion
  174.1 8.2 %shard_map.196 = bf16[2048,512]{1,0:T(8,128)(2,1)} custom-call(s32[36]{0:T(128)} %stack.147.meta, bf16[2048,768]{1,0:T(8,128)(2,1)} %get-tuple-element.92.ds_ref.ds1_ref, bf16[2048,768]{1,0:T(8,128)(2,1)} %get-tuple-element.106.ds_ref.ds2_ref, bf16[2048,1536]{1,0:T(8,128)(2,1)} %refs_10_.7, bf16[2048,1536]{1,0:T(8,128)(2,1)} %refs_10_.7, ...), custom_call_target="tpu_custom_call" | custom-call | flops 64424509440 | bytes 125829120 | tf_op jit(solution)/shard_map/pallas_call | solution.py:20
  182.3 2.7 collective-permute-start.20
  184.9 3.5 %collective-permute-start.25 = (bf16[2048,512]{1,0:T(8,128)(2,1)}, bf16[2048,512]{1,0:T(8,128)(2,1)S(1)}, u32[]{:S(2)}, u32[]{:S(2)}) collective-permute-start(bf16[2048,512]{1,0:T(8,128)(2,1)} %shard_map.196), channel_id=1, source_target_pairs={{0,1},{1,0},{2,3},{3,2},{4,5},{5,4},{6,7},{7,6},{8,9},{9,8},{10,11... | collective-permute-start | bytes 6291464 | tf_op jit(solution)/shard_map/ppermute | solution.py:763
  188.5 8.0 %shard_map.197.k_ref = bf16[2048,512]{1,0:T(8,128)(2,1)} custom-call(s32[36]{0:T(128)} %stack.147.meta, bf16[2048,768]{1,0:T(8,128)(2,1)} %get-tuple-element.92.ds_ref.ds1_ref, bf16[2048,768]{1,0:T(8,128)(2,1)} %get-tuple-element.106.ds_ref.ds2_ref, bf16[2048,1536]{1,0:T(8,128)(2,1)} %refs_10_.7, bf16[2048,1536]{1,0:T(8,128)(2,1)} %refs_10_.7, ...), custom_call_target="tpu_custom_call" | custom-call | flops 64424509440 | bytes 125829120 | tf_op jit(solution)/shard_map/pallas_call | solution.py:20
  197.4 2.6 shard_map.198
  200.5 5.4 %collective-permute-done.20 = bf16[2,128,768]{2,1,0:T(8,128)(2,1)} collective-permute-done((bf16[2,128,768]{2,1,0:T(8,128)(2,1)S(1)}, bf16[2,128,768]{2,1,0:T(8,128)(2,1)}, u32[]{:S(2)}, u32[]{:S(2)}) %collective-permute-start.20) | collective-permute-done | bytes 393248 | tf_op jit(solution)/shard_map/ppermute | solution.py:769
  210.0 1.8 collective-permute-start.23
  211.8 16.7 %collective-permute-done.22 = bf16[2,128,768]{2,1,0:T(8,128)(2,1)S(1)} collective-permute-done((bf16[2,128,768]{2,1,0:T(8,128)(2,1)S(1)}, bf16[2,128,768]{2,1,0:T(8,128)(2,1)S(1)}, u32[]{:S(2)}, u32[]{:S(2)}) %collective-permute-start.22) | collective-permute-done | bytes 393248 | tf_op jit(solution)/shard_map/ppermute | solution.py:769
  228.6 1.9 collective-permute-done.23.b_ref
  230.4 3.2 %shard_map.199 = (bf16[512,768]{1,0:T(8,128)(2,1)}, bf16[512,768]{1,0:T(8,128)(2,1)}) custom-call(s32[36]{0:T(128)} %stack.147.meta, bf16[2,256,768]{2,1,0:T(8,128)(2,1)} %copy-done.10, bf16[2,256,768]{2,1,0:T(8,128)(2,1)} %collective-permute-done.23.b_ref), custom_call_target="tpu_custom_call" | custom-call | bytes 3145728 | tf_op jit(solution)/shard_map/pallas_call | solution.py:20
  233.7 1.8 collective-permute-start.31
  235.5 10.4 %collective-permute-done.24.b_ref = bf16[2,256,768]{2,1,0:T(8,128)(2,1)} collective-permute-done((bf16[2,256,768]{2,1,0:T(8,128)(2,1)S(1)}, bf16[2,256,768]{2,1,0:T(8,128)(2,1)}, u32[]{:S(2)}, u32[]{:S(2)}) %collective-permute-start.24) | collective-permute-done | bytes 786464 | tf_op jit(solution)/shard_map/ppermute | solution.py:769
  245.9 3.2 %shard_map.200 = (bf16[512,768]{1,0:T(8,128)(2,1)}, bf16[512,768]{1,0:T(8,128)(2,1)}) custom-call(s32[36]{0:T(128)} %stack.147.meta, bf16[2,256,768]{2,1,0:T(8,128)(2,1)} %copy-done.5, bf16[2,256,768]{2,1,0:T(8,128)(2,1)} %collective-permute-done.24.b_ref), custom_call_target="tpu_custom_call" | custom-call | bytes 3145728 | tf_op jit(solution)/shard_map/pallas_call | solution.py:20
  251.4 9.5 %shard_map.201 = (f32[2048,512]{1,0:T(8,128)}, f32[8,2048]{1,0:T(8,128)}, f32[8,512]{1,0:T(8,128)}) custom-call(s32[36]{0:T(128)} %stack.147.meta, bf16[2048,512]{1,0:T(8,128)(2,1)} %shard_map.197.k_ref, bf16[2048,512]{1,0:T(8,128)(2,1)} %copy-done.9, bf16[512,512]{1,0:T(8,128)(2,1)} %copy-done.15, bf16[1536,512]{1,0:T(8,128)(2,1)} %collective-permute-done.26.r2_ref, ...), custom_call_target="tpu_custom_call" | custom-call | flops 20971520 | bytes 12582912 | tf_op jit(solution)/shard_map/pallas_call | solution.py:20
  265.6 3.7 %collective-permute-done.38 = f32[6,512]{1,0:T(8,128)S(1)} collective-permute-done((f32[6,512]{1,0:T(8,128)S(1)}, f32[6,512]{1,0:T(8,128)S(1)}, u32[]{:S(2)}, u32[]{:S(2)}) %collective-permute-start.38) | collective-permute-done | bytes 12320 | tf_op jit(solution)/shard_map/ppermute | solution.py:862
  271.4 2.8 collective-permute-done.39
  276.9 7.4 %shard_map.202 = bf16[2048,512]{1,0:T(8,128)(2,1)} custom-call(s32[36]{0:T(128)} %stack.147.meta, f32[2048,512]{1,0:T(8,128)} %get-tuple-element.144.dn_ref, f32[8,2048]{1,0:T(8,128)} %add.126.row_ref, bf16[2048,512]{1,0:T(8,128)(2,1)} %get-tuple-element.89.x_ref, f32[2048,128]{1,0:T(8,128)} %get-tuple-element.142.mu_ref, ...), custom_call_target="tpu_custom_call" | custom-call | flops 10485760 | bytes 12582912 | tf_op jit(solution)/shard_map/pallas_call | solution.py:20
  284.3 6.9 %collective-permute-done.33.refs_5_ = bf16[512,768]{1,0:T(8,128)(2,1)} collective-permute-done((bf16[512,768]{1,0:T(8,128)(2,1)S(1)}, bf16[512,768]{1,0:T(8,128)(2,1)}, u32[]{:S(2)}, u32[]{:S(2)}) %collective-permute-start.33) | collective-permute-done | bytes 786464 | tf_op jit(solution)/shard_map/ppermute | solution.py:769
  291.2 8.5 %shard_map.203 = f32[2048,1536]{1,0:T(8,128)} custom-call(s32[36]{0:T(128)} %stack.147.meta, bf16[512,768]{1,0:T(8,128)(2,1)} %get-tuple-element.138.refs_0_, bf16[512,768]{1,0:T(8,128)(2,1)} %copy-done.13, bf16[512,768]{1,0:T(8,128)(2,1)} %collective-permute-done.30.refs_2_, bf16[512,768]{1,0:T(8,128)(2,1)} %collective-permute-done.32.refs_3_, ...), custom_call_target="tpu_custom_call" | custom-call | flops 3145728 | bytes 18874368 | tf_op jit(solution)/shard_map/pallas_call | solution.py:20
  (129 shorter events, 29.1 us)
Async XLA Ops:
  6.2 26.9 %collective-permute-start = (bf16[2048,384]{1,0:T(8,128)(2,1)}, bf16[2048,384]{1,0:T(8,128)(2,1)S(1)}, u32[]{:S(2)}, u32[]{:S(2)}) collective-permute-start(bf16[2048,384]{1,0:T(8,128)(2,1)} %get-tuple-element.88), channel_id=1, source_target_pairs={{0,1},{1,0},{2,3},{3,2},{4,5},{5,4},{6,7},{7,6},{8,9},{9,8},{10,11... | collective-permute-start | bytes 4718600 | tf_op jit(solution)/shard_map/ppermute | solution.py:763
  6.7 24.7 %collective-permute-start.1 = (bf16[2048,128]{1,0:T(8,128)(2,1)}, bf16[2048,128]{1,0:T(8,128)(2,1)S(1)}, u32[]{:S(2)}, u32[]{:S(2)}) collective-permute-start(bf16[2048,128]{1,0:T(8,128)(2,1)} %get-tuple-element.80), channel_id=1, source_target_pairs={{0,2},{1,3},{2,0},{3,1},{4,6},{5,7},{6,4},{7,5},{8,10},{9,11},{10,... | collective-permute-start | bytes 1572872 | tf_op jit(solution)/shard_map/ppermute | solution.py:763
  9.2 23.9 %collective-permute-start.2 = (bf16[2048,128]{1,0:T(8,128)(2,1)}, bf16[2048,128]{1,0:T(8,128)(2,1)S(1)}, u32[]{:S(2)}, u32[]{:S(2)}) collective-permute-start(bf16[2048,128]{1,0:T(8,128)(2,1)} %get-tuple-element.81), channel_id=1, source_target_pairs={{0,3},{1,2},{2,1},{3,0},{4,7},{5,6},{6,5},{7,4},{8,11},{9,10},{10,... | collective-permute-start | bytes 1572872 | tf_op jit(solution)/shard_map/ppermute | solution.py:763
  29.0 50.2 %collective-permute-start.3 = (bf16[2048,256]{1,0:T(8,128)(2,1)}, bf16[2048,256]{1,0:T(8,128)(2,1)}, u32[]{:S(2)}, u32[]{:S(2)}) collective-permute-start(bf16[2048,256]{1,0:T(8,128)(2,1)} %get-tuple-element.85), channel_id=1, source_target_pairs={{0,2},{1,3},{2,0},{3,1},{4,6},{5,7},{6,4},{7,5},{8,10},{9,11},{10,... | collective-permute-start | bytes 3145736 | tf_op jit(solution)/shard_map/ppermute | solution.py:763
  30.7 48.5 %collective-permute-start.4 = (bf16[2048,256]{1,0:T(8,128)(2,1)}, bf16[2048,256]{1,0:T(8,128)(2,1)}, u32[]{:S(2)}, u32[]{:S(2)}) collective-permute-start(bf16[2048,256]{1,0:T(8,128)(2,1)} %get-tuple-element.86), channel_id=1, source_target_pairs={{0,3},{1,2},{2,1},{3,0},{4,7},{5,6},{6,5},{7,4},{8,11},{9,10},{10,... | collective-permute-start | bytes 3145736 | tf_op jit(solution)/shard_map/ppermute | solution.py:763
  67.6 23.8 %collective-permute-start.6 = (bf16[512,768]{1,0:T(8,128)(2,1)}, bf16[512,768]{1,0:T(8,128)(2,1)}, u32[]{:S(2)}, u32[]{:S(2)}) collective-permute-start(bf16[512,768]{1,0:T(8,128)(2,1)} %get-tuple-element.93), channel_id=1, source_target_pairs={{0,4},{1,9},{2,6},{3,11},{4,0},{5,13},{6,2},{7,15},{8,12},{9,1},{1... | collective-permute-start | bytes 2359304 | tf_op jit(solution)/shard_map/ppermute | solution.py:769
  69.1 8.6 %collective-permute-start.7 = (bf16[512,768]{1,0:T(8,128)(2,1)}, bf16[512,768]{1,0:T(8,128)(2,1)S(1)}, u32[]{:S(2)}, u32[]{:S(2)}) collective-permute-start(bf16[512,768]{1,0:T(8,128)(2,1)} %get-tuple-element.99), channel_id=1, source_target_pairs={{0,1},{1,0},{2,3},{3,2},{4,5},{5,4},{6,7},{7,6},{8,9},{9,8},{10,11... | collective-permute-start | bytes 2359304 | tf_op jit(solution)/shard_map/ppermute | solution.py:763
  77.7 13.7 %collective-permute-start.5 = (bf16[512,768]{1,0:T(8,128)(2,1)}, bf16[512,768]{1,0:T(8,128)(2,1)S(1)}, u32[]{:S(2)}, u32[]{:S(2)}) collective-permute-start(bf16[512,768]{1,0:T(8,128)(2,1)} %get-tuple-element.98), channel_id=1, source_target_pairs={{0,1},{1,0},{2,3},{3,2},{4,5},{5,4},{6,7},{7,6},{8,9},{9,8},{10,11... | collective-permute-start | bytes 2359304 | tf_op jit(solution)/shard_map/ppermute | solution.py:763
  77.7 13.7 %collective-permute-start.8 = (bf16[512,768]{1,0:T(8,128)(2,1)S(1)}, bf16[512,768]{1,0:T(8,128)(2,1)S(1)}, u32[]{:S(2)}, u32[]{:S(2)}) collective-permute-start(bf16[512,768]{1,0:T(8,128)(2,1)S(1)} %collective-permute-done.7), channel_id=1, source_target_pairs={{0,4},{1,9},{2,6},{3,11},{4,0},{5,13},{6,2},{7,15},{8,12},{9,1},{1... | collective-permute-start | bytes 2359304 | tf_op jit(solution)/shard_map/ppermute | solution.py:769
  96.9 13.0 %collective-permute-start.9 = (bf16[2,256,768]{2,1,0:T(8,128)(2,1)}, bf16[2,256,768]{2,1,0:T(8,128)(2,1)S(1)}, u32[]{:S(2)}, u32[]{:S(2)}) collective-permute-start(bf16[2,256,768]{2,1,0:T(8,128)(2,1)} %get-tuple-element.100), channel_id=1, source_target_pairs={{0,8},{1,5},{2,10},{3,7},{4,12},{5,1},{6,14},{7,3},{8,0},{9,13},{1... | collective-permute-start | bytes 2359304 | tf_op jit(solution)/shard_map/ppermute | solution.py:769
  113.8 38.0 %collective-permute-start.14 = (bf16[2,128,768]{2,1,0:T(8,128)(2,1)}, bf16[2,128,768]{2,1,0:T(8,128)(2,1)}, u32[]{:S(2)}, u32[]{:S(2)}) collective-permute-start(bf16[2,128,768]{2,1,0:T(8,128)(2,1)} %get-tuple-element.109), channel_id=1, source_target_pairs={{0,16},{1,17},{2,18},{3,19},{4,20},{5,21},{6,22},{7,23},{8,24},{9,... | collective-permute-start | bytes 1179656 | tf_op jit(solution)/shard_map/ppermute | solution.py:769
  124.5 18.7 %collective-permute-start.11 = (bf16[512,768]{1,0:T(8,128)(2,1)}, bf16[512,768]{1,0:T(8,128)(2,1)S(1)}, u32[]{:S(2)}, u32[]{:S(2)}) collective-permute-start(bf16[512,768]{1,0:T(8,128)(2,1)} %get-tuple-element.111), channel_id=1, source_target_pairs={{0,4},{1,9},{2,6},{3,11},{4,0},{5,13},{6,2},{7,15},{8,12},{9,1},{1... | collective-permute-start | bytes 2359304 | tf_op jit(solution)/shard_map/ppermute | solution.py:769
  126.0 8.6 %collective-permute-start.12 = (bf16[512,768]{1,0:T(8,128)(2,1)}, bf16[512,768]{1,0:T(8,128)(2,1)S(1)}, u32[]{:S(2)}, u32[]{:S(2)}) collective-permute-start(bf16[512,768]{1,0:T(8,128)(2,1)} %get-tuple-element.117), channel_id=1, source_target_pairs={{0,1},{1,0},{2,3},{3,2},{4,5},{5,4},{6,7},{7,6},{8,9},{9,8},{10,11... | collective-permute-start | bytes 2359304 | tf_op jit(solution)/shard_map/ppermute | solution.py:763
  134.1 9.1 %collective-permute-start.10 = (bf16[512,768]{1,0:T(8,128)(2,1)}, bf16[512,768]{1,0:T(8,128)(2,1)S(1)}, u32[]{:S(2)}, u32[]{:S(2)}) collective-permute-start(bf16[512,768]{1,0:T(8,128)(2,1)} %get-tuple-element.116), channel_id=1, source_target_pairs={{0,1},{1,0},{2,3},{3,2},{4,5},{5,4},{6,7},{7,6},{8,9},{9,8},{10,11... | collective-permute-start | bytes 2359304 | tf_op jit(solution)/shard_map/ppermute | solution.py:763
  134.6 12.0 %collective-permute-start.13 = (bf16[512,768]{1,0:T(8,128)(2,1)S(1)}, bf16[512,768]{1,0:T(8,128)(2,1)S(1)}, u32[]{:S(2)}, u32[]{:S(2)}) collective-permute-start(bf16[512,768]{1,0:T(8,128)(2,1)S(1)} %collective-permute-done.12), channel_id=1, source_target_pairs={{0,4},{1,9},{2,6},{3,11},{4,0},{5,13},{6,2},{7,15},{8,12},{9,1},{1... | collective-permute-start | bytes 2359304 | tf_op jit(solution)/shard_map/ppermute | solution.py:769
  143.2 25.4 %collective-permute-start.16 = (bf16[2048,512]{1,0:T(8,128)(2,1)}, bf16[2048,512]{1,0:T(8,128)(2,1)}, u32[]{:S(2)}, u32[]{:S(2)}) collective-permute-start(bf16[2048,512]{1,0:T(8,128)(2,1)} %shard_map.191), channel_id=1, source_target_pairs={{0,1},{1,0},{2,3},{3,2},{4,5},{5,4},{6,7},{7,6},{8,9},{9,8},{10,11... | collective-permute-start | bytes 6291464 | tf_op jit(solution)/shard_map/ppermute | solution.py:763
  151.3 12.9 %collective-permute-start.15 = (bf16[2,256,768]{2,1,0:T(8,128)(2,1)}, bf16[2,256,768]{2,1,0:T(8,128)(2,1)S(1)}, u32[]{:S(2)}, u32[]{:S(2)}) collective-permute-start(bf16[2,256,768]{2,1,0:T(8,128)(2,1)} %get-tuple-element.118), channel_id=1, source_target_pairs={{0,8},{1,5},{2,10},{3,7},{4,12},{5,1},{6,14},{7,3},{8,0},{9,13},{1... | collective-permute-start | bytes 2359304 | tf_op jit(solution)/shard_map/ppermute | solution.py:769
  154.4 27.8 %collective-permute-start.17 = (bf16[2,128,256]{2,1,0:T(8,128)(2,1)}, bf16[2,128,256]{2,1,0:T(8,128)(2,1)S(1)}, u32[]{:S(2)}, u32[]{:S(2)}) collective-permute-start(bf16[2,128,256]{2,1,0:T(8,128)(2,1)} %get-tuple-element.129), channel_id=1, source_target_pairs={{0,2},{1,3},{2,0},{3,1},{4,6},{5,7},{6,4},{7,5},{8,10},{9,11},{10,... | collective-permute-start | bytes 393224 | tf_op jit(solution)/shard_map/ppermute | solution.py:763
  168.3 29.2 %collective-permute-start.19 = (bf16[2,128,768]{2,1,0:T(8,128)(2,1)}, bf16[2,128,768]{2,1,0:T(8,128)(2,1)}, u32[]{:S(2)}, u32[]{:S(2)}) collective-permute-start(bf16[2,128,768]{2,1,0:T(8,128)(2,1)} %get-tuple-element.125), channel_id=1, source_target_pairs={{0,16},{1,17},{2,18},{3,19},{4,20},{5,21},{6,22},{7,23},{8,24},{9,... | collective-permute-start | bytes 1179656 | tf_op jit(solution)/shard_map/ppermute | solution.py:769
  170.6 25.9 %collective-permute-start.18 = (bf16[512,512]{1,0:T(8,128)(2,1)}, bf16[512,512]{1,0:T(8,128)(2,1)S(1)}, u32[]{:S(2)}, u32[]{:S(2)}) collective-permute-start(bf16[512,512]{1,0:T(8,128)(2,1)} %add_convert_fusion.1), channel_id=1, source_target_pairs={{0,2},{1,3},{2,0},{3,1},{4,6},{5,7},{6,4},{7,5},{8,10},{9,11},{10,... | collective-permute-start | bytes 1572872 | tf_op jit(solution)/shard_map/ppermute | solution.py:763
  174.1 8.2 %copy-start.16 = (bf16[2,128,512]{2,1,0:T(8,128)(2,1)S(1)}, bf16[2,128,512]{2,1,0:T(8,128)(2,1)}, u32[]{:S(2)}) copy-start(bf16[2,128,512]{2,1,0:T(8,128)(2,1)} %get-tuple-element.128) | copy-start | bytes 786436
  182.3 23.6 %collective-permute-start.20 = (bf16[2,128,768]{2,1,0:T(8,128)(2,1)S(1)}, bf16[2,128,768]{2,1,0:T(8,128)(2,1)}, u32[]{:S(2)}, u32[]{:S(2)}) collective-permute-start(bf16[2,128,768]{2,1,0:T(8,128)(2,1)S(1)} %constant_dynamic-update-slice_fusion), channel_id=1, source_target_pairs={{0,16},{1,17},{2,18},{3,19},{4,20},{5,21},{6,22},{7,23},{8,24},{9,... | collective-permute-start | bytes 1179656 | tf_op jit(solution)/shard_map/ppermute | solution.py:769
  184.9 65.2 %collective-permute-start.25 = (bf16[2048,512]{1,0:T(8,128)(2,1)}, bf16[2048,512]{1,0:T(8,128)(2,1)S(1)}, u32[]{:S(2)}, u32[]{:S(2)}) collective-permute-start(bf16[2048,512]{1,0:T(8,128)(2,1)} %shard_map.196), channel_id=1, source_target_pairs={{0,1},{1,0},{2,3},{3,2},{4,5},{5,4},{6,7},{7,6},{8,9},{9,8},{10,11... | collective-permute-start | bytes 6291464 | tf_op jit(solution)/shard_map/ppermute | solution.py:763
  196.5 15.2 %copy-start.15 = (bf16[512,512]{1,0:T(8,128)(2,1)}, bf16[512,512]{1,0:T(8,128)(2,1)S(1)}, u32[]{:S(2)}) copy-start(bf16[512,512]{1,0:T(8,128)(2,1)S(1)} %collective-permute-done.18.r1_ref) | copy-start | bytes 1572868
  200.1 8.5 %collective-permute-start.21 = (bf16[2,128,512]{2,1,0:T(8,128)(2,1)}, bf16[2,128,512]{2,1,0:T(8,128)(2,1)S(1)}, u32[]{:S(2)}, u32[]{:S(2)}) collective-permute-start(bf16[2,128,512]{2,1,0:T(8,128)(2,1)} %get-tuple-element.136), channel_id=1, source_target_pairs={{0,2},{1,3},{2,0},{3,1},{4,6},{5,7},{6,4},{7,5},{8,10},{9,11},{10,... | collective-permute-start | bytes 786440 | tf_op jit(solution)/shard_map/ppermute | solution.py:763
  206.9 23.5 %copy-start.10 = (bf16[2,256,768]{2,1,0:T(8,128)(2,1)}, bf16[2,256,768]{2,1,0:T(8,128)(2,1)S(1)}, u32[]{:S(2)}) copy-start(bf16[2,256,768]{2,1,0:T(8,128)(2,1)S(1)} %constant_dynamic-update-slice_fusion.2.a_ref) | copy-start | bytes 2359300
  208.6 41.5 %copy-start.17 = (f32[8,512]{1,0:T(8,128)S(1)}, f32[8,512]{1,0:T(8,128)}, u32[]{:S(2)}) copy-start(f32[8,512]{1,0:T(8,128)} %get-tuple-element.150) | copy-start | bytes 49156
  208.6 19.8 %collective-permute-start.22 = (bf16[2,128,768]{2,1,0:T(8,128)(2,1)S(1)}, bf16[2,128,768]{2,1,0:T(8,128)(2,1)S(1)}, u32[]{:S(2)}, u32[]{:S(2)}) collective-permute-start(bf16[2,128,768]{2,1,0:T(8,128)(2,1)S(1)} %constant_dynamic-update-slice_fusion.4), channel_id=1, source_target_pairs={{0,16},{1,17},{2,18},{3,19},{4,20},{5,21},{6,22},{7,23},{8,24},{9,... | collective-permute-start | bytes 1179656 | tf_op jit(solution)/shard_map/ppermute | solution.py:769
  208.7 41.5 %collective-permute-start.26 = (bf16[1536,512]{1,0:T(8,128)(2,1)}, bf16[1536,512]{1,0:T(8,128)(2,1)}, u32[]{:S(2)}, u32[]{:S(2)}) collective-permute-start(bf16[1536,512]{1,0:T(8,128)(2,1)} %add_convert_fusion), channel_id=1, source_target_pairs={{0,2},{1,3},{2,0},{3,1},{4,6},{5,7},{6,4},{7,5},{8,10},{9,11},{10,... | collective-permute-start | bytes 4718600 | tf_op jit(solution)/shard_map/ppermute | solution.py:763
  210.0 20.5 %collective-permute-start.23 = (bf16[2,256,768]{2,1,0:T(8,128)(2,1)S(1)}, bf16[2,256,768]{2,1,0:T(8,128)(2,1)}, u32[]{:S(2)}, u32[]{:S(2)}) collective-permute-start(bf16[2,256,768]{2,1,0:T(8,128)(2,1)S(1)} %constant_dynamic-update-slice_fusion.2.a_ref), channel_id=1, source_target_pairs={{0,8},{1,5},{2,10},{3,7},{4,12},{5,1},{6,14},{7,3},{8,0},{9,13},{1... | collective-permute-start | bytes 2359304 | tf_op jit(solution)/shard_map/ppermute | solution.py:769
  228.5 17.4 %copy-start.5 = (bf16[2,256,768]{2,1,0:T(8,128)(2,1)}, bf16[2,256,768]{2,1,0:T(8,128)(2,1)S(1)}, u32[]{:S(2)}) copy-start(bf16[2,256,768]{2,1,0:T(8,128)(2,1)S(1)} %pad_maximum_fusion.a_ref) | copy-start | bytes 2359300
  228.5 17.4 %collective-permute-start.24 = (bf16[2,256,768]{2,1,0:T(8,128)(2,1)S(1)}, bf16[2,256,768]{2,1,0:T(8,128)(2,1)}, u32[]{:S(2)}, u32[]{:S(2)}) collective-permute-start(bf16[2,256,768]{2,1,0:T(8,128)(2,1)S(1)} %pad_maximum_fusion.a_ref), channel_id=1, source_target_pairs={{0,8},{1,5},{2,10},{3,7},{4,12},{5,1},{6,14},{7,3},{8,0},{9,13},{1... | collective-permute-start | bytes 2359304 | tf_op jit(solution)/shard_map/ppermute | solution.py:769
  233.7 37.0 %collective-permute-start.31 = (bf16[512,768]{1,0:T(8,128)(2,1)}, bf16[512,768]{1,0:T(8,128)(2,1)}, u32[]{:S(2)}, u32[]{:S(2)}) collective-permute-start(bf16[512,768]{1,0:T(8,128)(2,1)} %get-tuple-element.147), channel_id=1, source_target_pairs={{0,4},{1,9},{2,6},{3,11},{4,0},{5,13},{6,2},{7,15},{8,12},{9,1},{1... | collective-permute-start | bytes 2359304 | tf_op jit(solution)/shard_map/ppermute | solution.py:769
  235.5 35.9 %collective-permute-start.30 = (bf16[512,768]{1,0:T(8,128)(2,1)}, bf16[512,768]{1,0:T(8,128)(2,1)}, u32[]{:S(2)}, u32[]{:S(2)}) collective-permute-start(bf16[512,768]{1,0:T(8,128)(2,1)} %get-tuple-element.147), channel_id=1, source_target_pairs={{0,1},{1,0},{2,3},{3,2},{4,5},{5,4},{6,7},{7,6},{8,9},{9,8},{10,11... | collective-permute-start | bytes 2359304 | tf_op jit(solution)/shard_map/ppermute | solution.py:763
  249.1 26.0 %collective-permute-start.35 = (bf16[512,768]{1,0:T(8,128)(2,1)}, bf16[512,768]{1,0:T(8,128)(2,1)}, u32[]{:S(2)}, u32[]{:S(2)}) collective-permute-start(bf16[512,768]{1,0:T(8,128)(2,1)} %get-tuple-element.148), channel_id=1, source_target_pairs={{0,4},{1,9},{2,6},{3,11},{4,0},{5,13},{6,2},{7,15},{8,12},{9,1},{1... | collective-permute-start | bytes 2359304 | tf_op jit(solution)/shard_map/ppermute | solution.py:769
  251.4 19.3 %copy-start.11 = (bf16[512,768]{1,0:T(8,128)(2,1)S(1)}, bf16[512,768]{1,0:T(8,128)(2,1)}, u32[]{:S(2)}) copy-start(bf16[512,768]{1,0:T(8,128)(2,1)} %get-tuple-element.138.refs_0_) | copy-start | bytes 2359300
  251.4 22.8 %copy-start.12 = (bf16[512,768]{1,0:T(8,128)(2,1)S(1)}, bf16[512,768]{1,0:T(8,128)(2,1)}, u32[]{:S(2)}) copy-start(bf16[512,768]{1,0:T(8,128)(2,1)} %get-tuple-element.140.refs_4_) | copy-start | bytes 2359300
  261.7 1.5 collective-permute-start.27
  261.7 3.8 %collective-permute-start.37 = (f32[6,512]{1,0:T(8,128)S(1)}, f32[6,512]{1,0:T(8,128)S(1)}, u32[]{:S(2)}, u32[]{:S(2)}) collective-permute-start(f32[6,512]{1,0:T(8,128)S(1)} %pad_maximum_fusion.1), channel_id=1, source_target_pairs={{0,4},{4,0},{8,12},{12,8},{16,20},{20,16},{24,28},{28,24},{1,5},{5... | collective-permute-start | bytes 36872 | tf_op jit(solution)/shard_map/ppermute | solution.py:862
  264.0 11.1 %collective-permute-start.28 = (f32[8,2048]{1,0:T(8,128)S(1)}, f32[8,2048]{1,0:T(8,128)S(1)}, u32[]{:S(2)}, u32[]{:S(2)}) collective-permute-start(f32[8,2048]{1,0:T(8,128)S(1)} %add.125), channel_id=1, source_target_pairs={{0,2},{1,3},{2,0},{3,1},{4,6},{5,7},{6,4},{7,5},{8,10},{9,11},{10,... | collective-permute-start | bytes 196616 | tf_op jit(solution)/shard_map/ppermute | solution.py:763
  265.5 3.8 %collective-permute-start.38 = (f32[6,512]{1,0:T(8,128)S(1)}, f32[6,512]{1,0:T(8,128)S(1)}, u32[]{:S(2)}, u32[]{:S(2)}) collective-permute-start(f32[6,512]{1,0:T(8,128)S(1)} %fusion), channel_id=1, source_target_pairs={{0,8},{4,12},{8,0},{12,4},{16,24},{20,28},{24,16},{28,20},{1,9},{5... | collective-permute-start | bytes 36872 | tf_op jit(solution)/shard_map/ppermute | solution.py:862
  269.3 4.9 %collective-permute-start.39 = (f32[6,512]{1,0:T(8,128)S(1)}, f32[6,512]{1,0:T(8,128)S(1)}, u32[]{:S(2)}, u32[]{:S(2)}) collective-permute-start(f32[6,512]{1,0:T(8,128)S(1)} %add.128), channel_id=1, source_target_pairs={{0,16},{4,20},{8,24},{12,28},{16,0},{20,4},{24,8},{28,12},{1,17},{... | collective-permute-start | bytes 36872 | tf_op jit(solution)/shard_map/ppermute | solution.py:862
  270.7 13.6 %collective-permute-start.29 = (bf16[512,768]{1,0:T(8,128)(2,1)S(1)}, bf16[512,768]{1,0:T(8,128)(2,1)S(1)}, u32[]{:S(2)}, u32[]{:S(2)}) collective-permute-start(bf16[512,768]{1,0:T(8,128)(2,1)S(1)} %copy-done.11), channel_id=1, source_target_pairs={{0,4},{1,9},{2,6},{3,11},{4,0},{5,13},{6,2},{7,15},{8,12},{9,1},{1... | collective-permute-start | bytes 2359304 | tf_op jit(solution)/shard_map/ppermute | solution.py:769
  271.4 12.9 %collective-permute-start.34 = (bf16[512,768]{1,0:T(8,128)(2,1)}, bf16[512,768]{1,0:T(8,128)(2,1)S(1)}, u32[]{:S(2)}, u32[]{:S(2)}) collective-permute-start(bf16[512,768]{1,0:T(8,128)(2,1)} %get-tuple-element.148), channel_id=1, source_target_pairs={{0,1},{1,0},{2,3},{3,2},{4,5},{5,4},{6,7},{7,6},{8,9},{9,8},{10,11... | collective-permute-start | bytes 2359304 | tf_op jit(solution)/shard_map/ppermute | solution.py:763
  274.2 17.0 %collective-permute-start.33 = (bf16[512,768]{1,0:T(8,128)(2,1)S(1)}, bf16[512,768]{1,0:T(8,128)(2,1)}, u32[]{:S(2)}, u32[]{:S(2)}) collective-permute-start(bf16[512,768]{1,0:T(8,128)(2,1)S(1)} %copy-done.12), channel_id=1, source_target_pairs={{0,4},{1,9},{2,6},{3,11},{4,0},{5,13},{6,2},{7,15},{8,12},{9,1},{1... | collective-permute-start | bytes 2359304 | tf_op jit(solution)/shard_map/ppermute | solution.py:769
  275.1 16.1 %collective-permute-start.32 = (bf16[512,768]{1,0:T(8,128)(2,1)}, bf16[512,768]{1,0:T(8,128)(2,1)}, u32[]{:S(2)}, u32[]{:S(2)}) collective-permute-start(bf16[512,768]{1,0:T(8,128)(2,1)} %collective-permute-done.31), channel_id=1, source_target_pairs={{0,1},{1,0},{2,3},{3,2},{4,5},{5,4},{6,7},{7,6},{8,9},{9,8},{10,11... | collective-permute-start | bytes 2359304 | tf_op jit(solution)/shard_map/ppermute | solution.py:763
  275.1 16.1 %collective-permute-start.36 = (bf16[512,768]{1,0:T(8,128)(2,1)}, bf16[512,768]{1,0:T(8,128)(2,1)}, u32[]{:S(2)}, u32[]{:S(2)}) collective-permute-start(bf16[512,768]{1,0:T(8,128)(2,1)} %collective-permute-done.35), channel_id=1, source_target_pairs={{0,1},{1,0},{2,3},{3,2},{4,5},{5,4},{6,7},{7,6},{8,9},{9,8},{10,11... | collective-permute-start | bytes 2359304 | tf_op jit(solution)/shard_map/ppermute | solution.py:763
  284.3 6.9 %copy-start.13 = (bf16[512,768]{1,0:T(8,128)(2,1)}, bf16[512,768]{1,0:T(8,128)(2,1)S(1)}, u32[]{:S(2)}) copy-start(bf16[512,768]{1,0:T(8,128)(2,1)S(1)} %collective-permute-done.29.refs_1_) | copy-start | bytes 2359300
  (17 other events, 53.9 us)

commit v6 on v5

--- a/solution.py
+++ b/solution.py
@@ -13,7 +13,7 @@
 LANES = 128
 VMEM_LIMIT = 60 * 1024 * 1024
 COVER = 20
-FIRST = 2
+FIRST = 3
 
 
 def call(kernel, meta, args, grid, in_specs, out_specs, out_shape, scratch=(), aliases=None, cost=None):
@@ -490,7 +490,7 @@
             pl.BlockSpec((8, channels), lambda t, m: (0, 0)),
         ],
         [struct((tokens, channels), F32), struct((8, tokens), F32), struct((8, channels), F32)],
-        cost=cost(20 * tokens * channels, 12 * tokens * channels),
+        cost=cost(20 * tokens * channels, 12 * tokens * channels, weight=COVER),
     )
 
 
@@ -824,10 +824,10 @@
     kept2 = first_keeps(after(meta, mine2), ds2)
     far_theirs = back(after(meta, kept2[0]), ds1, ds2, units, M_FAR)
     far_got = over_gate(far_theirs, 1)
-    away2, stay2 = halve(after(meta, far_theirs), M_BIT + 1, kept2, got2)
+    near1, far1 = gathered(after(meta, far_theirs), M_H1, False, stay1, step1)
+    away2, stay2 = halve(after(meta, near1), M_BIT + 1, kept2, got2)
     step2 = over_dp(away2, 1)
-    near1, far1 = gathered(after(meta, away2), M_H1, False, stay1, step1)
-    far_mine = back(after(meta, near1), ds1, ds2, units, M_FAR + 1)
+    far_mine = back(after(meta, away2), ds1, ds2, units, M_FAR + 1)
     for step in range(2, bits):
         away2, stay2 = halve(after(meta, far_mine), M_BIT + step, [stay2], [step2])
         step2 = over_dp(away2, step)
@@ -840,22 +840,25 @@
     theirs = back(after(meta, away2, *far_send), ds1, ds2, units, M_HERE)
     got = over_gate(theirs, 1)
     shard1 = jnp.concatenate([after(near1, theirs), far1], axis=2)
-    mine = back(after(meta, theirs, shard1), ds1, ds2, units, M_HERE + 1)
 
     def last_doubling(meta, shard):
         mine, theirs = join(meta, shard, over_dp(shard, 1))
         moved = over_dp(theirs, 0)
         return [mine, over_dp(mine, 0), over_gate(theirs, 1), over_gate(moved, 1)]
 
-    near2, far2 = gathered(after(meta, mine, far_part[0]), M_H2, True, stay2, step2)
-    shard1 = last_steps(shard1, near2)
-    shard2 = last_steps(jnp.concatenate([after(near2, shard1), far2], axis=2))
+    near2, far2 = gathered(after(meta, shard1, far_part[0]), M_H2, True, stay2, step2)
+    mine = back(after(meta, theirs, near2), ds1, ds2, units, M_HERE + 1)
+    shard2 = jnp.concatenate([after(near2, mine), far2], axis=2)
+    shard1 = last_steps(shard1, shard2)
     parts1 = last_doubling(after(meta, shard2), shard1)
-    parts2 = last_doubling(after(meta, parts1[0]), shard2)
-    dn, row_sums, col_sums = tail_sums(after(meta, parts2[0]), mine, got, far_part, own_x, mu, inv, ln_gain)
+    shard2 = last_steps(shard2, parts1[0])
+    parts2 = last_doubling(after(meta, far_part[1]), shard2)
+    dn, row_sums, col_sums = tail_sums(
+        after(meta, parts2[0], parts1[1]), mine, got, far_part, own_x, mu, inv, ln_gain
+    )
     for delta in (1, 2):
         row_sums = row_sums + over_gate(row_sums, delta)
-    dinputs = tail(after(meta, parts2[0]), dn, row_sums, own_x, mu, inv, ln_gain, direct, features)
+    dinputs = tail(after(meta, parts2[1], *parts1), dn, row_sums, own_x, mu, inv, ln_gain, direct, features)
 
     totals = jnp.concatenate([col_sums[:2], vecs[:4]], axis=0)
     for step in range(bits):

time: 301 us -> 309 us (1.027)
  waiting for transfers between devices: 55.6 us -> 65.3 us
  starting transfers between devices: 34.8 us -> 29.8 us
    ppermute x21, waiting for transfers between devices: 2.69 us -> 14 us  [over_gate(): return lax.ppermute(value, 'gate', [(g, g ^ delta) for g in range(n_gate)])]
    unnamed x53 -> x60, local copies, waits for them, and re-layouts: 8.84 us -> 10.7 us
  transfers between devices with their start and end apart: 40 -> 40, of which waited for: 13 -> 13; matrix products, arithmetic and copies ran while one was open for 4% -> 3% of each run, Pallas kernels for 56% -> 55%
where the time goes in v6:
time: 309 us; the launch traced here: 308 us
  Pallas kernels  190 us (61%)
  waiting for transfers between devices  65.3 us (21%)
  starting transfers between devices  29.8 us (10%)
  local copies, waits for them, and re-layouts  15.2 us (5%)
  other arithmetic  6.46 us (2%)
    pallas_call x26, Pallas kernels, call(): pl.pallas_call(kernel, grid_spec=pltpu.PrefetchScalarGridSpec(num_scalar_...  190 us
    ppermute x16, waiting for transfers between devices, over_dp(): return lax.ppermute(value, ('dp', 'gate'), pairs)  44 us
    ppermute x16, starting transfers between devices, over_dp(): return lax.ppermute(value, ('dp', 'gate'), pairs)  17.1 us
    ppermute x21, waiting for transfers between devices, over_gate(): return lax.ppermute(value, 'gate', [(g, g ^ delta) for g in range(n_gate)])  14 us
    ppermute x21, starting transfers between devices, over_gate(): return lax.ppermute(value, 'gate', [(g, g ^ delta) for g in range(n_gate)])  11.4 us
    unnamed x60, local copies, waits for them, and re-layouts  10.7 us
    ppermute x3, waiting for transfers between devices, shards(): lax.ppermute(totals, 'dp', [(d, d ^ 1 << step) for d in range(n_dp)])  7.38 us
  transfers between devices with their start and end apart: 40, of which 13 were waited for; matrix products, arithmetic and copies ran while one was open for 3% of the time, Pallas kernels for 55%

profile of v6, /device:TPU:0, one launch (start us, length us, event | category | flops | bytes accessed | tf_op | source)
XLA Modules:
  0.0 307.7 jit_solution(16317578446977890493)
XLA Ops:
  1.3 4.8 %shard_map.178 = (bf16[2048,128]{1,0:T(8,128)(2,1)}, bf16[2048,128]{1,0:T(8,128)(2,1)}, bf16[2048,384]{1,0:T(8,128)(2,1)}) custom-call(s32[36]{0:T(128)} %stack.147.meta, bf16[2048,1536]{1,0:T(8,128)(2,1)} %refs_10_.7, bf16[2048,1536]{1,0:T(8,128)(2,1)} %refs_10_.7, bf16[2048,1536]{1,0:T(8,128)(2,1)} %refs_10_.7, bf16[2048,1536]{1,0:T(8,128)(2,1)} %refs_10_.7, ...), custom_call_target="tpu_custom_call" | custom-call | bytes 5242880 | tf_op jit(solution)/shard_map/pallas_call | solution.py:20
  6.6 2.6 collective-permute-start.1
  9.3 14.8 %shard_map.179 = (bf16[2048,2048]{1,0:T(8,128)(2,1)}, f32[2048,128]{1,0:T(8,128)}, f32[2048,128]{1,0:T(8,128)}, bf16[2048,512]{1,0:T(8,128)(2,1)}, f32[2048,128]{1,0:T(8,128)}, /*index=5*/f32[2048,128]{1,0:T(8,128)}) custom-call(s32[36]{0:T(128)} %stack.147.meta, bf16[2048,2048]{1,0:T(8,128)(2,1)} %bitcast.50, f32[1,2048]{1,0:T(1,128)} %bitcast.55, ...), custom_call_target="tpu_custom_call" | custom-call | flops 671088640 | bytes 335544320 | tf_op jit(solution)/shard_map/pallas_call | solution.py:20
  24.2 4.8 %shard_map.180 = (bf16[2048,256]{1,0:T(8,128)(2,1)}, bf16[2048,256]{1,0:T(8,128)(2,1)}) custom-call(s32[36]{0:T(128)} %stack.147.meta, bf16[2048,1536]{1,0:T(8,128)(2,1)} %refs_10_.7, bf16[2048,1536]{1,0:T(8,128)(2,1)} %refs_10_.7, bf16[2048,1536]{1,0:T(8,128)(2,1)} %refs_10_.7, bf16[2048,1536]{1,0:T(8,128)(2,1)} %refs_10_.7), custom_call_target="tpu_custom_call" | custom-call | bytes 4194304 | tf_op jit(solution)/shard_map/pallas_call | solution.py:20
  29.0 1.7 collective-permute-start.3
  31.4 1.7 collective-permute-done.2.refs_5_
  35.1 11.9 %shard_map.181.u_ref = bf16[2048,768]{1,0:T(8,128)(2,1)} custom-call(s32[36]{0:T(128)} %stack.147.meta, bf16[2048,2048]{1,0:T(8,128)(2,1)} %get-tuple-element.85.normed_ref, bf16[2048,1536]{1,0:T(8,128)(2,1)} %refs_10_.7, bf16[2048,1536]{1,0:T(8,128)(2,1)} %refs_10_.7, bf16[2048,384]{1,0:T(8,128)(2,1)} %copy-done.25, bf16[2048,384]{1,0:T(8,128)(2,1)} %copy-done.25, ...), custom_call_target="tpu_custom_call" | custom-call | flops 128849018880 | bytes 293601280 | tf_op jit(solution)/shard_map/pallas_call | solution.py:20
  47.0 12.4 %shard_map.182 = (bf16[2048,512]{1,0:T(8,128)(2,1)}, bf16[2048,768]{1,0:T(8,128)(2,1)}, bf16[2048,512]{1,0:T(8,128)(2,1)}, f32[8,512]{1,0:T(8,128)}) custom-call(s32[36]{0:T(128)} %stack.147.meta, bf16[2048,768]{1,0:T(8,128)(2,1)} %shard_map.181.u_ref, bf16[2048,512]{1,0:T(8,128)(2,1)} %get-tuple-element.91.x_ref, bf16[2048,512]{1,0:T(8,128)(2,1)} %bitcast.51, ...), custom_call_target="tpu_custom_call" | custom-call | flops 629145600 | bytes 188743680 | tf_op jit(solution)/shard_map/pallas_call | solution.py:20
  59.4 8.2 %shard_map.183 = (bf16[512,768]{1,0:T(8,128)(2,1)}, bf16[512,768]{1,0:T(8,128)(2,1)}) custom-call(s32[36]{0:T(128)} %stack.147.meta, bf16[2048,2048]{1,0:T(8,128)(2,1)} %get-tuple-element.85.normed_ref, bf16[2048,768]{1,0:T(8,128)(2,1)} %get-tuple-element.94.ds_ref.ds1_ref), custom_call_target="tpu_custom_call" | custom-call | flops 64424509440 | bytes 146800640 | tf_op jit(solution)/shard_map/pallas_call | solution.py:20
  67.6 1.5 collective-permute-start.6
  69.6 8.1 %shard_map.184 = (bf16[512,768]{1,0:T(8,128)(2,1)}, bf16[512,768]{1,0:T(8,128)(2,1)}) custom-call(s32[36]{0:T(128)} %stack.147.meta, bf16[2048,2048]{1,0:T(8,128)(2,1)} %get-tuple-element.85.normed_ref, bf16[2048,768]{1,0:T(8,128)(2,1)} %get-tuple-element.94.ds_ref.ds1_ref), custom_call_target="tpu_custom_call" | custom-call | flops 64424509440 | bytes 146800640 | tf_op jit(solution)/shard_map/pallas_call | solution.py:20
  77.7 1.5 collective-permute-start.8
  79.3 12.1 %shard_map.185.u_ref = bf16[2048,768]{1,0:T(8,128)(2,1)} custom-call(s32[36]{0:T(128)} %stack.147.meta, bf16[2048,2048]{1,0:T(8,128)(2,1)} %get-tuple-element.85.normed_ref, bf16[2048,256]{1,0:T(8,128)(2,1)} %collective-permute-done.3.refs_0_.refs_1_.refs_6_.refs_7_, bf16[2048,256]{1,0:T(8,128)(2,1)} %collective-permute-done.3.refs_0_.refs_1_.refs_6_.refs_7_, ...), custom_call_target="tpu_custom_call" | custom-call | flops 128849018880 | bytes 293601280 | tf_op jit(solution)/shard_map/pallas_call | solution.py:20
  93.2 3.7 %shard_map.186 = (bf16[2,256,768]{2,1,0:T(8,128)(2,1)}, bf16[2,256,768]{2,1,0:T(8,128)(2,1)}) custom-call(s32[36]{0:T(128)} %stack.147.meta, bf16[512,768]{1,0:T(8,128)(2,1)} %get-tuple-element.97.refs_0_.refs_4_, bf16[512,768]{1,0:T(8,128)(2,1)} %copy-done.3, bf16[512,768]{1,0:T(8,128)(2,1)} %collective-permute-done.6.refs_2_.refs_6_, ...), custom_call_target="tpu_custom_call" | custom-call | flops 1572864 | bytes 4718592 | tf_op jit(solution)/shard_map/pallas_call | solution.py:20
  97.5 12.4 %shard_map.187 = (bf16[2048,512]{1,0:T(8,128)(2,1)}, bf16[2048,768]{1,0:T(8,128)(2,1)}, bf16[2048,512]{1,0:T(8,128)(2,1)}, f32[8,512]{1,0:T(8,128)}) custom-call(s32[36]{0:T(128)} %stack.147.meta, bf16[2048,768]{1,0:T(8,128)(2,1)} %shard_map.185.u_ref, ...), custom_call_target="tpu_custom_call", output_to_operand_aliasing={{0}: (7, {}), {2}: (8, {}), {3}: (9, {})} | custom-call | flops 629145600 | bytes 188743680 | tf_op jit(solution)/shard_map/pallas_call | solution.py:20
  110.8 3.1 shard_map.188
  113.9 2.6 collective-permute-start.10
  116.5 8.1 %shard_map.189 = (bf16[512,768]{1,0:T(8,128)(2,1)}, bf16[512,768]{1,0:T(8,128)(2,1)}) custom-call(s32[36]{0:T(128)} %stack.147.meta, bf16[2048,2048]{1,0:T(8,128)(2,1)} %get-tuple-element.85.normed_ref, bf16[2048,768]{1,0:T(8,128)(2,1)} %get-tuple-element.108.ds_ref.ds2_ref), custom_call_target="tpu_custom_call" | custom-call | flops 64424509440 | bytes 146800640 | tf_op jit(solution)/shard_map/pallas_call | solution.py:20
  124.6 1.5 collective-permute-start.12
  126.1 8.2 %shard_map.190 = (bf16[512,768]{1,0:T(8,128)(2,1)}, bf16[512,768]{1,0:T(8,128)(2,1)}) custom-call(s32[36]{0:T(128)} %stack.147.meta, bf16[2048,2048]{1,0:T(8,128)(2,1)} %get-tuple-element.85.normed_ref, bf16[2048,768]{1,0:T(8,128)(2,1)} %get-tuple-element.108.ds_ref.ds2_ref), custom_call_target="tpu_custom_call" | custom-call | flops 64424509440 | bytes 146800640 | tf_op jit(solution)/shard_map/pallas_call | solution.py:20
  135.3 8.0 %shard_map.191 = bf16[2048,512]{1,0:T(8,128)(2,1)} custom-call(s32[36]{0:T(128)} %stack.147.meta, bf16[2048,768]{1,0:T(8,128)(2,1)} %get-tuple-element.94.ds_ref.ds1_ref, bf16[2048,768]{1,0:T(8,128)(2,1)} %get-tuple-element.108.ds_ref.ds2_ref, bf16[2048,1536]{1,0:T(8,128)(2,1)} %refs_10_.7, bf16[2048,1536]{1,0:T(8,128)(2,1)} %refs_10_.7, ...), custom_call_target="tpu_custom_call" | custom-call | flops 64424509440 | bytes 125829120 | tf_op jit(solution)/shard_map/pallas_call | solution.py:20
  143.4 2.6 shard_map.192
  146.0 1.4 collective-permute-start.18
  149.5 3.7 %shard_map.193 = (bf16[2,256,768]{2,1,0:T(8,128)(2,1)}, bf16[2,256,768]{2,1,0:T(8,128)(2,1)}) custom-call(s32[36]{0:T(128)} %stack.147.meta, bf16[512,768]{1,0:T(8,128)(2,1)} %get-tuple-element.115.refs_0_.refs_4_, bf16[512,768]{1,0:T(8,128)(2,1)} %copy-done.1, bf16[512,768]{1,0:T(8,128)(2,1)} %copy-done, bf16[512,768]{1,0:T(8,128)(2,1)} %copy-done.2, ...), custom_call_target="tpu_custom_call" | custom-call | flops 1572864 | bytes 4718592 | tf_op jit(solution)/shard_map/pallas_call | solution.py:20
  153.2 1.6 collective-permute-start.15
  154.8 8.3 %shard_map.194 = bf16[2048,512]{1,0:T(8,128)(2,1)} custom-call(s32[36]{0:T(128)} %stack.147.meta, bf16[2048,768]{1,0:T(8,128)(2,1)} %get-tuple-element.94.ds_ref.ds1_ref, bf16[2048,768]{1,0:T(8,128)(2,1)} %get-tuple-element.108.ds_ref.ds2_ref, bf16[2048,1536]{1,0:T(8,128)(2,1)} %refs_10_.7, bf16[2048,1536]{1,0:T(8,128)(2,1)} %refs_10_.7, ...), custom_call_target="tpu_custom_call" | custom-call | flops 64424509440 | bytes 125829120 | tf_op jit(solution)/shard_map/pallas_call | solution.py:20
  163.0 2.4 collective-permute-done.15.refs_1_.refs_3_
  166.3 3.0 shard_map.195
  169.7 2.2 add_convert_fusion.1
  172.5 2.7 add_convert_fusion
  175.3 8.2 %shard_map.196 = bf16[2048,512]{1,0:T(8,128)(2,1)} custom-call(s32[36]{0:T(128)} %stack.147.meta, bf16[2048,768]{1,0:T(8,128)(2,1)} %get-tuple-element.94.ds_ref.ds1_ref, bf16[2048,768]{1,0:T(8,128)(2,1)} %get-tuple-element.108.ds_ref.ds2_ref, bf16[2048,1536]{1,0:T(8,128)(2,1)} %refs_10_.7, bf16[2048,1536]{1,0:T(8,128)(2,1)} %refs_10_.7, ...), custom_call_target="tpu_custom_call" | custom-call | flops 64424509440 | bytes 125829120 | tf_op jit(solution)/shard_map/pallas_call | solution.py:20
  184.4 2.7 collective-permute-start.22
  187.0 5.0 %collective-permute-done.19.r1_ref = bf16[768,512]{1,0:T(8,128)(2,1)S(1)} collective-permute-done((bf16[768,512]{1,0:T(8,128)(2,1)}, bf16[768,512]{1,0:T(8,128)(2,1)S(1)}, u32[]{:S(2)}, u32[]{:S(2)}) %collective-permute-start.19) | collective-permute-done | bytes 786464 | tf_op jit(solution)/shard_map/ppermute | solution.py:763
  192.0 6.9 %collective-permute-done.20.b_ref = bf16[2,128,768]{2,1,0:T(8,128)(2,1)S(1)} collective-permute-done((bf16[2,128,768]{2,1,0:T(8,128)(2,1)}, bf16[2,128,768]{2,1,0:T(8,128)(2,1)S(1)}, u32[]{:S(2)}, u32[]{:S(2)}) %collective-permute-start.20) | collective-permute-done | bytes 393248 | tf_op jit(solution)/shard_map/ppermute | solution.py:769
  199.7 2.6 shard_map.197
  202.3 8.2 %shard_map.198.k_ref = bf16[2048,512]{1,0:T(8,128)(2,1)} custom-call(s32[36]{0:T(128)} %stack.147.meta, bf16[2048,768]{1,0:T(8,128)(2,1)} %get-tuple-element.94.ds_ref.ds1_ref, bf16[2048,768]{1,0:T(8,128)(2,1)} %get-tuple-element.108.ds_ref.ds2_ref, bf16[2048,1536]{1,0:T(8,128)(2,1)} %refs_10_.7, bf16[2048,1536]{1,0:T(8,128)(2,1)} %refs_10_.7, ...), custom_call_target="tpu_custom_call" | custom-call | flops 64424509440 | bytes 125829120 | tf_op jit(solution)/shard_map/pallas_call | solution.py:20
  213.3 16.8 %collective-permute-done.23.b_ref = bf16[2,256,768]{2,1,0:T(8,128)(2,1)S(1)} collective-permute-done((bf16[2,256,768]{2,1,0:T(8,128)(2,1)S(1)}, bf16[2,256,768]{2,1,0:T(8,128)(2,1)S(1)}, u32[]{:S(2)}, u32[]{:S(2)}) %collective-permute-start.23) | collective-permute-done | bytes 786464 | tf_op jit(solution)/shard_map/ppermute | solution.py:769
  230.9 3.3 %shard_map.199 = (bf16[512,768]{1,0:T(8,128)(2,1)}, bf16[512,768]{1,0:T(8,128)(2,1)}) custom-call(s32[36]{0:T(128)} %stack.147.meta, bf16[2,256,768]{2,1,0:T(8,128)(2,1)} %copy-done.9, bf16[2,256,768]{2,1,0:T(8,128)(2,1)} %copy-done.16), custom_call_target="tpu_custom_call" | custom-call | bytes 3145728 | tf_op jit(solution)/shard_map/pallas_call | solution.py:20
  237.5 6.1 %collective-permute-done.17.r2_ref = bf16[1280,512]{1,0:T(8,128)(2,1)} collective-permute-done((bf16[1280,512]{1,0:T(8,128)(2,1)}, bf16[1280,512]{1,0:T(8,128)(2,1)}, u32[]{:S(2)}, u32[]{:S(2)}) %collective-permute-start.17) | collective-permute-done | bytes 1310752 | tf_op jit(solution)/shard_map/ppermute | solution.py:763
  243.6 12.3 %collective-permute-done.25.b_ref = bf16[2,256,768]{2,1,0:T(8,128)(2,1)} collective-permute-done((bf16[2,256,768]{2,1,0:T(8,128)(2,1)S(1)}, bf16[2,256,768]{2,1,0:T(8,128)(2,1)}, u32[]{:S(2)}, u32[]{:S(2)}) %collective-permute-start.25) | collective-permute-done | bytes 786464 | tf_op jit(solution)/shard_map/ppermute | solution.py:769
  256.0 3.2 %shard_map.200 = (bf16[512,768]{1,0:T(8,128)(2,1)}, bf16[512,768]{1,0:T(8,128)(2,1)}) custom-call(s32[36]{0:T(128)} %stack.147.meta, bf16[2,256,768]{2,1,0:T(8,128)(2,1)} %copy-done.10, bf16[2,256,768]{2,1,0:T(8,128)(2,1)} %collective-permute-done.25.b_ref), custom_call_target="tpu_custom_call" | custom-call | bytes 3145728 | tf_op jit(solution)/shard_map/pallas_call | solution.py:20
  260.0 1.3 copy-done.8
  261.4 9.8 %shard_map.201 = (f32[2048,512]{1,0:T(8,128)}, f32[8,2048]{1,0:T(8,128)}, f32[8,512]{1,0:T(8,128)}) custom-call(s32[36]{0:T(128)} %stack.147.meta, bf16[2048,512]{1,0:T(8,128)(2,1)} %shard_map.198.k_ref, bf16[2048,512]{1,0:T(8,128)(2,1)} %copy-done.8, bf16[768,512]{1,0:T(8,128)(2,1)} %copy-done.15, bf16[1280,512]{1,0:T(8,128)(2,1)} %collective-permute-done.17.r2_ref, ...), custom_call_target="tpu_custom_call" | custom-call | flops 419430400 | bytes 251658240 | tf_op jit(solution)/shard_map/pallas_call | solution.py:20
  275.8 3.7 %collective-permute-done.38 = f32[6,512]{1,0:T(8,128)S(1)} collective-permute-done((f32[6,512]{1,0:T(8,128)S(1)}, f32[6,512]{1,0:T(8,128)S(1)}, u32[]{:S(2)}, u32[]{:S(2)}) %collective-permute-start.38) | collective-permute-done | bytes 12320 | tf_op jit(solution)/shard_map/ppermute | solution.py:865
  280.9 3.4 %collective-permute-done.39 = f32[6,512]{1,0:T(8,128)S(1)} collective-permute-done((f32[6,512]{1,0:T(8,128)S(1)}, f32[6,512]{1,0:T(8,128)S(1)}, u32[]{:S(2)}, u32[]{:S(2)}) %collective-permute-start.39) | collective-permute-done | bytes 12320 | tf_op jit(solution)/shard_map/ppermute | solution.py:865
  286.1 5.6 %collective-permute-done.26.refs_5_ = bf16[512,768]{1,0:T(8,128)(2,1)S(1)} collective-permute-done((bf16[512,768]{1,0:T(8,128)(2,1)S(1)}, bf16[512,768]{1,0:T(8,128)(2,1)S(1)}, u32[]{:S(2)}, u32[]{:S(2)}) %collective-permute-start.26) | collective-permute-done | bytes 786464 | tf_op jit(solution)/shard_map/ppermute | solution.py:769
  291.7 7.4 %shard_map.202 = bf16[2048,512]{1,0:T(8,128)(2,1)} custom-call(s32[36]{0:T(128)} %stack.147.meta, f32[2048,512]{1,0:T(8,128)} %get-tuple-element.149.dn_ref, f32[8,2048]{1,0:T(8,128)} %add.126.row_ref, bf16[2048,512]{1,0:T(8,128)(2,1)} %get-tuple-element.91.x_ref, f32[2048,128]{1,0:T(8,128)} %get-tuple-element.147.mu_ref, ...), custom_call_target="tpu_custom_call" | custom-call | flops 10485760 | bytes 12582912 | tf_op jit(solution)/shard_map/pallas_call | solution.py:20
  299.2 8.5 %shard_map.203 = f32[2048,1536]{1,0:T(8,128)} custom-call(s32[36]{0:T(128)} %stack.147.meta, bf16[512,768]{1,0:T(8,128)(2,1)} %get-tuple-element.141.refs_0_, bf16[512,768]{1,0:T(8,128)(2,1)} %copy-done.11, bf16[512,768]{1,0:T(8,128)(2,1)} %copy-done.13, bf16[512,768]{1,0:T(8,128)(2,1)} %collective-permute-done.30.refs_3_, ...), custom_call_target="tpu_custom_call" | custom-call | flops 3145728 | bytes 18874368 | tf_op jit(solution)/shard_map/pallas_call | solution.py:20
  (136 shorter events, 29.7 us)
Async XLA Ops:
  6.2 26.9 %collective-permute-start = (bf16[2048,384]{1,0:T(8,128)(2,1)}, bf16[2048,384]{1,0:T(8,128)(2,1)S(1)}, u32[]{:S(2)}, u32[]{:S(2)}) collective-permute-start(bf16[2048,384]{1,0:T(8,128)(2,1)} %get-tuple-element.90), channel_id=1, source_target_pairs={{0,1},{1,0},{2,3},{3,2},{4,5},{5,4},{6,7},{7,6},{8,9},{9,8},{10,11... | collective-permute-start | bytes 4718600 | tf_op jit(solution)/shard_map/ppermute | solution.py:763
  6.6 24.7 %collective-permute-start.1 = (bf16[2048,128]{1,0:T(8,128)(2,1)}, bf16[2048,128]{1,0:T(8,128)(2,1)S(1)}, u32[]{:S(2)}, u32[]{:S(2)}) collective-permute-start(bf16[2048,128]{1,0:T(8,128)(2,1)} %get-tuple-element.82), channel_id=1, source_target_pairs={{0,2},{1,3},{2,0},{3,1},{4,6},{5,7},{6,4},{7,5},{8,10},{9,11},{10,... | collective-permute-start | bytes 1572872 | tf_op jit(solution)/shard_map/ppermute | solution.py:763
  9.2 23.9 %collective-permute-start.2 = (bf16[2048,128]{1,0:T(8,128)(2,1)}, bf16[2048,128]{1,0:T(8,128)(2,1)S(1)}, u32[]{:S(2)}, u32[]{:S(2)}) collective-permute-start(bf16[2048,128]{1,0:T(8,128)(2,1)} %get-tuple-element.83), channel_id=1, source_target_pairs={{0,3},{1,2},{2,1},{3,0},{4,7},{5,6},{6,5},{7,4},{8,11},{9,10},{10,... | collective-permute-start | bytes 1572872 | tf_op jit(solution)/shard_map/ppermute | solution.py:763
  29.0 50.3 %collective-permute-start.3 = (bf16[2048,256]{1,0:T(8,128)(2,1)}, bf16[2048,256]{1,0:T(8,128)(2,1)}, u32[]{:S(2)}, u32[]{:S(2)}) collective-permute-start(bf16[2048,256]{1,0:T(8,128)(2,1)} %get-tuple-element.87), channel_id=1, source_target_pairs={{0,2},{1,3},{2,0},{3,1},{4,6},{5,7},{6,4},{7,5},{8,10},{9,11},{10,... | collective-permute-start | bytes 3145736 | tf_op jit(solution)/shard_map/ppermute | solution.py:763
  30.7 48.6 %collective-permute-start.4 = (bf16[2048,256]{1,0:T(8,128)(2,1)}, bf16[2048,256]{1,0:T(8,128)(2,1)}, u32[]{:S(2)}, u32[]{:S(2)}) collective-permute-start(bf16[2048,256]{1,0:T(8,128)(2,1)} %get-tuple-element.88), channel_id=1, source_target_pairs={{0,3},{1,2},{2,1},{3,0},{4,7},{5,6},{6,5},{7,4},{8,11},{9,10},{10,... | collective-permute-start | bytes 3145736 | tf_op jit(solution)/shard_map/ppermute | solution.py:763
  67.6 23.8 %collective-permute-start.6 = (bf16[512,768]{1,0:T(8,128)(2,1)}, bf16[512,768]{1,0:T(8,128)(2,1)}, u32[]{:S(2)}, u32[]{:S(2)}) collective-permute-start(bf16[512,768]{1,0:T(8,128)(2,1)} %get-tuple-element.95), channel_id=1, source_target_pairs={{0,4},{1,9},{2,6},{3,11},{4,0},{5,13},{6,2},{7,15},{8,12},{9,1},{1... | collective-permute-start | bytes 2359304 | tf_op jit(solution)/shard_map/ppermute | solution.py:769
  69.1 8.6 %collective-permute-start.7 = (bf16[512,768]{1,0:T(8,128)(2,1)}, bf16[512,768]{1,0:T(8,128)(2,1)S(1)}, u32[]{:S(2)}, u32[]{:S(2)}) collective-permute-start(bf16[512,768]{1,0:T(8,128)(2,1)} %get-tuple-element.101), channel_id=1, source_target_pairs={{0,1},{1,0},{2,3},{3,2},{4,5},{5,4},{6,7},{7,6},{8,9},{9,8},{10,11... | collective-permute-start | bytes 2359304 | tf_op jit(solution)/shard_map/ppermute | solution.py:763
  77.7 13.7 %collective-permute-start.5 = (bf16[512,768]{1,0:T(8,128)(2,1)}, bf16[512,768]{1,0:T(8,128)(2,1)S(1)}, u32[]{:S(2)}, u32[]{:S(2)}) collective-permute-start(bf16[512,768]{1,0:T(8,128)(2,1)} %get-tuple-element.100), channel_id=1, source_target_pairs={{0,1},{1,0},{2,3},{3,2},{4,5},{5,4},{6,7},{7,6},{8,9},{9,8},{10,11... | collective-permute-start | bytes 2359304 | tf_op jit(solution)/shard_map/ppermute | solution.py:763
  77.7 13.7 %collective-permute-start.8 = (bf16[512,768]{1,0:T(8,128)(2,1)S(1)}, bf16[512,768]{1,0:T(8,128)(2,1)S(1)}, u32[]{:S(2)}, u32[]{:S(2)}) collective-permute-start(bf16[512,768]{1,0:T(8,128)(2,1)S(1)} %collective-permute-done.7), channel_id=1, source_target_pairs={{0,4},{1,9},{2,6},{3,11},{4,0},{5,13},{6,2},{7,15},{8,12},{9,1},{1... | collective-permute-start | bytes 2359304 | tf_op jit(solution)/shard_map/ppermute | solution.py:769
  96.9 13.0 %collective-permute-start.9 = (bf16[2,256,768]{2,1,0:T(8,128)(2,1)}, bf16[2,256,768]{2,1,0:T(8,128)(2,1)S(1)}, u32[]{:S(2)}, u32[]{:S(2)}) collective-permute-start(bf16[2,256,768]{2,1,0:T(8,128)(2,1)} %get-tuple-element.102), channel_id=1, source_target_pairs={{0,8},{1,5},{2,10},{3,7},{4,12},{5,1},{6,14},{7,3},{8,0},{9,13},{1... | collective-permute-start | bytes 2359304 | tf_op jit(solution)/shard_map/ppermute | solution.py:769
  113.9 29.5 %collective-permute-start.10 = (bf16[2,128,768]{2,1,0:T(8,128)(2,1)}, bf16[2,128,768]{2,1,0:T(8,128)(2,1)}, u32[]{:S(2)}, u32[]{:S(2)}) collective-permute-start(bf16[2,128,768]{2,1,0:T(8,128)(2,1)} %get-tuple-element.111), channel_id=1, source_target_pairs={{0,16},{1,17},{2,18},{3,19},{4,20},{5,21},{6,22},{7,23},{8,24},{9,... | collective-permute-start | bytes 1179656 | tf_op jit(solution)/shard_map/ppermute | solution.py:769
  124.6 22.8 %collective-permute-start.12 = (bf16[512,768]{1,0:T(8,128)(2,1)}, bf16[512,768]{1,0:T(8,128)(2,1)S(1)}, u32[]{:S(2)}, u32[]{:S(2)}) collective-permute-start(bf16[512,768]{1,0:T(8,128)(2,1)} %get-tuple-element.113), channel_id=1, source_target_pairs={{0,4},{1,9},{2,6},{3,11},{4,0},{5,13},{6,2},{7,15},{8,12},{9,1},{1... | collective-permute-start | bytes 2359304 | tf_op jit(solution)/shard_map/ppermute | solution.py:769
  126.1 8.7 %collective-permute-start.13 = (bf16[512,768]{1,0:T(8,128)(2,1)}, bf16[512,768]{1,0:T(8,128)(2,1)S(1)}, u32[]{:S(2)}, u32[]{:S(2)}) collective-permute-start(bf16[512,768]{1,0:T(8,128)(2,1)} %get-tuple-element.122), channel_id=1, source_target_pairs={{0,1},{1,0},{2,3},{3,2},{4,5},{5,4},{6,7},{7,6},{8,9},{9,8},{10,11... | collective-permute-start | bytes 2359304 | tf_op jit(solution)/shard_map/ppermute | solution.py:763
  134.3 13.1 %collective-permute-start.11 = (bf16[512,768]{1,0:T(8,128)(2,1)}, bf16[512,768]{1,0:T(8,128)(2,1)S(1)}, u32[]{:S(2)}, u32[]{:S(2)}) collective-permute-start(bf16[512,768]{1,0:T(8,128)(2,1)} %get-tuple-element.121), channel_id=1, source_target_pairs={{0,1},{1,0},{2,3},{3,2},{4,5},{5,4},{6,7},{7,6},{8,9},{9,8},{10,11... | collective-permute-start | bytes 2359304 | tf_op jit(solution)/shard_map/ppermute | solution.py:763
  134.8 12.6 %collective-permute-start.14 = (bf16[512,768]{1,0:T(8,128)(2,1)S(1)}, bf16[512,768]{1,0:T(8,128)(2,1)S(1)}, u32[]{:S(2)}, u32[]{:S(2)}) collective-permute-start(bf16[512,768]{1,0:T(8,128)(2,1)S(1)} %collective-permute-done.13), channel_id=1, source_target_pairs={{0,4},{1,9},{2,6},{3,11},{4,0},{5,13},{6,2},{7,15},{8,12},{9,1},{1... | collective-permute-start | bytes 2359304 | tf_op jit(solution)/shard_map/ppermute | solution.py:769
  143.3 26.3 %collective-permute-start.16 = (bf16[2048,512]{1,0:T(8,128)(2,1)}, bf16[2048,512]{1,0:T(8,128)(2,1)}, u32[]{:S(2)}, u32[]{:S(2)}) collective-permute-start(bf16[2048,512]{1,0:T(8,128)(2,1)} %shard_map.191), channel_id=1, source_target_pairs={{0,1},{1,0},{2,3},{3,2},{4,5},{5,4},{6,7},{7,6},{8,9},{9,8},{10,11... | collective-permute-start | bytes 6291464 | tf_op jit(solution)/shard_map/ppermute | solution.py:763
  146.0 37.5 %collective-permute-start.18 = (bf16[2,128,256]{2,1,0:T(8,128)(2,1)}, bf16[2,128,256]{2,1,0:T(8,128)(2,1)}, u32[]{:S(2)}, u32[]{:S(2)}) collective-permute-start(bf16[2,128,256]{2,1,0:T(8,128)(2,1)} %get-tuple-element.132), channel_id=1, source_target_pairs={{0,2},{1,3},{2,0},{3,1},{4,6},{5,7},{6,4},{7,5},{8,10},{9,11},{10,... | collective-permute-start | bytes 393224 | tf_op jit(solution)/shard_map/ppermute | solution.py:763
  153.2 12.2 %collective-permute-start.15 = (bf16[2,256,768]{2,1,0:T(8,128)(2,1)}, bf16[2,256,768]{2,1,0:T(8,128)(2,1)S(1)}, u32[]{:S(2)}, u32[]{:S(2)}) collective-permute-start(bf16[2,256,768]{2,1,0:T(8,128)(2,1)} %get-tuple-element.123), channel_id=1, source_target_pairs={{0,8},{1,5},{2,10},{3,7},{4,12},{5,1},{6,14},{7,3},{8,0},{9,13},{1... | collective-permute-start | bytes 2359304 | tf_op jit(solution)/shard_map/ppermute | solution.py:769
  169.3 29.6 %collective-permute-start.20 = (bf16[2,128,768]{2,1,0:T(8,128)(2,1)}, bf16[2,128,768]{2,1,0:T(8,128)(2,1)S(1)}, u32[]{:S(2)}, u32[]{:S(2)}) collective-permute-start(bf16[2,128,768]{2,1,0:T(8,128)(2,1)} %get-tuple-element.127), channel_id=1, source_target_pairs={{0,16},{1,17},{2,18},{3,19},{4,20},{5,21},{6,22},{7,23},{8,24},{9,... | collective-permute-start | bytes 1179656 | tf_op jit(solution)/shard_map/ppermute | solution.py:769
  171.9 20.1 %collective-permute-start.19 = (bf16[768,512]{1,0:T(8,128)(2,1)}, bf16[768,512]{1,0:T(8,128)(2,1)S(1)}, u32[]{:S(2)}, u32[]{:S(2)}) collective-permute-start(bf16[768,512]{1,0:T(8,128)(2,1)} %add_convert_fusion.1), channel_id=1, source_target_pairs={{0,2},{1,3},{2,0},{3,1},{4,6},{5,7},{6,4},{7,5},{8,10},{9,11},{10,... | collective-permute-start | bytes 2359304 | tf_op jit(solution)/shard_map/ppermute | solution.py:763
  184.4 27.2 %collective-permute-start.22 = (bf16[2,128,768]{2,1,0:T(8,128)(2,1)S(1)}, bf16[2,128,768]{2,1,0:T(8,128)(2,1)S(1)}, u32[]{:S(2)}, u32[]{:S(2)}) collective-permute-start(bf16[2,128,768]{2,1,0:T(8,128)(2,1)S(1)} %constant_dynamic-update-slice_fusion), channel_id=1, source_target_pairs={{0,16},{1,17},{2,18},{3,19},{4,20},{5,21},{6,22},{7,23},{8,24},{9,... | collective-permute-start | bytes 1179656 | tf_op jit(solution)/shard_map/ppermute | solution.py:769
  192.0 18.5 %copy-start.15 = (bf16[768,512]{1,0:T(8,128)(2,1)}, bf16[768,512]{1,0:T(8,128)(2,1)S(1)}, u32[]{:S(2)}) copy-start(bf16[768,512]{1,0:T(8,128)(2,1)S(1)} %collective-permute-done.19.r1_ref) | copy-start | bytes 2359300
  202.3 8.2 %copy-start.19 = (bf16[2,128,256]{2,1,0:T(8,128)(2,1)S(1)}, bf16[2,128,256]{2,1,0:T(8,128)(2,1)}, u32[]{:S(2)}) copy-start(bf16[2,128,256]{2,1,0:T(8,128)(2,1)} %get-tuple-element.137) | copy-start | bytes 393220
  202.3 9.2 %collective-permute-start.21 = (bf16[2,128,512]{2,1,0:T(8,128)(2,1)}, bf16[2,128,512]{2,1,0:T(8,128)(2,1)S(1)}, u32[]{:S(2)}, u32[]{:S(2)}) collective-permute-start(bf16[2,128,512]{2,1,0:T(8,128)(2,1)} %get-tuple-element.138), channel_id=1, source_target_pairs={{0,2},{1,3},{2,0},{3,1},{4,6},{5,7},{6,4},{7,5},{8,10},{9,11},{10,... | collective-permute-start | bytes 786440 | tf_op jit(solution)/shard_map/ppermute | solution.py:763
  211.6 18.4 %copy-start.9 = (bf16[2,256,768]{2,1,0:T(8,128)(2,1)}, bf16[2,256,768]{2,1,0:T(8,128)(2,1)S(1)}, u32[]{:S(2)}) copy-start(bf16[2,256,768]{2,1,0:T(8,128)(2,1)S(1)} %constant_dynamic-update-slice_fusion.4.a_ref) | copy-start | bytes 2359300
  211.6 48.4 %copy-start.20 = (f32[8,512]{1,0:T(8,128)S(1)}, f32[8,512]{1,0:T(8,128)}, u32[]{:S(2)}) copy-start(f32[8,512]{1,0:T(8,128)} %get-tuple-element.154) | copy-start | bytes 49156
  211.6 18.4 %collective-permute-start.23 = (bf16[2,256,768]{2,1,0:T(8,128)(2,1)S(1)}, bf16[2,256,768]{2,1,0:T(8,128)(2,1)S(1)}, u32[]{:S(2)}, u32[]{:S(2)}) collective-permute-start(bf16[2,256,768]{2,1,0:T(8,128)(2,1)S(1)} %constant_dynamic-update-slice_fusion.4.a_ref), channel_id=1, source_target_pairs={{0,8},{1,5},{2,10},{3,7},{4,12},{5,1},{6,14},{7,3},{8,0},{9,13},{1... | collective-permute-start | bytes 2359304 | tf_op jit(solution)/shard_map/ppermute | solution.py:769
  211.7 48.3 %collective-permute-start.31 = (bf16[2048,512]{1,0:T(8,128)(2,1)}, bf16[2048,512]{1,0:T(8,128)(2,1)S(1)}, u32[]{:S(2)}, u32[]{:S(2)}) collective-permute-start(bf16[2048,512]{1,0:T(8,128)(2,1)} %shard_map.196), channel_id=1, source_target_pairs={{0,1},{1,0},{2,3},{3,2},{4,5},{5,4},{6,7},{7,6},{8,9},{9,8},{10,11... | collective-permute-start | bytes 6291464 | tf_op jit(solution)/shard_map/ppermute | solution.py:763
  212.6 31.0 %collective-permute-start.17 = (bf16[1280,512]{1,0:T(8,128)(2,1)}, bf16[1280,512]{1,0:T(8,128)(2,1)}, u32[]{:S(2)}, u32[]{:S(2)}) collective-permute-start(bf16[1280,512]{1,0:T(8,128)(2,1)} %add_convert_fusion), channel_id=1, source_target_pairs={{0,2},{1,3},{2,0},{3,1},{4,6},{5,7},{6,4},{7,5},{8,10},{9,11},{10,... | collective-permute-start | bytes 3932168 | tf_op jit(solution)/shard_map/ppermute | solution.py:763
  213.3 21.1 %collective-permute-start.24 = (bf16[2,128,768]{2,1,0:T(8,128)(2,1)S(1)}, bf16[2,128,768]{2,1,0:T(8,128)(2,1)}, u32[]{:S(2)}, u32[]{:S(2)}) collective-permute-start(bf16[2,128,768]{2,1,0:T(8,128)(2,1)S(1)} %constant_dynamic-update-slice_fusion.2), channel_id=1, source_target_pairs={{0,16},{1,17},{2,18},{3,19},{4,20},{5,21},{6,22},{7,23},{8,24},{9,... | collective-permute-start | bytes 1179656 | tf_op jit(solution)/shard_map/ppermute | solution.py:769
  235.4 20.6 %copy-start.10 = (bf16[2,256,768]{2,1,0:T(8,128)(2,1)}, bf16[2,256,768]{2,1,0:T(8,128)(2,1)S(1)}, u32[]{:S(2)}) copy-start(bf16[2,256,768]{2,1,0:T(8,128)(2,1)S(1)} %constant_dynamic-update-slice_fusion.6.a_ref) | copy-start | bytes 2359300
  235.4 20.6 %collective-permute-start.25 = (bf16[2,256,768]{2,1,0:T(8,128)(2,1)S(1)}, bf16[2,256,768]{2,1,0:T(8,128)(2,1)}, u32[]{:S(2)}, u32[]{:S(2)}) collective-permute-start(bf16[2,256,768]{2,1,0:T(8,128)(2,1)S(1)} %constant_dynamic-update-slice_fusion.6.a_ref), channel_id=1, source_target_pairs={{0,8},{1,5},{2,10},{3,7},{4,12},{5,1},{6,14},{7,3},{8,0},{9,13},{1... | collective-permute-start | bytes 2359304 | tf_op jit(solution)/shard_map/ppermute | solution.py:769
  235.4 24.6 %collective-permute-start.27 = (bf16[512,768]{1,0:T(8,128)(2,1)}, bf16[512,768]{1,0:T(8,128)(2,1)S(1)}, u32[]{:S(2)}, u32[]{:S(2)}) collective-permute-start(bf16[512,768]{1,0:T(8,128)(2,1)} %get-tuple-element.141.refs_0_), channel_id=1, source_target_pairs={{0,4},{1,9},{2,6},{3,11},{4,0},{5,13},{6,2},{7,15},{8,12},{9,1},{1... | collective-permute-start | bytes 2359304 | tf_op jit(solution)/shard_map/ppermute | solution.py:769
  236.3 43.3 %collective-permute-start.29 = (bf16[512,768]{1,0:T(8,128)(2,1)}, bf16[512,768]{1,0:T(8,128)(2,1)}, u32[]{:S(2)}, u32[]{:S(2)}) collective-permute-start(bf16[512,768]{1,0:T(8,128)(2,1)} %get-tuple-element.144), channel_id=1, source_target_pairs={{0,4},{1,9},{2,6},{3,11},{4,0},{5,13},{6,2},{7,15},{8,12},{9,1},{1... | collective-permute-start | bytes 2359304 | tf_op jit(solution)/shard_map/ppermute | solution.py:769
  259.2 25.6 %collective-permute-start.35 = (bf16[512,768]{1,0:T(8,128)(2,1)}, bf16[512,768]{1,0:T(8,128)(2,1)}, u32[]{:S(2)}, u32[]{:S(2)}) collective-permute-start(bf16[512,768]{1,0:T(8,128)(2,1)} %get-tuple-element.152), channel_id=1, source_target_pairs={{0,4},{1,9},{2,6},{3,11},{4,0},{5,13},{6,2},{7,15},{8,12},{9,1},{1... | collective-permute-start | bytes 2359304 | tf_op jit(solution)/shard_map/ppermute | solution.py:769
  260.0 39.1 %copy-start.11 = (bf16[512,768]{1,0:T(8,128)(2,1)}, bf16[512,768]{1,0:T(8,128)(2,1)S(1)}, u32[]{:S(2)}) copy-start(bf16[512,768]{1,0:T(8,128)(2,1)S(1)} %collective-permute-done.27.refs_1_) | copy-start | bytes 2359300
  261.4 18.2 %copy-start.12 = (bf16[512,768]{1,0:T(8,128)(2,1)S(1)}, bf16[512,768]{1,0:T(8,128)(2,1)}, u32[]{:S(2)}) copy-start(bf16[512,768]{1,0:T(8,128)(2,1)} %get-tuple-element.143.refs_4_) | copy-start | bytes 2359300
  271.9 1.5 collective-permute-start.32
  271.9 3.8 %collective-permute-start.37 = (f32[6,512]{1,0:T(8,128)S(1)}, f32[6,512]{1,0:T(8,128)S(1)}, u32[]{:S(2)}, u32[]{:S(2)}) collective-permute-start(f32[6,512]{1,0:T(8,128)S(1)} %pad_maximum_fusion), channel_id=1, source_target_pairs={{0,4},{4,0},{8,12},{12,8},{16,20},{20,16},{24,28},{28,24},{1,5},{5... | collective-permute-start | bytes 36872 | tf_op jit(solution)/shard_map/ppermute | solution.py:865
  274.2 10.1 %collective-permute-start.33 = (f32[8,2048]{1,0:T(8,128)S(1)}, f32[8,2048]{1,0:T(8,128)S(1)}, u32[]{:S(2)}, u32[]{:S(2)}) collective-permute-start(f32[8,2048]{1,0:T(8,128)S(1)} %add.125), channel_id=1, source_target_pairs={{0,2},{1,3},{2,0},{3,1},{4,6},{5,7},{6,4},{7,5},{8,10},{9,11},{10,... | collective-permute-start | bytes 196616 | tf_op jit(solution)/shard_map/ppermute | solution.py:763
  275.7 3.8 %collective-permute-start.38 = (f32[6,512]{1,0:T(8,128)S(1)}, f32[6,512]{1,0:T(8,128)S(1)}, u32[]{:S(2)}, u32[]{:S(2)}) collective-permute-start(f32[6,512]{1,0:T(8,128)S(1)} %fusion), channel_id=1, source_target_pairs={{0,8},{4,12},{8,0},{12,4},{16,24},{20,28},{24,16},{28,20},{1,9},{5... | collective-permute-start | bytes 36872 | tf_op jit(solution)/shard_map/ppermute | solution.py:865
  279.5 4.7 %collective-permute-start.39 = (f32[6,512]{1,0:T(8,128)S(1)}, f32[6,512]{1,0:T(8,128)S(1)}, u32[]{:S(2)}, u32[]{:S(2)}) collective-permute-start(f32[6,512]{1,0:T(8,128)S(1)} %add.128), channel_id=1, source_target_pairs={{0,16},{4,20},{8,24},{12,28},{16,0},{20,4},{24,8},{28,12},{1,17},{... | collective-permute-start | bytes 36872 | tf_op jit(solution)/shard_map/ppermute | solution.py:865
  279.5 6.6 %collective-permute-start.28 = (bf16[512,768]{1,0:T(8,128)(2,1)}, bf16[512,768]{1,0:T(8,128)(2,1)S(1)}, u32[]{:S(2)}, u32[]{:S(2)}) collective-permute-start(bf16[512,768]{1,0:T(8,128)(2,1)} %get-tuple-element.144), channel_id=1, source_target_pairs={{0,1},{1,0},{2,3},{3,2},{4,5},{5,4},{6,7},{7,6},{8,9},{9,8},{10,11... | collective-permute-start | bytes 2359304 | tf_op jit(solution)/shard_map/ppermute | solution.py:763
  279.6 12.1 %collective-permute-start.26 = (bf16[512,768]{1,0:T(8,128)(2,1)S(1)}, bf16[512,768]{1,0:T(8,128)(2,1)S(1)}, u32[]{:S(2)}, u32[]{:S(2)}) collective-permute-start(bf16[512,768]{1,0:T(8,128)(2,1)S(1)} %copy-done.12), channel_id=1, source_target_pairs={{0,4},{1,9},{2,6},{3,11},{4,0},{5,13},{6,2},{7,15},{8,12},{9,1},{1... | collective-permute-start | bytes 2359304 | tf_op jit(solution)/shard_map/ppermute | solution.py:769
  284.3 7.4 %collective-permute-start.30 = (bf16[512,768]{1,0:T(8,128)(2,1)}, bf16[512,768]{1,0:T(8,128)(2,1)}, u32[]{:S(2)}, u32[]{:S(2)}) collective-permute-start(bf16[512,768]{1,0:T(8,128)(2,1)} %collective-permute-done.29), channel_id=1, source_target_pairs={{0,1},{1,0},{2,3},{3,2},{4,5},{5,4},{6,7},{7,6},{8,9},{9,8},{10,11... | collective-permute-start | bytes 2359304 | tf_op jit(solution)/shard_map/ppermute | solution.py:763
  284.3 14.9 %collective-permute-start.34 = (bf16[512,768]{1,0:T(8,128)(2,1)}, bf16[512,768]{1,0:T(8,128)(2,1)}, u32[]{:S(2)}, u32[]{:S(2)}) collective-permute-start(bf16[512,768]{1,0:T(8,128)(2,1)} %get-tuple-element.152), channel_id=1, source_target_pairs={{0,1},{1,0},{2,3},{3,2},{4,5},{5,4},{6,7},{7,6},{8,9},{9,8},{10,11... | collective-permute-start | bytes 2359304 | tf_op jit(solution)/shard_map/ppermute | solution.py:763
  284.8 14.4 %collective-permute-start.36 = (bf16[512,768]{1,0:T(8,128)(2,1)}, bf16[512,768]{1,0:T(8,128)(2,1)}, u32[]{:S(2)}, u32[]{:S(2)}) collective-permute-start(bf16[512,768]{1,0:T(8,128)(2,1)} %collective-permute-done.35), channel_id=1, source_target_pairs={{0,1},{1,0},{2,3},{3,2},{4,5},{5,4},{6,7},{7,6},{8,9},{9,8},{10,11... | collective-permute-start | bytes 2359304 | tf_op jit(solution)/shard_map/ppermute | solution.py:763
  286.1 13.0 %copy-start.13 = (bf16[512,768]{1,0:T(8,128)(2,1)}, bf16[512,768]{1,0:T(8,128)(2,1)S(1)}, u32[]{:S(2)}) copy-start(bf16[512,768]{1,0:T(8,128)(2,1)S(1)} %collective-permute-done.28.refs_2_) | copy-start | bytes 2359300
  (20 other events, 61.8 us)

commit v7 on v5

--- a/solution.py
+++ b/solution.py
@@ -13,7 +13,7 @@
 LANES = 128
 VMEM_LIMIT = 60 * 1024 * 1024
 COVER = 20
-FIRST = 2
+FIRST = 3
 
 
 def call(kernel, meta, args, grid, in_specs, out_specs, out_shape, scratch=(), aliases=None, cost=None):
@@ -490,7 +490,7 @@
             pl.BlockSpec((8, channels), lambda t, m: (0, 0)),
         ],
         [struct((tokens, channels), F32), struct((8, tokens), F32), struct((8, channels), F32)],
-        cost=cost(20 * tokens * channels, 12 * tokens * channels),
+        cost=cost(20 * tokens * channels, 12 * tokens * channels, weight=COVER),
     )
 
 
@@ -535,7 +535,7 @@
         wide,
         struct((tokens, channels), BF16),
         scratch=[pltpu.VMEM((TILE, TILE), BF16)],
-        cost=cost(10 * tokens * channels, 12 * tokens * channels),
+        cost=cost(10 * tokens * channels, 12 * tokens * channels, weight=COVER),
     )
 
 
@@ -851,17 +851,19 @@
     shard1 = last_steps(shard1, near2)
     shard2 = last_steps(jnp.concatenate([after(near2, shard1), far2], axis=2))
     parts1 = last_doubling(after(meta, shard2), shard1)
-    parts2 = last_doubling(after(meta, parts1[0]), shard2)
-    dn, row_sums, col_sums = tail_sums(after(meta, parts2[0]), mine, got, far_part, own_x, mu, inv, ln_gain)
+    dn, row_sums, col_sums = tail_sums(after(meta, parts1[0]), mine, got, far_part, own_x, mu, inv, ln_gain)
+    parts2 = last_doubling(after(meta, dn, parts1[1]), shard2)
     for delta in (1, 2):
         row_sums = row_sums + over_gate(row_sums, delta)
-    dinputs = tail(after(meta, parts2[0]), dn, row_sums, own_x, mu, inv, ln_gain, direct, features)
+    dinputs = tail(after(meta, parts2[1]), dn, row_sums, own_x, mu, inv, ln_gain, direct, features)
 
     totals = jnp.concatenate([col_sums[:2], vecs[:4]], axis=0)
     for step in range(bits):
+        if step == bits - 1:
+            totals = after(totals, dinputs)
         totals = totals + lax.ppermute(totals, "dp", [(d, d ^ (1 << step)) for d in range(n_dp)])
 
-    grad_weight = place(meta, parts1, parts2, n_dp, features, weight.shape[1])
+    grad_weight = place(after(meta, dinputs), parts1, parts2, n_dp, features, weight.shape[1])
     return (
         hidden.reshape(rows, tokens, channels),
         dinputs.reshape(rows, tokens, channels),

time: 301 us -> 309 us (1.027)
  waiting for transfers between devices: 55.6 us -> 60.8 us
    ppermute x3, waiting for transfers between devices: 7.51 us -> 23.1 us  [shards(): lax.ppermute(totals, 'dp', [(d, d ^ 1 << step) for d in range(n_dp)])]
    ppermute x16, waiting for transfers between devices: 45.4 us -> 30.8 us  [over_dp(): return lax.ppermute(value, ('dp', 'gate'), pairs)]
    ppermute x21, waiting for transfers between devices: 2.69 us -> 6.9 us  [over_gate(): return lax.ppermute(value, 'gate', [(g, g ^ delta) for g in range(n_gate)])]
    unnamed x53 -> x55, local copies, waits for them, and re-layouts: 8.84 us -> 10.7 us
  transfers between devices with their start and end apart: 40 -> 40, of which waited for: 13 -> 11; matrix products, arithmetic and copies ran while one was open for 4% -> 3% of each run, Pallas kernels for 56% -> 55%
where the time goes in v7:
time: 309 us; the launch traced here: 307 us
  Pallas kernels  190 us (61%)
  waiting for transfers between devices  60.8 us (20%)
  starting transfers between devices  34.5 us (11%)
  local copies, waits for them, and re-layouts  14.3 us (5%)
  other arithmetic  6.58 us (2%)
    pallas_call x26, Pallas kernels, call(): pl.pallas_call(kernel, grid_spec=pltpu.PrefetchScalarGridSpec(num_scalar_...  190 us
    ppermute x16, waiting for transfers between devices, over_dp(): return lax.ppermute(value, ('dp', 'gate'), pairs)  30.8 us
    ppermute x3, waiting for transfers between devices, shards(): lax.ppermute(totals, 'dp', [(d, d ^ 1 << step) for d in range(n_dp)])  23.1 us
    ppermute x16, starting transfers between devices, over_dp(): return lax.ppermute(value, ('dp', 'gate'), pairs)  17.3 us
    ppermute x21, starting transfers between devices, over_gate(): return lax.ppermute(value, 'gate', [(g, g ^ delta) for g in range(n_gate)])  16 us
    unnamed x55, local copies, waits for them, and re-layouts  10.7 us
    ppermute x21, waiting for transfers between devices, over_gate(): return lax.ppermute(value, 'gate', [(g, g ^ delta) for g in range(n_gate)])  6.9 us
  transfers between devices with their start and end apart: 40, of which 11 were waited for; matrix products, arithmetic and copies ran while one was open for 3% of the time, Pallas kernels for 55%

profile of v7, /device:TPU:0, one launch (start us, length us, event | category | flops | bytes accessed | tf_op | source)
XLA Modules:
  0.0 307.0 jit_solution(3323965073481822556)
XLA Ops:
  1.4 4.8 %shard_map.178 = (bf16[2048,128]{1,0:T(8,128)(2,1)}, bf16[2048,128]{1,0:T(8,128)(2,1)}, bf16[2048,384]{1,0:T(8,128)(2,1)}) custom-call(s32[36]{0:T(128)} %stack.147.meta, bf16[2048,1536]{1,0:T(8,128)(2,1)} %refs_10_.7, bf16[2048,1536]{1,0:T(8,128)(2,1)} %refs_10_.7, bf16[2048,1536]{1,0:T(8,128)(2,1)} %refs_10_.7, bf16[2048,1536]{1,0:T(8,128)(2,1)} %refs_10_.7, ...), custom_call_target="tpu_custom_call" | custom-call | bytes 5242880 | tf_op jit(solution)/shard_map/pallas_call | solution.py:20
  6.7 2.6 collective-permute-start.1
  9.3 14.8 %shard_map.179 = (bf16[2048,2048]{1,0:T(8,128)(2,1)}, f32[2048,128]{1,0:T(8,128)}, f32[2048,128]{1,0:T(8,128)}, bf16[2048,512]{1,0:T(8,128)(2,1)}, f32[2048,128]{1,0:T(8,128)}, /*index=5*/f32[2048,128]{1,0:T(8,128)}) custom-call(s32[36]{0:T(128)} %stack.147.meta, bf16[2048,2048]{1,0:T(8,128)(2,1)} %bitcast.50, f32[1,2048]{1,0:T(1,128)} %bitcast.55, ...), custom_call_target="tpu_custom_call" | custom-call | flops 671088640 | bytes 335544320 | tf_op jit(solution)/shard_map/pallas_call | solution.py:20
  24.2 4.8 %shard_map.180 = (bf16[2048,256]{1,0:T(8,128)(2,1)}, bf16[2048,256]{1,0:T(8,128)(2,1)}) custom-call(s32[36]{0:T(128)} %stack.147.meta, bf16[2048,1536]{1,0:T(8,128)(2,1)} %refs_10_.7, bf16[2048,1536]{1,0:T(8,128)(2,1)} %refs_10_.7, bf16[2048,1536]{1,0:T(8,128)(2,1)} %refs_10_.7, bf16[2048,1536]{1,0:T(8,128)(2,1)} %refs_10_.7), custom_call_target="tpu_custom_call" | custom-call | bytes 4194304 | tf_op jit(solution)/shard_map/pallas_call | solution.py:20
  29.0 1.7 collective-permute-start.3
  31.5 1.7 collective-permute-done.2.refs_5_
  35.1 12.0 %shard_map.181.u_ref = bf16[2048,768]{1,0:T(8,128)(2,1)} custom-call(s32[36]{0:T(128)} %stack.147.meta, bf16[2048,2048]{1,0:T(8,128)(2,1)} %get-tuple-element.86.normed_ref, bf16[2048,1536]{1,0:T(8,128)(2,1)} %refs_10_.7, bf16[2048,1536]{1,0:T(8,128)(2,1)} %refs_10_.7, bf16[2048,384]{1,0:T(8,128)(2,1)} %copy-done.23, bf16[2048,384]{1,0:T(8,128)(2,1)} %copy-done.23, ...), custom_call_target="tpu_custom_call" | custom-call | flops 128849018880 | bytes 293601280 | tf_op jit(solution)/shard_map/pallas_call | solution.py:20
  47.0 12.4 %shard_map.182 = (bf16[2048,512]{1,0:T(8,128)(2,1)}, bf16[2048,768]{1,0:T(8,128)(2,1)}, bf16[2048,512]{1,0:T(8,128)(2,1)}, f32[8,512]{1,0:T(8,128)}) custom-call(s32[36]{0:T(128)} %stack.147.meta, bf16[2048,768]{1,0:T(8,128)(2,1)} %shard_map.181.u_ref, bf16[2048,512]{1,0:T(8,128)(2,1)} %get-tuple-element.92.x_ref, bf16[2048,512]{1,0:T(8,128)(2,1)} %bitcast.51, ...), custom_call_target="tpu_custom_call" | custom-call | flops 629145600 | bytes 188743680 | tf_op jit(solution)/shard_map/pallas_call | solution.py:20
  59.5 8.2 %shard_map.183 = (bf16[512,768]{1,0:T(8,128)(2,1)}, bf16[512,768]{1,0:T(8,128)(2,1)}) custom-call(s32[36]{0:T(128)} %stack.147.meta, bf16[2048,2048]{1,0:T(8,128)(2,1)} %get-tuple-element.86.normed_ref, bf16[2048,768]{1,0:T(8,128)(2,1)} %get-tuple-element.95.ds_ref.ds1_ref), custom_call_target="tpu_custom_call" | custom-call | flops 64424509440 | bytes 146800640 | tf_op jit(solution)/shard_map/pallas_call | solution.py:20
  67.6 1.5 collective-permute-start.6
  69.6 8.1 %shard_map.184 = (bf16[512,768]{1,0:T(8,128)(2,1)}, bf16[512,768]{1,0:T(8,128)(2,1)}) custom-call(s32[36]{0:T(128)} %stack.147.meta, bf16[2048,2048]{1,0:T(8,128)(2,1)} %get-tuple-element.86.normed_ref, bf16[2048,768]{1,0:T(8,128)(2,1)} %get-tuple-element.95.ds_ref.ds1_ref), custom_call_target="tpu_custom_call" | custom-call | flops 64424509440 | bytes 146800640 | tf_op jit(solution)/shard_map/pallas_call | solution.py:20
  77.8 1.5 collective-permute-start.8
  79.3 12.1 %shard_map.185.u_ref = bf16[2048,768]{1,0:T(8,128)(2,1)} custom-call(s32[36]{0:T(128)} %stack.147.meta, bf16[2048,2048]{1,0:T(8,128)(2,1)} %get-tuple-element.86.normed_ref, bf16[2048,256]{1,0:T(8,128)(2,1)} %collective-permute-done.3.refs_0_.refs_1_.refs_6_.refs_7_, bf16[2048,256]{1,0:T(8,128)(2,1)} %collective-permute-done.3.refs_0_.refs_1_.refs_6_.refs_7_, ...), custom_call_target="tpu_custom_call" | custom-call | flops 128849018880 | bytes 293601280 | tf_op jit(solution)/shard_map/pallas_call | solution.py:20
  93.2 3.7 %shard_map.186 = (bf16[2,256,768]{2,1,0:T(8,128)(2,1)}, bf16[2,256,768]{2,1,0:T(8,128)(2,1)}) custom-call(s32[36]{0:T(128)} %stack.147.meta, bf16[512,768]{1,0:T(8,128)(2,1)} %get-tuple-element.98.refs_0_.refs_4_, bf16[512,768]{1,0:T(8,128)(2,1)} %copy-done.1, bf16[512,768]{1,0:T(8,128)(2,1)} %collective-permute-done.6.refs_2_.refs_6_, ...), custom_call_target="tpu_custom_call" | custom-call | flops 1572864 | bytes 4718592 | tf_op jit(solution)/shard_map/pallas_call | solution.py:20
  97.5 12.4 %shard_map.187 = (bf16[2048,512]{1,0:T(8,128)(2,1)}, bf16[2048,768]{1,0:T(8,128)(2,1)}, bf16[2048,512]{1,0:T(8,128)(2,1)}, f32[8,512]{1,0:T(8,128)}) custom-call(s32[36]{0:T(128)} %stack.147.meta, bf16[2048,768]{1,0:T(8,128)(2,1)} %shard_map.185.u_ref, ...), custom_call_target="tpu_custom_call", output_to_operand_aliasing={{0}: (7, {}), {2}: (8, {}), {3}: (9, {})} | custom-call | flops 629145600 | bytes 188743680 | tf_op jit(solution)/shard_map/pallas_call | solution.py:20
  110.8 3.0 shard_map.188
  113.9 2.6 collective-permute-start.14
  116.5 8.1 %shard_map.189 = (bf16[512,768]{1,0:T(8,128)(2,1)}, bf16[512,768]{1,0:T(8,128)(2,1)}) custom-call(s32[36]{0:T(128)} %stack.147.meta, bf16[2048,2048]{1,0:T(8,128)(2,1)} %get-tuple-element.86.normed_ref, bf16[2048,768]{1,0:T(8,128)(2,1)} %get-tuple-element.109.ds_ref.ds2_ref), custom_call_target="tpu_custom_call" | custom-call | flops 64424509440 | bytes 146800640 | tf_op jit(solution)/shard_map/pallas_call | solution.py:20
  126.1 8.2 %shard_map.190 = (bf16[512,768]{1,0:T(8,128)(2,1)}, bf16[512,768]{1,0:T(8,128)(2,1)}) custom-call(s32[36]{0:T(128)} %stack.147.meta, bf16[2048,2048]{1,0:T(8,128)(2,1)} %get-tuple-element.86.normed_ref, bf16[2048,768]{1,0:T(8,128)(2,1)} %get-tuple-element.109.ds_ref.ds2_ref), custom_call_target="tpu_custom_call" | custom-call | flops 64424509440 | bytes 146800640 | tf_op jit(solution)/shard_map/pallas_call | solution.py:20
  135.3 8.0 %shard_map.191 = bf16[2048,512]{1,0:T(8,128)(2,1)} custom-call(s32[36]{0:T(128)} %stack.147.meta, bf16[2048,768]{1,0:T(8,128)(2,1)} %get-tuple-element.95.ds_ref.ds1_ref, bf16[2048,768]{1,0:T(8,128)(2,1)} %get-tuple-element.109.ds_ref.ds2_ref, bf16[2048,1536]{1,0:T(8,128)(2,1)} %refs_10_.7, bf16[2048,1536]{1,0:T(8,128)(2,1)} %refs_10_.7, ...), custom_call_target="tpu_custom_call" | custom-call | flops 64424509440 | bytes 125829120 | tf_op jit(solution)/shard_map/pallas_call | solution.py:20
  143.4 3.4 %collective-permute-done.13.refs_3_.refs_7_ = bf16[512,768]{1,0:T(8,128)(2,1)S(1)} collective-permute-done((bf16[512,768]{1,0:T(8,128)(2,1)S(1)}, bf16[512,768]{1,0:T(8,128)(2,1)S(1)}, u32[]{:S(2)}, u32[]{:S(2)}) %collective-permute-start.13) | collective-permute-done | bytes 786464 | tf_op jit(solution)/shard_map/ppermute | solution.py:769
  147.7 3.8 %shard_map.192 = (bf16[2,256,768]{2,1,0:T(8,128)(2,1)}, bf16[2,256,768]{2,1,0:T(8,128)(2,1)}) custom-call(s32[36]{0:T(128)} %stack.147.meta, bf16[512,768]{1,0:T(8,128)(2,1)} %get-tuple-element.116.refs_0_.refs_4_, bf16[512,768]{1,0:T(8,128)(2,1)} %copy-done.2, bf16[512,768]{1,0:T(8,128)(2,1)} %copy-done, bf16[512,768]{1,0:T(8,128)(2,1)} %copy-done.4, ...), custom_call_target="tpu_custom_call" | custom-call | flops 1572864 | bytes 4718592 | tf_op jit(solution)/shard_map/pallas_call | solution.py:20
  152.0 2.6 shard_map.193
  154.6 1.5 collective-permute-start.17
  156.2 8.3 %shard_map.194 = bf16[2048,512]{1,0:T(8,128)(2,1)} custom-call(s32[36]{0:T(128)} %stack.147.meta, bf16[2048,768]{1,0:T(8,128)(2,1)} %get-tuple-element.95.ds_ref.ds1_ref, bf16[2048,768]{1,0:T(8,128)(2,1)} %get-tuple-element.109.ds_ref.ds2_ref, bf16[2048,1536]{1,0:T(8,128)(2,1)} %refs_10_.7, bf16[2048,1536]{1,0:T(8,128)(2,1)} %refs_10_.7, ...), custom_call_target="tpu_custom_call" | custom-call | flops 64424509440 | bytes 125829120 | tf_op jit(solution)/shard_map/pallas_call | solution.py:20
  165.3 3.2 %shard_map.195 = (bf16[2,128,768]{2,1,0:T(8,128)(2,1)}, bf16[2,128,768]{2,1,0:T(8,128)(2,1)}) custom-call(s32[36]{0:T(128)} %stack.147.meta, bf16[2,256,768]{2,1,0:T(8,128)(2,1)} %get-tuple-element.127.refs_0_.refs_2_, bf16[2,256,768]{2,1,0:T(8,128)(2,1)} %copy-done.6, bf16[2,256,768]{2,1,0:T(8,128)(2,1)} %get-tuple-element.127.refs_0_.refs_2_, ...), custom_call_target="tpu_custom_call" | custom-call | flops 786432 | bytes 2359296 | tf_op jit(solution)/shard_map/pallas_call | solution.py:20
  168.8 2.2 add_convert_fusion.1
  171.5 2.8 add_convert_fusion
  174.3 8.2 %shard_map.196 = bf16[2048,512]{1,0:T(8,128)(2,1)} custom-call(s32[36]{0:T(128)} %stack.147.meta, bf16[2048,768]{1,0:T(8,128)(2,1)} %get-tuple-element.95.ds_ref.ds1_ref, bf16[2048,768]{1,0:T(8,128)(2,1)} %get-tuple-element.109.ds_ref.ds2_ref, bf16[2048,1536]{1,0:T(8,128)(2,1)} %refs_10_.7, bf16[2048,1536]{1,0:T(8,128)(2,1)} %refs_10_.7, ...), custom_call_target="tpu_custom_call" | custom-call | flops 64424509440 | bytes 125829120 | tf_op jit(solution)/shard_map/pallas_call | solution.py:20
  183.4 2.7 collective-permute-start.20
  186.1 3.5 %collective-permute-start.24 = (bf16[2048,512]{1,0:T(8,128)(2,1)}, bf16[2048,512]{1,0:T(8,128)(2,1)S(1)}, u32[]{:S(2)}, u32[]{:S(2)}) collective-permute-start(bf16[2048,512]{1,0:T(8,128)(2,1)} %shard_map.196), channel_id=1, source_target_pairs={{0,1},{1,0},{2,3},{3,2},{4,5},{5,4},{6,7},{7,6},{8,9},{9,8},{10,11... | collective-permute-start | bytes 6291464 | tf_op jit(solution)/shard_map/ppermute | solution.py:763
  189.6 8.0 %shard_map.197.k_ref = bf16[2048,512]{1,0:T(8,128)(2,1)} custom-call(s32[36]{0:T(128)} %stack.147.meta, bf16[2048,768]{1,0:T(8,128)(2,1)} %get-tuple-element.95.ds_ref.ds1_ref, bf16[2048,768]{1,0:T(8,128)(2,1)} %get-tuple-element.109.ds_ref.ds2_ref, bf16[2048,1536]{1,0:T(8,128)(2,1)} %refs_10_.7, bf16[2048,1536]{1,0:T(8,128)(2,1)} %refs_10_.7, ...), custom_call_target="tpu_custom_call" | custom-call | flops 64424509440 | bytes 125829120 | tf_op jit(solution)/shard_map/pallas_call | solution.py:20
  198.4 2.6 shard_map.198
  202.4 3.6 %collective-permute-done.20 = bf16[2,128,768]{2,1,0:T(8,128)(2,1)S(1)} collective-permute-done((bf16[2,128,768]{2,1,0:T(8,128)(2,1)S(1)}, bf16[2,128,768]{2,1,0:T(8,128)(2,1)S(1)}, u32[]{:S(2)}, u32[]{:S(2)}) %collective-permute-start.20) | collective-permute-done | bytes 393248 | tf_op jit(solution)/shard_map/ppermute | solution.py:769
  207.7 2.0 collective-permute-done.21
  211.2 18.3 %collective-permute-done.22 = bf16[2,128,768]{2,1,0:T(8,128)(2,1)S(1)} collective-permute-done((bf16[2,128,768]{2,1,0:T(8,128)(2,1)S(1)}, bf16[2,128,768]{2,1,0:T(8,128)(2,1)S(1)}, u32[]{:S(2)}, u32[]{:S(2)}) %collective-permute-start.22) | collective-permute-done | bytes 393248 | tf_op jit(solution)/shard_map/ppermute | solution.py:769
  229.6 3.3 %shard_map.199 = (bf16[512,768]{1,0:T(8,128)(2,1)}, bf16[512,768]{1,0:T(8,128)(2,1)}) custom-call(s32[36]{0:T(128)} %stack.147.meta, bf16[2,256,768]{2,1,0:T(8,128)(2,1)} %copy-done.10, bf16[2,256,768]{2,1,0:T(8,128)(2,1)} %collective-permute-done.23.b_ref), custom_call_target="tpu_custom_call" | custom-call | bytes 3145728 | tf_op jit(solution)/shard_map/pallas_call | solution.py:20
  235.0 3.2 %collective-permute-done.25.r2_ref = bf16[1280,512]{1,0:T(8,128)(2,1)} collective-permute-done((bf16[1280,512]{1,0:T(8,128)(2,1)}, bf16[1280,512]{1,0:T(8,128)(2,1)}, u32[]{:S(2)}, u32[]{:S(2)}) %collective-permute-start.25) | collective-permute-done | bytes 1310752 | tf_op jit(solution)/shard_map/ppermute | solution.py:763
  239.5 9.8 %shard_map.200 = (f32[2048,512]{1,0:T(8,128)}, f32[8,2048]{1,0:T(8,128)}, f32[8,512]{1,0:T(8,128)}) custom-call(s32[36]{0:T(128)} %stack.147.meta, bf16[2048,512]{1,0:T(8,128)(2,1)} %shard_map.197.k_ref, bf16[2048,512]{1,0:T(8,128)(2,1)} %copy-done.9, bf16[768,512]{1,0:T(8,128)(2,1)} %copy-done.15, bf16[1280,512]{1,0:T(8,128)(2,1)} %collective-permute-done.25.r2_ref, ...), custom_call_target="tpu_custom_call" | custom-call | flops 419430400 | bytes 251658240 | tf_op jit(solution)/shard_map/pallas_call | solution.py:20
  249.3 3.2 %collective-permute-done.26.refs_1_ = bf16[512,768]{1,0:T(8,128)(2,1)S(1)} collective-permute-done((bf16[512,768]{1,0:T(8,128)(2,1)}, bf16[512,768]{1,0:T(8,128)(2,1)S(1)}, u32[]{:S(2)}, u32[]{:S(2)}) %collective-permute-start.26) | collective-permute-done | bytes 786464 | tf_op jit(solution)/shard_map/ppermute | solution.py:769
  252.5 2.3 collective-permute-done.27.b_ref
  254.8 3.2 %shard_map.201 = (bf16[512,768]{1,0:T(8,128)(2,1)}, bf16[512,768]{1,0:T(8,128)(2,1)}) custom-call(s32[36]{0:T(128)} %stack.147.meta, bf16[2,256,768]{2,1,0:T(8,128)(2,1)} %copy-done.5, bf16[2,256,768]{2,1,0:T(8,128)(2,1)} %collective-permute-done.27.b_ref), custom_call_target="tpu_custom_call" | custom-call | bytes 3145728 | tf_op jit(solution)/shard_map/pallas_call | solution.py:20
  262.4 1.6 collective-permute-start.30
  264.0 15.0 %collective-permute-done.37 = f32[6,512]{1,0:T(8,128)S(1)} collective-permute-done((f32[6,512]{1,0:T(8,128)S(1)}, f32[6,512]{1,0:T(8,128)S(1)}, u32[]{:S(2)}, u32[]{:S(2)}) %collective-permute-start.37) | collective-permute-done | bytes 12320 | tf_op jit(solution)/shard_map/ppermute | solution.py:864
  279.1 3.7 %collective-permute-done.38 = f32[6,512]{1,0:T(8,128)S(1)} collective-permute-done((f32[6,512]{1,0:T(8,128)S(1)}, f32[6,512]{1,0:T(8,128)S(1)}, u32[]{:S(2)}, u32[]{:S(2)}) %collective-permute-start.38) | collective-permute-done | bytes 12320 | tf_op jit(solution)/shard_map/ppermute | solution.py:864
  284.5 7.4 %shard_map.202 = bf16[2048,512]{1,0:T(8,128)(2,1)} custom-call(s32[36]{0:T(128)} %stack.147.meta, f32[2048,512]{1,0:T(8,128)} %get-tuple-element.145.dn_ref, f32[8,2048]{1,0:T(8,128)} %add.126.row_ref, bf16[2048,512]{1,0:T(8,128)(2,1)} %get-tuple-element.92.x_ref, f32[2048,128]{1,0:T(8,128)} %get-tuple-element.143.mu_ref, ...), custom_call_target="tpu_custom_call" | custom-call | flops 209715200 | bytes 251658240 | tf_op jit(solution)/shard_map/pallas_call | solution.py:20
  292.3 4.4 %collective-permute-done.39 = f32[6,512]{1,0:T(8,128)S(1)} collective-permute-done((f32[6,512]{1,0:T(8,128)S(1)}, f32[6,512]{1,0:T(8,128)S(1)}, u32[]{:S(2)}, u32[]{:S(2)}) %collective-permute-start.39) | collective-permute-done | bytes 12320 | tf_op jit(solution)/shard_map/ppermute | solution.py:864
  298.5 8.5 %shard_map.203 = f32[2048,1536]{1,0:T(8,128)} custom-call(s32[36]{0:T(128)} %stack.147.meta, bf16[512,768]{1,0:T(8,128)(2,1)} %get-tuple-element.141.refs_0_, bf16[512,768]{1,0:T(8,128)(2,1)} %copy-done.11, bf16[512,768]{1,0:T(8,128)(2,1)} %copy-done.13, bf16[512,768]{1,0:T(8,128)(2,1)} %collective-permute-done.33.refs_3_, ...), custom_call_target="tpu_custom_call" | custom-call | flops 3145728 | bytes 18874368 | tf_op jit(solution)/shard_map/pallas_call | solution.py:20
  (131 shorter events, 31.2 us)
Async XLA Ops:
  6.2 26.9 %collective-permute-start = (bf16[2048,384]{1,0:T(8,128)(2,1)}, bf16[2048,384]{1,0:T(8,128)(2,1)S(1)}, u32[]{:S(2)}, u32[]{:S(2)}) collective-permute-start(bf16[2048,384]{1,0:T(8,128)(2,1)} %get-tuple-element.91), channel_id=1, source_target_pairs={{0,1},{1,0},{2,3},{3,2},{4,5},{5,4},{6,7},{7,6},{8,9},{9,8},{10,11... | collective-permute-start | bytes 4718600 | tf_op jit(solution)/shard_map/ppermute | solution.py:763
  6.7 24.7 %collective-permute-start.1 = (bf16[2048,128]{1,0:T(8,128)(2,1)}, bf16[2048,128]{1,0:T(8,128)(2,1)S(1)}, u32[]{:S(2)}, u32[]{:S(2)}) collective-permute-start(bf16[2048,128]{1,0:T(8,128)(2,1)} %get-tuple-element.83), channel_id=1, source_target_pairs={{0,2},{1,3},{2,0},{3,1},{4,6},{5,7},{6,4},{7,5},{8,10},{9,11},{10,... | collective-permute-start | bytes 1572872 | tf_op jit(solution)/shard_map/ppermute | solution.py:763
  9.3 23.9 %collective-permute-start.2 = (bf16[2048,128]{1,0:T(8,128)(2,1)}, bf16[2048,128]{1,0:T(8,128)(2,1)S(1)}, u32[]{:S(2)}, u32[]{:S(2)}) collective-permute-start(bf16[2048,128]{1,0:T(8,128)(2,1)} %get-tuple-element.84), channel_id=1, source_target_pairs={{0,3},{1,2},{2,1},{3,0},{4,7},{5,6},{6,5},{7,4},{8,11},{9,10},{10,... | collective-permute-start | bytes 1572872 | tf_op jit(solution)/shard_map/ppermute | solution.py:763
  24.2 6.6 %copy-start.19 = (f32[512]{0:T(512)S(1)}, f32[512]{0:T(512)}, u32[]{:S(2)}) copy-start(f32[512]{0:T(512)} %param.15) | copy-start | bytes 6148
  24.2 6.6 %copy-start.20 = (f32[512]{0:T(512)S(1)}, f32[512]{0:T(512)}, u32[]{:S(2)}) copy-start(f32[512]{0:T(512)} %param.16) | copy-start | bytes 6148
  29.0 50.3 %collective-permute-start.3 = (bf16[2048,256]{1,0:T(8,128)(2,1)}, bf16[2048,256]{1,0:T(8,128)(2,1)}, u32[]{:S(2)}, u32[]{:S(2)}) collective-permute-start(bf16[2048,256]{1,0:T(8,128)(2,1)} %get-tuple-element.88), channel_id=1, source_target_pairs={{0,2},{1,3},{2,0},{3,1},{4,6},{5,7},{6,4},{7,5},{8,10},{9,11},{10,... | collective-permute-start | bytes 3145736 | tf_op jit(solution)/shard_map/ppermute | solution.py:763
  30.8 48.5 %collective-permute-start.4 = (bf16[2048,256]{1,0:T(8,128)(2,1)}, bf16[2048,256]{1,0:T(8,128)(2,1)}, u32[]{:S(2)}, u32[]{:S(2)}) collective-permute-start(bf16[2048,256]{1,0:T(8,128)(2,1)} %get-tuple-element.89), channel_id=1, source_target_pairs={{0,3},{1,2},{2,1},{3,0},{4,7},{5,6},{6,5},{7,4},{8,11},{9,10},{10,... | collective-permute-start | bytes 3145736 | tf_op jit(solution)/shard_map/ppermute | solution.py:763
  67.6 23.8 %collective-permute-start.6 = (bf16[512,768]{1,0:T(8,128)(2,1)}, bf16[512,768]{1,0:T(8,128)(2,1)}, u32[]{:S(2)}, u32[]{:S(2)}) collective-permute-start(bf16[512,768]{1,0:T(8,128)(2,1)} %get-tuple-element.96), channel_id=1, source_target_pairs={{0,4},{1,9},{2,6},{3,11},{4,0},{5,13},{6,2},{7,15},{8,12},{9,1},{1... | collective-permute-start | bytes 2359304 | tf_op jit(solution)/shard_map/ppermute | solution.py:769
  69.1 8.6 %collective-permute-start.7 = (bf16[512,768]{1,0:T(8,128)(2,1)}, bf16[512,768]{1,0:T(8,128)(2,1)S(1)}, u32[]{:S(2)}, u32[]{:S(2)}) collective-permute-start(bf16[512,768]{1,0:T(8,128)(2,1)} %get-tuple-element.102), channel_id=1, source_target_pairs={{0,1},{1,0},{2,3},{3,2},{4,5},{5,4},{6,7},{7,6},{8,9},{9,8},{10,11... | collective-permute-start | bytes 2359304 | tf_op jit(solution)/shard_map/ppermute | solution.py:763
  77.7 13.7 %collective-permute-start.5 = (bf16[512,768]{1,0:T(8,128)(2,1)}, bf16[512,768]{1,0:T(8,128)(2,1)S(1)}, u32[]{:S(2)}, u32[]{:S(2)}) collective-permute-start(bf16[512,768]{1,0:T(8,128)(2,1)} %get-tuple-element.101), channel_id=1, source_target_pairs={{0,1},{1,0},{2,3},{3,2},{4,5},{5,4},{6,7},{7,6},{8,9},{9,8},{10,11... | collective-permute-start | bytes 2359304 | tf_op jit(solution)/shard_map/ppermute | solution.py:763
  77.8 13.7 %collective-permute-start.8 = (bf16[512,768]{1,0:T(8,128)(2,1)S(1)}, bf16[512,768]{1,0:T(8,128)(2,1)S(1)}, u32[]{:S(2)}, u32[]{:S(2)}) collective-permute-start(bf16[512,768]{1,0:T(8,128)(2,1)S(1)} %collective-permute-done.7), channel_id=1, source_target_pairs={{0,4},{1,9},{2,6},{3,11},{4,0},{5,13},{6,2},{7,15},{8,12},{9,1},{1... | collective-permute-start | bytes 2359304 | tf_op jit(solution)/shard_map/ppermute | solution.py:769
  96.9 13.0 %collective-permute-start.9 = (bf16[2,256,768]{2,1,0:T(8,128)(2,1)}, bf16[2,256,768]{2,1,0:T(8,128)(2,1)S(1)}, u32[]{:S(2)}, u32[]{:S(2)}) collective-permute-start(bf16[2,256,768]{2,1,0:T(8,128)(2,1)} %get-tuple-element.103), channel_id=1, source_target_pairs={{0,8},{1,5},{2,10},{3,7},{4,12},{5,1},{6,14},{7,3},{8,0},{9,13},{1... | collective-permute-start | bytes 2359304 | tf_op jit(solution)/shard_map/ppermute | solution.py:769
  113.9 38.1 %collective-permute-start.14 = (bf16[2,128,768]{2,1,0:T(8,128)(2,1)}, bf16[2,128,768]{2,1,0:T(8,128)(2,1)}, u32[]{:S(2)}, u32[]{:S(2)}) collective-permute-start(bf16[2,128,768]{2,1,0:T(8,128)(2,1)} %get-tuple-element.112), channel_id=1, source_target_pairs={{0,16},{1,17},{2,18},{3,19},{4,20},{5,21},{6,22},{7,23},{8,24},{9,... | collective-permute-start | bytes 1179656 | tf_op jit(solution)/shard_map/ppermute | solution.py:769
  124.6 18.8 %collective-permute-start.11 = (bf16[512,768]{1,0:T(8,128)(2,1)}, bf16[512,768]{1,0:T(8,128)(2,1)S(1)}, u32[]{:S(2)}, u32[]{:S(2)}) collective-permute-start(bf16[512,768]{1,0:T(8,128)(2,1)} %get-tuple-element.114), channel_id=1, source_target_pairs={{0,4},{1,9},{2,6},{3,11},{4,0},{5,13},{6,2},{7,15},{8,12},{9,1},{1... | collective-permute-start | bytes 2359304 | tf_op jit(solution)/shard_map/ppermute | solution.py:769
  126.1 8.7 %collective-permute-start.12 = (bf16[512,768]{1,0:T(8,128)(2,1)}, bf16[512,768]{1,0:T(8,128)(2,1)S(1)}, u32[]{:S(2)}, u32[]{:S(2)}) collective-permute-start(bf16[512,768]{1,0:T(8,128)(2,1)} %get-tuple-element.120), channel_id=1, source_target_pairs={{0,1},{1,0},{2,3},{3,2},{4,5},{5,4},{6,7},{7,6},{8,9},{9,8},{10,11... | collective-permute-start | bytes 2359304 | tf_op jit(solution)/shard_map/ppermute | solution.py:763
  134.3 9.1 %collective-permute-start.10 = (bf16[512,768]{1,0:T(8,128)(2,1)}, bf16[512,768]{1,0:T(8,128)(2,1)S(1)}, u32[]{:S(2)}, u32[]{:S(2)}) collective-permute-start(bf16[512,768]{1,0:T(8,128)(2,1)} %get-tuple-element.119), channel_id=1, source_target_pairs={{0,1},{1,0},{2,3},{3,2},{4,5},{5,4},{6,7},{7,6},{8,9},{9,8},{10,11... | collective-permute-start | bytes 2359304 | tf_op jit(solution)/shard_map/ppermute | solution.py:763
  134.8 12.0 %collective-permute-start.13 = (bf16[512,768]{1,0:T(8,128)(2,1)S(1)}, bf16[512,768]{1,0:T(8,128)(2,1)S(1)}, u32[]{:S(2)}, u32[]{:S(2)}) collective-permute-start(bf16[512,768]{1,0:T(8,128)(2,1)S(1)} %collective-permute-done.12), channel_id=1, source_target_pairs={{0,4},{1,9},{2,6},{3,11},{4,0},{5,13},{6,2},{7,15},{8,12},{9,1},{1... | collective-permute-start | bytes 2359304 | tf_op jit(solution)/shard_map/ppermute | solution.py:769
  143.3 25.5 %collective-permute-start.16 = (bf16[2048,512]{1,0:T(8,128)(2,1)}, bf16[2048,512]{1,0:T(8,128)(2,1)}, u32[]{:S(2)}, u32[]{:S(2)}) collective-permute-start(bf16[2048,512]{1,0:T(8,128)(2,1)} %shard_map.191), channel_id=1, source_target_pairs={{0,1},{1,0},{2,3},{3,2},{4,5},{5,4},{6,7},{7,6},{8,9},{9,8},{10,11... | collective-permute-start | bytes 6291464 | tf_op jit(solution)/shard_map/ppermute | solution.py:763
  151.5 12.9 %collective-permute-start.15 = (bf16[2,256,768]{2,1,0:T(8,128)(2,1)}, bf16[2,256,768]{2,1,0:T(8,128)(2,1)S(1)}, u32[]{:S(2)}, u32[]{:S(2)}) collective-permute-start(bf16[2,256,768]{2,1,0:T(8,128)(2,1)} %get-tuple-element.121), channel_id=1, source_target_pairs={{0,8},{1,5},{2,10},{3,7},{4,12},{5,1},{6,14},{7,3},{8,0},{9,13},{1... | collective-permute-start | bytes 2359304 | tf_op jit(solution)/shard_map/ppermute | solution.py:769
  154.6 27.9 %collective-permute-start.17 = (bf16[2,128,256]{2,1,0:T(8,128)(2,1)}, bf16[2,128,256]{2,1,0:T(8,128)(2,1)}, u32[]{:S(2)}, u32[]{:S(2)}) collective-permute-start(bf16[2,128,256]{2,1,0:T(8,128)(2,1)} %get-tuple-element.132), channel_id=1, source_target_pairs={{0,2},{1,3},{2,0},{3,1},{4,6},{5,7},{6,4},{7,5},{8,10},{9,11},{10,... | collective-permute-start | bytes 393224 | tf_op jit(solution)/shard_map/ppermute | solution.py:763
  168.5 29.2 %collective-permute-start.19 = (bf16[2,128,768]{2,1,0:T(8,128)(2,1)}, bf16[2,128,768]{2,1,0:T(8,128)(2,1)S(1)}, u32[]{:S(2)}, u32[]{:S(2)}) collective-permute-start(bf16[2,128,768]{2,1,0:T(8,128)(2,1)} %get-tuple-element.128), channel_id=1, source_target_pairs={{0,16},{1,17},{2,18},{3,19},{4,20},{5,21},{6,22},{7,23},{8,24},{9,... | collective-permute-start | bytes 1179656 | tf_op jit(solution)/shard_map/ppermute | solution.py:769
  171.1 26.5 %collective-permute-start.18 = (bf16[768,512]{1,0:T(8,128)(2,1)}, bf16[768,512]{1,0:T(8,128)(2,1)S(1)}, u32[]{:S(2)}, u32[]{:S(2)}) collective-permute-start(bf16[768,512]{1,0:T(8,128)(2,1)} %add_convert_fusion.1), channel_id=1, source_target_pairs={{0,2},{1,3},{2,0},{3,1},{4,6},{5,7},{6,4},{7,5},{8,10},{9,11},{10,... | collective-permute-start | bytes 2359304 | tf_op jit(solution)/shard_map/ppermute | solution.py:763
  174.3 8.2 %copy-start.17 = (bf16[2,128,512]{2,1,0:T(8,128)(2,1)S(1)}, bf16[2,128,512]{2,1,0:T(8,128)(2,1)}, u32[]{:S(2)}) copy-start(bf16[2,128,512]{2,1,0:T(8,128)(2,1)} %get-tuple-element.131) | copy-start | bytes 786436
  183.4 22.6 %collective-permute-start.20 = (bf16[2,128,768]{2,1,0:T(8,128)(2,1)S(1)}, bf16[2,128,768]{2,1,0:T(8,128)(2,1)S(1)}, u32[]{:S(2)}, u32[]{:S(2)}) collective-permute-start(bf16[2,128,768]{2,1,0:T(8,128)(2,1)S(1)} %constant_dynamic-update-slice_fusion), channel_id=1, source_target_pairs={{0,16},{1,17},{2,18},{3,19},{4,20},{5,21},{6,22},{7,23},{8,24},{9,... | collective-permute-start | bytes 1179656 | tf_op jit(solution)/shard_map/ppermute | solution.py:769
  186.1 52.1 %collective-permute-start.24 = (bf16[2048,512]{1,0:T(8,128)(2,1)}, bf16[2048,512]{1,0:T(8,128)(2,1)S(1)}, u32[]{:S(2)}, u32[]{:S(2)}) collective-permute-start(bf16[2048,512]{1,0:T(8,128)(2,1)} %shard_map.196), channel_id=1, source_target_pairs={{0,1},{1,0},{2,3},{3,2},{4,5},{5,4},{6,7},{7,6},{8,9},{9,8},{10,11... | collective-permute-start | bytes 6291464 | tf_op jit(solution)/shard_map/ppermute | solution.py:763
  201.1 8.6 %collective-permute-start.21 = (bf16[2,128,512]{2,1,0:T(8,128)(2,1)}, bf16[2,128,512]{2,1,0:T(8,128)(2,1)S(1)}, u32[]{:S(2)}, u32[]{:S(2)}) collective-permute-start(bf16[2,128,512]{2,1,0:T(8,128)(2,1)} %get-tuple-element.139), channel_id=1, source_target_pairs={{0,2},{1,3},{2,0},{3,1},{4,6},{5,7},{6,4},{7,5},{8,10},{9,11},{10,... | collective-permute-start | bytes 786440 | tf_op jit(solution)/shard_map/ppermute | solution.py:763
  206.0 23.6 %copy-start.10 = (bf16[2,256,768]{2,1,0:T(8,128)(2,1)}, bf16[2,256,768]{2,1,0:T(8,128)(2,1)S(1)}, u32[]{:S(2)}) copy-start(bf16[2,256,768]{2,1,0:T(8,128)(2,1)S(1)} %constant_dynamic-update-slice_fusion.2.a_ref) | copy-start | bytes 2359300
  206.0 23.6 %collective-permute-start.23 = (bf16[2,256,768]{2,1,0:T(8,128)(2,1)S(1)}, bf16[2,256,768]{2,1,0:T(8,128)(2,1)}, u32[]{:S(2)}, u32[]{:S(2)}) collective-permute-start(bf16[2,256,768]{2,1,0:T(8,128)(2,1)S(1)} %constant_dynamic-update-slice_fusion.2.a_ref), channel_id=1, source_target_pairs={{0,8},{1,5},{2,10},{3,7},{4,12},{5,1},{6,14},{7,3},{8,0},{9,13},{1... | collective-permute-start | bytes 2359304 | tf_op jit(solution)/shard_map/ppermute | solution.py:769
  206.1 32.0 %collective-permute-start.25 = (bf16[1280,512]{1,0:T(8,128)(2,1)}, bf16[1280,512]{1,0:T(8,128)(2,1)}, u32[]{:S(2)}, u32[]{:S(2)}) collective-permute-start(bf16[1280,512]{1,0:T(8,128)(2,1)} %add_convert_fusion), channel_id=1, source_target_pairs={{0,2},{1,3},{2,0},{3,1},{4,6},{5,7},{6,4},{7,5},{8,10},{9,11},{10,... | collective-permute-start | bytes 3932168 | tf_op jit(solution)/shard_map/ppermute | solution.py:763
  209.7 19.8 %collective-permute-start.22 = (bf16[2,128,768]{2,1,0:T(8,128)(2,1)S(1)}, bf16[2,128,768]{2,1,0:T(8,128)(2,1)S(1)}, u32[]{:S(2)}, u32[]{:S(2)}) collective-permute-start(bf16[2,128,768]{2,1,0:T(8,128)(2,1)S(1)} %constant_dynamic-update-slice_fusion.4), channel_id=1, source_target_pairs={{0,16},{1,17},{2,18},{3,19},{4,20},{5,21},{6,22},{7,23},{8,24},{9,... | collective-permute-start | bytes 1179656 | tf_op jit(solution)/shard_map/ppermute | solution.py:769
  229.6 19.7 %copy-start.5 = (bf16[2,256,768]{2,1,0:T(8,128)(2,1)}, bf16[2,256,768]{2,1,0:T(8,128)(2,1)S(1)}, u32[]{:S(2)}) copy-start(bf16[2,256,768]{2,1,0:T(8,128)(2,1)S(1)} %pad_maximum_fusion.a_ref) | copy-start | bytes 2359300
  232.9 19.6 %collective-permute-start.26 = (bf16[512,768]{1,0:T(8,128)(2,1)}, bf16[512,768]{1,0:T(8,128)(2,1)S(1)}, u32[]{:S(2)}, u32[]{:S(2)}) collective-permute-start(bf16[512,768]{1,0:T(8,128)(2,1)} %get-tuple-element.141.refs_0_), channel_id=1, source_target_pairs={{0,4},{1,9},{2,6},{3,11},{4,0},{5,13},{6,2},{7,15},{8,12},{9,1},{1... | collective-permute-start | bytes 2359304 | tf_op jit(solution)/shard_map/ppermute | solution.py:769
  234.3 20.5 %collective-permute-start.27 = (bf16[2,256,768]{2,1,0:T(8,128)(2,1)S(1)}, bf16[2,256,768]{2,1,0:T(8,128)(2,1)}, u32[]{:S(2)}, u32[]{:S(2)}) collective-permute-start(bf16[2,256,768]{2,1,0:T(8,128)(2,1)S(1)} %pad_maximum_fusion.a_ref), channel_id=1, source_target_pairs={{0,8},{1,5},{2,10},{3,7},{4,12},{5,1},{6,14},{7,3},{8,0},{9,13},{1... | collective-permute-start | bytes 2359304 | tf_op jit(solution)/shard_map/ppermute | solution.py:769
  234.3 49.0 %collective-permute-start.32 = (bf16[512,768]{1,0:T(8,128)(2,1)}, bf16[512,768]{1,0:T(8,128)(2,1)}, u32[]{:S(2)}, u32[]{:S(2)}) collective-permute-start(bf16[512,768]{1,0:T(8,128)(2,1)} %get-tuple-element.152), channel_id=1, source_target_pairs={{0,4},{1,9},{2,6},{3,11},{4,0},{5,13},{6,2},{7,15},{8,12},{9,1},{1... | collective-permute-start | bytes 2359304 | tf_op jit(solution)/shard_map/ppermute | solution.py:769
  239.5 19.2 %copy-start.18 = (f32[8,512]{1,0:T(8,128)S(1)}, f32[8,512]{1,0:T(8,128)}, u32[]{:S(2)}) copy-start(f32[8,512]{1,0:T(8,128)} %get-tuple-element.155) | copy-start | bytes 49156
  252.5 39.4 %copy-start.11 = (bf16[512,768]{1,0:T(8,128)(2,1)}, bf16[512,768]{1,0:T(8,128)(2,1)S(1)}, u32[]{:S(2)}) copy-start(bf16[512,768]{1,0:T(8,128)(2,1)S(1)} %collective-permute-done.26.refs_1_) | copy-start | bytes 2359300
  258.0 25.4 %collective-permute-start.35 = (bf16[512,768]{1,0:T(8,128)(2,1)}, bf16[512,768]{1,0:T(8,128)(2,1)}, u32[]{:S(2)}, u32[]{:S(2)}) collective-permute-start(bf16[512,768]{1,0:T(8,128)(2,1)} %get-tuple-element.153), channel_id=1, source_target_pairs={{0,4},{1,9},{2,6},{3,11},{4,0},{5,13},{6,2},{7,15},{8,12},{9,1},{1... | collective-permute-start | bytes 2359304 | tf_op jit(solution)/shard_map/ppermute | solution.py:769
  259.4 2.1 collective-permute-start.29
  259.4 25.1 %collective-permute-start.28 = (bf16[512,768]{1,0:T(8,128)(2,1)}, bf16[512,768]{1,0:T(8,128)(2,1)S(1)}, u32[]{:S(2)}, u32[]{:S(2)}) collective-permute-start(bf16[512,768]{1,0:T(8,128)(2,1)} %get-tuple-element.147.refs_4_), channel_id=1, source_target_pairs={{0,4},{1,9},{2,6},{3,11},{4,0},{5,13},{6,2},{7,15},{8,12},{9,1},{1... | collective-permute-start | bytes 2359304 | tf_op jit(solution)/shard_map/ppermute | solution.py:769
  260.8 18.2 %collective-permute-start.37 = (f32[6,512]{1,0:T(8,128)S(1)}, f32[6,512]{1,0:T(8,128)S(1)}, u32[]{:S(2)}, u32[]{:S(2)}) collective-permute-start(f32[6,512]{1,0:T(8,128)S(1)} %pad_maximum_fusion.1), channel_id=1, source_target_pairs={{0,4},{4,0},{8,12},{12,8},{16,20},{20,16},{24,28},{28,24},{1,5},{5... | collective-permute-start | bytes 36872 | tf_op jit(solution)/shard_map/ppermute | solution.py:864
  262.4 20.4 %collective-permute-start.30 = (f32[8,2048]{1,0:T(8,128)S(1)}, f32[8,2048]{1,0:T(8,128)S(1)}, u32[]{:S(2)}, u32[]{:S(2)}) collective-permute-start(f32[8,2048]{1,0:T(8,128)S(1)} %add.125), channel_id=1, source_target_pairs={{0,2},{1,3},{2,0},{3,1},{4,6},{5,7},{6,4},{7,5},{8,10},{9,11},{10,... | collective-permute-start | bytes 196616 | tf_op jit(solution)/shard_map/ppermute | solution.py:763
  279.0 3.8 %collective-permute-start.38 = (f32[6,512]{1,0:T(8,128)S(1)}, f32[6,512]{1,0:T(8,128)S(1)}, u32[]{:S(2)}, u32[]{:S(2)}) collective-permute-start(f32[6,512]{1,0:T(8,128)S(1)} %fusion), channel_id=1, source_target_pairs={{0,8},{4,12},{8,0},{12,4},{16,24},{20,28},{24,16},{28,20},{1,9},{5... | collective-permute-start | bytes 36872 | tf_op jit(solution)/shard_map/ppermute | solution.py:864
  282.8 14.5 %collective-permute-start.31 = (bf16[512,768]{1,0:T(8,128)(2,1)}, bf16[512,768]{1,0:T(8,128)(2,1)S(1)}, u32[]{:S(2)}, u32[]{:S(2)}) collective-permute-start(bf16[512,768]{1,0:T(8,128)(2,1)} %get-tuple-element.152), channel_id=1, source_target_pairs={{0,1},{1,0},{2,3},{3,2},{4,5},{5,4},{6,7},{7,6},{8,9},{9,8},{10,11... | collective-permute-start | bytes 2359304 | tf_op jit(solution)/shard_map/ppermute | solution.py:763
  282.8 14.5 %collective-permute-start.34 = (bf16[512,768]{1,0:T(8,128)(2,1)}, bf16[512,768]{1,0:T(8,128)(2,1)S(1)}, u32[]{:S(2)}, u32[]{:S(2)}) collective-permute-start(bf16[512,768]{1,0:T(8,128)(2,1)} %get-tuple-element.153), channel_id=1, source_target_pairs={{0,1},{1,0},{2,3},{3,2},{4,5},{5,4},{6,7},{7,6},{8,9},{9,8},{10,11... | collective-permute-start | bytes 2359304 | tf_op jit(solution)/shard_map/ppermute | solution.py:763
  283.3 13.9 %collective-permute-start.33 = (bf16[512,768]{1,0:T(8,128)(2,1)}, bf16[512,768]{1,0:T(8,128)(2,1)}, u32[]{:S(2)}, u32[]{:S(2)}) collective-permute-start(bf16[512,768]{1,0:T(8,128)(2,1)} %collective-permute-done.32), channel_id=1, source_target_pairs={{0,1},{1,0},{2,3},{3,2},{4,5},{5,4},{6,7},{7,6},{8,9},{9,8},{10,11... | collective-permute-start | bytes 2359304 | tf_op jit(solution)/shard_map/ppermute | solution.py:763
  283.4 13.9 %collective-permute-start.36 = (bf16[512,768]{1,0:T(8,128)(2,1)}, bf16[512,768]{1,0:T(8,128)(2,1)}, u32[]{:S(2)}, u32[]{:S(2)}) collective-permute-start(bf16[512,768]{1,0:T(8,128)(2,1)} %collective-permute-done.35), channel_id=1, source_target_pairs={{0,1},{1,0},{2,3},{3,2},{4,5},{5,4},{6,7},{7,6},{8,9},{9,8},{10,11... | collective-permute-start | bytes 2359304 | tf_op jit(solution)/shard_map/ppermute | solution.py:763
  284.5 7.5 %copy-start.12 = (bf16[512,768]{1,0:T(8,128)(2,1)}, bf16[512,768]{1,0:T(8,128)(2,1)S(1)}, u32[]{:S(2)}) copy-start(bf16[512,768]{1,0:T(8,128)(2,1)S(1)} %collective-permute-done.28.refs_5_) | copy-start | bytes 2359300
  292.0 4.7 %collective-permute-start.39 = (f32[6,512]{1,0:T(8,128)S(1)}, f32[6,512]{1,0:T(8,128)S(1)}, u32[]{:S(2)}, u32[]{:S(2)}) collective-permute-start(f32[6,512]{1,0:T(8,128)S(1)} %add.128), channel_id=1, source_target_pairs={{0,16},{4,20},{8,24},{12,28},{16,0},{20,4},{24,8},{28,12},{1,17},{... | collective-permute-start | bytes 36872 | tf_op jit(solution)/shard_map/ppermute | solution.py:864
  (18 other events, 40.3 us)

commit v8 on v5

--- a/solution.py
+++ b/solution.py
@@ -490,7 +490,7 @@
             pl.BlockSpec((8, channels), lambda t, m: (0, 0)),
         ],
         [struct((tokens, channels), F32), struct((8, tokens), F32), struct((8, channels), F32)],
-        cost=cost(20 * tokens * channels, 12 * tokens * channels),
+        cost=cost(20 * tokens * channels, 12 * tokens * channels, weight=COVER),
     )
 
 
@@ -689,7 +689,7 @@
         [whole] * 8,
         pl.BlockSpec((features // 4, columns), where_to),
         struct((features, columns), F32),
-        cost=cost(features * columns, 6 * features * columns),
+        cost=cost(features * columns, 6 * features * columns, weight=COVER),
     )
 
 
@@ -852,16 +852,19 @@
     shard2 = last_steps(jnp.concatenate([after(near2, shard1), far2], axis=2))
     parts1 = last_doubling(after(meta, shard2), shard1)
     parts2 = last_doubling(after(meta, parts1[0]), shard2)
-    dn, row_sums, col_sums = tail_sums(after(meta, parts2[0]), mine, got, far_part, own_x, mu, inv, ln_gain)
+    dn, row_sums, col_sums = tail_sums(after(meta, parts2[0], parts1[1]), mine, got, far_part, own_x, mu, inv, ln_gain)
     for delta in (1, 2):
         row_sums = row_sums + over_gate(row_sums, delta)
-    dinputs = tail(after(meta, parts2[0]), dn, row_sums, own_x, mu, inv, ln_gain, direct, features)
+    dinputs = tail(after(meta, parts2[1]), dn, row_sums, own_x, mu, inv, ln_gain, direct, features)
 
     totals = jnp.concatenate([col_sums[:2], vecs[:4]], axis=0)
+    grad_weight = place(after(meta, dinputs), parts1, parts2, n_dp, features, weight.shape[1])
     for step in range(bits):
-        totals = totals + lax.ppermute(totals, "dp", [(d, d ^ (1 << step)) for d in range(n_dp)])
-
-    grad_weight = place(meta, parts1, parts2, n_dp, features, weight.shape[1])
+        last = step == bits - 1
+        got = lax.ppermute(
+            after(totals, dinputs) if last else totals, "dp", [(d, d ^ (1 << step)) for d in range(n_dp)]
+        )
+        totals = (after(totals, grad_weight) if last else totals) + got
     return (
         hidden.reshape(rows, tokens, channels),
         dinputs.reshape(rows, tokens, channels),

time: 301 us -> 300 us (level)
  waiting for transfers between devices: 55.6 us -> 51.3 us
  starting transfers between devices: 34.8 us -> 37.9 us
    ppermute x3, waiting for transfers between devices: 7.51 us -> 2.57 us  [shards(): lax.ppermute(after(totals, dinputs) if last else totals, 'dp', [(d, d ^ 1...]
  transfers between devices with their start and end apart: 40 -> 40, of which waited for: 13 -> 10; matrix products, arithmetic and copies ran while one was open for 4% -> 3% of each run, Pallas kernels for 56% -> 60%
where the time goes in v8:
time: 300 us; the launch traced here: 299 us
  Pallas kernels  189 us (63%)
  waiting for transfers between devices  51.3 us (17%)
  starting transfers between devices  37.9 us (13%)
  local copies, waits for them, and re-layouts  13.4 us (4%)
  other arithmetic  5.72 us (2%)
    pallas_call x26, Pallas kernels, call(): pl.pallas_call(kernel, grid_spec=pltpu.PrefetchScalarGridSpec(num_scalar_...  189 us
    ppermute x16, waiting for transfers between devices, over_dp(): return lax.ppermute(value, ('dp', 'gate'), pairs)  46.4 us
    ppermute x16, starting transfers between devices, over_dp(): return lax.ppermute(value, ('dp', 'gate'), pairs)  17.9 us
    ppermute x21, starting transfers between devices, over_gate(): return lax.ppermute(value, 'gate', [(g, g ^ delta) for g in range(n_gate)])  14.7 us
    unnamed x53, local copies, waits for them, and re-layouts  9.72 us
  transfers between devices with their start and end apart: 40, of which 10 were waited for; matrix products, arithmetic and copies ran while one was open for 3% of the time, Pallas kernels for 60%

profile of v8, /device:TPU:0, one launch (start us, length us, event | category | flops | bytes accessed | tf_op | source)
XLA Modules:
  0.0 298.6 jit_solution(14399188087377631609)
XLA Ops:
  1.4 4.8 %shard_map.178 = (bf16[2048,128]{1,0:T(8,128)(2,1)}, bf16[2048,128]{1,0:T(8,128)(2,1)}, bf16[2048,384]{1,0:T(8,128)(2,1)}) custom-call(s32[36]{0:T(128)} %stack.147.meta, bf16[2048,1536]{1,0:T(8,128)(2,1)} %refs_10_.7, bf16[2048,1536]{1,0:T(8,128)(2,1)} %refs_10_.7, bf16[2048,1536]{1,0:T(8,128)(2,1)} %refs_10_.7, bf16[2048,1536]{1,0:T(8,128)(2,1)} %refs_10_.7, ...), custom_call_target="tpu_custom_call" | custom-call | bytes 5242880 | tf_op jit(solution)/shard_map/pallas_call | solution.py:20
  6.7 2.6 collective-permute-start.1
  9.3 14.8 %shard_map.179 = (bf16[2048,2048]{1,0:T(8,128)(2,1)}, f32[2048,128]{1,0:T(8,128)}, f32[2048,128]{1,0:T(8,128)}, bf16[2048,512]{1,0:T(8,128)(2,1)}, f32[2048,128]{1,0:T(8,128)}, /*index=5*/f32[2048,128]{1,0:T(8,128)}) custom-call(s32[36]{0:T(128)} %stack.147.meta, bf16[2048,2048]{1,0:T(8,128)(2,1)} %bitcast.50, f32[1,2048]{1,0:T(1,128)} %bitcast.55, ...), custom_call_target="tpu_custom_call" | custom-call | flops 671088640 | bytes 335544320 | tf_op jit(solution)/shard_map/pallas_call | solution.py:20
  24.2 4.8 %shard_map.180 = (bf16[2048,256]{1,0:T(8,128)(2,1)}, bf16[2048,256]{1,0:T(8,128)(2,1)}) custom-call(s32[36]{0:T(128)} %stack.147.meta, bf16[2048,1536]{1,0:T(8,128)(2,1)} %refs_10_.7, bf16[2048,1536]{1,0:T(8,128)(2,1)} %refs_10_.7, bf16[2048,1536]{1,0:T(8,128)(2,1)} %refs_10_.7, bf16[2048,1536]{1,0:T(8,128)(2,1)} %refs_10_.7), custom_call_target="tpu_custom_call" | custom-call | bytes 4194304 | tf_op jit(solution)/shard_map/pallas_call | solution.py:20
  29.0 1.7 collective-permute-start.3
  31.4 1.7 collective-permute-done.2.refs_5_
  35.0 12.0 %shard_map.181.u_ref = bf16[2048,768]{1,0:T(8,128)(2,1)} custom-call(s32[36]{0:T(128)} %stack.147.meta, bf16[2048,2048]{1,0:T(8,128)(2,1)} %get-tuple-element.87.normed_ref, bf16[2048,1536]{1,0:T(8,128)(2,1)} %refs_10_.7, bf16[2048,1536]{1,0:T(8,128)(2,1)} %refs_10_.7, bf16[2048,384]{1,0:T(8,128)(2,1)} %copy-done.22, bf16[2048,384]{1,0:T(8,128)(2,1)} %copy-done.22, ...), custom_call_target="tpu_custom_call" | custom-call | flops 128849018880 | bytes 293601280 | tf_op jit(solution)/shard_map/pallas_call | solution.py:20
  47.0 12.4 %shard_map.182 = (bf16[2048,512]{1,0:T(8,128)(2,1)}, bf16[2048,768]{1,0:T(8,128)(2,1)}, bf16[2048,512]{1,0:T(8,128)(2,1)}, f32[8,512]{1,0:T(8,128)}) custom-call(s32[36]{0:T(128)} %stack.147.meta, bf16[2048,768]{1,0:T(8,128)(2,1)} %shard_map.181.u_ref, bf16[2048,512]{1,0:T(8,128)(2,1)} %get-tuple-element.93.x_ref, bf16[2048,512]{1,0:T(8,128)(2,1)} %bitcast.51, ...), custom_call_target="tpu_custom_call" | custom-call | flops 629145600 | bytes 188743680 | tf_op jit(solution)/shard_map/pallas_call | solution.py:20
  59.4 8.1 %shard_map.183 = (bf16[512,768]{1,0:T(8,128)(2,1)}, bf16[512,768]{1,0:T(8,128)(2,1)}) custom-call(s32[36]{0:T(128)} %stack.147.meta, bf16[2048,2048]{1,0:T(8,128)(2,1)} %get-tuple-element.87.normed_ref, bf16[2048,768]{1,0:T(8,128)(2,1)} %get-tuple-element.96.ds_ref.ds1_ref), custom_call_target="tpu_custom_call" | custom-call | flops 64424509440 | bytes 146800640 | tf_op jit(solution)/shard_map/pallas_call | solution.py:20
  67.6 1.5 collective-permute-start.6
  69.5 8.1 %shard_map.184 = (bf16[512,768]{1,0:T(8,128)(2,1)}, bf16[512,768]{1,0:T(8,128)(2,1)}) custom-call(s32[36]{0:T(128)} %stack.147.meta, bf16[2048,2048]{1,0:T(8,128)(2,1)} %get-tuple-element.87.normed_ref, bf16[2048,768]{1,0:T(8,128)(2,1)} %get-tuple-element.96.ds_ref.ds1_ref), custom_call_target="tpu_custom_call" | custom-call | flops 64424509440 | bytes 146800640 | tf_op jit(solution)/shard_map/pallas_call | solution.py:20
  77.7 1.5 collective-permute-start.8
  79.2 12.1 %shard_map.185.u_ref = bf16[2048,768]{1,0:T(8,128)(2,1)} custom-call(s32[36]{0:T(128)} %stack.147.meta, bf16[2048,2048]{1,0:T(8,128)(2,1)} %get-tuple-element.87.normed_ref, bf16[2048,256]{1,0:T(8,128)(2,1)} %collective-permute-done.3.refs_0_.refs_1_.refs_6_.refs_7_, bf16[2048,256]{1,0:T(8,128)(2,1)} %collective-permute-done.3.refs_0_.refs_1_.refs_6_.refs_7_, ...), custom_call_target="tpu_custom_call" | custom-call | flops 128849018880 | bytes 293601280 | tf_op jit(solution)/shard_map/pallas_call | solution.py:20
  93.1 3.7 %shard_map.186 = (bf16[2,256,768]{2,1,0:T(8,128)(2,1)}, bf16[2,256,768]{2,1,0:T(8,128)(2,1)}) custom-call(s32[36]{0:T(128)} %stack.147.meta, bf16[512,768]{1,0:T(8,128)(2,1)} %get-tuple-element.99.refs_0_.refs_4_, bf16[512,768]{1,0:T(8,128)(2,1)} %copy-done.1, bf16[512,768]{1,0:T(8,128)(2,1)} %collective-permute-done.6.refs_2_.refs_6_, ...), custom_call_target="tpu_custom_call" | custom-call | flops 1572864 | bytes 4718592 | tf_op jit(solution)/shard_map/pallas_call | solution.py:20
  97.4 12.4 %shard_map.187 = (bf16[2048,512]{1,0:T(8,128)(2,1)}, bf16[2048,768]{1,0:T(8,128)(2,1)}, bf16[2048,512]{1,0:T(8,128)(2,1)}, f32[8,512]{1,0:T(8,128)}) custom-call(s32[36]{0:T(128)} %stack.147.meta, bf16[2048,768]{1,0:T(8,128)(2,1)} %shard_map.185.u_ref, ...), custom_call_target="tpu_custom_call", output_to_operand_aliasing={{0}: (7, {}), {2}: (8, {}), {3}: (9, {})} | custom-call | flops 629145600 | bytes 188743680 | tf_op jit(solution)/shard_map/pallas_call | solution.py:20
  110.8 3.0 %shard_map.188 = (bf16[2,128,768]{2,1,0:T(8,128)(2,1)}, bf16[2,128,768]{2,1,0:T(8,128)(2,1)}) custom-call(s32[36]{0:T(128)} %stack.147.meta, bf16[2,256,768]{2,1,0:T(8,128)(2,1)} %get-tuple-element.112.refs_0_.refs_2_, bf16[2,256,768]{2,1,0:T(8,128)(2,1)} %copy-done.7, bf16[2,256,768]{2,1,0:T(8,128)(2,1)} %get-tuple-element.112.refs_0_.refs_2_, ...), custom_call_target="tpu_custom_call" | custom-call | flops 786432 | bytes 2359296 | tf_op jit(solution)/shard_map/pallas_call | solution.py:20
  113.8 2.6 collective-permute-start.14
  116.4 8.1 %shard_map.189 = (bf16[512,768]{1,0:T(8,128)(2,1)}, bf16[512,768]{1,0:T(8,128)(2,1)}) custom-call(s32[36]{0:T(128)} %stack.147.meta, bf16[2048,2048]{1,0:T(8,128)(2,1)} %get-tuple-element.87.normed_ref, bf16[2048,768]{1,0:T(8,128)(2,1)} %get-tuple-element.110.ds_ref.ds2_ref), custom_call_target="tpu_custom_call" | custom-call | flops 64424509440 | bytes 146800640 | tf_op jit(solution)/shard_map/pallas_call | solution.py:20
  126.0 8.1 %shard_map.190 = (bf16[512,768]{1,0:T(8,128)(2,1)}, bf16[512,768]{1,0:T(8,128)(2,1)}) custom-call(s32[36]{0:T(128)} %stack.147.meta, bf16[2048,2048]{1,0:T(8,128)(2,1)} %get-tuple-element.87.normed_ref, bf16[2048,768]{1,0:T(8,128)(2,1)} %get-tuple-element.110.ds_ref.ds2_ref), custom_call_target="tpu_custom_call" | custom-call | flops 64424509440 | bytes 146800640 | tf_op jit(solution)/shard_map/pallas_call | solution.py:20
  135.2 8.0 %shard_map.191 = bf16[2048,512]{1,0:T(8,128)(2,1)} custom-call(s32[36]{0:T(128)} %stack.147.meta, bf16[2048,768]{1,0:T(8,128)(2,1)} %get-tuple-element.96.ds_ref.ds1_ref, bf16[2048,768]{1,0:T(8,128)(2,1)} %get-tuple-element.110.ds_ref.ds2_ref, bf16[2048,1536]{1,0:T(8,128)(2,1)} %refs_10_.7, bf16[2048,1536]{1,0:T(8,128)(2,1)} %refs_10_.7, ...), custom_call_target="tpu_custom_call" | custom-call | flops 64424509440 | bytes 125829120 | tf_op jit(solution)/shard_map/pallas_call | solution.py:20
  143.3 3.4 %collective-permute-done.13.refs_3_.refs_7_ = bf16[512,768]{1,0:T(8,128)(2,1)S(1)} collective-permute-done((bf16[512,768]{1,0:T(8,128)(2,1)S(1)}, bf16[512,768]{1,0:T(8,128)(2,1)S(1)}, u32[]{:S(2)}, u32[]{:S(2)}) %collective-permute-start.13) | collective-permute-done | bytes 786464 | tf_op jit(solution)/shard_map/ppermute | solution.py:769
  147.6 3.7 %shard_map.192 = (bf16[2,256,768]{2,1,0:T(8,128)(2,1)}, bf16[2,256,768]{2,1,0:T(8,128)(2,1)}) custom-call(s32[36]{0:T(128)} %stack.147.meta, bf16[512,768]{1,0:T(8,128)(2,1)} %get-tuple-element.117.refs_0_.refs_4_, bf16[512,768]{1,0:T(8,128)(2,1)} %copy-done.2, bf16[512,768]{1,0:T(8,128)(2,1)} %copy-done, bf16[512,768]{1,0:T(8,128)(2,1)} %copy-done.4, ...), custom_call_target="tpu_custom_call" | custom-call | flops 1572864 | bytes 4718592 | tf_op jit(solution)/shard_map/pallas_call | solution.py:20
  151.8 2.6 shard_map.193
  154.5 1.5 collective-permute-start.17
  156.0 8.3 %shard_map.194 = bf16[2048,512]{1,0:T(8,128)(2,1)} custom-call(s32[36]{0:T(128)} %stack.147.meta, bf16[2048,768]{1,0:T(8,128)(2,1)} %get-tuple-element.96.ds_ref.ds1_ref, bf16[2048,768]{1,0:T(8,128)(2,1)} %get-tuple-element.110.ds_ref.ds2_ref, bf16[2048,1536]{1,0:T(8,128)(2,1)} %refs_10_.7, bf16[2048,1536]{1,0:T(8,128)(2,1)} %refs_10_.7, ...), custom_call_target="tpu_custom_call" | custom-call | flops 64424509440 | bytes 125829120 | tf_op jit(solution)/shard_map/pallas_call | solution.py:20
  165.1 3.2 %shard_map.195 = (bf16[2,128,768]{2,1,0:T(8,128)(2,1)}, bf16[2,128,768]{2,1,0:T(8,128)(2,1)}) custom-call(s32[36]{0:T(128)} %stack.147.meta, bf16[2,256,768]{2,1,0:T(8,128)(2,1)} %get-tuple-element.128.refs_0_.refs_2_, bf16[2,256,768]{2,1,0:T(8,128)(2,1)} %copy-done.6, bf16[2,256,768]{2,1,0:T(8,128)(2,1)} %get-tuple-element.128.refs_0_.refs_2_, ...), custom_call_target="tpu_custom_call" | custom-call | flops 786432 | bytes 2359296 | tf_op jit(solution)/shard_map/pallas_call | solution.py:20
  170.4 3.0 add_convert_fusion
  173.3 8.2 %shard_map.196 = bf16[2048,512]{1,0:T(8,128)(2,1)} custom-call(s32[36]{0:T(128)} %stack.147.meta, bf16[2048,768]{1,0:T(8,128)(2,1)} %get-tuple-element.96.ds_ref.ds1_ref, bf16[2048,768]{1,0:T(8,128)(2,1)} %get-tuple-element.110.ds_ref.ds2_ref, bf16[2048,1536]{1,0:T(8,128)(2,1)} %refs_10_.7, bf16[2048,1536]{1,0:T(8,128)(2,1)} %refs_10_.7, ...), custom_call_target="tpu_custom_call" | custom-call | flops 64424509440 | bytes 125829120 | tf_op jit(solution)/shard_map/pallas_call | solution.py:20
  181.6 2.7 collective-permute-start.20
  184.2 3.5 %collective-permute-start.27 = (bf16[2048,512]{1,0:T(8,128)(2,1)}, bf16[2048,512]{1,0:T(8,128)(2,1)S(1)}, u32[]{:S(2)}, u32[]{:S(2)}) collective-permute-start(bf16[2048,512]{1,0:T(8,128)(2,1)} %shard_map.196), channel_id=1, source_target_pairs={{0,1},{1,0},{2,3},{3,2},{4,5},{5,4},{6,7},{7,6},{8,9},{9,8},{10,11... | collective-permute-start | bytes 6291464 | tf_op jit(solution)/shard_map/ppermute | solution.py:763
  187.7 8.0 %shard_map.197.k_ref = bf16[2048,512]{1,0:T(8,128)(2,1)} custom-call(s32[36]{0:T(128)} %stack.147.meta, bf16[2048,768]{1,0:T(8,128)(2,1)} %get-tuple-element.96.ds_ref.ds1_ref, bf16[2048,768]{1,0:T(8,128)(2,1)} %get-tuple-element.110.ds_ref.ds2_ref, bf16[2048,1536]{1,0:T(8,128)(2,1)} %refs_10_.7, bf16[2048,1536]{1,0:T(8,128)(2,1)} %refs_10_.7, ...), custom_call_target="tpu_custom_call" | custom-call | flops 64424509440 | bytes 125829120 | tf_op jit(solution)/shard_map/pallas_call | solution.py:20
  195.8 1.7 collective-permute-done.19.b_ref
  197.5 2.6 shard_map.198
  200.4 5.5 %collective-permute-done.20 = bf16[2,128,768]{2,1,0:T(8,128)(2,1)} collective-permute-done((bf16[2,128,768]{2,1,0:T(8,128)(2,1)S(1)}, bf16[2,128,768]{2,1,0:T(8,128)(2,1)}, u32[]{:S(2)}, u32[]{:S(2)}) %collective-permute-start.20) | collective-permute-done | bytes 393248 | tf_op jit(solution)/shard_map/ppermute | solution.py:769
  208.7 2.8 collective-permute-start.23
  212.0 16.5 %collective-permute-done.22 = bf16[2,128,768]{2,1,0:T(8,128)(2,1)S(1)} collective-permute-done((bf16[2,128,768]{2,1,0:T(8,128)(2,1)S(1)}, bf16[2,128,768]{2,1,0:T(8,128)(2,1)S(1)}, u32[]{:S(2)}, u32[]{:S(2)}) %collective-permute-start.22) | collective-permute-done | bytes 393248 | tf_op jit(solution)/shard_map/ppermute | solution.py:769
  230.0 3.3 %shard_map.199 = (bf16[512,768]{1,0:T(8,128)(2,1)}, bf16[512,768]{1,0:T(8,128)(2,1)}) custom-call(s32[36]{0:T(128)} %stack.147.meta, bf16[2,256,768]{2,1,0:T(8,128)(2,1)} %copy-done.10, bf16[2,256,768]{2,1,0:T(8,128)(2,1)} %collective-permute-done.23.b_ref), custom_call_target="tpu_custom_call" | custom-call | bytes 3145728 | tf_op jit(solution)/shard_map/pallas_call | solution.py:20
  233.2 1.6 collective-permute-start.26
  235.3 11.0 %collective-permute-done.24.b_ref = bf16[2,256,768]{2,1,0:T(8,128)(2,1)} collective-permute-done((bf16[2,256,768]{2,1,0:T(8,128)(2,1)S(1)}, bf16[2,256,768]{2,1,0:T(8,128)(2,1)}, u32[]{:S(2)}, u32[]{:S(2)}) %collective-permute-start.24) | collective-permute-done | bytes 786464 | tf_op jit(solution)/shard_map/ppermute | solution.py:769
  246.3 3.2 %shard_map.200 = (bf16[512,768]{1,0:T(8,128)(2,1)}, bf16[512,768]{1,0:T(8,128)(2,1)}) custom-call(s32[36]{0:T(128)} %stack.147.meta, bf16[2,256,768]{2,1,0:T(8,128)(2,1)} %copy-done.5, bf16[2,256,768]{2,1,0:T(8,128)(2,1)} %collective-permute-done.24.b_ref), custom_call_target="tpu_custom_call" | custom-call | bytes 3145728 | tf_op jit(solution)/shard_map/pallas_call | solution.py:20
  250.9 9.5 %shard_map.201 = (f32[2048,512]{1,0:T(8,128)}, f32[8,2048]{1,0:T(8,128)}, f32[8,512]{1,0:T(8,128)}) custom-call(s32[36]{0:T(128)} %stack.147.meta, bf16[2048,512]{1,0:T(8,128)(2,1)} %shard_map.197.k_ref, bf16[2048,512]{1,0:T(8,128)(2,1)} %copy-done.9, bf16[512,512]{1,0:T(8,128)(2,1)} %copy-done.15, bf16[1536,512]{1,0:T(8,128)(2,1)} %collective-permute-done.28.r2_ref, ...), custom_call_target="tpu_custom_call" | custom-call | flops 419430400 | bytes 251658240 | tf_op jit(solution)/shard_map/pallas_call | solution.py:20
  261.2 2.1 collective-permute-start.37
  264.1 1.7 collective-permute-start.30
  267.3 2.6 collective-permute-done.38
  271.1 6.9 %collective-permute-done.25.refs_5_ = bf16[512,768]{1,0:T(8,128)(2,1)S(1)} collective-permute-done((bf16[512,768]{1,0:T(8,128)(2,1)S(1)}, bf16[512,768]{1,0:T(8,128)(2,1)S(1)}, u32[]{:S(2)}, u32[]{:S(2)}) %collective-permute-start.25) | collective-permute-done | bytes 786464 | tf_op jit(solution)/shard_map/ppermute | solution.py:769
  278.0 7.4 %shard_map.202 = bf16[2048,512]{1,0:T(8,128)(2,1)} custom-call(s32[36]{0:T(128)} %stack.147.meta, f32[2048,512]{1,0:T(8,128)} %get-tuple-element.149.dn_ref, f32[8,2048]{1,0:T(8,128)} %add.126.row_ref, bf16[2048,512]{1,0:T(8,128)(2,1)} %get-tuple-element.93.x_ref, f32[2048,128]{1,0:T(8,128)} %get-tuple-element.147.mu_ref, ...), custom_call_target="tpu_custom_call" | custom-call | flops 10485760 | bytes 12582912 | tf_op jit(solution)/shard_map/pallas_call | solution.py:20
  285.5 3.1 %collective-permute-start.39 = (f32[6,512]{1,0:T(8,128)S(1)}, f32[6,512]{1,0:T(8,128)S(1)}, u32[]{:S(2)}, u32[]{:S(2)}) collective-permute-start(f32[6,512]{1,0:T(8,128)S(1)} %add.128), channel_id=1, source_target_pairs={{0,16},{4,20},{8,24},{12,28},{16,0},{20,4},{24,8},{28,12},{1,17},{... | collective-permute-start | bytes 36872 | tf_op jit(solution)/shard_map/ppermute | solution.py:864
  289.5 8.5 %shard_map.203 = f32[2048,1536]{1,0:T(8,128)} custom-call(s32[36]{0:T(128)} %stack.147.meta, bf16[512,768]{1,0:T(8,128)(2,1)} %get-tuple-element.142.refs_0_, bf16[512,768]{1,0:T(8,128)(2,1)} %copy-done.11, bf16[512,768]{1,0:T(8,128)(2,1)} %copy-done.14, bf16[512,768]{1,0:T(8,128)(2,1)} %collective-permute-done.33.refs_3_, ...), custom_call_target="tpu_custom_call" | custom-call | flops 62914560 | bytes 377487360 | tf_op jit(solution)/shard_map/pallas_call | solution.py:20
  (129 shorter events, 27.1 us)
Async XLA Ops:
  6.2 26.9 %collective-permute-start = (bf16[2048,384]{1,0:T(8,128)(2,1)}, bf16[2048,384]{1,0:T(8,128)(2,1)S(1)}, u32[]{:S(2)}, u32[]{:S(2)}) collective-permute-start(bf16[2048,384]{1,0:T(8,128)(2,1)} %get-tuple-element.92), channel_id=1, source_target_pairs={{0,1},{1,0},{2,3},{3,2},{4,5},{5,4},{6,7},{7,6},{8,9},{9,8},{10,11... | collective-permute-start | bytes 4718600 | tf_op jit(solution)/shard_map/ppermute | solution.py:763
  6.7 24.7 %collective-permute-start.1 = (bf16[2048,128]{1,0:T(8,128)(2,1)}, bf16[2048,128]{1,0:T(8,128)(2,1)S(1)}, u32[]{:S(2)}, u32[]{:S(2)}) collective-permute-start(bf16[2048,128]{1,0:T(8,128)(2,1)} %get-tuple-element.84), channel_id=1, source_target_pairs={{0,2},{1,3},{2,0},{3,1},{4,6},{5,7},{6,4},{7,5},{8,10},{9,11},{10,... | collective-permute-start | bytes 1572872 | tf_op jit(solution)/shard_map/ppermute | solution.py:763
  9.2 23.9 %collective-permute-start.2 = (bf16[2048,128]{1,0:T(8,128)(2,1)}, bf16[2048,128]{1,0:T(8,128)(2,1)S(1)}, u32[]{:S(2)}, u32[]{:S(2)}) collective-permute-start(bf16[2048,128]{1,0:T(8,128)(2,1)} %get-tuple-element.85), channel_id=1, source_target_pairs={{0,3},{1,2},{2,1},{3,0},{4,7},{5,6},{6,5},{7,4},{8,11},{9,10},{10,... | collective-permute-start | bytes 1572872 | tf_op jit(solution)/shard_map/ppermute | solution.py:763
  24.1 6.6 %copy-start.18 = (f32[512]{0:T(512)S(1)}, f32[512]{0:T(512)}, u32[]{:S(2)}) copy-start(f32[512]{0:T(512)} %param.15) | copy-start | bytes 6148
  29.0 50.2 %collective-permute-start.3 = (bf16[2048,256]{1,0:T(8,128)(2,1)}, bf16[2048,256]{1,0:T(8,128)(2,1)}, u32[]{:S(2)}, u32[]{:S(2)}) collective-permute-start(bf16[2048,256]{1,0:T(8,128)(2,1)} %get-tuple-element.89), channel_id=1, source_target_pairs={{0,2},{1,3},{2,0},{3,1},{4,6},{5,7},{6,4},{7,5},{8,10},{9,11},{10,... | collective-permute-start | bytes 3145736 | tf_op jit(solution)/shard_map/ppermute | solution.py:763
  30.7 48.5 %collective-permute-start.4 = (bf16[2048,256]{1,0:T(8,128)(2,1)}, bf16[2048,256]{1,0:T(8,128)(2,1)}, u32[]{:S(2)}, u32[]{:S(2)}) collective-permute-start(bf16[2048,256]{1,0:T(8,128)(2,1)} %get-tuple-element.90), channel_id=1, source_target_pairs={{0,3},{1,2},{2,1},{3,0},{4,7},{5,6},{6,5},{7,4},{8,11},{9,10},{10,... | collective-permute-start | bytes 3145736 | tf_op jit(solution)/shard_map/ppermute | solution.py:763
  67.6 23.8 %collective-permute-start.6 = (bf16[512,768]{1,0:T(8,128)(2,1)}, bf16[512,768]{1,0:T(8,128)(2,1)}, u32[]{:S(2)}, u32[]{:S(2)}) collective-permute-start(bf16[512,768]{1,0:T(8,128)(2,1)} %get-tuple-element.97), channel_id=1, source_target_pairs={{0,4},{1,9},{2,6},{3,11},{4,0},{5,13},{6,2},{7,15},{8,12},{9,1},{1... | collective-permute-start | bytes 2359304 | tf_op jit(solution)/shard_map/ppermute | solution.py:769
  69.1 8.6 %collective-permute-start.7 = (bf16[512,768]{1,0:T(8,128)(2,1)}, bf16[512,768]{1,0:T(8,128)(2,1)S(1)}, u32[]{:S(2)}, u32[]{:S(2)}) collective-permute-start(bf16[512,768]{1,0:T(8,128)(2,1)} %get-tuple-element.103), channel_id=1, source_target_pairs={{0,1},{1,0},{2,3},{3,2},{4,5},{5,4},{6,7},{7,6},{8,9},{9,8},{10,11... | collective-permute-start | bytes 2359304 | tf_op jit(solution)/shard_map/ppermute | solution.py:763
  77.7 13.7 %collective-permute-start.5 = (bf16[512,768]{1,0:T(8,128)(2,1)}, bf16[512,768]{1,0:T(8,128)(2,1)S(1)}, u32[]{:S(2)}, u32[]{:S(2)}) collective-permute-start(bf16[512,768]{1,0:T(8,128)(2,1)} %get-tuple-element.102), channel_id=1, source_target_pairs={{0,1},{1,0},{2,3},{3,2},{4,5},{5,4},{6,7},{7,6},{8,9},{9,8},{10,11... | collective-permute-start | bytes 2359304 | tf_op jit(solution)/shard_map/ppermute | solution.py:763
  77.7 13.7 %collective-permute-start.8 = (bf16[512,768]{1,0:T(8,128)(2,1)S(1)}, bf16[512,768]{1,0:T(8,128)(2,1)S(1)}, u32[]{:S(2)}, u32[]{:S(2)}) collective-permute-start(bf16[512,768]{1,0:T(8,128)(2,1)S(1)} %collective-permute-done.7), channel_id=1, source_target_pairs={{0,4},{1,9},{2,6},{3,11},{4,0},{5,13},{6,2},{7,15},{8,12},{9,1},{1... | collective-permute-start | bytes 2359304 | tf_op jit(solution)/shard_map/ppermute | solution.py:769
  96.9 13.0 %collective-permute-start.9 = (bf16[2,256,768]{2,1,0:T(8,128)(2,1)}, bf16[2,256,768]{2,1,0:T(8,128)(2,1)S(1)}, u32[]{:S(2)}, u32[]{:S(2)}) collective-permute-start(bf16[2,256,768]{2,1,0:T(8,128)(2,1)} %get-tuple-element.104), channel_id=1, source_target_pairs={{0,8},{1,5},{2,10},{3,7},{4,12},{5,1},{6,14},{7,3},{8,0},{9,13},{1... | collective-permute-start | bytes 2359304 | tf_op jit(solution)/shard_map/ppermute | solution.py:769
  113.8 38.0 %collective-permute-start.14 = (bf16[2,128,768]{2,1,0:T(8,128)(2,1)}, bf16[2,128,768]{2,1,0:T(8,128)(2,1)}, u32[]{:S(2)}, u32[]{:S(2)}) collective-permute-start(bf16[2,128,768]{2,1,0:T(8,128)(2,1)} %get-tuple-element.113), channel_id=1, source_target_pairs={{0,16},{1,17},{2,18},{3,19},{4,20},{5,21},{6,22},{7,23},{8,24},{9,... | collective-permute-start | bytes 1179656 | tf_op jit(solution)/shard_map/ppermute | solution.py:769
  124.5 18.7 %collective-permute-start.11 = (bf16[512,768]{1,0:T(8,128)(2,1)}, bf16[512,768]{1,0:T(8,128)(2,1)S(1)}, u32[]{:S(2)}, u32[]{:S(2)}) collective-permute-start(bf16[512,768]{1,0:T(8,128)(2,1)} %get-tuple-element.115), channel_id=1, source_target_pairs={{0,4},{1,9},{2,6},{3,11},{4,0},{5,13},{6,2},{7,15},{8,12},{9,1},{1... | collective-permute-start | bytes 2359304 | tf_op jit(solution)/shard_map/ppermute | solution.py:769
  126.0 8.6 %collective-permute-start.12 = (bf16[512,768]{1,0:T(8,128)(2,1)}, bf16[512,768]{1,0:T(8,128)(2,1)S(1)}, u32[]{:S(2)}, u32[]{:S(2)}) collective-permute-start(bf16[512,768]{1,0:T(8,128)(2,1)} %get-tuple-element.121), channel_id=1, source_target_pairs={{0,1},{1,0},{2,3},{3,2},{4,5},{5,4},{6,7},{7,6},{8,9},{9,8},{10,11... | collective-permute-start | bytes 2359304 | tf_op jit(solution)/shard_map/ppermute | solution.py:763
  134.1 9.1 %collective-permute-start.10 = (bf16[512,768]{1,0:T(8,128)(2,1)}, bf16[512,768]{1,0:T(8,128)(2,1)S(1)}, u32[]{:S(2)}, u32[]{:S(2)}) collective-permute-start(bf16[512,768]{1,0:T(8,128)(2,1)} %get-tuple-element.120), channel_id=1, source_target_pairs={{0,1},{1,0},{2,3},{3,2},{4,5},{5,4},{6,7},{7,6},{8,9},{9,8},{10,11... | collective-permute-start | bytes 2359304 | tf_op jit(solution)/shard_map/ppermute | solution.py:763
  134.7 12.0 %collective-permute-start.13 = (bf16[512,768]{1,0:T(8,128)(2,1)S(1)}, bf16[512,768]{1,0:T(8,128)(2,1)S(1)}, u32[]{:S(2)}, u32[]{:S(2)}) collective-permute-start(bf16[512,768]{1,0:T(8,128)(2,1)S(1)} %collective-permute-done.12), channel_id=1, source_target_pairs={{0,4},{1,9},{2,6},{3,11},{4,0},{5,13},{6,2},{7,15},{8,12},{9,1},{1... | collective-permute-start | bytes 2359304 | tf_op jit(solution)/shard_map/ppermute | solution.py:769
  143.2 25.4 %collective-permute-start.16 = (bf16[2048,512]{1,0:T(8,128)(2,1)}, bf16[2048,512]{1,0:T(8,128)(2,1)}, u32[]{:S(2)}, u32[]{:S(2)}) collective-permute-start(bf16[2048,512]{1,0:T(8,128)(2,1)} %shard_map.191), channel_id=1, source_target_pairs={{0,1},{1,0},{2,3},{3,2},{4,5},{5,4},{6,7},{7,6},{8,9},{9,8},{10,11... | collective-permute-start | bytes 6291464 | tf_op jit(solution)/shard_map/ppermute | solution.py:763
  151.3 12.9 %collective-permute-start.15 = (bf16[2,256,768]{2,1,0:T(8,128)(2,1)}, bf16[2,256,768]{2,1,0:T(8,128)(2,1)S(1)}, u32[]{:S(2)}, u32[]{:S(2)}) collective-permute-start(bf16[2,256,768]{2,1,0:T(8,128)(2,1)} %get-tuple-element.122), channel_id=1, source_target_pairs={{0,8},{1,5},{2,10},{3,7},{4,12},{5,1},{6,14},{7,3},{8,0},{9,13},{1... | collective-permute-start | bytes 2359304 | tf_op jit(solution)/shard_map/ppermute | solution.py:769
  154.5 27.1 %collective-permute-start.17 = (bf16[2,128,256]{2,1,0:T(8,128)(2,1)}, bf16[2,128,256]{2,1,0:T(8,128)(2,1)S(1)}, u32[]{:S(2)}, u32[]{:S(2)}) collective-permute-start(bf16[2,128,256]{2,1,0:T(8,128)(2,1)} %get-tuple-element.133), channel_id=1, source_target_pairs={{0,2},{1,3},{2,0},{3,1},{4,6},{5,7},{6,4},{7,5},{8,10},{9,11},{10,... | collective-permute-start | bytes 393224 | tf_op jit(solution)/shard_map/ppermute | solution.py:763
  168.3 29.2 %collective-permute-start.19 = (bf16[2,128,768]{2,1,0:T(8,128)(2,1)}, bf16[2,128,768]{2,1,0:T(8,128)(2,1)}, u32[]{:S(2)}, u32[]{:S(2)}) collective-permute-start(bf16[2,128,768]{2,1,0:T(8,128)(2,1)} %get-tuple-element.129), channel_id=1, source_target_pairs={{0,16},{1,17},{2,18},{3,19},{4,20},{5,21},{6,22},{7,23},{8,24},{9,... | collective-permute-start | bytes 1179656 | tf_op jit(solution)/shard_map/ppermute | solution.py:769
  169.8 26.0 %collective-permute-start.18 = (bf16[512,512]{1,0:T(8,128)(2,1)S(1)}, bf16[512,512]{1,0:T(8,128)(2,1)S(1)}, u32[]{:S(2)}, u32[]{:S(2)}) collective-permute-start(bf16[512,512]{1,0:T(8,128)(2,1)S(1)} %add_convert_fusion.1), channel_id=1, source_target_pairs={{0,2},{1,3},{2,0},{3,1},{4,6},{5,7},{6,4},{7,5},{8,10},{9,11},{10,... | collective-permute-start | bytes 1572872 | tf_op jit(solution)/shard_map/ppermute | solution.py:763
  173.3 8.2 %copy-start.16 = (bf16[2,128,512]{2,1,0:T(8,128)(2,1)S(1)}, bf16[2,128,512]{2,1,0:T(8,128)(2,1)}, u32[]{:S(2)}) copy-start(bf16[2,128,512]{2,1,0:T(8,128)(2,1)} %get-tuple-element.132) | copy-start | bytes 786436
  181.6 24.3 %collective-permute-start.20 = (bf16[2,128,768]{2,1,0:T(8,128)(2,1)S(1)}, bf16[2,128,768]{2,1,0:T(8,128)(2,1)}, u32[]{:S(2)}, u32[]{:S(2)}) collective-permute-start(bf16[2,128,768]{2,1,0:T(8,128)(2,1)S(1)} %constant_dynamic-update-slice_fusion), channel_id=1, source_target_pairs={{0,16},{1,17},{2,18},{3,19},{4,20},{5,21},{6,22},{7,23},{8,24},{9,... | collective-permute-start | bytes 1179656 | tf_op jit(solution)/shard_map/ppermute | solution.py:769
  184.2 65.3 %collective-permute-start.27 = (bf16[2048,512]{1,0:T(8,128)(2,1)}, bf16[2048,512]{1,0:T(8,128)(2,1)S(1)}, u32[]{:S(2)}, u32[]{:S(2)}) collective-permute-start(bf16[2048,512]{1,0:T(8,128)(2,1)} %shard_map.196), channel_id=1, source_target_pairs={{0,1},{1,0},{2,3},{3,2},{4,5},{5,4},{6,7},{7,6},{8,9},{9,8},{10,11... | collective-permute-start | bytes 6291464 | tf_op jit(solution)/shard_map/ppermute | solution.py:763
  200.1 8.5 %collective-permute-start.21 = (bf16[2,128,512]{2,1,0:T(8,128)(2,1)}, bf16[2,128,512]{2,1,0:T(8,128)(2,1)S(1)}, u32[]{:S(2)}, u32[]{:S(2)}) collective-permute-start(bf16[2,128,512]{2,1,0:T(8,128)(2,1)} %get-tuple-element.140), channel_id=1, source_target_pairs={{0,2},{1,3},{2,0},{3,1},{4,6},{5,7},{6,4},{7,5},{8,10},{9,11},{10,... | collective-permute-start | bytes 786440 | tf_op jit(solution)/shard_map/ppermute | solution.py:763
  206.9 23.1 %copy-start.10 = (bf16[2,256,768]{2,1,0:T(8,128)(2,1)}, bf16[2,256,768]{2,1,0:T(8,128)(2,1)S(1)}, u32[]{:S(2)}) copy-start(bf16[2,256,768]{2,1,0:T(8,128)(2,1)S(1)} %constant_dynamic-update-slice_fusion.2.a_ref) | copy-start | bytes 2359300
  208.6 40.9 %copy-start.17 = (f32[8,512]{1,0:T(8,128)S(1)}, f32[8,512]{1,0:T(8,128)}, u32[]{:S(2)}) copy-start(f32[8,512]{1,0:T(8,128)} %get-tuple-element.156) | copy-start | bytes 49156
  208.6 19.8 %collective-permute-start.22 = (bf16[2,128,768]{2,1,0:T(8,128)(2,1)S(1)}, bf16[2,128,768]{2,1,0:T(8,128)(2,1)S(1)}, u32[]{:S(2)}, u32[]{:S(2)}) collective-permute-start(bf16[2,128,768]{2,1,0:T(8,128)(2,1)S(1)} %constant_dynamic-update-slice_fusion.4), channel_id=1, source_target_pairs={{0,16},{1,17},{2,18},{3,19},{4,20},{5,21},{6,22},{7,23},{8,24},{9,... | collective-permute-start | bytes 1179656 | tf_op jit(solution)/shard_map/ppermute | solution.py:769
  208.7 21.3 %collective-permute-start.23 = (bf16[2,256,768]{2,1,0:T(8,128)(2,1)S(1)}, bf16[2,256,768]{2,1,0:T(8,128)(2,1)}, u32[]{:S(2)}, u32[]{:S(2)}) collective-permute-start(bf16[2,256,768]{2,1,0:T(8,128)(2,1)S(1)} %constant_dynamic-update-slice_fusion.2.a_ref), channel_id=1, source_target_pairs={{0,8},{1,5},{2,10},{3,7},{4,12},{5,1},{6,14},{7,3},{8,0},{9,13},{1... | collective-permute-start | bytes 2359304 | tf_op jit(solution)/shard_map/ppermute | solution.py:769
  211.5 38.1 %collective-permute-start.28 = (bf16[1536,512]{1,0:T(8,128)(2,1)}, bf16[1536,512]{1,0:T(8,128)(2,1)}, u32[]{:S(2)}, u32[]{:S(2)}) collective-permute-start(bf16[1536,512]{1,0:T(8,128)(2,1)} %add_convert_fusion), channel_id=1, source_target_pairs={{0,2},{1,3},{2,0},{3,1},{4,6},{5,7},{6,4},{7,5},{8,10},{9,11},{10,... | collective-permute-start | bytes 4718600 | tf_op jit(solution)/shard_map/ppermute | solution.py:763
  228.5 17.8 %copy-start.5 = (bf16[2,256,768]{2,1,0:T(8,128)(2,1)}, bf16[2,256,768]{2,1,0:T(8,128)(2,1)S(1)}, u32[]{:S(2)}) copy-start(bf16[2,256,768]{2,1,0:T(8,128)(2,1)S(1)} %pad_maximum_fusion.a_ref) | copy-start | bytes 2359300
  228.5 17.8 %collective-permute-start.24 = (bf16[2,256,768]{2,1,0:T(8,128)(2,1)S(1)}, bf16[2,256,768]{2,1,0:T(8,128)(2,1)}, u32[]{:S(2)}, u32[]{:S(2)}) collective-permute-start(bf16[2,256,768]{2,1,0:T(8,128)(2,1)S(1)} %pad_maximum_fusion.a_ref), channel_id=1, source_target_pairs={{0,8},{1,5},{2,10},{3,7},{4,12},{5,1},{6,14},{7,3},{8,0},{9,13},{1... | collective-permute-start | bytes 2359304 | tf_op jit(solution)/shard_map/ppermute | solution.py:769
  233.2 16.3 %collective-permute-start.26 = (bf16[512,768]{1,0:T(8,128)(2,1)}, bf16[512,768]{1,0:T(8,128)(2,1)S(1)}, u32[]{:S(2)}, u32[]{:S(2)}) collective-permute-start(bf16[512,768]{1,0:T(8,128)(2,1)} %get-tuple-element.142.refs_0_), channel_id=1, source_target_pairs={{0,4},{1,9},{2,6},{3,11},{4,0},{5,13},{6,2},{7,15},{8,12},{9,1},{1... | collective-permute-start | bytes 2359304 | tf_op jit(solution)/shard_map/ppermute | solution.py:769
  234.9 32.3 %collective-permute-start.32 = (bf16[512,768]{1,0:T(8,128)(2,1)}, bf16[512,768]{1,0:T(8,128)(2,1)}, u32[]{:S(2)}, u32[]{:S(2)}) collective-permute-start(bf16[512,768]{1,0:T(8,128)(2,1)} %get-tuple-element.153), channel_id=1, source_target_pairs={{0,4},{1,9},{2,6},{3,11},{4,0},{5,13},{6,2},{7,15},{8,12},{9,1},{1... | collective-permute-start | bytes 2359304 | tf_op jit(solution)/shard_map/ppermute | solution.py:769
  249.5 20.8 %collective-permute-start.35 = (bf16[512,768]{1,0:T(8,128)(2,1)}, bf16[512,768]{1,0:T(8,128)(2,1)}, u32[]{:S(2)}, u32[]{:S(2)}) collective-permute-start(bf16[512,768]{1,0:T(8,128)(2,1)} %get-tuple-element.154), channel_id=1, source_target_pairs={{0,4},{1,9},{2,6},{3,11},{4,0},{5,13},{6,2},{7,15},{8,12},{9,1},{1... | collective-permute-start | bytes 2359304 | tf_op jit(solution)/shard_map/ppermute | solution.py:769
  249.5 35.9 %copy-start.11 = (bf16[512,768]{1,0:T(8,128)(2,1)}, bf16[512,768]{1,0:T(8,128)(2,1)S(1)}, u32[]{:S(2)}) copy-start(bf16[512,768]{1,0:T(8,128)(2,1)S(1)} %collective-permute-done.26.refs_1_) | copy-start | bytes 2359300
  250.9 15.0 %copy-start.12 = (bf16[512,768]{1,0:T(8,128)(2,1)S(1)}, bf16[512,768]{1,0:T(8,128)(2,1)}, u32[]{:S(2)}) copy-start(bf16[512,768]{1,0:T(8,128)(2,1)} %get-tuple-element.144.refs_4_) | copy-start | bytes 2359300
  261.2 2.1 collective-permute-start.29
  261.2 4.7 %collective-permute-start.37 = (f32[6,512]{1,0:T(8,128)S(1)}, f32[6,512]{1,0:T(8,128)S(1)}, u32[]{:S(2)}, u32[]{:S(2)}) collective-permute-start(f32[6,512]{1,0:T(8,128)S(1)} %pad_maximum_fusion.1), channel_id=1, source_target_pairs={{0,4},{4,0},{8,12},{12,8},{16,20},{20,16},{24,28},{28,24},{1,5},{5... | collective-permute-start | bytes 36872 | tf_op jit(solution)/shard_map/ppermute | solution.py:864
  264.1 5.7 %collective-permute-start.30 = (f32[8,2048]{1,0:T(8,128)S(1)}, f32[8,2048]{1,0:T(8,128)S(1)}, u32[]{:S(2)}, u32[]{:S(2)}) collective-permute-start(f32[8,2048]{1,0:T(8,128)S(1)} %add.125), channel_id=1, source_target_pairs={{0,2},{1,3},{2,0},{3,1},{4,6},{5,7},{6,4},{7,5},{8,10},{9,11},{10,... | collective-permute-start | bytes 196616 | tf_op jit(solution)/shard_map/ppermute | solution.py:763
  265.9 4.0 %collective-permute-start.38 = (f32[6,512]{1,0:T(8,128)S(1)}, f32[6,512]{1,0:T(8,128)S(1)}, u32[]{:S(2)}, u32[]{:S(2)}) collective-permute-start(f32[6,512]{1,0:T(8,128)S(1)} %fusion), channel_id=1, source_target_pairs={{0,8},{4,12},{8,0},{12,4},{16,24},{20,28},{24,16},{28,20},{1,9},{5... | collective-permute-start | bytes 36872 | tf_op jit(solution)/shard_map/ppermute | solution.py:864
  266.0 12.1 %collective-permute-start.25 = (bf16[512,768]{1,0:T(8,128)(2,1)S(1)}, bf16[512,768]{1,0:T(8,128)(2,1)S(1)}, u32[]{:S(2)}, u32[]{:S(2)}) collective-permute-start(bf16[512,768]{1,0:T(8,128)(2,1)S(1)} %copy-done.12), channel_id=1, source_target_pairs={{0,4},{1,9},{2,6},{3,11},{4,0},{5,13},{6,2},{7,15},{8,12},{9,1},{1... | collective-permute-start | bytes 2359304 | tf_op jit(solution)/shard_map/ppermute | solution.py:769
  267.2 21.4 %collective-permute-start.31 = (bf16[512,768]{1,0:T(8,128)(2,1)}, bf16[512,768]{1,0:T(8,128)(2,1)S(1)}, u32[]{:S(2)}, u32[]{:S(2)}) collective-permute-start(bf16[512,768]{1,0:T(8,128)(2,1)} %get-tuple-element.153), channel_id=1, source_target_pairs={{0,1},{1,0},{2,3},{3,2},{4,5},{5,4},{6,7},{7,6},{8,9},{9,8},{10,11... | collective-permute-start | bytes 2359304 | tf_op jit(solution)/shard_map/ppermute | solution.py:763
  269.8 18.8 %collective-permute-start.34 = (bf16[512,768]{1,0:T(8,128)(2,1)}, bf16[512,768]{1,0:T(8,128)(2,1)}, u32[]{:S(2)}, u32[]{:S(2)}) collective-permute-start(bf16[512,768]{1,0:T(8,128)(2,1)} %get-tuple-element.154), channel_id=1, source_target_pairs={{0,1},{1,0},{2,3},{3,2},{4,5},{5,4},{6,7},{7,6},{8,9},{9,8},{10,11... | collective-permute-start | bytes 2359304 | tf_op jit(solution)/shard_map/ppermute | solution.py:763
  269.8 18.8 %collective-permute-start.33 = (bf16[512,768]{1,0:T(8,128)(2,1)}, bf16[512,768]{1,0:T(8,128)(2,1)}, u32[]{:S(2)}, u32[]{:S(2)}) collective-permute-start(bf16[512,768]{1,0:T(8,128)(2,1)} %collective-permute-done.32), channel_id=1, source_target_pairs={{0,1},{1,0},{2,3},{3,2},{4,5},{5,4},{6,7},{7,6},{8,9},{9,8},{10,11... | collective-permute-start | bytes 2359304 | tf_op jit(solution)/shard_map/ppermute | solution.py:763
  270.4 18.3 %collective-permute-start.36 = (bf16[512,768]{1,0:T(8,128)(2,1)}, bf16[512,768]{1,0:T(8,128)(2,1)}, u32[]{:S(2)}, u32[]{:S(2)}) collective-permute-start(bf16[512,768]{1,0:T(8,128)(2,1)} %collective-permute-done.35), channel_id=1, source_target_pairs={{0,1},{1,0},{2,3},{3,2},{4,5},{5,4},{6,7},{7,6},{8,9},{9,8},{10,11... | collective-permute-start | bytes 2359304 | tf_op jit(solution)/shard_map/ppermute | solution.py:763
  278.0 7.5 %copy-start.13 = (bf16[512,768]{1,0:T(8,128)(2,1)}, bf16[512,768]{1,0:T(8,128)(2,1)S(1)}, u32[]{:S(2)}) copy-start(bf16[512,768]{1,0:T(8,128)(2,1)S(1)} %collective-permute-done.25.refs_5_) | copy-start | bytes 2359300
  285.5 12.6 %collective-permute-start.39 = (f32[6,512]{1,0:T(8,128)S(1)}, f32[6,512]{1,0:T(8,128)S(1)}, u32[]{:S(2)}, u32[]{:S(2)}) collective-permute-start(f32[6,512]{1,0:T(8,128)S(1)} %add.128), channel_id=1, source_target_pairs={{0,16},{4,20},{8,24},{12,28},{16,0},{20,4},{24,8},{28,12},{1,17},{... | collective-permute-start | bytes 36872 | tf_op jit(solution)/shard_map/ppermute | solution.py:864
  (17 other events, 45.6 us)

commit v9 on v8

--- a/solution.py
+++ b/solution.py
@@ -858,6 +858,7 @@
     dinputs = tail(after(meta, parts2[1]), dn, row_sums, own_x, mu, inv, ln_gain, direct, features)
 
     totals = jnp.concatenate([col_sums[:2], vecs[:4]], axis=0)
+    totals = after(totals, parts2[1])
     grad_weight = place(after(meta, dinputs), parts1, parts2, n_dp, features, weight.shape[1])
     for step in range(bits):
         last = step == bits - 1

time: 300 us -> 308 us (1.027)
  waiting for transfers between devices: 51.3 us -> 66.5 us
  starting transfers between devices: 37.9 us -> 33.2 us
  local copies, waits for them, and re-layouts: 13.4 us -> 10.3 us
    ppermute x16, waiting for transfers between devices: 46.4 us -> 55 us  [over_dp(): return lax.ppermute(value, ('dp', 'gate'), pairs)]
    ppermute x21, waiting for transfers between devices: 2.33 us -> 8.88 us  [over_gate(): return lax.ppermute(value, 'gate', [(g, g ^ delta) for g in range(n_gate)])]
    unnamed x53 -> x49, local copies, waits for them, and re-layouts: 9.72 us -> 7.58 us
  transfers between devices with their start and end apart: 40 -> 40, of which waited for: 10 -> 13; matrix products, arithmetic and copies ran while one was open for 3% -> 3% of each run, Pallas kernels for 60% -> 58%
where the time goes in v9:
time: 308 us; the launch traced here: 306 us
  Pallas kernels  189 us (61%)
  waiting for transfers between devices  66.5 us (22%)
  starting transfers between devices  33.2 us (11%)
  local copies, waits for them, and re-layouts  10.3 us (3%)
  other arithmetic  5.71 us (2%)
    pallas_call x26, Pallas kernels, call(): pl.pallas_call(kernel, grid_spec=pltpu.PrefetchScalarGridSpec(num_scalar_...  189 us
    ppermute x16, waiting for transfers between devices, over_dp(): return lax.ppermute(value, ('dp', 'gate'), pairs)  55 us
    ppermute x16, starting transfers between devices, over_dp(): return lax.ppermute(value, ('dp', 'gate'), pairs)  18 us
    ppermute x21, starting transfers between devices, over_gate(): return lax.ppermute(value, 'gate', [(g, g ^ delta) for g in range(n_gate)])  11.7 us
    ppermute x21, waiting for transfers between devices, over_gate(): return lax.ppermute(value, 'gate', [(g, g ^ delta) for g in range(n_gate)])  8.88 us
    unnamed x49, local copies, waits for them, and re-layouts  7.58 us
  transfers between devices with their start and end apart: 40, of which 13 were waited for; matrix products, arithmetic and copies ran while one was open for 3% of the time, Pallas kernels for 58%

profile of v9, /device:TPU:0, one launch (start us, length us, event | category | flops | bytes accessed | tf_op | source)
XLA Modules:
  0.0 305.9 jit_solution(16556958991385003463)
XLA Ops:
  1.4 4.8 %shard_map.178 = (bf16[2048,128]{1,0:T(8,128)(2,1)}, bf16[2048,128]{1,0:T(8,128)(2,1)}, bf16[2048,384]{1,0:T(8,128)(2,1)}) custom-call(s32[36]{0:T(128)} %stack.147.meta, bf16[2048,1536]{1,0:T(8,128)(2,1)} %refs_10_.7, bf16[2048,1536]{1,0:T(8,128)(2,1)} %refs_10_.7, bf16[2048,1536]{1,0:T(8,128)(2,1)} %refs_10_.7, bf16[2048,1536]{1,0:T(8,128)(2,1)} %refs_10_.7, ...), custom_call_target="tpu_custom_call" | custom-call | bytes 5242880 | tf_op jit(solution)/shard_map/pallas_call | solution.py:20
  6.7 2.6 collective-permute-start.1
  9.3 14.9 %shard_map.179 = (bf16[2048,2048]{1,0:T(8,128)(2,1)}, f32[2048,128]{1,0:T(8,128)}, f32[2048,128]{1,0:T(8,128)}, bf16[2048,512]{1,0:T(8,128)(2,1)}, f32[2048,128]{1,0:T(8,128)}, /*index=5*/f32[2048,128]{1,0:T(8,128)}) custom-call(s32[36]{0:T(128)} %stack.147.meta, bf16[2048,2048]{1,0:T(8,128)(2,1)} %bitcast.50, f32[1,2048]{1,0:T(1,128)} %bitcast.55, ...), custom_call_target="tpu_custom_call" | custom-call | flops 671088640 | bytes 335544320 | tf_op jit(solution)/shard_map/pallas_call | solution.py:20
  24.2 4.8 %shard_map.180 = (bf16[2048,256]{1,0:T(8,128)(2,1)}, bf16[2048,256]{1,0:T(8,128)(2,1)}) custom-call(s32[36]{0:T(128)} %stack.147.meta, bf16[2048,1536]{1,0:T(8,128)(2,1)} %refs_10_.7, bf16[2048,1536]{1,0:T(8,128)(2,1)} %refs_10_.7, bf16[2048,1536]{1,0:T(8,128)(2,1)} %refs_10_.7, bf16[2048,1536]{1,0:T(8,128)(2,1)} %refs_10_.7), custom_call_target="tpu_custom_call" | custom-call | bytes 4194304 | tf_op jit(solution)/shard_map/pallas_call | solution.py:20
  29.0 1.7 collective-permute-start.3
  31.5 1.7 collective-permute-done.2.refs_5_
  35.1 11.9 %shard_map.181.u_ref = bf16[2048,768]{1,0:T(8,128)(2,1)} custom-call(s32[36]{0:T(128)} %stack.147.meta, bf16[2048,2048]{1,0:T(8,128)(2,1)} %get-tuple-element.88.normed_ref, bf16[2048,1536]{1,0:T(8,128)(2,1)} %refs_10_.7, bf16[2048,1536]{1,0:T(8,128)(2,1)} %refs_10_.7, bf16[2048,384]{1,0:T(8,128)(2,1)} %copy-done.20, bf16[2048,384]{1,0:T(8,128)(2,1)} %copy-done.20, ...), custom_call_target="tpu_custom_call" | custom-call | flops 128849018880 | bytes 293601280 | tf_op jit(solution)/shard_map/pallas_call | solution.py:20
  47.0 12.4 %shard_map.182 = (bf16[2048,512]{1,0:T(8,128)(2,1)}, bf16[2048,768]{1,0:T(8,128)(2,1)}, bf16[2048,512]{1,0:T(8,128)(2,1)}, f32[8,512]{1,0:T(8,128)}) custom-call(s32[36]{0:T(128)} %stack.147.meta, bf16[2048,768]{1,0:T(8,128)(2,1)} %shard_map.181.u_ref, bf16[2048,512]{1,0:T(8,128)(2,1)} %get-tuple-element.94.x_ref, bf16[2048,512]{1,0:T(8,128)(2,1)} %bitcast.51, ...), custom_call_target="tpu_custom_call" | custom-call | flops 629145600 | bytes 188743680 | tf_op jit(solution)/shard_map/pallas_call | solution.py:20
  59.5 8.1 %shard_map.183 = (bf16[512,768]{1,0:T(8,128)(2,1)}, bf16[512,768]{1,0:T(8,128)(2,1)}) custom-call(s32[36]{0:T(128)} %stack.147.meta, bf16[2048,2048]{1,0:T(8,128)(2,1)} %get-tuple-element.88.normed_ref, bf16[2048,768]{1,0:T(8,128)(2,1)} %get-tuple-element.97.ds_ref.ds1_ref), custom_call_target="tpu_custom_call" | custom-call | flops 64424509440 | bytes 146800640 | tf_op jit(solution)/shard_map/pallas_call | solution.py:20
  69.6 8.1 %shard_map.184 = (bf16[512,768]{1,0:T(8,128)(2,1)}, bf16[512,768]{1,0:T(8,128)(2,1)}) custom-call(s32[36]{0:T(128)} %stack.147.meta, bf16[2048,2048]{1,0:T(8,128)(2,1)} %get-tuple-element.88.normed_ref, bf16[2048,768]{1,0:T(8,128)(2,1)} %get-tuple-element.97.ds_ref.ds1_ref), custom_call_target="tpu_custom_call" | custom-call | flops 64424509440 | bytes 146800640 | tf_op jit(solution)/shard_map/pallas_call | solution.py:20
  77.7 1.5 collective-permute-start.8
  79.3 12.1 %shard_map.185.u_ref = bf16[2048,768]{1,0:T(8,128)(2,1)} custom-call(s32[36]{0:T(128)} %stack.147.meta, bf16[2048,2048]{1,0:T(8,128)(2,1)} %get-tuple-element.88.normed_ref, bf16[2048,256]{1,0:T(8,128)(2,1)} %collective-permute-done.3.refs_0_.refs_1_.refs_6_.refs_7_, bf16[2048,256]{1,0:T(8,128)(2,1)} %collective-permute-done.3.refs_0_.refs_1_.refs_6_.refs_7_, ...), custom_call_target="tpu_custom_call" | custom-call | flops 128849018880 | bytes 293601280 | tf_op jit(solution)/shard_map/pallas_call | solution.py:20
  93.2 3.8 %shard_map.186 = (bf16[2,256,768]{2,1,0:T(8,128)(2,1)}, bf16[2,256,768]{2,1,0:T(8,128)(2,1)}) custom-call(s32[36]{0:T(128)} %stack.147.meta, bf16[512,768]{1,0:T(8,128)(2,1)} %get-tuple-element.100.refs_0_.refs_4_, bf16[512,768]{1,0:T(8,128)(2,1)} %copy-done.1, bf16[512,768]{1,0:T(8,128)(2,1)} %collective-permute-done.6.refs_2_.refs_6_, ...), custom_call_target="tpu_custom_call" | custom-call | flops 1572864 | bytes 4718592 | tf_op jit(solution)/shard_map/pallas_call | solution.py:20
  97.5 12.4 %shard_map.187 = (bf16[2048,512]{1,0:T(8,128)(2,1)}, bf16[2048,768]{1,0:T(8,128)(2,1)}, bf16[2048,512]{1,0:T(8,128)(2,1)}, f32[8,512]{1,0:T(8,128)}) custom-call(s32[36]{0:T(128)} %stack.147.meta, bf16[2048,768]{1,0:T(8,128)(2,1)} %shard_map.185.u_ref, ...), custom_call_target="tpu_custom_call", output_to_operand_aliasing={{0}: (7, {}), {2}: (8, {}), {3}: (9, {})} | custom-call | flops 629145600 | bytes 188743680 | tf_op jit(solution)/shard_map/pallas_call | solution.py:20
  110.8 3.0 shard_map.188
  113.9 2.6 collective-permute-start.14
  116.4 8.1 %shard_map.189 = (bf16[512,768]{1,0:T(8,128)(2,1)}, bf16[512,768]{1,0:T(8,128)(2,1)}) custom-call(s32[36]{0:T(128)} %stack.147.meta, bf16[2048,2048]{1,0:T(8,128)(2,1)} %get-tuple-element.88.normed_ref, bf16[2048,768]{1,0:T(8,128)(2,1)} %get-tuple-element.111.ds_ref.ds2_ref), custom_call_target="tpu_custom_call" | custom-call | flops 64424509440 | bytes 146800640 | tf_op jit(solution)/shard_map/pallas_call | solution.py:20
  126.1 8.1 %shard_map.190 = (bf16[512,768]{1,0:T(8,128)(2,1)}, bf16[512,768]{1,0:T(8,128)(2,1)}) custom-call(s32[36]{0:T(128)} %stack.147.meta, bf16[2048,2048]{1,0:T(8,128)(2,1)} %get-tuple-element.88.normed_ref, bf16[2048,768]{1,0:T(8,128)(2,1)} %get-tuple-element.111.ds_ref.ds2_ref), custom_call_target="tpu_custom_call" | custom-call | flops 64424509440 | bytes 146800640 | tf_op jit(solution)/shard_map/pallas_call | solution.py:20
  135.2 8.0 %shard_map.191 = bf16[2048,512]{1,0:T(8,128)(2,1)} custom-call(s32[36]{0:T(128)} %stack.147.meta, bf16[2048,768]{1,0:T(8,128)(2,1)} %get-tuple-element.97.ds_ref.ds1_ref, bf16[2048,768]{1,0:T(8,128)(2,1)} %get-tuple-element.111.ds_ref.ds2_ref, bf16[2048,1536]{1,0:T(8,128)(2,1)} %refs_10_.7, bf16[2048,1536]{1,0:T(8,128)(2,1)} %refs_10_.7, ...), custom_call_target="tpu_custom_call" | custom-call | flops 64424509440 | bytes 125829120 | tf_op jit(solution)/shard_map/pallas_call | solution.py:20
  143.3 3.4 %collective-permute-done.13.refs_3_.refs_7_ = bf16[512,768]{1,0:T(8,128)(2,1)S(1)} collective-permute-done((bf16[512,768]{1,0:T(8,128)(2,1)S(1)}, bf16[512,768]{1,0:T(8,128)(2,1)S(1)}, u32[]{:S(2)}, u32[]{:S(2)}) %collective-permute-start.13) | collective-permute-done | bytes 786464 | tf_op jit(solution)/shard_map/ppermute | solution.py:769
  147.7 3.7 %shard_map.192 = (bf16[2,256,768]{2,1,0:T(8,128)(2,1)}, bf16[2,256,768]{2,1,0:T(8,128)(2,1)}) custom-call(s32[36]{0:T(128)} %stack.147.meta, bf16[512,768]{1,0:T(8,128)(2,1)} %get-tuple-element.118.refs_0_.refs_4_, bf16[512,768]{1,0:T(8,128)(2,1)} %copy-done.2, bf16[512,768]{1,0:T(8,128)(2,1)} %copy-done, bf16[512,768]{1,0:T(8,128)(2,1)} %copy-done.4, ...), custom_call_target="tpu_custom_call" | custom-call | flops 1572864 | bytes 4718592 | tf_op jit(solution)/shard_map/pallas_call | solution.py:20
  151.9 2.6 shard_map.193
  156.0 8.3 %shard_map.194 = bf16[2048,512]{1,0:T(8,128)(2,1)} custom-call(s32[36]{0:T(128)} %stack.147.meta, bf16[2048,768]{1,0:T(8,128)(2,1)} %get-tuple-element.97.ds_ref.ds1_ref, bf16[2048,768]{1,0:T(8,128)(2,1)} %get-tuple-element.111.ds_ref.ds2_ref, bf16[2048,1536]{1,0:T(8,128)(2,1)} %refs_10_.7, bf16[2048,1536]{1,0:T(8,128)(2,1)} %refs_10_.7, ...), custom_call_target="tpu_custom_call" | custom-call | flops 64424509440 | bytes 125829120 | tf_op jit(solution)/shard_map/pallas_call | solution.py:20
  165.2 3.2 %shard_map.195 = (bf16[2,128,768]{2,1,0:T(8,128)(2,1)}, bf16[2,128,768]{2,1,0:T(8,128)(2,1)}) custom-call(s32[36]{0:T(128)} %stack.147.meta, bf16[2,256,768]{2,1,0:T(8,128)(2,1)} %get-tuple-element.129.refs_0_.refs_2_, bf16[2,256,768]{2,1,0:T(8,128)(2,1)} %copy-done.6, bf16[2,256,768]{2,1,0:T(8,128)(2,1)} %get-tuple-element.129.refs_0_.refs_2_, ...), custom_call_target="tpu_custom_call" | custom-call | flops 786432 | bytes 2359296 | tf_op jit(solution)/shard_map/pallas_call | solution.py:20
  170.4 3.0 add_convert_fusion
  173.4 8.2 %shard_map.196 = bf16[2048,512]{1,0:T(8,128)(2,1)} custom-call(s32[36]{0:T(128)} %stack.147.meta, bf16[2048,768]{1,0:T(8,128)(2,1)} %get-tuple-element.97.ds_ref.ds1_ref, bf16[2048,768]{1,0:T(8,128)(2,1)} %get-tuple-element.111.ds_ref.ds2_ref, bf16[2048,1536]{1,0:T(8,128)(2,1)} %refs_10_.7, bf16[2048,1536]{1,0:T(8,128)(2,1)} %refs_10_.7, ...), custom_call_target="tpu_custom_call" | custom-call | flops 64424509440 | bytes 125829120 | tf_op jit(solution)/shard_map/pallas_call | solution.py:20
  181.6 2.7 collective-permute-start.20
  184.3 8.0 %shard_map.197.k_ref = bf16[2048,512]{1,0:T(8,128)(2,1)} custom-call(s32[36]{0:T(128)} %stack.147.meta, bf16[2048,768]{1,0:T(8,128)(2,1)} %get-tuple-element.97.ds_ref.ds1_ref, bf16[2048,768]{1,0:T(8,128)(2,1)} %get-tuple-element.111.ds_ref.ds2_ref, bf16[2048,1536]{1,0:T(8,128)(2,1)} %refs_10_.7, bf16[2048,1536]{1,0:T(8,128)(2,1)} %refs_10_.7, ...), custom_call_target="tpu_custom_call" | custom-call | flops 64424509440 | bytes 125829120 | tf_op jit(solution)/shard_map/pallas_call | solution.py:20
  192.3 5.2 %collective-permute-done.19.b_ref = bf16[2,128,768]{2,1,0:T(8,128)(2,1)} collective-permute-done((bf16[2,128,768]{2,1,0:T(8,128)(2,1)}, bf16[2,128,768]{2,1,0:T(8,128)(2,1)}, u32[]{:S(2)}, u32[]{:S(2)}) %collective-permute-start.19) | collective-permute-done | bytes 393248 | tf_op jit(solution)/shard_map/ppermute | solution.py:769
  197.5 2.6 shard_map.198
  200.4 5.4 %collective-permute-done.20 = bf16[2,128,768]{2,1,0:T(8,128)(2,1)S(1)} collective-permute-done((bf16[2,128,768]{2,1,0:T(8,128)(2,1)S(1)}, bf16[2,128,768]{2,1,0:T(8,128)(2,1)S(1)}, u32[]{:S(2)}, u32[]{:S(2)}) %collective-permute-start.20) | collective-permute-done | bytes 393248 | tf_op jit(solution)/shard_map/ppermute | solution.py:769
  206.9 1.8 collective-permute-done.21
  209.8 2.1 collective-permute-start.23
  211.9 16.3 %collective-permute-done.22 = bf16[2,128,768]{2,1,0:T(8,128)(2,1)S(1)} collective-permute-done((bf16[2,128,768]{2,1,0:T(8,128)(2,1)S(1)}, bf16[2,128,768]{2,1,0:T(8,128)(2,1)S(1)}, u32[]{:S(2)}, u32[]{:S(2)}) %collective-permute-start.22) | collective-permute-done | bytes 393248 | tf_op jit(solution)/shard_map/ppermute | solution.py:769
  228.4 2.0 collective-permute-done.23.b_ref
  230.4 3.3 %shard_map.199 = (bf16[512,768]{1,0:T(8,128)(2,1)}, bf16[512,768]{1,0:T(8,128)(2,1)}) custom-call(s32[36]{0:T(128)} %stack.147.meta, bf16[2,256,768]{2,1,0:T(8,128)(2,1)} %copy-done.10, bf16[2,256,768]{2,1,0:T(8,128)(2,1)} %collective-permute-done.23.b_ref), custom_call_target="tpu_custom_call" | custom-call | bytes 3145728 | tf_op jit(solution)/shard_map/pallas_call | solution.py:20
  233.6 1.9 collective-permute-start.26
  235.7 10.6 %collective-permute-done.24.b_ref = bf16[2,256,768]{2,1,0:T(8,128)(2,1)} collective-permute-done((bf16[2,256,768]{2,1,0:T(8,128)(2,1)S(1)}, bf16[2,256,768]{2,1,0:T(8,128)(2,1)}, u32[]{:S(2)}, u32[]{:S(2)}) %collective-permute-start.24) | collective-permute-done | bytes 786464 | tf_op jit(solution)/shard_map/ppermute | solution.py:769
  246.3 3.2 %shard_map.200 = (bf16[512,768]{1,0:T(8,128)(2,1)}, bf16[512,768]{1,0:T(8,128)(2,1)}) custom-call(s32[36]{0:T(128)} %stack.147.meta, bf16[2,256,768]{2,1,0:T(8,128)(2,1)} %copy-done.5, bf16[2,256,768]{2,1,0:T(8,128)(2,1)} %collective-permute-done.24.b_ref), custom_call_target="tpu_custom_call" | custom-call | bytes 3145728 | tf_op jit(solution)/shard_map/pallas_call | solution.py:20
  249.5 2.0 collective-permute-start.25
  251.6 4.8 %collective-permute-done.32 = bf16[512,768]{1,0:T(8,128)(2,1)} collective-permute-done((bf16[512,768]{1,0:T(8,128)(2,1)}, bf16[512,768]{1,0:T(8,128)(2,1)}, u32[]{:S(2)}, u32[]{:S(2)}) %collective-permute-start.32) | collective-permute-done | bytes 786464 | tf_op jit(solution)/shard_map/ppermute | solution.py:769
  257.5 7.3 %collective-permute-done.35 = bf16[512,768]{1,0:T(8,128)(2,1)} collective-permute-done((bf16[512,768]{1,0:T(8,128)(2,1)}, bf16[512,768]{1,0:T(8,128)(2,1)}, u32[]{:S(2)}, u32[]{:S(2)}) %collective-permute-start.35) | collective-permute-done | bytes 786464 | tf_op jit(solution)/shard_map/ppermute | solution.py:769
  265.8 9.4 %shard_map.201 = (f32[2048,512]{1,0:T(8,128)}, f32[8,2048]{1,0:T(8,128)}, f32[8,512]{1,0:T(8,128)}) custom-call(s32[36]{0:T(128)} %stack.147.meta, bf16[2048,512]{1,0:T(8,128)(2,1)} %shard_map.197.k_ref, bf16[2048,512]{1,0:T(8,128)(2,1)} %copy-done.9, bf16[512,512]{1,0:T(8,128)(2,1)} %copy-done.13, bf16[1536,512]{1,0:T(8,128)(2,1)} %collective-permute-done.28.r2_ref, ...), custom_call_target="tpu_custom_call" | custom-call | flops 419430400 | bytes 251658240 | tf_op jit(solution)/shard_map/pallas_call | solution.py:20
  278.5 2.6 collective-permute-done.37
  281.4 3.9 %collective-permute-done.30 = f32[8,2048]{1,0:T(8,128)S(1)} collective-permute-done((f32[8,2048]{1,0:T(8,128)S(1)}, f32[8,2048]{1,0:T(8,128)S(1)}, u32[]{:S(2)}, u32[]{:S(2)}) %collective-permute-start.30) | collective-permute-done | bytes 65568 | tf_op jit(solution)/shard_map/ppermute | solution.py:763
  286.0 7.4 %shard_map.202 = bf16[2048,512]{1,0:T(8,128)(2,1)} custom-call(s32[36]{0:T(128)} %stack.147.meta, f32[2048,512]{1,0:T(8,128)} %get-tuple-element.150.dn_ref, f32[8,2048]{1,0:T(8,128)} %add.126.row_ref, bf16[2048,512]{1,0:T(8,128)(2,1)} %get-tuple-element.94.x_ref, f32[2048,128]{1,0:T(8,128)} %get-tuple-element.148.mu_ref, ...), custom_call_target="tpu_custom_call" | custom-call | flops 10485760 | bytes 12582912 | tf_op jit(solution)/shard_map/pallas_call | solution.py:20
  293.5 3.3 %collective-permute-start.39 = (f32[6,512]{1,0:T(8,128)S(1)}, f32[6,512]{1,0:T(8,128)S(1)}, u32[]{:S(2)}, u32[]{:S(2)}) collective-permute-start(f32[6,512]{1,0:T(8,128)S(1)} %add.128), channel_id=1, source_target_pairs={{0,16},{4,20},{8,24},{12,28},{16,0},{20,4},{24,8},{28,12},{1,17},{... | collective-permute-start | bytes 36872 | tf_op jit(solution)/shard_map/ppermute | solution.py:865
  296.8 8.5 %shard_map.203 = f32[2048,1536]{1,0:T(8,128)} custom-call(s32[36]{0:T(128)} %stack.147.meta, bf16[512,768]{1,0:T(8,128)(2,1)} %get-tuple-element.143.refs_0_, bf16[512,768]{1,0:T(8,128)(2,1)} %copy-done.11, bf16[512,768]{1,0:T(8,128)(2,1)} %collective-permute-done.31.refs_2_, bf16[512,768]{1,0:T(8,128)(2,1)} %collective-permute-done.33.refs_3_, ...), custom_call_target="tpu_custom_call" | custom-call | flops 62914560 | bytes 377487360 | tf_op jit(solution)/shard_map/pallas_call | solution.py:20
  (125 shorter events, 27.3 us)
Async XLA Ops:
  6.2 26.9 %collective-permute-start = (bf16[2048,384]{1,0:T(8,128)(2,1)}, bf16[2048,384]{1,0:T(8,128)(2,1)S(1)}, u32[]{:S(2)}, u32[]{:S(2)}) collective-permute-start(bf16[2048,384]{1,0:T(8,128)(2,1)} %get-tuple-element.93), channel_id=1, source_target_pairs={{0,1},{1,0},{2,3},{3,2},{4,5},{5,4},{6,7},{7,6},{8,9},{9,8},{10,11... | collective-permute-start | bytes 4718600 | tf_op jit(solution)/shard_map/ppermute | solution.py:763
  6.7 24.7 %collective-permute-start.1 = (bf16[2048,128]{1,0:T(8,128)(2,1)}, bf16[2048,128]{1,0:T(8,128)(2,1)S(1)}, u32[]{:S(2)}, u32[]{:S(2)}) collective-permute-start(bf16[2048,128]{1,0:T(8,128)(2,1)} %get-tuple-element.85), channel_id=1, source_target_pairs={{0,2},{1,3},{2,0},{3,1},{4,6},{5,7},{6,4},{7,5},{8,10},{9,11},{10,... | collective-permute-start | bytes 1572872 | tf_op jit(solution)/shard_map/ppermute | solution.py:763
  9.3 23.9 %collective-permute-start.2 = (bf16[2048,128]{1,0:T(8,128)(2,1)}, bf16[2048,128]{1,0:T(8,128)(2,1)S(1)}, u32[]{:S(2)}, u32[]{:S(2)}) collective-permute-start(bf16[2048,128]{1,0:T(8,128)(2,1)} %get-tuple-element.86), channel_id=1, source_target_pairs={{0,3},{1,2},{2,1},{3,0},{4,7},{5,6},{6,5},{7,4},{8,11},{9,10},{10,... | collective-permute-start | bytes 1572872 | tf_op jit(solution)/shard_map/ppermute | solution.py:763
  29.0 50.2 %collective-permute-start.3 = (bf16[2048,256]{1,0:T(8,128)(2,1)}, bf16[2048,256]{1,0:T(8,128)(2,1)}, u32[]{:S(2)}, u32[]{:S(2)}) collective-permute-start(bf16[2048,256]{1,0:T(8,128)(2,1)} %get-tuple-element.90), channel_id=1, source_target_pairs={{0,2},{1,3},{2,0},{3,1},{4,6},{5,7},{6,4},{7,5},{8,10},{9,11},{10,... | collective-permute-start | bytes 3145736 | tf_op jit(solution)/shard_map/ppermute | solution.py:763
  30.8 48.5 %collective-permute-start.4 = (bf16[2048,256]{1,0:T(8,128)(2,1)}, bf16[2048,256]{1,0:T(8,128)(2,1)}, u32[]{:S(2)}, u32[]{:S(2)}) collective-permute-start(bf16[2048,256]{1,0:T(8,128)(2,1)} %get-tuple-element.91), channel_id=1, source_target_pairs={{0,3},{1,2},{2,1},{3,0},{4,7},{5,6},{6,5},{7,4},{8,11},{9,10},{10,... | collective-permute-start | bytes 3145736 | tf_op jit(solution)/shard_map/ppermute | solution.py:763
  67.6 23.8 %collective-permute-start.6 = (bf16[512,768]{1,0:T(8,128)(2,1)}, bf16[512,768]{1,0:T(8,128)(2,1)}, u32[]{:S(2)}, u32[]{:S(2)}) collective-permute-start(bf16[512,768]{1,0:T(8,128)(2,1)} %get-tuple-element.98), channel_id=1, source_target_pairs={{0,4},{1,9},{2,6},{3,11},{4,0},{5,13},{6,2},{7,15},{8,12},{9,1},{1... | collective-permute-start | bytes 2359304 | tf_op jit(solution)/shard_map/ppermute | solution.py:769
  69.1 8.6 %collective-permute-start.7 = (bf16[512,768]{1,0:T(8,128)(2,1)}, bf16[512,768]{1,0:T(8,128)(2,1)S(1)}, u32[]{:S(2)}, u32[]{:S(2)}) collective-permute-start(bf16[512,768]{1,0:T(8,128)(2,1)} %get-tuple-element.104), channel_id=1, source_target_pairs={{0,1},{1,0},{2,3},{3,2},{4,5},{5,4},{6,7},{7,6},{8,9},{9,8},{10,11... | collective-permute-start | bytes 2359304 | tf_op jit(solution)/shard_map/ppermute | solution.py:763
  77.7 13.7 %collective-permute-start.5 = (bf16[512,768]{1,0:T(8,128)(2,1)}, bf16[512,768]{1,0:T(8,128)(2,1)S(1)}, u32[]{:S(2)}, u32[]{:S(2)}) collective-permute-start(bf16[512,768]{1,0:T(8,128)(2,1)} %get-tuple-element.103), channel_id=1, source_target_pairs={{0,1},{1,0},{2,3},{3,2},{4,5},{5,4},{6,7},{7,6},{8,9},{9,8},{10,11... | collective-permute-start | bytes 2359304 | tf_op jit(solution)/shard_map/ppermute | solution.py:763
  77.7 13.7 %collective-permute-start.8 = (bf16[512,768]{1,0:T(8,128)(2,1)S(1)}, bf16[512,768]{1,0:T(8,128)(2,1)S(1)}, u32[]{:S(2)}, u32[]{:S(2)}) collective-permute-start(bf16[512,768]{1,0:T(8,128)(2,1)S(1)} %collective-permute-done.7), channel_id=1, source_target_pairs={{0,4},{1,9},{2,6},{3,11},{4,0},{5,13},{6,2},{7,15},{8,12},{9,1},{1... | collective-permute-start | bytes 2359304 | tf_op jit(solution)/shard_map/ppermute | solution.py:769
  96.9 13.0 %collective-permute-start.9 = (bf16[2,256,768]{2,1,0:T(8,128)(2,1)}, bf16[2,256,768]{2,1,0:T(8,128)(2,1)S(1)}, u32[]{:S(2)}, u32[]{:S(2)}) collective-permute-start(bf16[2,256,768]{2,1,0:T(8,128)(2,1)} %get-tuple-element.105), channel_id=1, source_target_pairs={{0,8},{1,5},{2,10},{3,7},{4,12},{5,1},{6,14},{7,3},{8,0},{9,13},{1... | collective-permute-start | bytes 2359304 | tf_op jit(solution)/shard_map/ppermute | solution.py:769
  113.9 38.0 %collective-permute-start.14 = (bf16[2,128,768]{2,1,0:T(8,128)(2,1)}, bf16[2,128,768]{2,1,0:T(8,128)(2,1)}, u32[]{:S(2)}, u32[]{:S(2)}) collective-permute-start(bf16[2,128,768]{2,1,0:T(8,128)(2,1)} %get-tuple-element.114), channel_id=1, source_target_pairs={{0,16},{1,17},{2,18},{3,19},{4,20},{5,21},{6,22},{7,23},{8,24},{9,... | collective-permute-start | bytes 1179656 | tf_op jit(solution)/shard_map/ppermute | solution.py:769
  124.6 18.7 %collective-permute-start.11 = (bf16[512,768]{1,0:T(8,128)(2,1)}, bf16[512,768]{1,0:T(8,128)(2,1)S(1)}, u32[]{:S(2)}, u32[]{:S(2)}) collective-permute-start(bf16[512,768]{1,0:T(8,128)(2,1)} %get-tuple-element.116), channel_id=1, source_target_pairs={{0,4},{1,9},{2,6},{3,11},{4,0},{5,13},{6,2},{7,15},{8,12},{9,1},{1... | collective-permute-start | bytes 2359304 | tf_op jit(solution)/shard_map/ppermute | solution.py:769
  126.1 8.6 %collective-permute-start.12 = (bf16[512,768]{1,0:T(8,128)(2,1)}, bf16[512,768]{1,0:T(8,128)(2,1)S(1)}, u32[]{:S(2)}, u32[]{:S(2)}) collective-permute-start(bf16[512,768]{1,0:T(8,128)(2,1)} %get-tuple-element.122), channel_id=1, source_target_pairs={{0,1},{1,0},{2,3},{3,2},{4,5},{5,4},{6,7},{7,6},{8,9},{9,8},{10,11... | collective-permute-start | bytes 2359304 | tf_op jit(solution)/shard_map/ppermute | solution.py:763
  134.2 9.1 %collective-permute-start.10 = (bf16[512,768]{1,0:T(8,128)(2,1)}, bf16[512,768]{1,0:T(8,128)(2,1)S(1)}, u32[]{:S(2)}, u32[]{:S(2)}) collective-permute-start(bf16[512,768]{1,0:T(8,128)(2,1)} %get-tuple-element.121), channel_id=1, source_target_pairs={{0,1},{1,0},{2,3},{3,2},{4,5},{5,4},{6,7},{7,6},{8,9},{9,8},{10,11... | collective-permute-start | bytes 2359304 | tf_op jit(solution)/shard_map/ppermute | solution.py:763
  134.7 12.0 %collective-permute-start.13 = (bf16[512,768]{1,0:T(8,128)(2,1)S(1)}, bf16[512,768]{1,0:T(8,128)(2,1)S(1)}, u32[]{:S(2)}, u32[]{:S(2)}) collective-permute-start(bf16[512,768]{1,0:T(8,128)(2,1)S(1)} %collective-permute-done.12), channel_id=1, source_target_pairs={{0,4},{1,9},{2,6},{3,11},{4,0},{5,13},{6,2},{7,15},{8,12},{9,1},{1... | collective-permute-start | bytes 2359304 | tf_op jit(solution)/shard_map/ppermute | solution.py:769
  143.3 25.4 %collective-permute-start.16 = (bf16[2048,512]{1,0:T(8,128)(2,1)}, bf16[2048,512]{1,0:T(8,128)(2,1)}, u32[]{:S(2)}, u32[]{:S(2)}) collective-permute-start(bf16[2048,512]{1,0:T(8,128)(2,1)} %shard_map.191), channel_id=1, source_target_pairs={{0,1},{1,0},{2,3},{3,2},{4,5},{5,4},{6,7},{7,6},{8,9},{9,8},{10,11... | collective-permute-start | bytes 6291464 | tf_op jit(solution)/shard_map/ppermute | solution.py:763
  151.4 12.9 %collective-permute-start.15 = (bf16[2,256,768]{2,1,0:T(8,128)(2,1)}, bf16[2,256,768]{2,1,0:T(8,128)(2,1)S(1)}, u32[]{:S(2)}, u32[]{:S(2)}) collective-permute-start(bf16[2,256,768]{2,1,0:T(8,128)(2,1)} %get-tuple-element.123), channel_id=1, source_target_pairs={{0,8},{1,5},{2,10},{3,7},{4,12},{5,1},{6,14},{7,3},{8,0},{9,13},{1... | collective-permute-start | bytes 2359304 | tf_op jit(solution)/shard_map/ppermute | solution.py:769
  154.5 27.1 %collective-permute-start.17 = (bf16[2,128,256]{2,1,0:T(8,128)(2,1)}, bf16[2,128,256]{2,1,0:T(8,128)(2,1)S(1)}, u32[]{:S(2)}, u32[]{:S(2)}) collective-permute-start(bf16[2,128,256]{2,1,0:T(8,128)(2,1)} %get-tuple-element.134), channel_id=1, source_target_pairs={{0,2},{1,3},{2,0},{3,1},{4,6},{5,7},{6,4},{7,5},{8,10},{9,11},{10,... | collective-permute-start | bytes 393224 | tf_op jit(solution)/shard_map/ppermute | solution.py:763
  168.3 29.2 %collective-permute-start.19 = (bf16[2,128,768]{2,1,0:T(8,128)(2,1)}, bf16[2,128,768]{2,1,0:T(8,128)(2,1)}, u32[]{:S(2)}, u32[]{:S(2)}) collective-permute-start(bf16[2,128,768]{2,1,0:T(8,128)(2,1)} %get-tuple-element.130), channel_id=1, source_target_pairs={{0,16},{1,17},{2,18},{3,19},{4,20},{5,21},{6,22},{7,23},{8,24},{9,... | collective-permute-start | bytes 1179656 | tf_op jit(solution)/shard_map/ppermute | solution.py:769
  169.8 22.5 %collective-permute-start.18 = (bf16[512,512]{1,0:T(8,128)(2,1)S(1)}, bf16[512,512]{1,0:T(8,128)(2,1)S(1)}, u32[]{:S(2)}, u32[]{:S(2)}) collective-permute-start(bf16[512,512]{1,0:T(8,128)(2,1)S(1)} %add_convert_fusion.1), channel_id=1, source_target_pairs={{0,2},{1,3},{2,0},{3,1},{4,6},{5,7},{6,4},{7,5},{8,10},{9,11},{10,... | collective-permute-start | bytes 1572872 | tf_op jit(solution)/shard_map/ppermute | solution.py:763
  173.4 8.2 %copy-start.14 = (bf16[2,128,512]{2,1,0:T(8,128)(2,1)S(1)}, bf16[2,128,512]{2,1,0:T(8,128)(2,1)}, u32[]{:S(2)}) copy-start(bf16[2,128,512]{2,1,0:T(8,128)(2,1)} %get-tuple-element.133) | copy-start | bytes 786436
  181.6 24.2 %collective-permute-start.20 = (bf16[2,128,768]{2,1,0:T(8,128)(2,1)S(1)}, bf16[2,128,768]{2,1,0:T(8,128)(2,1)S(1)}, u32[]{:S(2)}, u32[]{:S(2)}) collective-permute-start(bf16[2,128,768]{2,1,0:T(8,128)(2,1)S(1)} %constant_dynamic-update-slice_fusion), channel_id=1, source_target_pairs={{0,16},{1,17},{2,18},{3,19},{4,20},{5,21},{6,22},{7,23},{8,24},{9,... | collective-permute-start | bytes 1179656 | tf_op jit(solution)/shard_map/ppermute | solution.py:769
  192.3 19.6 %copy-start.13 = (bf16[512,512]{1,0:T(8,128)(2,1)}, bf16[512,512]{1,0:T(8,128)(2,1)S(1)}, u32[]{:S(2)}) copy-start(bf16[512,512]{1,0:T(8,128)(2,1)S(1)} %collective-permute-done.18.r1_ref) | copy-start | bytes 1572868
  200.1 8.6 %collective-permute-start.21 = (bf16[2,128,512]{2,1,0:T(8,128)(2,1)}, bf16[2,128,512]{2,1,0:T(8,128)(2,1)S(1)}, u32[]{:S(2)}, u32[]{:S(2)}) collective-permute-start(bf16[2,128,512]{2,1,0:T(8,128)(2,1)} %get-tuple-element.141), channel_id=1, source_target_pairs={{0,2},{1,3},{2,0},{3,1},{4,6},{5,7},{6,4},{7,5},{8,10},{9,11},{10,... | collective-permute-start | bytes 786440 | tf_op jit(solution)/shard_map/ppermute | solution.py:763
  205.8 24.5 %copy-start.10 = (bf16[2,256,768]{2,1,0:T(8,128)(2,1)}, bf16[2,256,768]{2,1,0:T(8,128)(2,1)S(1)}, u32[]{:S(2)}) copy-start(bf16[2,256,768]{2,1,0:T(8,128)(2,1)S(1)} %constant_dynamic-update-slice_fusion.2.a_ref) | copy-start | bytes 2359300
  208.7 57.1 %copy-start.15 = (f32[8,512]{1,0:T(8,128)S(1)}, f32[8,512]{1,0:T(8,128)}, u32[]{:S(2)}) copy-start(f32[8,512]{1,0:T(8,128)} %get-tuple-element.157) | copy-start | bytes 49156
  208.7 19.5 %collective-permute-start.22 = (bf16[2,128,768]{2,1,0:T(8,128)(2,1)S(1)}, bf16[2,128,768]{2,1,0:T(8,128)(2,1)S(1)}, u32[]{:S(2)}, u32[]{:S(2)}) collective-permute-start(bf16[2,128,768]{2,1,0:T(8,128)(2,1)S(1)} %constant_dynamic-update-slice_fusion.4), channel_id=1, source_target_pairs={{0,16},{1,17},{2,18},{3,19},{4,20},{5,21},{6,22},{7,23},{8,24},{9,... | collective-permute-start | bytes 1179656 | tf_op jit(solution)/shard_map/ppermute | solution.py:769
  208.8 42.8 %collective-permute-start.27 = (bf16[2048,512]{1,0:T(8,128)(2,1)}, bf16[2048,512]{1,0:T(8,128)(2,1)S(1)}, u32[]{:S(2)}, u32[]{:S(2)}) collective-permute-start(bf16[2048,512]{1,0:T(8,128)(2,1)} %shard_map.196), channel_id=1, source_target_pairs={{0,1},{1,0},{2,3},{3,2},{4,5},{5,4},{6,7},{7,6},{8,9},{9,8},{10,11... | collective-permute-start | bytes 6291464 | tf_op jit(solution)/shard_map/ppermute | solution.py:763
  209.5 40.0 %collective-permute-start.28 = (bf16[1536,512]{1,0:T(8,128)(2,1)}, bf16[1536,512]{1,0:T(8,128)(2,1)}, u32[]{:S(2)}, u32[]{:S(2)}) collective-permute-start(bf16[1536,512]{1,0:T(8,128)(2,1)} %add_convert_fusion), channel_id=1, source_target_pairs={{0,2},{1,3},{2,0},{3,1},{4,6},{5,7},{6,4},{7,5},{8,10},{9,11},{10,... | collective-permute-start | bytes 4718600 | tf_op jit(solution)/shard_map/ppermute | solution.py:763
  209.8 20.6 %collective-permute-start.23 = (bf16[2,256,768]{2,1,0:T(8,128)(2,1)S(1)}, bf16[2,256,768]{2,1,0:T(8,128)(2,1)}, u32[]{:S(2)}, u32[]{:S(2)}) collective-permute-start(bf16[2,256,768]{2,1,0:T(8,128)(2,1)S(1)} %constant_dynamic-update-slice_fusion.2.a_ref), channel_id=1, source_target_pairs={{0,8},{1,5},{2,10},{3,7},{4,12},{5,1},{6,14},{7,3},{8,0},{9,13},{1... | collective-permute-start | bytes 2359304 | tf_op jit(solution)/shard_map/ppermute | solution.py:769
  228.3 18.0 %copy-start.5 = (bf16[2,256,768]{2,1,0:T(8,128)(2,1)}, bf16[2,256,768]{2,1,0:T(8,128)(2,1)S(1)}, u32[]{:S(2)}) copy-start(bf16[2,256,768]{2,1,0:T(8,128)(2,1)S(1)} %pad_maximum_fusion.a_ref) | copy-start | bytes 2359300
  228.3 18.0 %collective-permute-start.24 = (bf16[2,256,768]{2,1,0:T(8,128)(2,1)S(1)}, bf16[2,256,768]{2,1,0:T(8,128)(2,1)}, u32[]{:S(2)}, u32[]{:S(2)}) collective-permute-start(bf16[2,256,768]{2,1,0:T(8,128)(2,1)S(1)} %pad_maximum_fusion.a_ref), channel_id=1, source_target_pairs={{0,8},{1,5},{2,10},{3,7},{4,12},{5,1},{6,14},{7,3},{8,0},{9,13},{1... | collective-permute-start | bytes 2359304 | tf_op jit(solution)/shard_map/ppermute | solution.py:769
  233.6 23.8 %collective-permute-start.26 = (bf16[512,768]{1,0:T(8,128)(2,1)}, bf16[512,768]{1,0:T(8,128)(2,1)S(1)}, u32[]{:S(2)}, u32[]{:S(2)}) collective-permute-start(bf16[512,768]{1,0:T(8,128)(2,1)} %get-tuple-element.143.refs_0_), channel_id=1, source_target_pairs={{0,4},{1,9},{2,6},{3,11},{4,0},{5,13},{6,2},{7,15},{8,12},{9,1},{1... | collective-permute-start | bytes 2359304 | tf_op jit(solution)/shard_map/ppermute | solution.py:769
  235.6 20.8 %collective-permute-start.32 = (bf16[512,768]{1,0:T(8,128)(2,1)}, bf16[512,768]{1,0:T(8,128)(2,1)}, u32[]{:S(2)}, u32[]{:S(2)}) collective-permute-start(bf16[512,768]{1,0:T(8,128)(2,1)} %get-tuple-element.154), channel_id=1, source_target_pairs={{0,4},{1,9},{2,6},{3,11},{4,0},{5,13},{6,2},{7,15},{8,12},{9,1},{1... | collective-permute-start | bytes 2359304 | tf_op jit(solution)/shard_map/ppermute | solution.py:769
  249.5 15.3 %collective-permute-start.35 = (bf16[512,768]{1,0:T(8,128)(2,1)}, bf16[512,768]{1,0:T(8,128)(2,1)}, u32[]{:S(2)}, u32[]{:S(2)}) collective-permute-start(bf16[512,768]{1,0:T(8,128)(2,1)} %get-tuple-element.155), channel_id=1, source_target_pairs={{0,4},{1,9},{2,6},{3,11},{4,0},{5,13},{6,2},{7,15},{8,12},{9,1},{1... | collective-permute-start | bytes 2359304 | tf_op jit(solution)/shard_map/ppermute | solution.py:769
  249.5 26.4 %collective-permute-start.25 = (bf16[512,768]{1,0:T(8,128)(2,1)}, bf16[512,768]{1,0:T(8,128)(2,1)S(1)}, u32[]{:S(2)}, u32[]{:S(2)}) collective-permute-start(bf16[512,768]{1,0:T(8,128)(2,1)} %get-tuple-element.145.refs_4_), channel_id=1, source_target_pairs={{0,4},{1,9},{2,6},{3,11},{4,0},{5,13},{6,2},{7,15},{8,12},{9,1},{1... | collective-permute-start | bytes 2359304 | tf_op jit(solution)/shard_map/ppermute | solution.py:769
  251.5 14.2 %copy-start.9 = (bf16[2048,512]{1,0:T(8,128)(2,1)}, bf16[2048,512]{1,0:T(8,128)(2,1)S(1)}, u32[]{:S(2)}) copy-start(bf16[2048,512]{1,0:T(8,128)(2,1)S(1)} %collective-permute-done.27.rc_ref) | copy-start | bytes 6291460
  251.5 45.2 %collective-permute-start.31 = (bf16[512,768]{1,0:T(8,128)(2,1)}, bf16[512,768]{1,0:T(8,128)(2,1)}, u32[]{:S(2)}, u32[]{:S(2)}) collective-permute-start(bf16[512,768]{1,0:T(8,128)(2,1)} %get-tuple-element.154), channel_id=1, source_target_pairs={{0,1},{1,0},{2,3},{3,2},{4,5},{5,4},{6,7},{7,6},{8,9},{9,8},{10,11... | collective-permute-start | bytes 2359304 | tf_op jit(solution)/shard_map/ppermute | solution.py:763
  256.4 40.4 %collective-permute-start.34 = (bf16[512,768]{1,0:T(8,128)(2,1)}, bf16[512,768]{1,0:T(8,128)(2,1)}, u32[]{:S(2)}, u32[]{:S(2)}) collective-permute-start(bf16[512,768]{1,0:T(8,128)(2,1)} %get-tuple-element.155), channel_id=1, source_target_pairs={{0,1},{1,0},{2,3},{3,2},{4,5},{5,4},{6,7},{7,6},{8,9},{9,8},{10,11... | collective-permute-start | bytes 2359304 | tf_op jit(solution)/shard_map/ppermute | solution.py:763
  257.4 17.7 %copy-start.11 = (bf16[512,768]{1,0:T(8,128)(2,1)}, bf16[512,768]{1,0:T(8,128)(2,1)S(1)}, u32[]{:S(2)}) copy-start(bf16[512,768]{1,0:T(8,128)(2,1)S(1)} %collective-permute-done.26.refs_1_) | copy-start | bytes 2359300
  257.4 39.3 %collective-permute-start.33 = (bf16[512,768]{1,0:T(8,128)(2,1)}, bf16[512,768]{1,0:T(8,128)(2,1)}, u32[]{:S(2)}, u32[]{:S(2)}) collective-permute-start(bf16[512,768]{1,0:T(8,128)(2,1)} %collective-permute-done.32), channel_id=1, source_target_pairs={{0,1},{1,0},{2,3},{3,2},{4,5},{5,4},{6,7},{7,6},{8,9},{9,8},{10,11... | collective-permute-start | bytes 2359304 | tf_op jit(solution)/shard_map/ppermute | solution.py:763
  264.8 32.0 %collective-permute-start.36 = (bf16[512,768]{1,0:T(8,128)(2,1)}, bf16[512,768]{1,0:T(8,128)(2,1)}, u32[]{:S(2)}, u32[]{:S(2)}) collective-permute-start(bf16[512,768]{1,0:T(8,128)(2,1)} %collective-permute-done.35), channel_id=1, source_target_pairs={{0,1},{1,0},{2,3},{3,2},{4,5},{5,4},{6,7},{7,6},{8,9},{9,8},{10,11... | collective-permute-start | bytes 2359304 | tf_op jit(solution)/shard_map/ppermute | solution.py:763
  275.9 17.6 %copy-start.12 = (bf16[512,768]{1,0:T(8,128)(2,1)}, bf16[512,768]{1,0:T(8,128)(2,1)S(1)}, u32[]{:S(2)}) copy-start(bf16[512,768]{1,0:T(8,128)(2,1)S(1)} %collective-permute-done.25.refs_5_) | copy-start | bytes 2359300
  275.9 1.5 collective-permute-start.29
  277.4 3.7 %collective-permute-start.37 = (f32[6,512]{1,0:T(8,128)S(1)}, f32[6,512]{1,0:T(8,128)S(1)}, u32[]{:S(2)}, u32[]{:S(2)}) collective-permute-start(f32[6,512]{1,0:T(8,128)S(1)} %pad_maximum_fusion.1), channel_id=1, source_target_pairs={{0,4},{4,0},{8,12},{12,8},{16,20},{20,16},{24,28},{28,24},{1,5},{5... | collective-permute-start | bytes 36872 | tf_op jit(solution)/shard_map/ppermute | solution.py:865
  281.1 4.3 %collective-permute-start.30 = (f32[8,2048]{1,0:T(8,128)S(1)}, f32[8,2048]{1,0:T(8,128)S(1)}, u32[]{:S(2)}, u32[]{:S(2)}) collective-permute-start(f32[8,2048]{1,0:T(8,128)S(1)} %add.125), channel_id=1, source_target_pairs={{0,2},{1,3},{2,0},{3,1},{4,6},{5,7},{6,4},{7,5},{8,10},{9,11},{10,... | collective-permute-start | bytes 196616 | tf_op jit(solution)/shard_map/ppermute | solution.py:763
  285.4 8.1 %collective-permute-start.38 = (f32[6,512]{1,0:T(8,128)S(1)}, f32[6,512]{1,0:T(8,128)S(1)}, u32[]{:S(2)}, u32[]{:S(2)}) collective-permute-start(f32[6,512]{1,0:T(8,128)S(1)} %add.127), channel_id=1, source_target_pairs={{0,8},{4,12},{8,0},{12,4},{16,24},{20,28},{24,16},{28,20},{1,9},{5... | collective-permute-start | bytes 36872 | tf_op jit(solution)/shard_map/ppermute | solution.py:865
  293.5 11.8 %collective-permute-start.39 = (f32[6,512]{1,0:T(8,128)S(1)}, f32[6,512]{1,0:T(8,128)S(1)}, u32[]{:S(2)}, u32[]{:S(2)}) collective-permute-start(f32[6,512]{1,0:T(8,128)S(1)} %add.128), channel_id=1, source_target_pairs={{0,16},{4,20},{8,24},{12,28},{16,0},{20,4},{24,8},{28,12},{1,17},{... | collective-permute-start | bytes 36872 | tf_op jit(solution)/shard_map/ppermute | solution.py:865
  (15 other events, 45.8 us)
